TPU v7x, 256 devices: a whole 4x4x8 slice. The times are simulated.
256 devices in a mesh: patch: 32 (over z, x), frame: 8 (over y, core).
Axes of the slice: x: 4, y: 4, z: 8, core: 2. Of those that a mesh axis runs over, the one named last changes fastest.
Arguments:
- screens: float32 [2, 2048, 4096], P(None, 'patch'), may hold values from -6 to 6
- row_offsets: int32 [8, 2, 32], replicated, may hold values from 0 to 1792
- col_offsets: int32 [8, 2, 32], replicated, may hold values from 0 to 3840
- amplitude: float32 [256, 256], replicated, may hold values from 0.5 to 1.5
- object_strip: float32 [384, 8192], P(None, 'patch'), may hold values from 0.5 to 1.5
- observed: float32 [8, 256, 8192], P('frame', None, 'patch'), may hold values from 0.5 to 1.5
Outputs:
- screen_grad: float32 [2, 2048, 4096], P(None, 'patch', 'frame')
All inputs are finite; a program needn't handle non-finite values.
Results may differ from a plain program's by a relative error of at most 0.0003.
Values sent between devices are 32-bit elements; how exact they have to be, the bound alone decides.
No kernel may reach another device: no remote copies, remote signals or barrier semaphores. Data moves between devices by JAX's collectives and lax.ppermute only.
A program may use at most 128 MiB of HBM per device.

v0:
```python
import math

import jax
import jax.numpy as jnp
from jax import lax
from jax.sharding import PartitionSpec as P

CORE = 256
HALO = 64


def padded(cells, sides, width):
    for axis, dim in sides:
        count = lax.axis_size(axis)
        ends = count - 1
        head = lax.slice_in_dim(cells, 0, width, axis=dim)
        tail = lax.slice_in_dim(cells, cells.shape[dim] - width, cells.shape[dim], axis=dim)
        cells = jnp.concatenate(
            [
                lax.ppermute(tail, axis, [(i, (i + 1) % count) for i in range(ends)]),
                cells,
                lax.ppermute(head, axis, [((i + 1) % count, i) for i in range(ends)]),
            ],
            axis=dim,
        )
    return cells


def matmul_high(left_op, right_op):
    return jnp.dot(
        left_op, right_op, precision=lax.Precision.HIGHEST, preferred_element_type=jnp.float32
    )


def complex_product(left_re, left_im, right_re, right_im):
    return (
        matmul_high(left_re, right_re) - matmul_high(left_im, right_im),
        matmul_high(left_re, right_im) + matmul_high(left_im, right_re),
    )


def real_left(left_re, left_im, right_op):
    return (matmul_high(left_re, right_op), matmul_high(left_im, right_op))


def phase_gradient(phases, window, target, amplitude, cosine, sine_neg):
    extent = window.shape[0]
    win_size = phases.shape[0]
    core_size = target.shape[0]
    margin = (extent - core_size) // 2
    core_rows = slice(margin, margin + core_size)
    inverse_total = 1.0 / (extent * extent * jnp.sum(amplitude * amplitude))
    pupil_re = amplitude * jnp.cos(phases)
    pupil_im = amplitude * jnp.sin(phases)
    half_re, half_im = complex_product(
        cosine[:, :win_size], sine_neg[:, :win_size], pupil_re, pupil_im
    )
    far_re, far_im = complex_product(half_re, half_im, cosine[:win_size, :], sine_neg[:win_size, :])
    spread = (far_re * far_re + far_im * far_im) * inverse_total

    def spectrum(values):
        part_re, part_im = real_left(cosine, sine_neg, values)
        return complex_product(part_re, part_im, cosine, sine_neg)

    spread_re, spread_im = spectrum(spread)
    object_re, object_im = spectrum(window)
    prod_re = spread_re * object_re - spread_im * object_im
    prod_im = spread_re * object_im + spread_im * object_re
    rows_re, rows_im = complex_product(cosine[core_rows], -sine_neg[core_rows], prod_re, prod_im)
    model_image = (
        matmul_high(rows_re, cosine[:, core_rows]) + matmul_high(rows_im, sine_neg[:, core_rows])
    ) / (extent * extent)
    residual = (model_image - target) * (win_size * extent / core_size)
    grad_re, grad_im = real_left(cosine[:, core_rows], sine_neg[:, core_rows], residual)
    spec_re, spec_im = complex_product(
        grad_re, grad_im, cosine[core_rows, :], sine_neg[core_rows, :]
    )
    corr_re = spec_re * object_re + spec_im * object_im
    corr_im = spec_im * object_re - spec_re * object_im
    wave_re, wave_im = complex_product(cosine, -sine_neg, corr_re, corr_im)
    spread_grad = (matmul_high(wave_re, cosine) + matmul_high(wave_im, sine_neg)) / (
        extent * extent
    )
    back_re, back_im = complex_product(
        cosine[:win_size, :], -sine_neg[:win_size, :], far_re * spread_grad, far_im * spread_grad
    )
    out_re, out_im = complex_product(
        back_re, back_im, cosine[:, :win_size], -sine_neg[:, :win_size]
    )
    return 2.0 * inverse_total * (pupil_re * out_im - pupil_im * out_re)


def frame_total(values):
    return lax.psum_scatter(values, "frame", scatter_dimension=2, tiled=True)


def body(screens, row_offsets, col_offsets, amplitude, object_strip, observed):
    patch_count = lax.axis_size("patch")
    place = lax.axis_index("patch")
    frame_id = lax.axis_index("frame")
    layer_count, tile_rows, screen_cols = screens.shape
    win_size = amplitude.shape[0]
    extent = object_strip.shape[0]
    per_device = observed.shape[2] // CORE
    angle_index = jnp.arange(extent, dtype=jnp.int32)
    angles = (angle_index[:, None] * angle_index[None, :] % extent).astype(jnp.float32) * (
        2.0 * math.pi / extent
    )
    cosine = jnp.cos(angles)
    sine_neg = -jnp.sin(angles)
    patch_ids = (
        jnp.arange(patch_count, dtype=jnp.int32)[None, :] * per_device
        + jnp.arange(per_device, dtype=jnp.int32)[:, None]
    )
    rows_by = jnp.moveaxis(row_offsets[frame_id][:, patch_ids], 1, 0)
    cols_by = jnp.moveaxis(col_offsets[frame_id][:, patch_ids], 1, 0)
    my_rows = rows_by[:, :, place]
    extended = padded(object_strip, (("patch", 1),), HALO)
    windows = jnp.stack([extended])
    targets = observed[0].reshape(CORE, per_device, CORE).transpose(1, 0, 2)

    def cut_band(sheet, column):
        return lax.dynamic_slice_in_dim(sheet, column, win_size, 1)

    bands = jax.vmap(
        lambda member_cols: jax.vmap(
            lambda sheet, layer_cols: jax.vmap(lambda column: cut_band(sheet, column))(layer_cols)
        )(screens, member_cols)
    )(cols_by)
    received = lax.all_to_all(bands, "patch", split_axis=2, concat_axis=2, tiled=True)
    columns = received.reshape(per_device, layer_count, patch_count * tile_rows, win_size)

    def pick_rows(column_band, top_row):
        return lax.dynamic_slice_in_dim(column_band, top_row, win_size, 0)

    phases = jax.vmap(jax.vmap(pick_rows))(columns, my_rows).sum(axis=1)
    gradients = lax.map(
        lambda packed: phase_gradient(packed[0], packed[1], packed[2], amplitude, cosine, sine_neg),
        (phases, windows, targets),
    )

    def place_band(gradient, top_row):
        return lax.dynamic_update_slice_in_dim(
            jnp.zeros((patch_count * tile_rows, win_size), jnp.float32), gradient, top_row, 0
        )

    outgoing = jax.vmap(
        lambda gradient, member_rows: jax.vmap(lambda top_row: place_band(gradient, top_row))(
            member_rows
        )
    )(gradients, my_rows)
    returned = lax.all_to_all(
        outgoing.reshape(per_device, layer_count, patch_count, tile_rows, win_size),
        "patch",
        split_axis=2,
        concat_axis=2,
        tiled=True,
    )

    def add_band(source, running):
        for layer_id in range(layer_count):
            corner = (jnp.int32(layer_id), jnp.int32(0), cols_by[0, layer_id, source])
            current = lax.dynamic_slice(running, corner, (1, tile_rows, win_size))
            running = lax.dynamic_update_slice(
                running, current + returned[0, layer_id, source][None], corner
            )
        return running

    summed = lax.fori_loop(0, patch_count, add_band, jnp.zeros_like(screens))
    result = frame_total(summed)
    return result


def solution(mesh):
    in_specs = (P(None, "patch", None), P(), P(), P(), P(None, "patch"), P("frame", None, "patch"))
    out_specs = P(None, "patch", "frame")
    return jax.shard_map(body, mesh=mesh, in_specs=in_specs, out_specs=out_specs, check_vma=False)
```

profile of v0, /device:TPU:64, one launch (start us, length us, event | category | flops | bytes accessed | tf_op | source)
XLA Modules:
  0.0 685.6 jit_solution(5704596793613604520)
XLA Ops:
  8.1 6.2 copy.38
  14.3 17.7 %gather_fusion.2 = f32[64,64,256]{1,0,2:T(8,128)} fusion(f32[2,64,4096]{1,0,2:T(2,128)} %copy.38, s32[64]{0:T(128)S(1)} %reshape.144), kind=kCustom, calls=%fused_computation.2 | custom fusion | bytes 8389376 | tf_op jit(solution)/shard_map/vmap(vmap(vmap()))/gather | solution.py:123
  32.1 7.7 %copy.39 = f32[1,2,32,64,256]{4,3,1,0,2:T(8,128)} copy(f32[1,2,32,64,256]{3,2,1,4,0:T(8,128)} %bitcast.94) | data formatting | bytes 8388608 | tf_op jit(solution)/shard_map/vmap(vmap(vmap()))/gather | solution.py:123
  39.8 10.9 %all-to-all-start = ((f32[1,2,32,64,256]{4,3,1,0,2:T(8,128)}), f32[1,2,32,64,256]{4,3,1,0,2:T(8,128)}, u32[]{:S(2)}, u32[]{:S(2)}) async-start(f32[1,2,32,64,256]{4,3,1,0,2:T(8,128)} %copy.39), calls=%async_computation | async-start | bytes 8388608 | tf_op jit(solution)/shard_map/all_to_all | solution.py:130
  50.8 3.4 collective-permute-start
  54.2 4.8 collective-permute-start.1
  61.4 2.2 fusion.13
  63.7 2.3 fusion.16
  66.1 81.8 %collective-permute-done = f32[384,64]{1,0:T(8,128)S(1)} collective-permute-done((f32[384,64]{1,0:T(8,128)S(1)}, f32[384,64]{1,0:T(8,128)S(1)}, u32[]{:S(2)}, u32[]{:S(2)}) %collective-permute-start) | collective-permute-done | bytes 98336 | tf_op jit(solution)/shard_map/ppermute | solution.py:20
  148.0 3.7 fusion.68
  151.6 4.1 fusion.67
  155.7 3.5 fusion.91
  159.2 3.5 fusion.83
  162.7 3.5 convolution_add_fusion.2
  166.2 3.7 convolution_subtract_fusion.1
  169.9 7.5 %copy.40 = f32[1,2,32,64,256]{4,1,3,2,0:T(2,128)} copy(f32[1,2,32,64,256]{4,3,1,0,2:T(8,128)} %all-to-all-done) | data formatting | bytes 8388608 | tf_op jit(solution)/shard_map/all_to_all | solution.py:130
  177.4 2.9 gather_fusion.3
  182.3 1.3 fusion.56
  183.7 1.3 convolution_subtract_fusion.5
  186.9 1.3 convolution_add_fusion.6
  189.8 3.6 fusion.98
  193.4 3.6 fusion.88
  197.0 3.9 fusion.86
  200.9 3.5 fusion.93
  204.5 3.5 convolution_subtract_fusion.2
  208.0 3.7 multiply_add_fusion.1
  221.1 4.1 fusion.75
  225.3 4.1 fusion.79
  229.4 4.1 convolution_add_fusion.1
  233.5 4.3 convolution_subtract_fusion
  237.8 3.5 fusion.77
  241.3 3.5 fusion
  251.3 1.4 fusion.5
  252.7 2.2 broadcast_in_dim.11
  255.0 19.7 %while.19 = (s32[]{:T(128)}, f32[1,2,2048,256]{3,2,1,0:T(8,128)}, s32[2,4]{1,0:T(2,128)S(1)}, f32[2,256,256]{2,1,0:T(8,128)S(1)}, s32[]{:T(128)}, /*index=5*/s32[4]{0:T(128)S(1)}, s32[]{:T(128)}) while((s32[]{:T(128)}, f32[1,2,2048,256]{3,2,1,0:T(8,128)}, s32[2,4]{1,0:T(2,128)S(1)}, f32[2,256,256]{2,1,0:T(8,128)S(1)}, s32[]{:T(128)}, ...), condition=%wide.while_cond, body=%wide.while_body.sunk | while | flops 65565 | bytes 1310915 | solution.py:143
  255.6 3.2 and_reduce_fusion.2
  258.8 2.9 bitcast_select_fusion.2
  261.7 3.1 dynamic-update-slice.3
  265.5 3.2 and_reduce_fusion.2
  268.7 2.9 bitcast_select_fusion.2
  271.6 3.1 dynamic-update-slice.3
  274.7 4.6 copy.42
  279.3 7.6 %all-to-all-start.1 = ((f32[1,2,32,64,256]{4,3,1,0,2:T(8,128)}), f32[1,2,32,64,256]{4,3,1,0,2:T(8,128)}, u32[]{:S(2)}, u32[]{:S(2)}) async-start(f32[1,2,32,64,256]{4,3,1,0,2:T(8,128)} %copy.42), calls=%async_computation.1 | async-start | bytes 8388608 | tf_op jit(solution)/shard_map/all_to_all | solution.py:152
  287.0 93.9 %all-to-all-done.1 = f32[1,2,32,64,256]{4,3,1,0,2:T(8,128)} async-done(((f32[1,2,32,64,256]{4,3,1,0,2:T(8,128)}), f32[1,2,32,64,256]{4,3,1,0,2:T(8,128)}, u32[]{:S(2)}, u32[]{:S(2)}) %all-to-all-start.1) | async-done | bytes 4194336 | tf_op jit(solution)/shard_map/all_to_all | solution.py:152
  380.9 4.6 copy.43
  385.7 255.1 %while.18 = (s32[]{:T(128)}, f32[2,64,4096]{2,1,0:T(8,128)S(1)}, s32[1,2,32]{2,1,0:T(2,128)S(1)}, f32[1,2,32,64,256]{4,3,2,1,0:T(8,128)}, s32[]{:T(128)}, /*index=5*/s32[]{:T(128)}, s32[]{:T(128)}) while((s32[]{:T(128)}, f32[2,64,4096]{2,1,0:T(8,128)S(1)}, s32[1,2,32]{2,1,0:T(2,128)S(1)}, f32[1,2,32,64,256]{4,3,2,1,0:T(8,128)}, s32[]{:T(128)}, ...), condition=%wide.region_4.5_spmd, body=%wide.region_3.4_spmd.sunk | while | flops 32776 | bytes 655549 | solution.py:169
  640.8 1.3 copy-done.1
  642.1 36.2 %reduce-scatter.2.cloned.1.call-done = f32[2,64,512]{2,1,0:T(8,128)} async-done(((f32[2,64,4096]{2,1,0:T(8,128)}), f32[2,64,512]{2,1,0:T(8,128)}) %reduce-scatter.2.cloned.1.call-update) | async-done | bytes 262160 | tf_op jit(solution)/shard_map/reduce_scatter | solution.py:94
  (229 shorter events, 159.8 us)
Async XLA Ops:
  39.8 10.9 %copy-start.2 = (f32[384,256]{1,0:T(8,128)S(1)}, f32[384,256]{1,0:T(8,128)}, u32[]{:S(2)}) copy-start(f32[384,256]{1,0:T(8,128)} %param.12) | copy-start | bytes 1179652
  39.8 19.9 %copy-start.5 = (s32[2]{0:T(128)S(1)}, s32[2]{0:T(128)}, u32[]{:S(2)}) copy-start(s32[2]{0:T(128)} %constant.97.clone.1) | copy-start | bytes 28
  39.8 20.2 %copy-start = (f32[256,256]{1,0:T(8,128)S(1)}, f32[256,256]{1,0:T(8,128)}, u32[]{:S(2)}) copy-start(f32[256,256]{1,0:T(8,128)} %param.11) | copy-start | bytes 786436
  39.8 130.1 %all-to-all-start = ((f32[1,2,32,64,256]{4,3,1,0,2:T(8,128)}), f32[1,2,32,64,256]{4,3,1,0,2:T(8,128)}, u32[]{:S(2)}, u32[]{:S(2)}) async-start(f32[1,2,32,64,256]{4,3,1,0,2:T(8,128)} %copy.39), calls=%async_computation | async-start | bytes 8388608 | tf_op jit(solution)/shard_map/all_to_all | solution.py:130
  50.8 97.1 %collective-permute-start = (f32[384,64]{1,0:T(8,128)S(1)}, f32[384,64]{1,0:T(8,128)S(1)}, u32[]{:S(2)}, u32[]{:S(2)}) collective-permute-start(f32[384,64]{1,0:T(8,128)S(1)} %get-tuple-element.151), channel_id=1, source_target_pairs={{0,8},{8,16},{16,24},{24,32},{32,40},{40,48},{48,56},{56,64},{64,7... | collective-permute-start | bytes 294920 | tf_op jit(solution)/shard_map/ppermute | solution.py:20
  54.2 93.7 %collective-permute-start.1 = (f32[384,64]{1,0:T(8,128)S(1)}, f32[384,64]{1,0:T(8,128)S(1)}, u32[]{:S(2)}, u32[]{:S(2)}) collective-permute-start(f32[384,64]{1,0:T(8,128)S(1)} %get-tuple-element.152), channel_id=1, source_target_pairs={{8,0},{16,8},{24,16},{32,24},{40,32},{48,40},{56,48},{64,56},{72,6... | collective-permute-start | bytes 294920 | tf_op jit(solution)/shard_map/ppermute | solution.py:22
  211.7 4.4 copy-start.3
  250.0 5.0 copy-start.4
  279.3 101.6 %all-to-all-start.1 = ((f32[1,2,32,64,256]{4,3,1,0,2:T(8,128)}), f32[1,2,32,64,256]{4,3,1,0,2:T(8,128)}, u32[]{:S(2)}, u32[]{:S(2)}) async-start(f32[1,2,32,64,256]{4,3,1,0,2:T(8,128)} %copy.42), calls=%async_computation.1 | async-start | bytes 8388608 | tf_op jit(solution)/shard_map/all_to_all | solution.py:152
  286.9 391.5 %reduce-scatter.2.cloned.1.call-start = ((), (), s32[]{:S(2)}) async-start(), calls=%async_computation.3 | async-start | bytes 2359296 | tf_op jit(solution)/shard_map/reduce_scatter | solution.py:94
  640.8 1.3 copy-start.1
Sparse Core Ops, SparseCore 0:
  642.2 36.0 reduce-scatter.1
where the time goes:
time: 697 us; the launch traced here: 686 us
  waiting for transfers between devices  212 us (30%)
  local copies, waits for them, and re-layouts  139 us (20%)
  loops' own time  122 us (18%)
  matrix products  93.3 us (13%)
  other arithmetic  78 us (11%)
  starting transfers between devices  26.7 us (4%)
  between operations  15 us (2%)
    another operation x1, loops' own time, body(): summed = lax.fori_loop(0, patch_count, add_band, jnp.zeros_like(screens))  122 us
    all_to_all x1, waiting for transfers between devices, body(): lax.all_to_all(outgoing.reshape(per_device, layer_count, patch_count, til...  93.9 us
    dot_general x46, matrix products, matmul_high(): jnp.dot(left_op, right_op, precision=lax.Precision.HIGHEST, preferred_ele...  93.3 us
    ppermute x1, waiting for transfers between devices, padded(): lax.ppermute(tail, axis, [(i, (i + 1) % count) for i in range(ends)])  81.8 us
    add x64, other arithmetic, add_band(): current + returned[0, layer_id, source][None]  59.7 us
    dynamic_update_slice x64, local copies, waits for them, and re-layouts, add_band(): lax.dynamic_update_slice(running, current + returned[0, layer_id, source]...  52.9 us
    reduce_scatter x1, waiting for transfers between devices, frame_total(): return lax.psum_scatter(values, 'frame', scatter_dimension=2, tiled=True)  36.2 us
    gather x3, local copies, waits for them, and re-layouts, cut_band(): return lax.dynamic_slice_in_dim(sheet, column, win_size, 1)  25.5 us
  transfers between devices with their start and end apart: 5, of which 3 were waited for; matrix products, arithmetic and copies ran while one was open for 4% of the time, Pallas kernels for 0%

commit v1 on v0

v1 whole, which is shorter than its diff:
```python
import functools
import math

import jax
import jax.numpy as jnp
import numpy as np
from jax import lax
from jax.experimental import pallas as pl
from jax.experimental.pallas import tpu as pltpu
from jax.sharding import Mesh, PartitionSpec as P

CORE = 256
HALO = 64
SPAN = 384
HALF = 256
SLAB = ("x", "y", "core")
FRAME = ("y", "core")


def split_constants():
    index = np.arange(SPAN)
    angles = (np.outer(index, index) % SPAN) * (2.0 * np.pi / SPAN)
    cosine, sine = np.cos(angles), np.sin(angles)
    parts = []
    for values in (cosine, sine):
        high = values.astype(jnp.bfloat16)
        low = (values - high.astype(np.float64)).astype(jnp.bfloat16)
        parts += [high, low]
    return parts


def split(values):
    high = values.astype(jnp.bfloat16)
    low = (values - high.astype(jnp.float32)).astype(jnp.bfloat16)
    return high, low


def dot(left, right):
    return jnp.dot(left, right, preferred_element_type=jnp.float32)


def product(left, right):
    return dot(left[0], right[0]) + (dot(left[0], right[1]) + dot(left[1], right[0]))


class Pair:
    def __init__(self, high, low):
        self.refs = (high, low)

    def __getitem__(self, index):
        return tuple(ref[index] for ref in self.refs)

    def put(self, index, values):
        for ref, part in zip(self.refs, split(values)):
            ref[index] = part


def sine_cosine(angle):
    turns = jnp.round(angle * (2.0 / math.pi))
    rest = angle - turns * 1.5703125
    rest = rest - turns * 4.837512969970703125e-4
    rest = rest - turns * 7.549789948768648e-8
    square = rest * rest
    sine = rest + rest * square * (
        -1.6666654611e-1 + square * (8.3321608736e-3 + square * -1.9515295891e-4)
    )
    cosine = 1.0 - 0.5 * square + square * square * (
        4.166664568298827e-2 + square * (-1.388731625493765e-3 + square * 2.443315711809948e-5)
    )
    quarter = turns.astype(jnp.int32)
    odd = (quarter & 1) == 1
    sine, cosine = jnp.where(odd, cosine, sine), jnp.where(odd, sine, cosine)
    sine = jnp.where((quarter & 2) == 2, -sine, sine)
    cosine = jnp.where(((quarter + 1) & 2) == 2, -cosine, cosine)
    return sine, cosine


LOW = slice(0, CORE)
HIGH = slice(SPAN, SPAN + CORE)
FULL = slice(0, SPAN)
REST = slice(SPAN, 2 * SPAN)
ALL = slice(None)


def object_kernel(ch, cl, sh, sl, window, forward_h, forward_l, inverse_h, inverse_l, spec_re, spec_im):
    for target_f, target_i, cos_ref, sin_ref in (
        (forward_h, inverse_h, ch, sh),
        (forward_l, inverse_l, cl, sl),
    ):
        cosine, sine = cos_ref[...], sin_ref[...]
        target_f[FULL, FULL] = cosine
        target_f[FULL, REST] = sine
        target_f[REST, FULL] = -sine
        target_f[REST, REST] = cosine
        target_i[FULL, FULL] = cosine
        target_i[FULL, REST] = -sine
        target_i[REST, FULL] = sine
        target_i[REST, REST] = cosine
    forward, inverse = Pair(forward_h, forward_l), Pair(inverse_h, inverse_l)
    seen = split(window[...])
    part_re = split(product(seen, inverse[FULL, LOW]))
    part_im = split(product(seen, inverse[FULL, HIGH]))
    out = product(forward[ALL, FULL], part_re) + product(forward[ALL, REST], part_im)
    column = lax.broadcasted_iota(jnp.int32, (SPAN, HALF), 1)
    ends = (column == 0) | (column == SPAN // 2)
    weight = jnp.where(ends, 1.0, jnp.where(column < SPAN // 2, 2.0, 0.0)) / (SPAN * SPAN)
    spec_re[...] = out[FULL] * weight
    spec_im[...] = out[REST] * weight


def select_kernel(place, rows, cols, gathered, out):
    slab, first = place[0], place[1]
    row_index = first + lax.broadcasted_iota(jnp.int32, (8, CORE), 0)
    lane = lax.broadcasted_iota(jnp.int32, (8, CORE), 1)

    def one(member, carry):
        patch = slab * 4 + member // 8
        frame = member % 8
        for layer in range(2):
            row = rows[frame, layer, patch]
            col = cols[frame, layer, patch]
            block, residue = row // CORE, row % CORE
            after = jnp.minimum(block + 1, 7)
            strip, turn = col // CORE, col % CORE
            at = pl.ds(pl.multiple_of(strip * CORE, CORE), CORE)
            beside = pl.ds(pl.multiple_of(jnp.minimum(strip + 1, 15) * CORE, CORE), CORE)
            right = lane >= turn
            upper = jnp.where(
                right, gathered[block * 2 + layer, :, at], gathered[block * 2 + layer, :, beside]
            )
            lower = jnp.where(
                right, gathered[after * 2 + layer, :, at], gathered[after * 2 + layer, :, beside]
            )
            out[member, layer] = jnp.where(row_index >= residue, upper, lower)
        return carry

    lax.fori_loop(0, 32, one, 0, unroll=4)


def scatter_kernel(place, rows, cols, values, out):
    slab, first = place[0], place[1]
    row_index = first + lax.broadcasted_iota(jnp.int32, (8, CORE), 0)
    lane = lax.broadcasted_iota(jnp.int32, (8, CORE), 1)
    out[...] = jnp.zeros_like(out)

    def one(member, carry):
        patch = slab * 4 + member // 8
        frame = member % 8
        for layer in range(2):
            row = rows[frame, layer, patch]
            col = cols[frame, layer, patch]
            block, residue = row // CORE, row % CORE
            after = jnp.minimum(block + 1, 7)
            strip, turn = col // CORE, col % CORE
            beside = jnp.minimum(strip + 1, 15)
            value = values[member, layer]
            here = row_index >= residue
            right = lane >= turn
            for where, keep_row in ((block, here), (after, ~here)):
                for place_col, keep_col in ((strip, right), (beside, ~right)):
                    at = pl.ds(pl.multiple_of((place_col % 2) * CORE, CORE), CORE)
                    chunk = place_col // 2
                    out[where, chunk, layer, :, at] = out[where, chunk, layer, :, at] + jnp.where(
                        keep_row & keep_col, value, 0.0
                    )
        return carry

    lax.fori_loop(0, 32, one, 0, unroll=2)


def gradient_kernel(
    turns, received, amp_ref, observed, forward_h, forward_l, inverse_h, inverse_l, spec_re, spec_im,
    out, pupil_re, pupil_im, far_re, far_im, mix_h, mix_l, wide_h, wide_l,
):
    forward, inverse = Pair(forward_h, forward_l), Pair(inverse_h, inverse_l)
    mix, wide = Pair(mix_h, mix_l), Pair(wide_h, wide_l)
    phases = None
    for layer in range(2):
        sheet = received[:, layer].reshape(CORE, CORE)
        sheet = pltpu.roll(sheet, (CORE - turns[layer, 0]) % CORE, 0)
        sheet = pltpu.roll(sheet, (CORE - turns[layer, 1]) % CORE, 1)
        phases = sheet if phases is None else phases + sheet
    amplitude = amp_ref[...]
    inverse_total = 1.0 / (SPAN * SPAN * jnp.sum(amplitude * amplitude))
    sine, cosine = sine_cosine(phases)
    pupil_re[...] = amplitude * cosine
    pupil_im[...] = amplitude * sine
    half = product(forward[ALL, LOW], split(pupil_re[...])) + product(
        forward[ALL, HIGH], split(pupil_im[...])
    )
    half_re, half_im = split(half[FULL]), split(half[REST])
    far_re[...] = product(half_re, inverse[LOW, FULL]) + product(half_im, inverse[HIGH, FULL])
    far_im[...] = product(half_re, inverse[LOW, REST]) + product(half_im, inverse[HIGH, REST])
    spread = split((far_re[...] * far_re[...] + far_im[...] * far_im[...]) * inverse_total)
    mix.put((FULL, ALL), product(spread, inverse[FULL, LOW]))
    mix.put((REST, ALL), product(spread, inverse[FULL, HIGH]))
    spectrum = product(forward[ALL, ALL], mix[ALL, ALL])
    first, second = spectrum[FULL], spectrum[REST]
    mix.put((FULL, ALL), first * spec_re[...] - second * spec_im[...])
    mix.put((REST, ALL), first * spec_im[...] + second * spec_re[...])
    rows_re = split(product(inverse[LOW, ALL], mix[ALL, ALL]))
    rows_im = split(product(inverse[HIGH, ALL], mix[ALL, ALL]))
    model = product(rows_re, forward[LOW, LOW]) + product(rows_im, forward[HIGH, LOW])
    residual = split((model - observed[0]) * float(SPAN))
    grad_re = split(product(residual, inverse[LOW, LOW]))
    grad_im = split(product(residual, inverse[LOW, HIGH]))
    spectrum = product(forward[ALL, LOW], grad_re) + product(forward[ALL, HIGH], grad_im)
    first, second = spectrum[FULL], spectrum[REST]
    mix.put((FULL, ALL), first * spec_re[...] + second * spec_im[...])
    mix.put((REST, ALL), second * spec_re[...] - first * spec_im[...])
    wave = product(inverse[ALL, ALL], mix[ALL, ALL])
    spread_grad = product(split(wave[FULL]), forward[LOW, FULL]) + product(
        split(wave[REST]), forward[HIGH, FULL]
    )
    wide.put((FULL, ALL), far_re[...] * spread_grad)
    wide.put((REST, ALL), far_im[...] * spread_grad)
    back_re = split(product(inverse[LOW, ALL], wide[ALL, ALL]))
    back_im = split(product(inverse[HIGH, ALL], wide[ALL, ALL]))
    out_re = product(back_re, forward[FULL, LOW]) + product(back_im, forward[REST, LOW])
    out_im = product(back_re, forward[FULL, HIGH]) + product(back_im, forward[REST, HIGH])
    gradient = (2.0 * inverse_total) * (pupil_re[...] * out_im - pupil_im[...] * out_re)
    for layer in range(2):
        sheet = pltpu.roll(gradient, turns[layer, 1], 1)
        sheet = pltpu.roll(sheet, turns[layer, 0], 0)
        out[:, layer] = sheet.reshape(32, 8, CORE)


SMEM = pl.BlockSpec(memory_space=pltpu.SMEM)
VMEM = pl.BlockSpec(memory_space=pltpu.VMEM)


def cost(flops, moved):
    return pl.CostEstimate(flops=flops, bytes_accessed=moved, transcendentals=0)


def f32(*shape):
    return jax.ShapeDtypeStruct(shape, jnp.float32)


def body(screens, row_offsets, col_offsets, amplitude, object_strip, observed):
    slab = lax.axis_index("z")
    across = lax.axis_index("x")
    frame_id = lax.axis_index(FRAME)
    patch = slab * 4 + across
    patches = lax.axis_size("z") * lax.axis_size("x")
    rows = lax.dynamic_slice_in_dim(screens, frame_id * 8, 8, 1)
    gathered = lax.all_gather(rows, "z", axis=0, tiled=True)
    ends = patches - 1
    left_tail = lax.ppermute(
        object_strip[:, CORE - HALO :], ("z", "x"), [(i, i + 1) for i in range(ends)]
    )
    right_head = lax.ppermute(object_strip[:, :HALO], ("z", "x"), [(i + 1, i) for i in range(ends)])
    window = jnp.concatenate([object_strip, right_head, left_tail], axis=1)
    window = jnp.concatenate([window[HALO:], window[:HALO]], axis=0)
    constants = [jnp.asarray(part) for part in split_constants()]
    big = jax.ShapeDtypeStruct((2 * SPAN, 2 * SPAN), jnp.bfloat16)
    forward_h, forward_l, inverse_h, inverse_l, spec_re, spec_im = pl.pallas_call(
        object_kernel,
        out_shape=[big] * 4 + [f32(SPAN, HALF)] * 2,
        in_specs=[VMEM] * 5,
        out_specs=[VMEM] * 6,
        cost_estimate=cost(3 * 2 * 226 * 10**6, 7 * 10**6),
        name="object_spectrum",
    )(*constants, window)

    place = jnp.stack([slab, across * 64 + frame_id * 8]).astype(jnp.int32)
    sent = pl.pallas_call(
        select_kernel,
        out_shape=f32(32, 2, 8, CORE),
        in_specs=[SMEM] * 3 + [VMEM],
        out_specs=VMEM,
        cost_estimate=cost(0, 3 * 10**6),
        name="select_rows",
    )(place, row_offsets, col_offsets, gathered)
    received = lax.all_to_all(sent, SLAB, split_axis=0, concat_axis=0, tiled=True)

    row_turns = lax.dynamic_slice(row_offsets, (frame_id, 0, patch), (1, 2, 1))[0, :, 0] % CORE
    col_turns = lax.dynamic_slice(col_offsets, (frame_id, 0, patch), (1, 2, 1))[0, :, 0] % CORE
    turns = jnp.stack([row_turns, col_turns], axis=1)
    placed = pl.pallas_call(
        gradient_kernel,
        out_shape=f32(32, 2, 8, CORE),
        in_specs=[SMEM] + [VMEM] * 9,
        out_specs=VMEM,
        scratch_shapes=[
            pltpu.VMEM((CORE, CORE), jnp.float32),
            pltpu.VMEM((CORE, CORE), jnp.float32),
            pltpu.VMEM((SPAN, SPAN), jnp.float32),
            pltpu.VMEM((SPAN, SPAN), jnp.float32),
            pltpu.VMEM((2 * SPAN, HALF), jnp.bfloat16),
            pltpu.VMEM((2 * SPAN, HALF), jnp.bfloat16),
            pltpu.VMEM((2 * SPAN, SPAN), jnp.bfloat16),
            pltpu.VMEM((2 * SPAN, SPAN), jnp.bfloat16),
        ],
        cost_estimate=cost(3 * 2 * 1222 * 10**6, 7 * 10**6),
        name="gradient",
    )(turns, received, amplitude, observed, forward_h, forward_l, inverse_h, inverse_l, spec_re, spec_im)
    returned = lax.all_to_all(placed, SLAB, split_axis=0, concat_axis=0, tiled=True)

    partial = pl.pallas_call(
        scatter_kernel,
        out_shape=f32(8, 8, 2, 8, 512),
        in_specs=[SMEM] * 3 + [VMEM],
        out_specs=VMEM,
        cost_estimate=cost(0, 3 * 10**6),
        name="scatter_rows",
    )(place, row_offsets, col_offsets, returned)
    summed = lax.psum_scatter(partial, "z", scatter_dimension=0, tiled=False)
    turned = lax.all_to_all(summed, FRAME, split_axis=0, concat_axis=0, tiled=True)
    return turned.transpose(1, 0, 2, 3).reshape(2, 64, 512)


def solution(mesh):
    fine = Mesh(mesh.devices.reshape(8, 4, 4, 2), ("z", "x", "y", "core"))
    patch = ("z", "x")
    in_specs = (
        P(None, patch, None), P(), P(), P(), P(None, patch), P(FRAME, None, patch),
    )
    out_specs = P(None, patch, FRAME)
    return jax.shard_map(body, mesh=fine, in_specs=in_specs, out_specs=out_specs, check_vma=False)
```

time: 697 us -> 174 us (0.25); the launches traced: 686 us -> 171 us
  waiting for transfers between devices: 212 us -> 75.1 us
  local copies, waits for them, and re-layouts: 139 us -> 5.78 us
  loops' own time: 122 us -> 0 us
  matrix products: 93.3 us -> 0 us
  other arithmetic: 78 us -> 3.1 us
  Pallas kernels: 0 us -> 32.2 us
  blocking collectives: 0 us -> 27.4 us
  starting transfers between devices: 26.7 us -> 13.8 us
    another operation x2 -> x0, loops' own time: 122 us -> none  [the longest x1 122 us: body(): summed = lax.fori_loop(0, patch_count, add_band, jnp.zeros_like(screens))]
    dot_general x46 -> x0, matrix products: 93.3 us -> none  [matmul_high(): jnp.dot(left_op, right_op, precision=lax.Precision.HIGHEST, preferred_ele...]
    all_to_all x2 -> x1, waiting for transfers between devices: 93.9 us -> 3.59 us  [body(): lax.all_to_all(sent, SLAB, split_axis=0, concat_axis=0, tiled=True)]
    ppermute x2, waiting for transfers between devices: 81.8 us -> 0.01 us  [the longest x1 0.01 us: body(): lax.ppermute(object_strip[:, :HALO], ('z', 'x'), [(i + 1, i) for i in ran...]
    add x64 -> x0, other arithmetic: 59.7 us -> none  [add_band(): current + returned[0, layer_id, source][None]]
    dynamic_update_slice x64 -> x0, local copies, waits for them, and re-layouts: 52.9 us -> none  [add_band(): lax.dynamic_update_slice(running, current + returned[0, layer_id, source]...]
    all_gather x0 -> x1, waiting for transfers between devices: none -> 33.4 us  [body(): gathered = lax.all_gather(rows, 'z', axis=0, tiled=True)]
    pallas_call x0 -> x4, Pallas kernels: none -> 32.2 us  [the longest x1 18.7 us: body(): pl.pallas_call(gradient_kernel, out_shape=f32(32, 2, 8, CORE), in_specs=[...]
  transfers between devices with their start and end apart: 5 -> 5, of which waited for: 3 -> 3; matrix products, arithmetic and copies ran while one was open for 4% -> 3% of each run, Pallas kernels for 0% -> 5%
where the time goes in v1:
time: 174 us; the launch traced here: 171 us
  waiting for transfers between devices  75.1 us (43%)
  Pallas kernels  32.2 us (19%)
  blocking collectives  27.4 us (16%)
  starting transfers between devices  13.8 us (8%)
  between operations  13.5 us (8%)
  local copies, waits for them, and re-layouts  5.78 us (3%)
  other arithmetic  3.1 us (2%)
    reduce_scatter x1, waiting for transfers between devices, body(): summed = lax.psum_scatter(partial, 'z', scatter_dimension=0, tiled=False)  38.1 us
    all_gather x1, waiting for transfers between devices, body(): gathered = lax.all_gather(rows, 'z', axis=0, tiled=True)  33.4 us
    pallas_call x1, Pallas kernels, body(): pl.pallas_call(gradient_kernel, out_shape=f32(32, 2, 8, CORE), in_specs=[...  18.7 us
    all_to_all x1, blocking collectives, body(): lax.all_to_all(placed, SLAB, split_axis=0, concat_axis=0, tiled=True)  15.7 us
    all_to_all x1, blocking collectives, body(): lax.all_to_all(summed, FRAME, split_axis=0, concat_axis=0, tiled=True)  11.7 us
    all_to_all x1, starting transfers between devices, body(): lax.all_to_all(sent, SLAB, split_axis=0, concat_axis=0, tiled=True)  7.65 us
    pallas_call x1, Pallas kernels, body(): pl.pallas_call(object_kernel, out_shape=[big] * 4 + [f32(SPAN, HALF)] * 2...  4.92 us
    pallas_call x1, Pallas kernels, body(): pl.pallas_call(scatter_kernel, out_shape=f32(8, 8, 2, 8, 512), in_specs=[...  4.75 us
  transfers between devices with their start and end apart: 5, of which 3 were waited for; matrix products, arithmetic and copies ran while one was open for 3% of the time, Pallas kernels for 5%

profile of v1, /device:TPU:64, one launch (start us, length us, event | category | flops | bytes accessed | tf_op | source)
XLA Modules:
  0.0 170.9 jit_solution(6800816377942657243)
XLA Ops:
  6.5 0.0 copy-start
  6.5 0.0 all-gather.2.cloned.1.call-start
  6.5 1.6 copy-done
  8.1 0.7 constant_dynamic-slice_fusion
  8.8 0.0 all-gather.2.cloned.1.call-update
  8.9 0.0 copy-start.1
  8.9 1.9 %fusion.3 = (f32[384,64]{1,0:T(8,128)}, f32[384,64]{1,0:T(8,128)}) fusion(f32[384,256]{1,0:T(8,128)} %param.14), kind=kLoop, calls=%fused_computation.16 | loop fusion | bytes 393216 | tf_op jit(solution)/shard_map/slice | solution.py:252
  10.8 4.2 %collective-permute-start = (f32[384,64]{1,0:T(8,128)}, f32[384,64]{1,0:T(8,128)S(1)}, u32[]{:S(2)}, u32[]{:S(2)}) collective-permute-start(f32[384,64]{1,0:T(8,128)} %get-tuple-element.17), channel_id=1, source_target_pairs={{8,0},{16,8},{24,16},{32,24},{40,32},{48,40},{56,48},{64,56},{72,6... | collective-permute-start | bytes 294920 | tf_op jit(solution)/shard_map/ppermute | solution.py:252
  15.0 1.9 %collective-permute-start.1 = (f32[384,64]{1,0:T(8,128)}, f32[384,64]{1,0:T(8,128)S(1)}, u32[]{:S(2)}, u32[]{:S(2)}) collective-permute-start(f32[384,64]{1,0:T(8,128)} %get-tuple-element.18), channel_id=1, source_target_pairs={{0,8},{8,16},{16,24},{24,32},{32,40},{40,48},{48,56},{56,64},{64,7... | collective-permute-start | bytes 294920 | tf_op jit(solution)/shard_map/ppermute | solution.py:249
  16.9 0.6 pad_add_fusion.1.place
  17.5 33.4 %all-gather.2.cloned.1.call-done.gathered = f32[16,8,4096]{2,1,0:T(8,128)} async-done(((f32[2,8,4096]{2,1,0:T(8,128)}), f32[16,8,4096]{2,1,0:T(8,128)}) %all-gather.2.cloned.1.call-update) | async-done | bytes 2097168 | tf_op jit(solution)/shard_map/all_gather | solution.py:247
  50.9 3.8 %select_rows.1 = f32[32,2,8,256]{3,2,1,0:T(8,128)} custom-call(s32[2]{0:T(128)} %pad_add_fusion.1.place, s32[8,2,32]{2,1,0:T(2,128)} %rows.3, s32[8,2,32]{2,1,0:T(2,128)} %cols.3, f32[16,8,4096]{2,1,0:T(8,128)} %all-gather.2.cloned.1.call-done.gathered), custom_call_target="tpu_custom_call" | custom-call | bytes 3000000 | tf_op jit(solution)/shard_map/select_rows/pallas_call | solution.py:267
  54.7 7.6 %all-to-all-start = ((f32[32,2,8,256]{3,2,1,0:T(8,128)}), f32[32,2,8,256]{3,2,1,0:T(8,128)S(1)}, u32[]{:S(2)}, u32[]{:S(2)}) async-start(f32[32,2,8,256]{3,2,1,0:T(8,128)} %select_rows.1), calls=%async_computation | async-start | bytes 1048576 | tf_op jit(solution)/shard_map/all_to_all | solution.py:275
  62.4 0.0 reduce-scatter.2.cloned.1.call-start
  62.4 0.8 and_select_fusion
  63.2 0.6 pad_add_fusion.turns
  63.9 0.0 collective-permute-done
  63.9 0.0 collective-permute-done.1
  63.9 0.0 copy-done.1
  63.9 0.1 pad_maximum_fusion.2
  64.0 0.9 fusion.window
  65.0 4.9 %object_spectrum.1 = (bf16[768,768]{1,0:T(8,128)(2,1)}, bf16[768,768]{1,0:T(8,128)(2,1)}, bf16[768,768]{1,0:T(8,128)(2,1)}, bf16[768,768]{1,0:T(8,128)(2,1)}, f32[384,256]{1,0:T(8,128)}, /*index=5*/f32[384,256]{1,0:T(8,128)}) custom-call(bf16[384,384]{1,0:T(8,128)(2,1)} %constant.55.clone.ch, bf16[384,384]{1,0:T(8,128)(2,1)} %constant.56.clone.cl, ...), custom_call_target="tpu_custom_call" | custom-call | flops 1356000000 | bytes 7000000 | tf_op jit(solution)/shard_map/object_spectrum/pallas_call | solution.py:257
  69.9 3.6 %all-to-all-done.received = f32[32,2,8,256]{3,2,1,0:T(8,128)S(1)} async-done(((f32[32,2,8,256]{3,2,1,0:T(8,128)}), f32[32,2,8,256]{3,2,1,0:T(8,128)S(1)}, u32[]{:S(2)}, u32[]{:S(2)}) %all-to-all-start) | async-done | bytes 524320 | tf_op jit(solution)/shard_map/all_to_all | solution.py:275
  73.5 0.0 copy-start.2
  73.5 0.8 copy-done.2
  74.3 18.7 %gradient.1 = f32[32,2,8,256]{3,2,1,0:T(8,128)} custom-call(s32[2,2]{1,0:T(2,128)} %pad_add_fusion.turns, f32[32,2,8,256]{3,2,1,0:T(8,128)} %copy-done.2, f32[256,256]{1,0:T(8,128)} %amp_ref.1, f32[1,256,256]{2,1,0:T(8,128)} %observed.1, bf16[768,768]{1,0:T(8,128)(2,1)} %get-tuple-element.11.forward_h, bf16[768,768]{1,0:T(8,128)(2,1)} %get-tuple-element.12.forward_l, ...), custom_call_target="tpu_custom_call" | custom-call | flops 7331999744 | bytes 7000000 | tf_op jit(solution)/shard_map/gradient/pallas_call | solution.py:280
  93.0 15.7 %all_to_all.15.values = f32[32,2,8,256]{3,2,1,0:T(8,128)} all-to-all(f32[32,2,8,256]{3,2,1,0:T(8,128)} %gradient.1), channel_id=1, replica_groups=mesh['z'=8,'x'=4,'y'=4,'core'=2] {'x','y','core'}, dimensions={0} | all-to-all | bytes 1048576 | tf_op jit(solution)/shard_map/all_to_all | solution.py:298
  108.7 4.8 %scatter_rows.1 = f32[8,8,2,8,512]{4,3,2,1,0:T(8,128)} custom-call(s32[2]{0:T(128)} %pad_add_fusion.1.place, s32[8,2,32]{2,1,0:T(2,128)} %rows.3, s32[8,2,32]{2,1,0:T(2,128)} %cols.3, f32[32,2,8,256]{3,2,1,0:T(8,128)} %all_to_all.15.values), custom_call_target="tpu_custom_call" | custom-call | bytes 3000000 | tf_op jit(solution)/shard_map/scatter_rows/pallas_call | solution.py:300
  113.4 0.0 reduce-scatter.2.cloned.1.call-update
  113.4 38.1 %reduce-scatter.2.cloned.1.call-done = f32[1,8,2,8,512]{4,3,2,1,0:T(8,128)} async-done(((f32[8,8,2,8,512]{4,3,2,1,0:T(8,128)}), f32[1,8,2,8,512]{4,3,2,1,0:T(8,128)}) %reduce-scatter.2.cloned.1.call-update) | async-done | bytes 262160 | tf_op jit(solution)/shard_map/reduce_scatter | solution.py:308
  151.6 11.7 %all_to_all.16 = f32[8,2,8,512]{3,2,1,0:T(8,128)S(1)} all-to-all(f32[8,2,8,512]{3,2,1,0:T(8,128)} %bitcast.12), channel_id=1, replica_groups=mesh['z'=8,'x'=4,'y'=4,'core'=2] {'y','core'}, dimensions={0} | all-to-all | bytes 524288 | tf_op jit(solution)/shard_map/all_to_all | solution.py:309
  163.3 0.7 copy_bitcast_fusion
  (1 shorter events, 0.0 us)
Async XLA Ops:
  6.5 1.6 copy-start
  6.5 44.4 %all-gather.2.cloned.1.call-start = ((), (), s32[]{:S(2)}) async-start(), calls=%async_computation.4 | async-start | bytes 2359296 | tf_op jit(solution)/shard_map/all_gather | solution.py:247
  8.9 55.0 %copy-start.1 = (f32[384,256]{1,0:T(8,128)S(1)}, f32[384,256]{1,0:T(8,128)}, u32[]{:S(2)}) copy-start(f32[384,256]{1,0:T(8,128)} %param.14) | copy-start | bytes 1179652
  10.8 53.1 %collective-permute-start = (f32[384,64]{1,0:T(8,128)}, f32[384,64]{1,0:T(8,128)S(1)}, u32[]{:S(2)}, u32[]{:S(2)}) collective-permute-start(f32[384,64]{1,0:T(8,128)} %get-tuple-element.17), channel_id=1, source_target_pairs={{8,0},{16,8},{24,16},{32,24},{40,32},{48,40},{56,48},{64,56},{72,6... | collective-permute-start | bytes 294920 | tf_op jit(solution)/shard_map/ppermute | solution.py:252
  15.0 48.9 %collective-permute-start.1 = (f32[384,64]{1,0:T(8,128)}, f32[384,64]{1,0:T(8,128)S(1)}, u32[]{:S(2)}, u32[]{:S(2)}) collective-permute-start(f32[384,64]{1,0:T(8,128)} %get-tuple-element.18), channel_id=1, source_target_pairs={{0,8},{8,16},{16,24},{24,32},{32,40},{40,48},{48,56},{56,64},{64,7... | collective-permute-start | bytes 294920 | tf_op jit(solution)/shard_map/ppermute | solution.py:249
  54.7 18.7 %all-to-all-start = ((f32[32,2,8,256]{3,2,1,0:T(8,128)}), f32[32,2,8,256]{3,2,1,0:T(8,128)S(1)}, u32[]{:S(2)}, u32[]{:S(2)}) async-start(f32[32,2,8,256]{3,2,1,0:T(8,128)} %select_rows.1), calls=%async_computation | async-start | bytes 1048576 | tf_op jit(solution)/shard_map/all_to_all | solution.py:275
  62.4 89.2 %reduce-scatter.2.cloned.1.call-start = ((), (), s32[]{:S(2)}) async-start(), calls=%async_computation.5 | async-start | bytes 2359296 | tf_op jit(solution)/shard_map/reduce_scatter | solution.py:308
  73.5 0.8 copy-start.2
Sparse Core Ops, SparseCore 0:
  9.1 41.7 all-gather.1
  113.6 37.9 reduce-scatter.1

commit v2 on v1

--- a/solution.py
+++ b/solution.py
@@ -3,7 +3,6 @@
 
 import jax
 import jax.numpy as jnp
-import numpy as np
 from jax import lax
 from jax.experimental import pallas as pl
 from jax.experimental.pallas import tpu as pltpu
@@ -15,18 +14,6 @@
 HALF = 256
 SLAB = ("x", "y", "core")
 FRAME = ("y", "core")
-
-
-def split_constants():
-    index = np.arange(SPAN)
-    angles = (np.outer(index, index) % SPAN) * (2.0 * np.pi / SPAN)
-    cosine, sine = np.cos(angles), np.sin(angles)
-    parts = []
-    for values in (cosine, sine):
-        high = values.astype(jnp.bfloat16)
-        low = (values - high.astype(np.float64)).astype(jnp.bfloat16)
-        parts += [high, low]
-    return parts
 
 
 def split(values):
@@ -82,12 +69,15 @@
 ALL = slice(None)
 
 
-def object_kernel(ch, cl, sh, sl, window, forward_h, forward_l, inverse_h, inverse_l, spec_re, spec_im):
-    for target_f, target_i, cos_ref, sin_ref in (
-        (forward_h, inverse_h, ch, sh),
-        (forward_l, inverse_l, cl, sl),
+def object_kernel(window, forward_h, forward_l, inverse_h, inverse_l, spec_re, spec_im):
+    row = lax.broadcasted_iota(jnp.int32, (SPAN, SPAN), 0)
+    column = lax.broadcasted_iota(jnp.int32, (SPAN, SPAN), 1)
+    steps = (row * column).astype(jnp.float32)
+    steps = steps - SPAN * jnp.floor((steps + 0.5) * (1.0 / SPAN))
+    sine, cosine = sine_cosine(steps * (2.0 * math.pi / SPAN))
+    for target_f, target_i, cosine, sine in zip(
+        (forward_h, forward_l), (inverse_h, inverse_l), split(cosine), split(sine)
     ):
-        cosine, sine = cos_ref[...], sin_ref[...]
         target_f[FULL, FULL] = cosine
         target_f[FULL, REST] = sine
         target_f[REST, FULL] = -sine
@@ -108,8 +98,22 @@
     spec_im[...] = out[REST] * weight
 
 
-def select_kernel(place, rows, cols, gathered, out):
+def cut_kernel(place, screens, out, sem):
+    at = pl.ds(pl.multiple_of(place[2], 8), 8)
+    copy = pltpu.make_async_copy(screens.at[:, at, :], out, sem)
+    copy.start()
+    copy.wait()
+
+
+def select_kernel(place, rows, cols, *refs):
+    chunks, out, gathered = refs[:9], refs[9], refs[10]
     slab, first = place[0], place[1]
+    for step, chunk in zip((0, 1, 2, 3, 5, 6, 7), chunks):
+        source = (slab + step) % 8
+        gathered[pl.ds(source * 2, 2)] = chunk[...]
+    source = (slab + 4) % 8
+    gathered[pl.ds(source * 2, 1)] = chunks[7][...]
+    gathered[pl.ds(source * 2 + 1, 1)] = chunks[8][...]
     row_index = first + lax.broadcasted_iota(jnp.int32, (8, CORE), 0)
     lane = lax.broadcasted_iota(jnp.int32, (8, CORE), 1)
 
@@ -137,7 +141,7 @@
     lax.fori_loop(0, 32, one, 0, unroll=4)
 
 
-def scatter_kernel(place, rows, cols, values, out):
+def scatter_kernel(place, rows, cols, values, out, above, below):
     slab, first = place[0], place[1]
     row_index = first + lax.broadcasted_iota(jnp.int32, (8, CORE), 0)
     lane = lax.broadcasted_iota(jnp.int32, (8, CORE), 1)
@@ -156,7 +160,8 @@
             value = values[member, layer]
             here = row_index >= residue
             right = lane >= turn
-            for where, keep_row in ((block, here), (after, ~here)):
+            for target, keep_row in ((block, here), (after, ~here)):
+                where = (target + 8 - slab) % 8
                 for place_col, keep_col in ((strip, right), (beside, ~right)):
                     at = pl.ds(pl.multiple_of((place_col % 2) * CORE, CORE), CORE)
                     chunk = place_col // 2
@@ -166,6 +171,8 @@
         return carry
 
     lax.fori_loop(0, 32, one, 0, unroll=2)
+    above[...] = out[4, 0:4]
+    below[...] = out[4, 4:8]
 
 
 def gradient_kernel(
@@ -229,12 +236,49 @@
 VMEM = pl.BlockSpec(memory_space=pltpu.VMEM)
 
 
+def limit(mib):
+    return pltpu.CompilerParams(vmem_limit_bytes=mib << 20)
+
+
 def cost(flops, moved):
     return pl.CostEstimate(flops=flops, bytes_accessed=moved, transcendentals=0)
 
 
 def f32(*shape):
     return jax.ShapeDtypeStruct(shape, jnp.float32)
+
+
+def up(values):
+    count = lax.axis_size("z")
+    return lax.ppermute(values, "z", [(i, (i + 1) % count) for i in range(count)])
+
+
+def down(values):
+    count = lax.axis_size("z")
+    return lax.ppermute(values, "z", [((i + 1) % count, i) for i in range(count)])
+
+
+def ring_gather(own):
+    rise, fall = [own], [own]
+    for _ in range(3):
+        rise.append(up(rise[-1]))
+        fall.append(down(fall[-1]))
+    halves = [up(rise[3][0:1]), down(fall[3][1:2])]
+    return fall + [rise[3], rise[2], rise[1]] + halves
+
+
+def ring_scatter(partial, above, below):
+    above = up(above)
+    below = down(below)
+    rise = jnp.concatenate([partial[3, :4] + above, partial[3, 4:]])
+    fall = jnp.concatenate([partial[5, :4], partial[5, 4:] + below])
+    for step in (2, 1, 0):
+        rise = up(rise)
+        fall = down(fall)
+        if step:
+            rise = rise + partial[step]
+            fall = fall + partial[8 - step]
+    return partial[0] + rise + fall
 
 
 def body(screens, row_offsets, col_offsets, amplitude, object_strip, observed):
@@ -243,8 +287,17 @@
     frame_id = lax.axis_index(FRAME)
     patch = slab * 4 + across
     patches = lax.axis_size("z") * lax.axis_size("x")
-    rows = lax.dynamic_slice_in_dim(screens, frame_id * 8, 8, 1)
-    gathered = lax.all_gather(rows, "z", axis=0, tiled=True)
+    place = jnp.stack([slab, across * 64 + frame_id * 8, frame_id * 8]).astype(jnp.int32)
+    own = pl.pallas_call(
+        cut_kernel,
+        out_shape=f32(2, 8, screens.shape[2]),
+        in_specs=[SMEM, pl.BlockSpec(memory_space=pltpu.HBM)],
+        out_specs=VMEM,
+        scratch_shapes=[pltpu.SemaphoreType.DMA],
+        compiler_params=limit(61),
+        name="cut_rows",
+    )(place, screens)
+    chunks = ring_gather(own)
     ends = patches - 1
     left_tail = lax.ppermute(
         object_strip[:, CORE - HALO :], ("z", "x"), [(i, i + 1) for i in range(ends)]
@@ -252,26 +305,27 @@
     right_head = lax.ppermute(object_strip[:, :HALO], ("z", "x"), [(i + 1, i) for i in range(ends)])
     window = jnp.concatenate([object_strip, right_head, left_tail], axis=1)
     window = jnp.concatenate([window[HALO:], window[:HALO]], axis=0)
-    constants = [jnp.asarray(part) for part in split_constants()]
     big = jax.ShapeDtypeStruct((2 * SPAN, 2 * SPAN), jnp.bfloat16)
     forward_h, forward_l, inverse_h, inverse_l, spec_re, spec_im = pl.pallas_call(
         object_kernel,
         out_shape=[big] * 4 + [f32(SPAN, HALF)] * 2,
-        in_specs=[VMEM] * 5,
+        in_specs=[VMEM],
         out_specs=[VMEM] * 6,
+        compiler_params=limit(20),
         cost_estimate=cost(3 * 2 * 226 * 10**6, 7 * 10**6),
         name="object_spectrum",
-    )(*constants, window)
-
-    place = jnp.stack([slab, across * 64 + frame_id * 8]).astype(jnp.int32)
+    )(window)
+
     sent = pl.pallas_call(
         select_kernel,
         out_shape=f32(32, 2, 8, CORE),
-        in_specs=[SMEM] * 3 + [VMEM],
+        in_specs=[SMEM] * 3 + [VMEM] * 9,
         out_specs=VMEM,
+        scratch_shapes=[pltpu.VMEM((16, 8, screens.shape[2]), jnp.float32)],
+        compiler_params=limit(20),
         cost_estimate=cost(0, 3 * 10**6),
         name="select_rows",
-    )(place, row_offsets, col_offsets, gathered)
+    )(place, row_offsets, col_offsets, *chunks)
     received = lax.all_to_all(sent, SLAB, split_axis=0, concat_axis=0, tiled=True)
 
     row_turns = lax.dynamic_slice(row_offsets, (frame_id, 0, patch), (1, 2, 1))[0, :, 0] % CORE
@@ -292,20 +346,22 @@
             pltpu.VMEM((2 * SPAN, SPAN), jnp.bfloat16),
             pltpu.VMEM((2 * SPAN, SPAN), jnp.bfloat16),
         ],
+        compiler_params=limit(20),
         cost_estimate=cost(3 * 2 * 1222 * 10**6, 7 * 10**6),
         name="gradient",
     )(turns, received, amplitude, observed, forward_h, forward_l, inverse_h, inverse_l, spec_re, spec_im)
     returned = lax.all_to_all(placed, SLAB, split_axis=0, concat_axis=0, tiled=True)
 
-    partial = pl.pallas_call(
+    partial, above, below = pl.pallas_call(
         scatter_kernel,
-        out_shape=f32(8, 8, 2, 8, 512),
+        out_shape=[f32(8, 8, 2, 8, 512)] + [f32(4, 2, 8, 512)] * 2,
         in_specs=[SMEM] * 3 + [VMEM],
-        out_specs=VMEM,
+        out_specs=[VMEM] * 3,
+        compiler_params=limit(20),
         cost_estimate=cost(0, 3 * 10**6),
         name="scatter_rows",
     )(place, row_offsets, col_offsets, returned)
-    summed = lax.psum_scatter(partial, "z", scatter_dimension=0, tiled=False)
+    summed = ring_scatter(partial, above, below)
     turned = lax.all_to_all(summed, FRAME, split_axis=0, concat_axis=0, tiled=True)
     return turned.transpose(1, 0, 2, 3).reshape(2, 64, 512)
 

time: 174 us -> 151 us (0.87); the launches traced: 171 us -> 150 us
  waiting for transfers between devices: 75.1 us -> 46.2 us
  starting transfers between devices: 13.8 us -> 40.8 us
  between operations: 13.5 us -> 0.25 us
  Pallas kernels: 32.2 us -> 27.9 us
  local copies, waits for them, and re-layouts: 5.78 us -> 8.76 us
  blocking collectives: 27.4 us -> 24.9 us
  other arithmetic: 3.1 us -> 1.29 us
    ppermute x0 -> x16, waiting for transfers between devices: none -> 41.9 us  [the longest x8 26.4 us: up(): lax.ppermute(values, 'z', [(i, (i + 1) % count) for i in range(count)])]
    reduce_scatter x1 -> x0, waiting for transfers between devices: 38.1 us -> none  [body(): summed = lax.psum_scatter(partial, 'z', scatter_dimension=0, tiled=False)]
    all_gather x1 -> x0, waiting for transfers between devices: 33.4 us -> none  [body(): gathered = lax.all_gather(rows, 'z', axis=0, tiled=True)]
    ppermute x0 -> x16, starting transfers between devices: none -> 25.7 us  [the longest x8 25.4 us: up(): lax.ppermute(values, 'z', [(i, (i + 1) % count) for i in range(count)])]
    unnamed x6 -> x26, local copies, waits for them, and re-layouts: 2.43 us -> 7.86 us
    pallas_call x1, Pallas kernels: 18.7 us -> 15.7 us  [body(): pl.pallas_call(gradient_kernel, out_shape=f32(32, 2, 8, CORE), in_specs=[...]
    pallas_call x1, Pallas kernels: 4.92 us -> 3.01 us  [body(): pl.pallas_call(object_kernel, out_shape=[big] * 4 + [f32(SPAN, HALF)] * 2...]
    ppermute x1, starting transfers between devices: 4.2 us -> 6.03 us  [body(): lax.ppermute(object_strip[:, :HALO], ('z', 'x'), [(i + 1, i) for i in ran...]
  transfers between devices with their start and end apart: 5 -> 19, of which waited for: 3 -> 14; matrix products, arithmetic and copies ran while one was open for 3% -> 0% of each run, Pallas kernels for 5% -> 4%
where the time goes in v2:
time: 151 us; the launch traced here: 150 us
  waiting for transfers between devices  46.2 us (31%)
  starting transfers between devices  40.8 us (27%)
  Pallas kernels  27.9 us (18%)
  blocking collectives  24.9 us (16%)
  local copies, waits for them, and re-layouts  8.76 us (6%)
    ppermute x8, waiting for transfers between devices, up(): lax.ppermute(values, 'z', [(i, (i + 1) % count) for i in range(count)])  26.4 us
    ppermute x8, starting transfers between devices, up(): lax.ppermute(values, 'z', [(i, (i + 1) % count) for i in range(count)])  25.4 us
    pallas_call x1, Pallas kernels, body(): pl.pallas_call(gradient_kernel, out_shape=f32(32, 2, 8, CORE), in_specs=[...  15.7 us
    ppermute x8, waiting for transfers between devices, down(): lax.ppermute(values, 'z', [((i + 1) % count, i) for i in range(count)])  15.4 us
    all_to_all x1, blocking collectives, body(): lax.all_to_all(placed, SLAB, split_axis=0, concat_axis=0, tiled=True)  15 us
    all_to_all x1, blocking collectives, body(): lax.all_to_all(summed, FRAME, split_axis=0, concat_axis=0, tiled=True)  9.91 us
    unnamed x26, local copies, waits for them, and re-layouts  7.86 us
    all_to_all x1, starting transfers between devices, body(): lax.all_to_all(sent, SLAB, split_axis=0, concat_axis=0, tiled=True)  7.24 us
  transfers between devices with their start and end apart: 19, of which 14 were waited for; matrix products, arithmetic and copies ran while one was open for 0% of the time, Pallas kernels for 4%

profile of v2, /device:TPU:64, one launch (start us, length us, event | category | flops | bytes accessed | tf_op | source)
XLA Modules:
  0.0 150.2 jit_solution(9654199723433387825)
XLA Ops:
  0.0 0.6 pad_add_fusion.1.place
  0.6 2.5 %cut_rows.1.refs_0_ = f32[2,8,4096]{2,1,0:T(8,128)} custom-call(s32[3]{0:T(128)} %pad_add_fusion.1.place, f32[2,64,4096]{2,1,0:T(8,128)} %screens.1), custom_call_target="tpu_custom_call" | custom-call | tf_op jit(solution)/shard_map/cut_rows/pallas_call | solution.py:291
  3.1 2.0 %collective-permute-start.3 = (f32[2,8,4096]{2,1,0:T(8,128)}, f32[2,8,4096]{2,1,0:T(8,128)S(1)}, u32[]{:S(2)}, u32[]{:S(2)}) collective-permute-start(f32[2,8,4096]{2,1,0:T(8,128)} %cut_rows.1.refs_0_), channel_id=1, source_target_pairs={{0,32},{32,64},{64,96},{96,128},{128,160},{160,192},{192,224},{224... | collective-permute-start | bytes 786440 | tf_op jit(solution)/shard_map/ppermute | solution.py:253
  5.1 0.1 collective-permute-start
  5.2 6.2 %collective-permute-done.3.refs_6_ = f32[2,8,4096]{2,1,0:T(8,128)S(1)} collective-permute-done((f32[2,8,4096]{2,1,0:T(8,128)}, f32[2,8,4096]{2,1,0:T(8,128)S(1)}, u32[]{:S(2)}, u32[]{:S(2)}) %collective-permute-start.3) | collective-permute-done | bytes 262176 | tf_op jit(solution)/shard_map/ppermute | solution.py:253
  11.4 2.7 %collective-permute-start.4 = (f32[2,8,4096]{2,1,0:T(8,128)S(1)}, f32[2,8,4096]{2,1,0:T(8,128)S(1)}, u32[]{:S(2)}, u32[]{:S(2)}) collective-permute-start(f32[2,8,4096]{2,1,0:T(8,128)S(1)} %collective-permute-done.3.refs_6_), channel_id=1, source_target_pairs={{0,32},{32,64},{64,96},{96,128},{128,160},{160,192},{192,224},{224... | collective-permute-start | bytes 786440 | tf_op jit(solution)/shard_map/ppermute | solution.py:253
  14.1 0.4 collective-permute-done.refs_1_
  14.5 4.3 %collective-permute-done.4.refs_5_ = f32[2,8,4096]{2,1,0:T(8,128)S(1)} collective-permute-done((f32[2,8,4096]{2,1,0:T(8,128)S(1)}, f32[2,8,4096]{2,1,0:T(8,128)S(1)}, u32[]{:S(2)}, u32[]{:S(2)}) %collective-permute-start.4) | collective-permute-done | bytes 262176 | tf_op jit(solution)/shard_map/ppermute | solution.py:253
  18.8 3.6 %collective-permute-start.5 = (f32[2,8,4096]{2,1,0:T(8,128)S(1)}, f32[2,8,4096]{2,1,0:T(8,128)S(1)}, u32[]{:S(2)}, u32[]{:S(2)}) collective-permute-start(f32[2,8,4096]{2,1,0:T(8,128)S(1)} %collective-permute-done.4.refs_5_), channel_id=1, source_target_pairs={{0,32},{32,64},{64,96},{96,128},{128,160},{160,192},{192,224},{224... | collective-permute-start | bytes 786440 | tf_op jit(solution)/shard_map/ppermute | solution.py:253
  22.4 0.5 collective-permute-done.1.refs_2_
  22.9 3.8 %collective-permute-done.5.refs_4_ = f32[2,8,4096]{2,1,0:T(8,128)S(1)} collective-permute-done((f32[2,8,4096]{2,1,0:T(8,128)S(1)}, f32[2,8,4096]{2,1,0:T(8,128)S(1)}, u32[]{:S(2)}, u32[]{:S(2)}) %collective-permute-start.5) | collective-permute-done | bytes 262176 | tf_op jit(solution)/shard_map/ppermute | solution.py:253
  26.7 3.4 %collective-permute-start.6 = (f32[1,8,4096]{2,1,0:T(8,128)S(1)}, f32[1,8,4096]{2,1,0:T(8,128)S(1)}, u32[]{:S(2)}, u32[]{:S(2)}) collective-permute-start(f32[1,8,4096]{2,1,0:T(8,128)S(1)} %slice.60), channel_id=1, source_target_pairs={{0,32},{32,64},{64,96},{96,128},{128,160},{160,192},{192,224},{224... | collective-permute-start | bytes 393224 | tf_op jit(solution)/shard_map/ppermute | solution.py:253
  30.1 0.4 collective-permute-done.2.refs_3_
  30.6 0.1 fusion.4
  30.7 6.0 %collective-permute-start.8 = (f32[384,64]{1,0:T(8,128)S(1)}, f32[384,64]{1,0:T(8,128)S(1)}, u32[]{:S(2)}, u32[]{:S(2)}) collective-permute-start(f32[384,64]{1,0:T(8,128)S(1)} %get-tuple-element.31), channel_id=1, source_target_pairs={{8,0},{16,8},{24,16},{32,24},{40,32},{48,40},{56,48},{64,56},{72,6... | collective-permute-start | bytes 294920 | tf_op jit(solution)/shard_map/ppermute | solution.py:305
  36.7 1.9 %collective-permute-start.9 = (f32[384,64]{1,0:T(8,128)S(1)}, f32[384,64]{1,0:T(8,128)S(1)}, u32[]{:S(2)}, u32[]{:S(2)}) collective-permute-start(f32[384,64]{1,0:T(8,128)S(1)} %get-tuple-element.32), channel_id=1, source_target_pairs={{0,8},{8,16},{16,24},{24,32},{32,40},{40,48},{48,56},{56,64},{64,7... | collective-permute-start | bytes 294920 | tf_op jit(solution)/shard_map/ppermute | solution.py:302
  38.7 0.9 copy-done
  39.7 3.2 %select_rows.1 = f32[32,2,8,256]{3,2,1,0:T(8,128)} custom-call(s32[3]{0:T(128)S(1)} %copy-done.3, s32[8,2,32]{2,1,0:T(2,128)S(1)} %copy-done.1, s32[8,2,32]{2,1,0:T(2,128)S(1)} %copy-done.2, f32[2,8,4096]{2,1,0:T(8,128)S(1)} %copy-done, f32[2,8,4096]{2,1,0:T(8,128)S(1)} %collective-permute-done.refs_1_, f32[2,8,4096]{2,1,0:T(8,128)S(1)} %collective-permute-done.1.refs_2_, ...), custom_call_target="tpu_custom_call" | custom-call | bytes 3000000 | tf_op jit(solution)/shard_map/select_rows/pallas_call | solution.py:319
  42.8 7.2 %all-to-all-start = ((f32[32,2,8,256]{3,2,1,0:T(8,128)}), f32[32,2,8,256]{3,2,1,0:T(8,128)S(1)}, u32[]{:S(2)}, u32[]{:S(2)}) async-start(f32[32,2,8,256]{3,2,1,0:T(8,128)} %select_rows.1), calls=%async_computation | async-start | bytes 1048576 | tf_op jit(solution)/shard_map/all_to_all | solution.py:329
  50.1 0.1 and_select_fusion
  50.2 0.1 pad_maximum_fusion.2
  50.5 3.0 %object_spectrum.1 = (bf16[768,768]{1,0:T(8,128)(2,1)S(1)}, bf16[768,768]{1,0:T(8,128)(2,1)S(1)}, bf16[768,768]{1,0:T(8,128)(2,1)S(1)}, bf16[768,768]{1,0:T(8,12...) custom-call(f32[384,384]{1,0:T(8,128)S(1)} %fusion.window), custom_call_target="tpu_custom_call" | custom-call | flops 1356000000 | bytes 7000000 | tf_op jit(solution)/shard_map/object_spectrum/pallas_call | solution.py:309
  53.5 1.0 copy-done.6
  54.6 1.0 copy-done.8
  55.6 1.0 copy-done.10
  56.6 4.4 %all-to-all-done.received = f32[32,2,8,256]{3,2,1,0:T(8,128)S(1)} async-done(((f32[32,2,8,256]{3,2,1,0:T(8,128)}), f32[32,2,8,256]{3,2,1,0:T(8,128)S(1)}, u32[]{:S(2)}, u32[]{:S(2)}) %all-to-all-start) | async-done | bytes 524320 | tf_op jit(solution)/shard_map/all_to_all | solution.py:329
  61.0 1.3 copy-done.7
  62.2 1.3 copy-done.9
  63.5 1.3 copy-done.11
  64.8 15.7 %gradient.1 = f32[32,2,8,256]{3,2,1,0:T(8,128)S(1)} custom-call(s32[2,2]{1,0:T(2,128)S(1)} %pad_add_fusion.turns, f32[32,2,8,256]{3,2,1,0:T(8,128)S(1)} %all-to-all-done.received, f32[256,256]{1,0:T(8,128)S(1)} %copy-done.4, f32[1,256,256]{2,1,0:T(8,128)S(1)} %copy-done.5, bf16[768,768]{1,0:T(8,128)(2,1)S(1)} %get-tuple-element.14.forward_h, ...), custom_call_target="tpu_custom_call" | custom-call | flops 7331999744 | bytes 7000000 | tf_op jit(solution)/shard_map/gradient/pallas_call | solution.py:334
  80.5 15.0 %all_to_all.15.values = f32[32,2,8,256]{3,2,1,0:T(8,128)S(1)} all-to-all(f32[32,2,8,256]{3,2,1,0:T(8,128)S(1)} %gradient.1), channel_id=1, replica_groups=mesh['z'=8,'x'=4,'y'=4,'core'=2] {'x','y','core'}, dimensions={0} | all-to-all | bytes 1048576 | tf_op jit(solution)/shard_map/all_to_all | solution.py:353
  95.5 3.5 %scatter_rows.1 = (f32[8,8,2,8,512]{4,3,2,1,0:T(8,128)S(1)}, f32[4,2,8,512]{3,2,1,0:T(8,128)S(1)}, f32[4,2,8,512]{3,2,1,0:T(8,128)S(1)}) custom-call(s32[3]{0:T(128)S(1)} %copy-done.3, s32[8,2,32]{2,1,0:T(2,128)S(1)} %copy-done.1, s32[8,2,32]{2,1,0:T(2,128)S(1)} %copy-done.2, f32[32,2,8,256]{3,2,1,0:T(8,128)S(1)} %all_to_all.15.values), custom_call_target="tpu_custom_call" | custom-call | bytes 3000000 | tf_op jit(solution)/shard_map/scatter_rows/pallas_call | solution.py:355
  99.1 4.6 %collective-permute-start.10 = (f32[4,2,8,512]{3,2,1,0:T(8,128)S(1)}, f32[4,2,8,512]{3,2,1,0:T(8,128)S(1)}, u32[]{:S(2)}, u32[]{:S(2)}) collective-permute-start(f32[4,2,8,512]{3,2,1,0:T(8,128)S(1)} %get-tuple-element.21), channel_id=1, source_target_pairs={{0,32},{32,64},{64,96},{96,128},{128,160},{160,192},{192,224},{224... | collective-permute-start | bytes 393224 | tf_op jit(solution)/shard_map/ppermute | solution.py:253
  103.7 3.7 %collective-permute-done.10 = f32[4,2,8,512]{3,2,1,0:T(8,128)S(1)} collective-permute-done((f32[4,2,8,512]{3,2,1,0:T(8,128)S(1)}, f32[4,2,8,512]{3,2,1,0:T(8,128)S(1)}, u32[]{:S(2)}, u32[]{:S(2)}) %collective-permute-start.10) | collective-permute-done | bytes 131104 | tf_op jit(solution)/shard_map/ppermute | solution.py:253
  107.4 2.5 %collective-permute-done.14 = f32[4,2,8,512]{3,2,1,0:T(8,128)S(1)} collective-permute-done((f32[4,2,8,512]{3,2,1,0:T(8,128)S(1)}, f32[4,2,8,512]{3,2,1,0:T(8,128)S(1)}, u32[]{:S(2)}, u32[]{:S(2)}) %collective-permute-start.14) | collective-permute-done | bytes 131104 | tf_op jit(solution)/shard_map/ppermute | solution.py:258
  109.9 0.1 collective-permute-start.15
  110.0 3.0 %collective-permute-start.11 = (f32[8,2,8,512]{3,2,1,0:T(8,128)S(1)}, f32[8,2,8,512]{3,2,1,0:T(8,128)S(1)}, u32[]{:S(2)}, u32[]{:S(2)}) collective-permute-start(f32[8,2,8,512]{3,2,1,0:T(8,128)S(1)} %pad_maximum_fusion.3), channel_id=1, source_target_pairs={{0,32},{32,64},{64,96},{96,128},{128,160},{160,192},{192,224},{224... | collective-permute-start | bytes 786440 | tf_op jit(solution)/shard_map/ppermute | solution.py:253
  113.1 6.0 %collective-permute-done.15 = f32[8,2,8,512]{3,2,1,0:T(8,128)S(1)} collective-permute-done((f32[8,2,8,512]{3,2,1,0:T(8,128)S(1)}, f32[8,2,8,512]{3,2,1,0:T(8,128)S(1)}, u32[]{:S(2)}, u32[]{:S(2)}) %collective-permute-start.15) | collective-permute-done | bytes 262176 | tf_op jit(solution)/shard_map/ppermute | solution.py:258
  119.1 0.1 bitcast_add_fusion.3
  119.2 3.0 %collective-permute-start.12 = (f32[8,2,8,512]{3,2,1,0:T(8,128)S(1)}, f32[8,2,8,512]{3,2,1,0:T(8,128)S(1)}, u32[]{:S(2)}, u32[]{:S(2)}) collective-permute-start(f32[8,2,8,512]{3,2,1,0:T(8,128)S(1)} %get-tuple-element.25), channel_id=1, source_target_pairs={{0,32},{32,64},{64,96},{96,128},{128,160},{160,192},{192,224},{224... | collective-permute-start | bytes 786440 | tf_op jit(solution)/shard_map/ppermute | solution.py:253
  122.2 4.5 %collective-permute-done.12 = f32[8,2,8,512]{3,2,1,0:T(8,128)S(1)} collective-permute-done((f32[8,2,8,512]{3,2,1,0:T(8,128)S(1)}, f32[8,2,8,512]{3,2,1,0:T(8,128)S(1)}, u32[]{:S(2)}, u32[]{:S(2)}) %collective-permute-start.12) | collective-permute-done | bytes 262176 | tf_op jit(solution)/shard_map/ppermute | solution.py:253
  126.7 3.2 %collective-permute-done.16 = f32[8,2,8,512]{3,2,1,0:T(8,128)S(1)} collective-permute-done((f32[8,2,8,512]{3,2,1,0:T(8,128)S(1)}, f32[8,2,8,512]{3,2,1,0:T(8,128)S(1)}, u32[]{:S(2)}, u32[]{:S(2)}) %collective-permute-start.16) | collective-permute-done | bytes 262176 | tf_op jit(solution)/shard_map/ppermute | solution.py:258
  130.0 0.1 bitcast_add_fusion.2
  130.1 3.0 %collective-permute-start.13 = (f32[8,2,8,512]{3,2,1,0:T(8,128)S(1)}, f32[8,2,8,512]{3,2,1,0:T(8,128)S(1)}, u32[]{:S(2)}, u32[]{:S(2)}) collective-permute-start(f32[8,2,8,512]{3,2,1,0:T(8,128)S(1)} %get-tuple-element.23), channel_id=1, source_target_pairs={{0,32},{32,64},{64,96},{96,128},{128,160},{160,192},{192,224},{224... | collective-permute-start | bytes 786440 | tf_op jit(solution)/shard_map/ppermute | solution.py:253
  133.1 3.9 %collective-permute-done.13 = f32[8,2,8,512]{3,2,1,0:T(8,128)S(1)} collective-permute-done((f32[8,2,8,512]{3,2,1,0:T(8,128)S(1)}, f32[8,2,8,512]{3,2,1,0:T(8,128)S(1)}, u32[]{:S(2)}, u32[]{:S(2)}) %collective-permute-start.13) | collective-permute-done | bytes 262176 | tf_op jit(solution)/shard_map/ppermute | solution.py:253
  137.0 2.5 %collective-permute-done.17 = f32[8,2,8,512]{3,2,1,0:T(8,128)S(1)} collective-permute-done((f32[8,2,8,512]{3,2,1,0:T(8,128)S(1)}, f32[8,2,8,512]{3,2,1,0:T(8,128)S(1)}, u32[]{:S(2)}, u32[]{:S(2)}) %collective-permute-start.17) | collective-permute-done | bytes 262176 | tf_op jit(solution)/shard_map/ppermute | solution.py:258
  139.5 9.9 %all_to_all.16 = f32[8,2,8,512]{3,2,1,0:T(8,128)S(1)} all-to-all(f32[8,2,8,512]{3,2,1,0:T(8,128)S(1)} %fusion.1), channel_id=1, replica_groups=mesh['z'=8,'x'=4,'y'=4,'core'=2] {'y','core'}, dimensions={0} | all-to-all | bytes 524288 | tf_op jit(solution)/shard_map/all_to_all | solution.py:365
  149.4 0.7 copy_bitcast_fusion
  (40 shorter events, 0.5 us)
Async XLA Ops:
  0.0 30.6 %copy-start.12 = (f32[384,256]{1,0:T(8,128)S(1)}, f32[384,256]{1,0:T(8,128)}, u32[]{:S(2)}) copy-start(f32[384,256]{1,0:T(8,128)} %param.10) | copy-start | bytes 1179652
  0.0 38.7 %copy-start.2 = (s32[8,2,32]{2,1,0:T(2,128)S(1)}, s32[8,2,32]{2,1,0:T(2,128)}, u32[]{:S(2)}) copy-start(s32[8,2,32]{2,1,0:T(2,128)} %cols.3) | copy-start | bytes 6148
  0.0 38.7 %copy-start.1 = (s32[8,2,32]{2,1,0:T(2,128)S(1)}, s32[8,2,32]{2,1,0:T(2,128)}, u32[]{:S(2)}) copy-start(s32[8,2,32]{2,1,0:T(2,128)} %rows.3) | copy-start | bytes 6148
  0.6 38.1 %copy-start.3 = (s32[3]{0:T(128)S(1)}, s32[3]{0:T(128)}, u32[]{:S(2)}) copy-start(s32[3]{0:T(128)} %pad_add_fusion.1.place) | copy-start | bytes 40
  3.1 8.3 %collective-permute-start.3 = (f32[2,8,4096]{2,1,0:T(8,128)}, f32[2,8,4096]{2,1,0:T(8,128)S(1)}, u32[]{:S(2)}, u32[]{:S(2)}) collective-permute-start(f32[2,8,4096]{2,1,0:T(8,128)} %cut_rows.1.refs_0_), channel_id=1, source_target_pairs={{0,32},{32,64},{64,96},{96,128},{128,160},{160,192},{192,224},{224... | collective-permute-start | bytes 786440 | tf_op jit(solution)/shard_map/ppermute | solution.py:253
  5.1 9.4 %collective-permute-start = (f32[2,8,4096]{2,1,0:T(8,128)}, f32[2,8,4096]{2,1,0:T(8,128)S(1)}, u32[]{:S(2)}, u32[]{:S(2)}) collective-permute-start(f32[2,8,4096]{2,1,0:T(8,128)} %cut_rows.1.refs_0_), channel_id=1, source_target_pairs={{32,0},{64,32},{96,64},{128,96},{160,128},{192,160},{224,192},{0,2... | collective-permute-start | bytes 786440 | tf_op jit(solution)/shard_map/ppermute | solution.py:258
  11.4 7.4 %collective-permute-start.4 = (f32[2,8,4096]{2,1,0:T(8,128)S(1)}, f32[2,8,4096]{2,1,0:T(8,128)S(1)}, u32[]{:S(2)}, u32[]{:S(2)}) collective-permute-start(f32[2,8,4096]{2,1,0:T(8,128)S(1)} %collective-permute-done.3.refs_6_), channel_id=1, source_target_pairs={{0,32},{32,64},{64,96},{96,128},{128,160},{160,192},{192,224},{224... | collective-permute-start | bytes 786440 | tf_op jit(solution)/shard_map/ppermute | solution.py:253
  14.5 8.4 %collective-permute-start.1 = (f32[2,8,4096]{2,1,0:T(8,128)S(1)}, f32[2,8,4096]{2,1,0:T(8,128)S(1)}, u32[]{:S(2)}, u32[]{:S(2)}) collective-permute-start(f32[2,8,4096]{2,1,0:T(8,128)S(1)} %collective-permute-done.refs_1_), channel_id=1, source_target_pairs={{32,0},{64,32},{96,64},{128,96},{160,128},{192,160},{224,192},{0,2... | collective-permute-start | bytes 786440 | tf_op jit(solution)/shard_map/ppermute | solution.py:258
  18.8 7.8 %collective-permute-start.5 = (f32[2,8,4096]{2,1,0:T(8,128)S(1)}, f32[2,8,4096]{2,1,0:T(8,128)S(1)}, u32[]{:S(2)}, u32[]{:S(2)}) collective-permute-start(f32[2,8,4096]{2,1,0:T(8,128)S(1)} %collective-permute-done.4.refs_5_), channel_id=1, source_target_pairs={{0,32},{32,64},{64,96},{96,128},{128,160},{160,192},{192,224},{224... | collective-permute-start | bytes 786440 | tf_op jit(solution)/shard_map/ppermute | solution.py:253
  22.9 7.6 %collective-permute-start.2 = (f32[2,8,4096]{2,1,0:T(8,128)S(1)}, f32[2,8,4096]{2,1,0:T(8,128)S(1)}, u32[]{:S(2)}, u32[]{:S(2)}) collective-permute-start(f32[2,8,4096]{2,1,0:T(8,128)S(1)} %collective-permute-done.1.refs_2_), channel_id=1, source_target_pairs={{32,0},{64,32},{96,64},{128,96},{160,128},{192,160},{224,192},{0,2... | collective-permute-start | bytes 786440 | tf_op jit(solution)/shard_map/ppermute | solution.py:258
  26.7 12.0 %collective-permute-start.6 = (f32[1,8,4096]{2,1,0:T(8,128)S(1)}, f32[1,8,4096]{2,1,0:T(8,128)S(1)}, u32[]{:S(2)}, u32[]{:S(2)}) collective-permute-start(f32[1,8,4096]{2,1,0:T(8,128)S(1)} %slice.60), channel_id=1, source_target_pairs={{0,32},{32,64},{64,96},{96,128},{128,160},{160,192},{192,224},{224... | collective-permute-start | bytes 393224 | tf_op jit(solution)/shard_map/ppermute | solution.py:253
  30.5 8.2 %collective-permute-start.7 = (f32[1,8,4096]{2,1,0:T(8,128)S(1)}, f32[1,8,4096]{2,1,0:T(8,128)S(1)}, u32[]{:S(2)}, u32[]{:S(2)}) collective-permute-start(f32[1,8,4096]{2,1,0:T(8,128)S(1)} %slice.61), channel_id=1, source_target_pairs={{32,0},{64,32},{96,64},{128,96},{160,128},{192,160},{224,192},{0,2... | collective-permute-start | bytes 393224 | tf_op jit(solution)/shard_map/ppermute | solution.py:258
  30.7 19.5 %collective-permute-start.8 = (f32[384,64]{1,0:T(8,128)S(1)}, f32[384,64]{1,0:T(8,128)S(1)}, u32[]{:S(2)}, u32[]{:S(2)}) collective-permute-start(f32[384,64]{1,0:T(8,128)S(1)} %get-tuple-element.31), channel_id=1, source_target_pairs={{8,0},{16,8},{24,16},{32,24},{40,32},{48,40},{56,48},{64,56},{72,6... | collective-permute-start | bytes 294920 | tf_op jit(solution)/shard_map/ppermute | solution.py:305
  36.7 13.5 %collective-permute-start.9 = (f32[384,64]{1,0:T(8,128)S(1)}, f32[384,64]{1,0:T(8,128)S(1)}, u32[]{:S(2)}, u32[]{:S(2)}) collective-permute-start(f32[384,64]{1,0:T(8,128)S(1)} %get-tuple-element.32), channel_id=1, source_target_pairs={{0,8},{8,16},{16,24},{24,32},{32,40},{40,48},{48,56},{56,64},{64,7... | collective-permute-start | bytes 294920 | tf_op jit(solution)/shard_map/ppermute | solution.py:302
  38.7 1.0 copy-start
  42.8 18.1 %all-to-all-start = ((f32[32,2,8,256]{3,2,1,0:T(8,128)}), f32[32,2,8,256]{3,2,1,0:T(8,128)S(1)}, u32[]{:S(2)}, u32[]{:S(2)}) async-start(f32[32,2,8,256]{3,2,1,0:T(8,128)} %select_rows.1), calls=%async_computation | async-start | bytes 1048576 | tf_op jit(solution)/shard_map/all_to_all | solution.py:329
  50.5 10.5 %copy-start.4 = (f32[256,256]{1,0:T(8,128)S(1)}, f32[256,256]{1,0:T(8,128)}, u32[]{:S(2)}) copy-start(f32[256,256]{1,0:T(8,128)} %amp_ref.1) | copy-start | bytes 786436
  50.5 10.5 %copy-start.5 = (f32[1,256,256]{2,1,0:T(8,128)S(1)}, f32[1,256,256]{2,1,0:T(8,128)}, u32[]{:S(2)}) copy-start(f32[1,256,256]{2,1,0:T(8,128)} %observed.1) | copy-start | bytes 786436
  53.5 1.0 copy-start.6
  54.5 1.0 copy-start.8
  55.6 1.0 copy-start.10
  61.0 1.3 copy-start.7
  62.2 1.3 copy-start.9
  63.5 1.3 copy-start.11
  99.1 8.3 %collective-permute-start.10 = (f32[4,2,8,512]{3,2,1,0:T(8,128)S(1)}, f32[4,2,8,512]{3,2,1,0:T(8,128)S(1)}, u32[]{:S(2)}, u32[]{:S(2)}) collective-permute-start(f32[4,2,8,512]{3,2,1,0:T(8,128)S(1)} %get-tuple-element.21), channel_id=1, source_target_pairs={{0,32},{32,64},{64,96},{96,128},{128,160},{160,192},{192,224},{224... | collective-permute-start | bytes 393224 | tf_op jit(solution)/shard_map/ppermute | solution.py:253
  103.7 6.2 %collective-permute-start.14 = (f32[4,2,8,512]{3,2,1,0:T(8,128)S(1)}, f32[4,2,8,512]{3,2,1,0:T(8,128)S(1)}, u32[]{:S(2)}, u32[]{:S(2)}) collective-permute-start(f32[4,2,8,512]{3,2,1,0:T(8,128)S(1)} %get-tuple-element.22), channel_id=1, source_target_pairs={{32,0},{64,32},{96,64},{128,96},{160,128},{192,160},{224,192},{0,2... | collective-permute-start | bytes 393224 | tf_op jit(solution)/shard_map/ppermute | solution.py:258
  109.9 9.2 %collective-permute-start.15 = (f32[8,2,8,512]{3,2,1,0:T(8,128)S(1)}, f32[8,2,8,512]{3,2,1,0:T(8,128)S(1)}, u32[]{:S(2)}, u32[]{:S(2)}) collective-permute-start(f32[8,2,8,512]{3,2,1,0:T(8,128)S(1)} %pad_maximum_fusion.4), channel_id=1, source_target_pairs={{32,0},{64,32},{96,64},{128,96},{160,128},{192,160},{224,192},{0,2... | collective-permute-start | bytes 786440 | tf_op jit(solution)/shard_map/ppermute | solution.py:258
  110.0 9.0 %collective-permute-start.11 = (f32[8,2,8,512]{3,2,1,0:T(8,128)S(1)}, f32[8,2,8,512]{3,2,1,0:T(8,128)S(1)}, u32[]{:S(2)}, u32[]{:S(2)}) collective-permute-start(f32[8,2,8,512]{3,2,1,0:T(8,128)S(1)} %pad_maximum_fusion.3), channel_id=1, source_target_pairs={{0,32},{32,64},{64,96},{96,128},{128,160},{160,192},{192,224},{224... | collective-permute-start | bytes 786440 | tf_op jit(solution)/shard_map/ppermute | solution.py:253
  119.2 7.6 %collective-permute-start.12 = (f32[8,2,8,512]{3,2,1,0:T(8,128)S(1)}, f32[8,2,8,512]{3,2,1,0:T(8,128)S(1)}, u32[]{:S(2)}, u32[]{:S(2)}) collective-permute-start(f32[8,2,8,512]{3,2,1,0:T(8,128)S(1)} %get-tuple-element.25), channel_id=1, source_target_pairs={{0,32},{32,64},{64,96},{96,128},{128,160},{160,192},{192,224},{224... | collective-permute-start | bytes 786440 | tf_op jit(solution)/shard_map/ppermute | solution.py:253
  122.2 7.8 %collective-permute-start.16 = (f32[8,2,8,512]{3,2,1,0:T(8,128)S(1)}, f32[8,2,8,512]{3,2,1,0:T(8,128)S(1)}, u32[]{:S(2)}, u32[]{:S(2)}) collective-permute-start(f32[8,2,8,512]{3,2,1,0:T(8,128)S(1)} %get-tuple-element.26), channel_id=1, source_target_pairs={{32,0},{64,32},{96,64},{128,96},{160,128},{192,160},{224,192},{0,2... | collective-permute-start | bytes 786440 | tf_op jit(solution)/shard_map/ppermute | solution.py:258
  130.1 6.9 %collective-permute-start.13 = (f32[8,2,8,512]{3,2,1,0:T(8,128)S(1)}, f32[8,2,8,512]{3,2,1,0:T(8,128)S(1)}, u32[]{:S(2)}, u32[]{:S(2)}) collective-permute-start(f32[8,2,8,512]{3,2,1,0:T(8,128)S(1)} %get-tuple-element.23), channel_id=1, source_target_pairs={{0,32},{32,64},{64,96},{96,128},{128,160},{160,192},{192,224},{224... | collective-permute-start | bytes 786440 | tf_op jit(solution)/shard_map/ppermute | solution.py:253
  133.1 6.4 %collective-permute-start.17 = (f32[8,2,8,512]{3,2,1,0:T(8,128)S(1)}, f32[8,2,8,512]{3,2,1,0:T(8,128)S(1)}, u32[]{:S(2)}, u32[]{:S(2)}) collective-permute-start(f32[8,2,8,512]{3,2,1,0:T(8,128)S(1)} %get-tuple-element.24), channel_id=1, source_target_pairs={{32,0},{64,32},{96,64},{128,96},{160,128},{192,160},{224,192},{0,2... | collective-permute-start | bytes 786440 | tf_op jit(solution)/shard_map/ppermute | solution.py:258

commit v3 on v2

--- a/solution.py
+++ b/solution.py
@@ -176,9 +176,20 @@
 
 
 def gradient_kernel(
-    turns, received, amp_ref, observed, forward_h, forward_l, inverse_h, inverse_l, spec_re, spec_im,
-    out, pupil_re, pupil_im, far_re, far_im, mix_h, mix_l, wide_h, wide_l,
+    turns, received, amp_ref, observed, far_fh, far_fl, far_ih, far_il, spec_re, spec_im, out,
+    forward_h, forward_l, inverse_h, inverse_l, pupil_re, pupil_im, far_re, far_im,
+    mix_h, mix_l, wide_h, wide_l, sems,
 ):
+    copies = [
+        pltpu.make_async_copy(source, target, sems.at[index])
+        for index, (source, target) in enumerate(
+            (
+                (far_fh, forward_h), (far_fl, forward_l), (far_ih, inverse_h), (far_il, inverse_l),
+            )
+        )
+    ]
+    for copy in copies:
+        copy.start()
     forward, inverse = Pair(forward_h, forward_l), Pair(inverse_h, inverse_l)
     mix, wide = Pair(mix_h, mix_l), Pair(wide_h, wide_l)
     phases = None
@@ -192,6 +203,8 @@
     sine, cosine = sine_cosine(phases)
     pupil_re[...] = amplitude * cosine
     pupil_im[...] = amplitude * sine
+    for copy in copies:
+        copy.wait()
     half = product(forward[ALL, LOW], split(pupil_re[...])) + product(
         forward[ALL, HIGH], split(pupil_im[...])
     )
@@ -234,6 +247,7 @@
 
 SMEM = pl.BlockSpec(memory_space=pltpu.SMEM)
 VMEM = pl.BlockSpec(memory_space=pltpu.VMEM)
+ANY = pl.BlockSpec(memory_space=pl.ANY)
 
 
 def limit(mib):
@@ -246,6 +260,33 @@
 
 def f32(*shape):
     return jax.ShapeDtypeStruct(shape, jnp.float32)
+
+
+def gradient_call(*operands, name="gradient"):
+    return pl.pallas_call(
+        gradient_kernel,
+        out_shape=f32(32, 2, 8, CORE),
+        in_specs=[SMEM] + [VMEM] * 3 + [ANY] * 4 + [VMEM] * 2,
+        out_specs=VMEM,
+        scratch_shapes=[
+            pltpu.VMEM((2 * SPAN, 2 * SPAN), jnp.bfloat16),
+            pltpu.VMEM((2 * SPAN, 2 * SPAN), jnp.bfloat16),
+            pltpu.VMEM((2 * SPAN, 2 * SPAN), jnp.bfloat16),
+            pltpu.VMEM((2 * SPAN, 2 * SPAN), jnp.bfloat16),
+            pltpu.VMEM((CORE, CORE), jnp.float32),
+            pltpu.VMEM((CORE, CORE), jnp.float32),
+            pltpu.VMEM((SPAN, SPAN), jnp.float32),
+            pltpu.VMEM((SPAN, SPAN), jnp.float32),
+            pltpu.VMEM((2 * SPAN, HALF), jnp.bfloat16),
+            pltpu.VMEM((2 * SPAN, HALF), jnp.bfloat16),
+            pltpu.VMEM((2 * SPAN, SPAN), jnp.bfloat16),
+            pltpu.VMEM((2 * SPAN, SPAN), jnp.bfloat16),
+            pltpu.SemaphoreType.DMA((4,)),
+        ],
+        compiler_params=limit(61),
+        cost_estimate=cost(3 * 2 * 1222 * 10**6, 7 * 10**6),
+        name=name,
+    )(*operands)
 
 
 def up(values):
@@ -258,13 +299,14 @@
     return lax.ppermute(values, "z", [((i + 1) % count, i) for i in range(count)])
 
 
-def ring_gather(own):
+def ring_gather(own, beside):
     rise, fall = [own], [own]
-    for _ in range(3):
+    for step in range(3):
         rise.append(up(rise[-1]))
         fall.append(down(fall[-1]))
+    rise[3], fall[3], beside = lax.optimization_barrier((rise[3], fall[3], beside))
     halves = [up(rise[3][0:1]), down(fall[3][1:2])]
-    return fall + [rise[3], rise[2], rise[1]] + halves
+    return fall + [rise[3], rise[2], rise[1]] + halves, beside
 
 
 def ring_scatter(partial, above, below):
@@ -291,31 +333,33 @@
     own = pl.pallas_call(
         cut_kernel,
         out_shape=f32(2, 8, screens.shape[2]),
-        in_specs=[SMEM, pl.BlockSpec(memory_space=pltpu.HBM)],
+        in_specs=[SMEM, ANY],
         out_specs=VMEM,
         scratch_shapes=[pltpu.SemaphoreType.DMA],
         compiler_params=limit(61),
         name="cut_rows",
     )(place, screens)
-    chunks = ring_gather(own)
     ends = patches - 1
+    own, strip = lax.optimization_barrier((own, object_strip))
     left_tail = lax.ppermute(
-        object_strip[:, CORE - HALO :], ("z", "x"), [(i, i + 1) for i in range(ends)]
-    )
-    right_head = lax.ppermute(object_strip[:, :HALO], ("z", "x"), [(i + 1, i) for i in range(ends)])
+        strip[:, CORE - HALO :], ("z", "x"), [(i, i + 1) for i in range(ends)]
+    )
+    right_head = lax.ppermute(strip[:, :HALO], ("z", "x"), [(i + 1, i) for i in range(ends)])
     window = jnp.concatenate([object_strip, right_head, left_tail], axis=1)
     window = jnp.concatenate([window[HALO:], window[:HALO]], axis=0)
     big = jax.ShapeDtypeStruct((2 * SPAN, 2 * SPAN), jnp.bfloat16)
-    forward_h, forward_l, inverse_h, inverse_l, spec_re, spec_im = pl.pallas_call(
+    object_parts = pl.pallas_call(
         object_kernel,
         out_shape=[big] * 4 + [f32(SPAN, HALF)] * 2,
         in_specs=[VMEM],
         out_specs=[VMEM] * 6,
-        compiler_params=limit(20),
+        compiler_params=limit(61),
         cost_estimate=cost(3 * 2 * 226 * 10**6, 7 * 10**6),
         name="object_spectrum",
     )(window)
 
+    chunks, object_parts = ring_gather(own, object_parts)
+    forward_h, forward_l, inverse_h, inverse_l, spec_re, spec_im = object_parts
     sent = pl.pallas_call(
         select_kernel,
         out_shape=f32(32, 2, 8, CORE),
@@ -331,25 +375,9 @@
     row_turns = lax.dynamic_slice(row_offsets, (frame_id, 0, patch), (1, 2, 1))[0, :, 0] % CORE
     col_turns = lax.dynamic_slice(col_offsets, (frame_id, 0, patch), (1, 2, 1))[0, :, 0] % CORE
     turns = jnp.stack([row_turns, col_turns], axis=1)
-    placed = pl.pallas_call(
-        gradient_kernel,
-        out_shape=f32(32, 2, 8, CORE),
-        in_specs=[SMEM] + [VMEM] * 9,
-        out_specs=VMEM,
-        scratch_shapes=[
-            pltpu.VMEM((CORE, CORE), jnp.float32),
-            pltpu.VMEM((CORE, CORE), jnp.float32),
-            pltpu.VMEM((SPAN, SPAN), jnp.float32),
-            pltpu.VMEM((SPAN, SPAN), jnp.float32),
-            pltpu.VMEM((2 * SPAN, HALF), jnp.bfloat16),
-            pltpu.VMEM((2 * SPAN, HALF), jnp.bfloat16),
-            pltpu.VMEM((2 * SPAN, SPAN), jnp.bfloat16),
-            pltpu.VMEM((2 * SPAN, SPAN), jnp.bfloat16),
-        ],
-        compiler_params=limit(20),
-        cost_estimate=cost(3 * 2 * 1222 * 10**6, 7 * 10**6),
-        name="gradient",
-    )(turns, received, amplitude, observed, forward_h, forward_l, inverse_h, inverse_l, spec_re, spec_im)
+    placed = gradient_call(
+        turns, received, amplitude, observed, forward_h, forward_l, inverse_h, inverse_l, spec_re, spec_im
+    )
     returned = lax.all_to_all(placed, SLAB, split_axis=0, concat_axis=0, tiled=True)
 
     partial, above, below = pl.pallas_call(

time: 151 us -> 155 us (1.026)
  waiting for transfers between devices: 46.2 us -> 56.9 us
  local copies, waits for them, and re-layouts: 8.76 us -> 1.73 us
  starting transfers between devices: 40.8 us -> 34.1 us
  Pallas kernels: 27.9 us -> 33.6 us
    ppermute x8, starting transfers between devices: 25.4 us -> 17.5 us  [up(): lax.ppermute(values, 'z', [(i, (i + 1) % count) for i in range(count)])]
    unnamed x26 -> x12, local copies, waits for them, and re-layouts: 7.86 us -> 0.83 us
    ppermute x2, waiting for transfers between devices: 0.01 us -> 6.42 us  [the longest x1 6.42 us: body(): lax.ppermute(strip[:, CORE - HALO:], ('z', 'x'), [(i, i + 1) for i in ran...]
    all_to_all x1, waiting for transfers between devices: 4.36 us -> 10.2 us  [body(): lax.all_to_all(sent, SLAB, split_axis=0, concat_axis=0, tiled=True)]
    ppermute x8, waiting for transfers between devices: 26.4 us -> 22 us  [up(): lax.ppermute(values, 'z', [(i, (i + 1) % count) for i in range(count)])]
    ppermute x8, starting transfers between devices: 0.29 us -> 4.29 us  [down(): lax.ppermute(values, 'z', [((i + 1) % count, i) for i in range(count)])]
    pallas_call x1, Pallas kernels: 15.7 us -> 19.2 us  [gradient_call(): pl.pallas_call(gradient_kernel, out_shape=f32(32, 2, 8, CORE), in_specs=[...]
    ppermute x8, waiting for transfers between devices: 15.4 us -> 18.4 us  [down(): lax.ppermute(values, 'z', [((i + 1) % count, i) for i in range(count)])]
  transfers between devices with their start and end apart: 19 -> 19, of which waited for: 14 -> 15; matrix products, arithmetic and copies ran while one was open for 0% -> 1% of each run, Pallas kernels for 4% -> 4%
where the time goes in v3:
time: 155 us; the launch traced here: 154 us
  waiting for transfers between devices  56.9 us (37%)
  starting transfers between devices  34.1 us (22%)
  Pallas kernels  33.6 us (22%)
  blocking collectives  25.1 us (16%)
  other arithmetic  2.64 us (2%)
  local copies, waits for them, and re-layouts  1.73 us (1%)
    ppermute x8, waiting for transfers between devices, up(): lax.ppermute(values, 'z', [(i, (i + 1) % count) for i in range(count)])  22 us
    pallas_call x1, Pallas kernels, gradient_call(): pl.pallas_call(gradient_kernel, out_shape=f32(32, 2, 8, CORE), in_specs=[...  19.2 us
    ppermute x8, waiting for transfers between devices, down(): lax.ppermute(values, 'z', [((i + 1) % count, i) for i in range(count)])  18.4 us
    ppermute x8, starting transfers between devices, up(): lax.ppermute(values, 'z', [(i, (i + 1) % count) for i in range(count)])  17.5 us
    all_to_all x1, blocking collectives, body(): lax.all_to_all(placed, SLAB, split_axis=0, concat_axis=0, tiled=True)  15.2 us
    all_to_all x1, waiting for transfers between devices, body(): lax.all_to_all(sent, SLAB, split_axis=0, concat_axis=0, tiled=True)  10.2 us
    all_to_all x1, blocking collectives, body(): lax.all_to_all(summed, FRAME, split_axis=0, concat_axis=0, tiled=True)  9.91 us
    ppermute x1, waiting for transfers between devices, body(): lax.ppermute(strip[:, CORE - HALO:], ('z', 'x'), [(i, i + 1) for i in ran...  6.42 us
  transfers between devices with their start and end apart: 19, of which 15 were waited for; matrix products, arithmetic and copies ran while one was open for 1% of the time, Pallas kernels for 4%

profile of v3, /device:TPU:64, one launch (start us, length us, event | category | flops | bytes accessed | tf_op | source)
XLA Modules:
  0.0 154.4 jit_solution(4459166526085961231)
XLA Ops:
  0.0 0.6 pad_add_fusion.1.place
  0.6 2.3 %cut_rows.1.refs_0_ = f32[2,8,4096]{2,1,0:T(8,128)} custom-call(s32[3]{0:T(128)} %pad_add_fusion.1.place, f32[2,64,4096]{2,1,0:T(8,128)} %screens.1), custom_call_target="tpu_custom_call" | custom-call | tf_op jit(solution)/shard_map/cut_rows/pallas_call | solution.py:333
  2.9 2.0 %collective-permute-start.2 = (f32[2,8,4096]{2,1,0:T(8,128)}, f32[2,8,4096]{2,1,0:T(8,128)S(1)}, u32[]{:S(2)}, u32[]{:S(2)}) collective-permute-start(f32[2,8,4096]{2,1,0:T(8,128)} %cut_rows.1.refs_0_), channel_id=1, source_target_pairs={{0,32},{32,64},{64,96},{96,128},{128,160},{160,192},{192,224},{224... | collective-permute-start | bytes 786440 | tf_op jit(solution)/shard_map/ppermute | solution.py:294
  4.9 0.1 collective-permute-start
  5.0 6.2 %collective-permute-done.2.refs_6_ = f32[2,8,4096]{2,1,0:T(8,128)S(1)} collective-permute-done((f32[2,8,4096]{2,1,0:T(8,128)}, f32[2,8,4096]{2,1,0:T(8,128)S(1)}, u32[]{:S(2)}, u32[]{:S(2)}) %collective-permute-start.2) | collective-permute-done | bytes 262176 | tf_op jit(solution)/shard_map/ppermute | solution.py:294
  11.2 2.7 %collective-permute-start.3 = (f32[2,8,4096]{2,1,0:T(8,128)S(1)}, f32[2,8,4096]{2,1,0:T(8,128)S(1)}, u32[]{:S(2)}, u32[]{:S(2)}) collective-permute-start(f32[2,8,4096]{2,1,0:T(8,128)S(1)} %collective-permute-done.2.refs_6_), channel_id=1, source_target_pairs={{0,32},{32,64},{64,96},{96,128},{128,160},{160,192},{192,224},{224... | collective-permute-start | bytes 786440 | tf_op jit(solution)/shard_map/ppermute | solution.py:294
  13.9 0.4 collective-permute-done.refs_1_
  14.3 0.1 fusion.4
  14.4 5.4 %collective-permute-start.6 = (f32[384,64]{1,0:T(8,128)S(1)}, f32[384,64]{1,0:T(8,128)S(1)}, u32[]{:S(2)}, u32[]{:S(2)}) collective-permute-start(f32[384,64]{1,0:T(8,128)S(1)} %get-tuple-element.51), channel_id=1, source_target_pairs={{8,0},{16,8},{24,16},{32,24},{40,32},{48,40},{56,48},{64,56},{72,6... | collective-permute-start | bytes 294920 | tf_op jit(solution)/shard_map/ppermute | solution.py:347
  19.8 1.9 %collective-permute-start.7 = (f32[384,64]{1,0:T(8,128)S(1)}, f32[384,64]{1,0:T(8,128)S(1)}, u32[]{:S(2)}, u32[]{:S(2)}) collective-permute-start(f32[384,64]{1,0:T(8,128)S(1)} %get-tuple-element.52), channel_id=1, source_target_pairs={{0,8},{8,16},{16,24},{24,32},{32,40},{40,48},{48,56},{56,64},{64,7... | collective-permute-start | bytes 294920 | tf_op jit(solution)/shard_map/ppermute | solution.py:344
  21.8 1.8 %collective-permute-start.4 = (f32[2,8,4096]{2,1,0:T(8,128)S(1)}, f32[2,8,4096]{2,1,0:T(8,128)S(1)}, u32[]{:S(2)}, u32[]{:S(2)}) collective-permute-start(f32[2,8,4096]{2,1,0:T(8,128)S(1)} %collective-permute-done.3.refs_5_), channel_id=1, source_target_pairs={{0,32},{32,64},{64,96},{96,128},{128,160},{160,192},{192,224},{224... | collective-permute-start | bytes 786440 | tf_op jit(solution)/shard_map/ppermute | solution.py:294
  23.6 1.1 collective-permute-done.1.refs_2_
  24.7 0.5 collective-permute-start.5
  25.2 6.4 %collective-permute-done.7 = f32[384,64]{1,0:T(8,128)S(1)} collective-permute-done((f32[384,64]{1,0:T(8,128)S(1)}, f32[384,64]{1,0:T(8,128)S(1)}, u32[]{:S(2)}, u32[]{:S(2)}) %collective-permute-start.7) | collective-permute-done | bytes 98336 | tf_op jit(solution)/shard_map/ppermute | solution.py:344
  31.6 0.1 pad_maximum_fusion.2
  31.8 0.9 fusion.window
  32.7 5.4 %object_spectrum.1 = (bf16[768,768]{1,0:T(8,128)(2,1)}, bf16[768,768]{1,0:T(8,128)(2,1)}, bf16[768,768]{1,0:T(8,128)(2,1)}, bf16[768,768]{1,0:T(8,128)(2,1)}, f32[384,256]{1,0:T(8,128)}, /*index=5*/f32[384,256]{1,0:T(8,128)}) custom-call(f32[384,384]{1,0:T(8,128)} %fusion.window), custom_call_target="tpu_custom_call" | custom-call | flops 1356000000 | bytes 7000000 | tf_op jit(solution)/shard_map/object_spectrum/pallas_call | solution.py:351
  38.1 0.1 collective-permute-start.8
  38.2 3.3 %collective-permute-start.9 = (f32[1,8,4096]{2,1,0:T(8,128)S(1)}, f32[1,8,4096]{2,1,0:T(8,128)S(1)}, u32[]{:S(2)}, u32[]{:S(2)}) collective-permute-start(f32[1,8,4096]{2,1,0:T(8,128)S(1)} %slice.50), channel_id=1, source_target_pairs={{32,0},{64,32},{96,64},{128,96},{160,128},{192,160},{224,192},{0,2... | collective-permute-start | bytes 393224 | tf_op jit(solution)/shard_map/ppermute | solution.py:299
  41.5 2.9 %collective-permute-done.8.refs_7_ = f32[1,8,4096]{2,1,0:T(8,128)S(1)} collective-permute-done((f32[1,8,4096]{2,1,0:T(8,128)S(1)}, f32[1,8,4096]{2,1,0:T(8,128)S(1)}, u32[]{:S(2)}, u32[]{:S(2)}) %collective-permute-start.8) | collective-permute-done | bytes 131104 | tf_op jit(solution)/shard_map/ppermute | solution.py:294
  44.4 3.1 %collective-permute-done.9.refs_8_ = f32[1,8,4096]{2,1,0:T(8,128)S(1)} collective-permute-done((f32[1,8,4096]{2,1,0:T(8,128)S(1)}, f32[1,8,4096]{2,1,0:T(8,128)S(1)}, u32[]{:S(2)}, u32[]{:S(2)}) %collective-permute-start.9) | collective-permute-done | bytes 131104 | tf_op jit(solution)/shard_map/ppermute | solution.py:299
  47.6 3.2 %select_rows.1 = f32[32,2,8,256]{3,2,1,0:T(8,128)} custom-call(s32[3]{0:T(128)S(1)} %copy-done.3, s32[8,2,32]{2,1,0:T(2,128)S(1)} %copy-done.1, s32[8,2,32]{2,1,0:T(2,128)S(1)} %copy-done.2, f32[2,8,4096]{2,1,0:T(8,128)S(1)} %copy-done, f32[2,8,4096]{2,1,0:T(8,128)S(1)} %collective-permute-done.refs_1_, f32[2,8,4096]{2,1,0:T(8,128)S(1)} %collective-permute-done.1.refs_2_, ...), custom_call_target="tpu_custom_call" | custom-call | bytes 3000000 | tf_op jit(solution)/shard_map/select_rows/pallas_call | solution.py:363
  50.7 5.0 %all-to-all-start = ((f32[32,2,8,256]{3,2,1,0:T(8,128)}), f32[32,2,8,256]{3,2,1,0:T(8,128)S(1)}, u32[]{:S(2)}, u32[]{:S(2)}) async-start(f32[32,2,8,256]{3,2,1,0:T(8,128)} %select_rows.1), calls=%async_computation | async-start | bytes 1048576 | tf_op jit(solution)/shard_map/all_to_all | solution.py:373
  55.8 0.1 and_select_fusion
  55.9 0.6 pad_add_fusion.turns
  56.5 10.2 %all-to-all-done.received = f32[32,2,8,256]{3,2,1,0:T(8,128)S(1)} async-done(((f32[32,2,8,256]{3,2,1,0:T(8,128)}), f32[32,2,8,256]{3,2,1,0:T(8,128)S(1)}, u32[]{:S(2)}, u32[]{:S(2)}) %all-to-all-start) | async-done | bytes 524320 | tf_op jit(solution)/shard_map/all_to_all | solution.py:373
  66.7 0.8 copy-done.5
  67.5 19.2 %gradient.1 = f32[32,2,8,256]{3,2,1,0:T(8,128)} custom-call(s32[2,2]{1,0:T(2,128)} %pad_add_fusion.turns, f32[32,2,8,256]{3,2,1,0:T(8,128)} %copy-done.5, f32[256,256]{1,0:T(8,128)} %amp_ref.1, f32[1,256,256]{2,1,0:T(8,128)} %observed.1, bf16[768,768]{1,0:T(8,128)(2,1)} %get-tuple-element.34.far_fh, bf16[768,768]{1,0:T(8,128)(2,1)} %get-tuple-element.35.far_fl, ...), custom_call_target="tpu_custom_call" | custom-call | flops 7331999744 | bytes 7000000 | tf_op jit(solution)/shard_map/gradient/pallas_call | solution.py:266
  86.7 15.2 %all_to_all.15.values = f32[32,2,8,256]{3,2,1,0:T(8,128)S(1)} all-to-all(f32[32,2,8,256]{3,2,1,0:T(8,128)} %gradient.1), channel_id=1, replica_groups=mesh['z'=8,'x'=4,'y'=4,'core'=2] {'x','y','core'}, dimensions={0} | all-to-all | bytes 1048576 | tf_op jit(solution)/shard_map/all_to_all | solution.py:381
  101.9 3.5 %scatter_rows.1 = (f32[8,8,2,8,512]{4,3,2,1,0:T(8,128)S(1)}, f32[4,2,8,512]{3,2,1,0:T(8,128)S(1)}, f32[4,2,8,512]{3,2,1,0:T(8,128)S(1)}) custom-call(s32[3]{0:T(128)S(1)} %copy-done.3, s32[8,2,32]{2,1,0:T(2,128)S(1)} %copy-done.1, s32[8,2,32]{2,1,0:T(2,128)S(1)} %copy-done.2, f32[32,2,8,256]{3,2,1,0:T(8,128)S(1)} %all_to_all.15.values), custom_call_target="tpu_custom_call" | custom-call | bytes 3000000 | tf_op jit(solution)/shard_map/scatter_rows/pallas_call | solution.py:383
  105.4 3.3 %collective-permute-start.10 = (f32[4,2,8,512]{3,2,1,0:T(8,128)S(1)}, f32[4,2,8,512]{3,2,1,0:T(8,128)S(1)}, u32[]{:S(2)}, u32[]{:S(2)}) collective-permute-start(f32[4,2,8,512]{3,2,1,0:T(8,128)S(1)} %get-tuple-element.41), channel_id=1, source_target_pairs={{0,32},{32,64},{64,96},{96,128},{128,160},{160,192},{192,224},{224... | collective-permute-start | bytes 393224 | tf_op jit(solution)/shard_map/ppermute | solution.py:294
  108.8 3.7 %collective-permute-done.10 = f32[4,2,8,512]{3,2,1,0:T(8,128)S(1)} collective-permute-done((f32[4,2,8,512]{3,2,1,0:T(8,128)S(1)}, f32[4,2,8,512]{3,2,1,0:T(8,128)S(1)}, u32[]{:S(2)}, u32[]{:S(2)}) %collective-permute-start.10) | collective-permute-done | bytes 131104 | tf_op jit(solution)/shard_map/ppermute | solution.py:294
  112.5 2.2 %collective-permute-done.14 = f32[4,2,8,512]{3,2,1,0:T(8,128)S(1)} collective-permute-done((f32[4,2,8,512]{3,2,1,0:T(8,128)S(1)}, f32[4,2,8,512]{3,2,1,0:T(8,128)S(1)}, u32[]{:S(2)}, u32[]{:S(2)}) %collective-permute-start.14) | collective-permute-done | bytes 131104 | tf_op jit(solution)/shard_map/ppermute | solution.py:299
  114.7 0.4 collective-permute-start.15
  115.1 2.0 %collective-permute-start.11 = (f32[8,2,8,512]{3,2,1,0:T(8,128)S(1)}, f32[8,2,8,512]{3,2,1,0:T(8,128)S(1)}, u32[]{:S(2)}, u32[]{:S(2)}) collective-permute-start(f32[8,2,8,512]{3,2,1,0:T(8,128)S(1)} %pad_maximum_fusion.3), channel_id=1, source_target_pairs={{0,32},{32,64},{64,96},{96,128},{128,160},{160,192},{192,224},{224... | collective-permute-start | bytes 786440 | tf_op jit(solution)/shard_map/ppermute | solution.py:294
  117.2 5.6 %collective-permute-done.15 = f32[8,2,8,512]{3,2,1,0:T(8,128)S(1)} collective-permute-done((f32[8,2,8,512]{3,2,1,0:T(8,128)S(1)}, f32[8,2,8,512]{3,2,1,0:T(8,128)S(1)}, u32[]{:S(2)}, u32[]{:S(2)}) %collective-permute-start.15) | collective-permute-done | bytes 262176 | tf_op jit(solution)/shard_map/ppermute | solution.py:299
  122.8 0.5 collective-permute-done.11
  123.3 0.1 bitcast_add_fusion.3
  123.4 2.5 %collective-permute-start.12 = (f32[8,2,8,512]{3,2,1,0:T(8,128)S(1)}, f32[8,2,8,512]{3,2,1,0:T(8,128)S(1)}, u32[]{:S(2)}, u32[]{:S(2)}) collective-permute-start(f32[8,2,8,512]{3,2,1,0:T(8,128)S(1)} %get-tuple-element.45), channel_id=1, source_target_pairs={{0,32},{32,64},{64,96},{96,128},{128,160},{160,192},{192,224},{224... | collective-permute-start | bytes 786440 | tf_op jit(solution)/shard_map/ppermute | solution.py:294
  125.9 4.8 %collective-permute-done.12 = f32[8,2,8,512]{3,2,1,0:T(8,128)S(1)} collective-permute-done((f32[8,2,8,512]{3,2,1,0:T(8,128)S(1)}, f32[8,2,8,512]{3,2,1,0:T(8,128)S(1)}, u32[]{:S(2)}, u32[]{:S(2)}) %collective-permute-start.12) | collective-permute-done | bytes 262176 | tf_op jit(solution)/shard_map/ppermute | solution.py:294
  130.7 3.5 %collective-permute-done.16 = f32[8,2,8,512]{3,2,1,0:T(8,128)S(1)} collective-permute-done((f32[8,2,8,512]{3,2,1,0:T(8,128)S(1)}, f32[8,2,8,512]{3,2,1,0:T(8,128)S(1)}, u32[]{:S(2)}, u32[]{:S(2)}) %collective-permute-start.16) | collective-permute-done | bytes 262176 | tf_op jit(solution)/shard_map/ppermute | solution.py:299
  134.2 0.1 bitcast_add_fusion.2
  134.3 3.0 %collective-permute-start.13 = (f32[8,2,8,512]{3,2,1,0:T(8,128)S(1)}, f32[8,2,8,512]{3,2,1,0:T(8,128)S(1)}, u32[]{:S(2)}, u32[]{:S(2)}) collective-permute-start(f32[8,2,8,512]{3,2,1,0:T(8,128)S(1)} %get-tuple-element.43), channel_id=1, source_target_pairs={{0,32},{32,64},{64,96},{96,128},{128,160},{160,192},{192,224},{224... | collective-permute-start | bytes 786440 | tf_op jit(solution)/shard_map/ppermute | solution.py:294
  137.3 3.9 %collective-permute-done.13 = f32[8,2,8,512]{3,2,1,0:T(8,128)S(1)} collective-permute-done((f32[8,2,8,512]{3,2,1,0:T(8,128)S(1)}, f32[8,2,8,512]{3,2,1,0:T(8,128)S(1)}, u32[]{:S(2)}, u32[]{:S(2)}) %collective-permute-start.13) | collective-permute-done | bytes 262176 | tf_op jit(solution)/shard_map/ppermute | solution.py:294
  141.2 2.5 %collective-permute-done.17 = f32[8,2,8,512]{3,2,1,0:T(8,128)S(1)} collective-permute-done((f32[8,2,8,512]{3,2,1,0:T(8,128)S(1)}, f32[8,2,8,512]{3,2,1,0:T(8,128)S(1)}, u32[]{:S(2)}, u32[]{:S(2)}) %collective-permute-start.17) | collective-permute-done | bytes 262176 | tf_op jit(solution)/shard_map/ppermute | solution.py:299
  143.7 0.1 fusion.1
  143.8 9.9 %all_to_all.16 = f32[8,2,8,512]{3,2,1,0:T(8,128)S(1)} all-to-all(f32[8,2,8,512]{3,2,1,0:T(8,128)S(1)} %fusion.1), channel_id=1, replica_groups=mesh['z'=8,'x'=4,'y'=4,'core'=2] {'y','core'}, dimensions={0} | all-to-all | bytes 524288 | tf_op jit(solution)/shard_map/all_to_all | solution.py:393
  153.7 0.7 copy_bitcast_fusion
  (26 shorter events, 0.2 us)
Async XLA Ops:
  0.0 14.3 %copy-start.4 = (f32[384,256]{1,0:T(8,128)S(1)}, f32[384,256]{1,0:T(8,128)}, u32[]{:S(2)}) copy-start(f32[384,256]{1,0:T(8,128)} %param.10) | copy-start | bytes 1179652
  2.9 8.3 %collective-permute-start.2 = (f32[2,8,4096]{2,1,0:T(8,128)}, f32[2,8,4096]{2,1,0:T(8,128)S(1)}, u32[]{:S(2)}, u32[]{:S(2)}) collective-permute-start(f32[2,8,4096]{2,1,0:T(8,128)} %cut_rows.1.refs_0_), channel_id=1, source_target_pairs={{0,32},{32,64},{64,96},{96,128},{128,160},{160,192},{192,224},{224... | collective-permute-start | bytes 786440 | tf_op jit(solution)/shard_map/ppermute | solution.py:294
  4.9 9.4 %collective-permute-start = (f32[2,8,4096]{2,1,0:T(8,128)}, f32[2,8,4096]{2,1,0:T(8,128)S(1)}, u32[]{:S(2)}, u32[]{:S(2)}) collective-permute-start(f32[2,8,4096]{2,1,0:T(8,128)} %cut_rows.1.refs_0_), channel_id=1, source_target_pairs={{32,0},{64,32},{96,64},{128,96},{160,128},{192,160},{224,192},{0,2... | collective-permute-start | bytes 786440 | tf_op jit(solution)/shard_map/ppermute | solution.py:299
  11.2 10.5 %collective-permute-start.3 = (f32[2,8,4096]{2,1,0:T(8,128)S(1)}, f32[2,8,4096]{2,1,0:T(8,128)S(1)}, u32[]{:S(2)}, u32[]{:S(2)}) collective-permute-start(f32[2,8,4096]{2,1,0:T(8,128)S(1)} %collective-permute-done.2.refs_6_), channel_id=1, source_target_pairs={{0,32},{32,64},{64,96},{96,128},{128,160},{160,192},{192,224},{224... | collective-permute-start | bytes 786440 | tf_op jit(solution)/shard_map/ppermute | solution.py:294
  14.3 10.4 %collective-permute-start.1 = (f32[2,8,4096]{2,1,0:T(8,128)S(1)}, f32[2,8,4096]{2,1,0:T(8,128)S(1)}, u32[]{:S(2)}, u32[]{:S(2)}) collective-permute-start(f32[2,8,4096]{2,1,0:T(8,128)S(1)} %collective-permute-done.refs_1_), channel_id=1, source_target_pairs={{32,0},{64,32},{96,64},{128,96},{160,128},{192,160},{224,192},{0,2... | collective-permute-start | bytes 786440 | tf_op jit(solution)/shard_map/ppermute | solution.py:299
  14.4 10.7 %collective-permute-start.6 = (f32[384,64]{1,0:T(8,128)S(1)}, f32[384,64]{1,0:T(8,128)S(1)}, u32[]{:S(2)}, u32[]{:S(2)}) collective-permute-start(f32[384,64]{1,0:T(8,128)S(1)} %get-tuple-element.51), channel_id=1, source_target_pairs={{8,0},{16,8},{24,16},{32,24},{40,32},{48,40},{56,48},{64,56},{72,6... | collective-permute-start | bytes 294920 | tf_op jit(solution)/shard_map/ppermute | solution.py:347
  19.8 11.8 %collective-permute-start.7 = (f32[384,64]{1,0:T(8,128)S(1)}, f32[384,64]{1,0:T(8,128)S(1)}, u32[]{:S(2)}, u32[]{:S(2)}) collective-permute-start(f32[384,64]{1,0:T(8,128)S(1)} %get-tuple-element.52), channel_id=1, source_target_pairs={{0,8},{8,16},{16,24},{24,32},{32,40},{40,48},{48,56},{56,64},{64,7... | collective-permute-start | bytes 294920 | tf_op jit(solution)/shard_map/ppermute | solution.py:344
  21.8 16.3 %collective-permute-start.4 = (f32[2,8,4096]{2,1,0:T(8,128)S(1)}, f32[2,8,4096]{2,1,0:T(8,128)S(1)}, u32[]{:S(2)}, u32[]{:S(2)}) collective-permute-start(f32[2,8,4096]{2,1,0:T(8,128)S(1)} %collective-permute-done.3.refs_5_), channel_id=1, source_target_pairs={{0,32},{32,64},{64,96},{96,128},{128,160},{160,192},{192,224},{224... | collective-permute-start | bytes 786440 | tf_op jit(solution)/shard_map/ppermute | solution.py:294
  24.7 13.4 %collective-permute-start.5 = (f32[2,8,4096]{2,1,0:T(8,128)S(1)}, f32[2,8,4096]{2,1,0:T(8,128)S(1)}, u32[]{:S(2)}, u32[]{:S(2)}) collective-permute-start(f32[2,8,4096]{2,1,0:T(8,128)S(1)} %collective-permute-done.1.refs_2_), channel_id=1, source_target_pairs={{32,0},{64,32},{96,64},{128,96},{160,128},{192,160},{224,192},{0,2... | collective-permute-start | bytes 786440 | tf_op jit(solution)/shard_map/ppermute | solution.py:299
  32.7 14.9 %copy-start = (f32[2,8,4096]{2,1,0:T(8,128)S(1)}, f32[2,8,4096]{2,1,0:T(8,128)}, u32[]{:S(2)}) copy-start(f32[2,8,4096]{2,1,0:T(8,128)} %cut_rows.1.refs_0_) | copy-start | bytes 786436
  32.7 14.9 %copy-start.1 = (s32[8,2,32]{2,1,0:T(2,128)S(1)}, s32[8,2,32]{2,1,0:T(2,128)}, u32[]{:S(2)}) copy-start(s32[8,2,32]{2,1,0:T(2,128)} %rows.3) | copy-start | bytes 6148
  32.7 14.9 %copy-start.2 = (s32[8,2,32]{2,1,0:T(2,128)S(1)}, s32[8,2,32]{2,1,0:T(2,128)}, u32[]{:S(2)}) copy-start(s32[8,2,32]{2,1,0:T(2,128)} %cols.3) | copy-start | bytes 6148
  32.7 14.9 %copy-start.3 = (s32[3]{0:T(128)S(1)}, s32[3]{0:T(128)}, u32[]{:S(2)}) copy-start(s32[3]{0:T(128)} %pad_add_fusion.1.place) | copy-start | bytes 40
  38.1 6.3 %collective-permute-start.8 = (f32[1,8,4096]{2,1,0:T(8,128)S(1)}, f32[1,8,4096]{2,1,0:T(8,128)S(1)}, u32[]{:S(2)}, u32[]{:S(2)}) collective-permute-start(f32[1,8,4096]{2,1,0:T(8,128)S(1)} %slice.49), channel_id=1, source_target_pairs={{0,32},{32,64},{64,96},{96,128},{128,160},{160,192},{192,224},{224... | collective-permute-start | bytes 393224 | tf_op jit(solution)/shard_map/ppermute | solution.py:294
  38.2 9.3 %collective-permute-start.9 = (f32[1,8,4096]{2,1,0:T(8,128)S(1)}, f32[1,8,4096]{2,1,0:T(8,128)S(1)}, u32[]{:S(2)}, u32[]{:S(2)}) collective-permute-start(f32[1,8,4096]{2,1,0:T(8,128)S(1)} %slice.50), channel_id=1, source_target_pairs={{32,0},{64,32},{96,64},{128,96},{160,128},{192,160},{224,192},{0,2... | collective-permute-start | bytes 393224 | tf_op jit(solution)/shard_map/ppermute | solution.py:299
  50.7 15.9 %all-to-all-start = ((f32[32,2,8,256]{3,2,1,0:T(8,128)}), f32[32,2,8,256]{3,2,1,0:T(8,128)S(1)}, u32[]{:S(2)}, u32[]{:S(2)}) async-start(f32[32,2,8,256]{3,2,1,0:T(8,128)} %select_rows.1), calls=%async_computation | async-start | bytes 1048576 | tf_op jit(solution)/shard_map/all_to_all | solution.py:373
  66.7 0.8 copy-start.5
  105.4 7.0 %collective-permute-start.10 = (f32[4,2,8,512]{3,2,1,0:T(8,128)S(1)}, f32[4,2,8,512]{3,2,1,0:T(8,128)S(1)}, u32[]{:S(2)}, u32[]{:S(2)}) collective-permute-start(f32[4,2,8,512]{3,2,1,0:T(8,128)S(1)} %get-tuple-element.41), channel_id=1, source_target_pairs={{0,32},{32,64},{64,96},{96,128},{128,160},{160,192},{192,224},{224... | collective-permute-start | bytes 393224 | tf_op jit(solution)/shard_map/ppermute | solution.py:294
  108.8 5.9 %collective-permute-start.14 = (f32[4,2,8,512]{3,2,1,0:T(8,128)S(1)}, f32[4,2,8,512]{3,2,1,0:T(8,128)S(1)}, u32[]{:S(2)}, u32[]{:S(2)}) collective-permute-start(f32[4,2,8,512]{3,2,1,0:T(8,128)S(1)} %get-tuple-element.42), channel_id=1, source_target_pairs={{32,0},{64,32},{96,64},{128,96},{160,128},{192,160},{224,192},{0,2... | collective-permute-start | bytes 393224 | tf_op jit(solution)/shard_map/ppermute | solution.py:299
  114.7 8.1 %collective-permute-start.15 = (f32[8,2,8,512]{3,2,1,0:T(8,128)S(1)}, f32[8,2,8,512]{3,2,1,0:T(8,128)S(1)}, u32[]{:S(2)}, u32[]{:S(2)}) collective-permute-start(f32[8,2,8,512]{3,2,1,0:T(8,128)S(1)} %pad_maximum_fusion.4), channel_id=1, source_target_pairs={{32,0},{64,32},{96,64},{128,96},{160,128},{192,160},{224,192},{0,2... | collective-permute-start | bytes 786440 | tf_op jit(solution)/shard_map/ppermute | solution.py:299
  115.1 8.2 %collective-permute-start.11 = (f32[8,2,8,512]{3,2,1,0:T(8,128)S(1)}, f32[8,2,8,512]{3,2,1,0:T(8,128)S(1)}, u32[]{:S(2)}, u32[]{:S(2)}) collective-permute-start(f32[8,2,8,512]{3,2,1,0:T(8,128)S(1)} %pad_maximum_fusion.3), channel_id=1, source_target_pairs={{0,32},{32,64},{64,96},{96,128},{128,160},{160,192},{192,224},{224... | collective-permute-start | bytes 786440 | tf_op jit(solution)/shard_map/ppermute | solution.py:294
  123.4 7.4 %collective-permute-start.12 = (f32[8,2,8,512]{3,2,1,0:T(8,128)S(1)}, f32[8,2,8,512]{3,2,1,0:T(8,128)S(1)}, u32[]{:S(2)}, u32[]{:S(2)}) collective-permute-start(f32[8,2,8,512]{3,2,1,0:T(8,128)S(1)} %get-tuple-element.45), channel_id=1, source_target_pairs={{0,32},{32,64},{64,96},{96,128},{128,160},{160,192},{192,224},{224... | collective-permute-start | bytes 786440 | tf_op jit(solution)/shard_map/ppermute | solution.py:294
  125.9 8.3 %collective-permute-start.16 = (f32[8,2,8,512]{3,2,1,0:T(8,128)S(1)}, f32[8,2,8,512]{3,2,1,0:T(8,128)S(1)}, u32[]{:S(2)}, u32[]{:S(2)}) collective-permute-start(f32[8,2,8,512]{3,2,1,0:T(8,128)S(1)} %get-tuple-element.46), channel_id=1, source_target_pairs={{32,0},{64,32},{96,64},{128,96},{160,128},{192,160},{224,192},{0,2... | collective-permute-start | bytes 786440 | tf_op jit(solution)/shard_map/ppermute | solution.py:299
  134.3 6.9 %collective-permute-start.13 = (f32[8,2,8,512]{3,2,1,0:T(8,128)S(1)}, f32[8,2,8,512]{3,2,1,0:T(8,128)S(1)}, u32[]{:S(2)}, u32[]{:S(2)}) collective-permute-start(f32[8,2,8,512]{3,2,1,0:T(8,128)S(1)} %get-tuple-element.43), channel_id=1, source_target_pairs={{0,32},{32,64},{64,96},{96,128},{128,160},{160,192},{192,224},{224... | collective-permute-start | bytes 786440 | tf_op jit(solution)/shard_map/ppermute | solution.py:294
  137.3 6.4 %collective-permute-start.17 = (f32[8,2,8,512]{3,2,1,0:T(8,128)S(1)}, f32[8,2,8,512]{3,2,1,0:T(8,128)S(1)}, u32[]{:S(2)}, u32[]{:S(2)}) collective-permute-start(f32[8,2,8,512]{3,2,1,0:T(8,128)S(1)} %get-tuple-element.44), channel_id=1, source_target_pairs={{32,0},{64,32},{96,64},{128,96},{160,128},{192,160},{224,192},{0,2... | collective-permute-start | bytes 786440 | tf_op jit(solution)/shard_map/ppermute | solution.py:299

commit v4 on v3

v4 whole, which is shorter than its diff:
```python
import functools
import math

import jax
import jax.numpy as jnp
from jax import lax
from jax.experimental import pallas as pl
from jax.experimental.pallas import tpu as pltpu
from jax.sharding import Mesh, PartitionSpec as P

CORE = 256
HALO = 64
SPAN = 384
HALF = 256
SLAB = ("x", "y", "core")
FRAME = ("y", "core")


def split(values):
    high = values.astype(jnp.bfloat16)
    low = (values - high.astype(jnp.float32)).astype(jnp.bfloat16)
    return high, low


def dot(left, right):
    return jnp.dot(left, right, preferred_element_type=jnp.float32)


def product(left, right):
    return dot(left[0], right[0]) + (dot(left[0], right[1]) + dot(left[1], right[0]))


def left(matrix, rows, parts):
    stacked, extra = None, None
    for lanes, (high, low) in parts:
        four = matrix[:, 0:rows, lanes].reshape(4 * rows, high.shape[0])
        term, small = dot(four, high), dot(four[0 : 2 * rows], low)
        stacked = term if stacked is None else stacked + term
        extra = small if extra is None else extra + small
    real = stacked[0:rows] + (stacked[2 * rows : 3 * rows] + extra[0:rows])
    imag = stacked[rows : 2 * rows] + (stacked[3 * rows : 4 * rows] + extra[rows : 2 * rows])
    return real, imag


def right(parts, matrix, lanes):
    stacked, extra = None, None
    for part, (high, low) in enumerate(parts):
        depth = high.shape[1]
        term = dot(jnp.concatenate([high, low], axis=0), matrix[part, 0:depth, lanes])
        small = dot(high, matrix[2 + part, 0:depth, lanes])
        stacked = term if stacked is None else stacked + term
        extra = small if extra is None else extra + small
    rows = extra.shape[0]
    return stacked[0:rows] + (stacked[rows : 2 * rows] + extra)


def build(matrix, base, sign):
    for part in range(2):
        cosine, sine = base[2 * part], base[2 * part + 1]
        matrix[2 * part, :, FULL] = cosine
        matrix[2 * part, :, REST] = sine if sign > 0 else -sine
        matrix[2 * part + 1, :, FULL] = -sine if sign > 0 else sine
        matrix[2 * part + 1, :, REST] = cosine


def sine_cosine(angle):
    turns = jnp.round(angle * (2.0 / math.pi))
    rest = angle - turns * 1.5703125
    rest = rest - turns * 4.837512969970703125e-4
    rest = rest - turns * 7.549789948768648e-8
    square = rest * rest
    sine = rest + rest * square * (
        -1.6666654611e-1 + square * (8.3321608736e-3 + square * -1.9515295891e-4)
    )
    cosine = 1.0 - 0.5 * square + square * square * (
        4.166664568298827e-2 + square * (-1.388731625493765e-3 + square * 2.443315711809948e-5)
    )
    quarter = turns.astype(jnp.int32)
    odd = (quarter & 1) == 1
    sine, cosine = jnp.where(odd, cosine, sine), jnp.where(odd, sine, cosine)
    sine = jnp.where((quarter & 2) == 2, -sine, sine)
    cosine = jnp.where(((quarter + 1) & 2) == 2, -cosine, cosine)
    return sine, cosine


LOW = slice(0, CORE)
HIGH = slice(SPAN, SPAN + CORE)
FULL = slice(0, SPAN)
REST = slice(SPAN, 2 * SPAN)
ALL = slice(None)


def object_kernel(window, base, spec_re, spec_im, forward, inverse):
    block = SPAN // 8
    row = lax.broadcasted_iota(jnp.int32, (block, SPAN), 0)
    column = lax.broadcasted_iota(jnp.int32, (block, SPAN), 1)

    def fill(index, carry):
        begin = pl.multiple_of(index * block, block)
        steps = ((row + begin) * column).astype(jnp.float32)
        steps = steps - SPAN * jnp.floor((steps + 0.5) * (1.0 / SPAN))
        sine, cosine = sine_cosine(steps * (2.0 * math.pi / SPAN))
        at = pl.ds(begin, block)
        base[0, at], base[2, at] = split(cosine)
        base[1, at], base[3, at] = split(sine)
        return carry

    lax.fori_loop(0, 8, fill, 0)
    build(forward, base, 1)
    build(inverse, base, -1)
    seen = split(window[...])
    part_re = split(right([seen], inverse, LOW))
    part_im = split(right([seen], inverse, HIGH))
    real, imag = left(forward, SPAN, [(FULL, part_re), (REST, part_im)])
    column = lax.broadcasted_iota(jnp.int32, (SPAN, HALF), 1)
    ends = (column == 0) | (column == SPAN // 2)
    weight = jnp.where(ends, 1.0, jnp.where(column < SPAN // 2, 2.0, 0.0)) / (SPAN * SPAN)
    spec_re[...] = real * weight
    spec_im[...] = imag * weight


def cut_kernel(place, screens, first, second, sems):
    at = pl.ds(pl.multiple_of(place[2], 8), 8)
    copies = [
        pltpu.make_async_copy(screens.at[layer, at, :], target, sems.at[layer])
        for layer, target in enumerate((first, second))
    ]
    for copy in copies:
        copy.start()
    for copy in copies:
        copy.wait()


def select_kernel(place, rows, cols, *refs):
    chunks, out, gathered = refs[:16], refs[16], refs[17]
    slab, first = place[0], place[1]
    for step in range(8):
        source = (slab + step) % 8
        for layer in range(2):
            gathered[source * 2 + layer] = chunks[step * 2 + layer][...]
    row_index = first + lax.broadcasted_iota(jnp.int32, (8, CORE), 0)
    lane = lax.broadcasted_iota(jnp.int32, (8, CORE), 1)

    def one(member, carry):
        patch = slab * 4 + member // 8
        frame = member % 8
        for layer in range(2):
            row = rows[frame, layer, patch]
            col = cols[frame, layer, patch]
            block, residue = row // CORE, row % CORE
            after = jnp.minimum(block + 1, 7)
            strip, turn = col // CORE, col % CORE
            at = pl.ds(pl.multiple_of(strip * CORE, CORE), CORE)
            beside = pl.ds(pl.multiple_of(jnp.minimum(strip + 1, 15) * CORE, CORE), CORE)
            right = lane >= turn
            upper = jnp.where(
                right, gathered[block * 2 + layer, :, at], gathered[block * 2 + layer, :, beside]
            )
            lower = jnp.where(
                right, gathered[after * 2 + layer, :, at], gathered[after * 2 + layer, :, beside]
            )
            out[member, layer] = jnp.where(row_index >= residue, upper, lower)
        return carry

    lax.fori_loop(0, 32, one, 0, unroll=2)


def scatter_kernel(place, rows, cols, values, *refs):
    pieces, out = refs[:16], refs[16]
    slab, first = place[0], place[1]
    row_index = first + lax.broadcasted_iota(jnp.int32, (8, CORE), 0)
    lane = lax.broadcasted_iota(jnp.int32, (8, CORE), 1)
    out[...] = jnp.zeros_like(out)

    def one(member, carry):
        patch = slab * 4 + member // 8
        frame = member % 8
        for layer in range(2):
            row = rows[frame, layer, patch]
            col = cols[frame, layer, patch]
            block, residue = row // CORE, row % CORE
            after = jnp.minimum(block + 1, 7)
            strip, turn = col // CORE, col % CORE
            beside = jnp.minimum(strip + 1, 15)
            value = values[member, layer]
            here = row_index >= residue
            right = lane >= turn
            for target, keep_row in ((block, here), (after, ~here)):
                where = (target + 8 - slab) % 8
                for place_col, keep_col in ((strip, right), (beside, ~right)):
                    at = pl.ds(pl.multiple_of((place_col % 2) * CORE, CORE), CORE)
                    chunk = place_col // 2
                    out[where, chunk, layer, :, at] = out[where, chunk, layer, :, at] + jnp.where(
                        keep_row & keep_col, value, 0.0
                    )
        return carry

    lax.fori_loop(0, 32, one, 0, unroll=2)
    for index, piece in enumerate(pieces):
        piece[...] = out[index // 2, 4 * (index % 2) : 4 * (index % 2) + 4]


def gradient_kernel(
    turns, received, amp_ref, observed, base, spec_re, spec_im, out,
    forward, inverse, pupil_re, pupil_im, far_re, far_im, mix_h, mix_l, wide_h, wide_l,
):
    def put(high, low, at, values):
        high[at], low[at] = split(values)

    build(forward, base, 1)
    build(inverse, base, -1)
    phases = None
    for layer in range(2):
        sheet = received[:, layer].reshape(CORE, CORE)
        sheet = pltpu.roll(sheet, (CORE - turns[layer, 0]) % CORE, 0)
        sheet = pltpu.roll(sheet, (CORE - turns[layer, 1]) % CORE, 1)
        phases = sheet if phases is None else phases + sheet
    amplitude = amp_ref[...]
    inverse_total = 1.0 / (SPAN * SPAN * jnp.sum(amplitude * amplitude))
    sine, cosine = sine_cosine(phases)
    pupil_re[...] = amplitude * cosine
    pupil_im[...] = amplitude * sine
    half_re, half_im = left(
        forward, SPAN, [(LOW, split(pupil_re[...])), (HIGH, split(pupil_im[...]))]
    )
    half = [split(half_re), split(half_im)]
    far_re[...] = right(half, inverse, FULL)
    far_im[...] = right(half, inverse, REST)
    spread = [split((far_re[...] * far_re[...] + far_im[...] * far_im[...]) * inverse_total)]
    put(mix_h, mix_l, FULL, right(spread, inverse, LOW))
    put(mix_h, mix_l, REST, right(spread, inverse, HIGH))
    first, second = left(forward, SPAN, [(ALL, (mix_h[...], mix_l[...]))])
    put(mix_h, mix_l, FULL, first * spec_re[...] - second * spec_im[...])
    put(mix_h, mix_l, REST, first * spec_im[...] + second * spec_re[...])
    first, second = left(inverse, CORE, [(ALL, (mix_h[...], mix_l[...]))])
    model = right([split(first), split(second)], forward, LOW)
    residual = [split((model - observed[0]) * float(SPAN))]
    grad_re = split(right(residual, inverse, LOW))
    grad_im = split(right(residual, inverse, HIGH))
    first, second = left(forward, SPAN, [(LOW, grad_re), (HIGH, grad_im)])
    put(mix_h, mix_l, FULL, first * spec_re[...] + second * spec_im[...])
    put(mix_h, mix_l, REST, second * spec_re[...] - first * spec_im[...])
    first, second = left(inverse, SPAN, [(ALL, (mix_h[...], mix_l[...]))])
    spread_grad = right([split(first), split(second)], forward, FULL)
    put(wide_h, wide_l, FULL, far_re[...] * spread_grad)
    put(wide_h, wide_l, REST, far_im[...] * spread_grad)
    first, second = left(inverse, CORE, [(ALL, (wide_h[...], wide_l[...]))])
    back = [split(first), split(second)]
    out_re = right(back, forward, LOW)
    out_im = right(back, forward, HIGH)
    gradient = (2.0 * inverse_total) * (pupil_re[...] * out_im - pupil_im[...] * out_re)
    for layer in range(2):
        sheet = pltpu.roll(gradient, turns[layer, 1], 1)
        sheet = pltpu.roll(sheet, turns[layer, 0], 0)
        out[:, layer] = sheet.reshape(32, 8, CORE)


SMEM = pl.BlockSpec(memory_space=pltpu.SMEM)
VMEM = pl.BlockSpec(memory_space=pltpu.VMEM)
ANY = pl.BlockSpec(memory_space=pl.ANY)


def limit(mib):
    return pltpu.CompilerParams(vmem_limit_bytes=mib << 20)


def cost(flops, moved):
    return pl.CostEstimate(flops=flops, bytes_accessed=moved, transcendentals=0)


def f32(*shape):
    return jax.ShapeDtypeStruct(shape, jnp.float32)


def gradient_call(*operands, name="gradient"):
    return pl.pallas_call(
        gradient_kernel,
        out_shape=f32(32, 2, 8, CORE),
        in_specs=[SMEM] + [VMEM] * 6,
        out_specs=VMEM,
        scratch_shapes=[
            pltpu.VMEM((4, SPAN, 2 * SPAN), jnp.bfloat16),
            pltpu.VMEM((4, SPAN, 2 * SPAN), jnp.bfloat16),
            pltpu.VMEM((CORE, CORE), jnp.float32),
            pltpu.VMEM((CORE, CORE), jnp.float32),
            pltpu.VMEM((SPAN, SPAN), jnp.float32),
            pltpu.VMEM((SPAN, SPAN), jnp.float32),
            pltpu.VMEM((2 * SPAN, HALF), jnp.bfloat16),
            pltpu.VMEM((2 * SPAN, HALF), jnp.bfloat16),
            pltpu.VMEM((2 * SPAN, SPAN), jnp.bfloat16),
            pltpu.VMEM((2 * SPAN, SPAN), jnp.bfloat16),
        ],
        compiler_params=limit(28),
        cost_estimate=cost(3 * 2 * 1222 * 10**6, 7 * 10**6),
        name=name,
    )(*operands)


def up(values):
    count = lax.axis_size("z")
    return lax.ppermute(values, "z", [(i, (i + 1) % count) for i in range(count)])


def down(values):
    count = lax.axis_size("z")
    return lax.ppermute(values, "z", [((i + 1) % count, i) for i in range(count)])


def ring_gather(own):
    chunks = {(0, 0): own[0], (0, 1): own[1]}
    for step in range(1, 4):
        for layer in range(2):
            chunks[8 - step, layer] = up(chunks[(9 - step) % 8, layer])
            chunks[step, layer] = down(chunks[step - 1, layer])
    chunks[4, 0] = up(chunks[5, 0])
    chunks[4, 1] = down(chunks[3, 1])
    return [chunks[step, layer] for step in range(8) for layer in range(2)]


def ring_scatter(partial):
    top, bottom = (4, 3), (3, 4)
    rise = [partial[2 * top[half] + half] for half in range(2)]
    fall = [partial[2 * (8 - bottom[half]) + half] for half in range(2)]
    for step in range(1, 5):
        for half in range(2):
            if step <= top[half]:
                rise[half] = up(rise[half])
                if step < top[half]:
                    rise[half] = rise[half] + partial[2 * (top[half] - step) + half]
            if step <= bottom[half]:
                fall[half] = down(fall[half])
                if step < bottom[half]:
                    fall[half] = fall[half] + partial[2 * (8 - bottom[half] + step) + half]
    return jnp.concatenate([partial[half] + rise[half] + fall[half] for half in range(2)])


def body(screens, row_offsets, col_offsets, amplitude, object_strip, observed):
    slab = lax.axis_index("z")
    across = lax.axis_index("x")
    frame_id = lax.axis_index(FRAME)
    patch = slab * 4 + across
    patches = lax.axis_size("z") * lax.axis_size("x")
    place = jnp.stack([slab, across * 64 + frame_id * 8, frame_id * 8]).astype(jnp.int32)
    own = pl.pallas_call(
        cut_kernel,
        out_shape=[f32(8, screens.shape[2])] * 2,
        in_specs=[SMEM, ANY],
        out_specs=[VMEM] * 2,
        scratch_shapes=[pltpu.SemaphoreType.DMA((2,))],
        compiler_params=limit(61),
        name="cut_rows",
    )(place, screens)
    chunks = ring_gather(own)
    sent = pl.pallas_call(
        select_kernel,
        out_shape=f32(32, 2, 8, CORE),
        in_specs=[SMEM] * 3 + [VMEM] * 16,
        out_specs=VMEM,
        scratch_shapes=[pltpu.VMEM((16, 8, screens.shape[2]), jnp.float32)],
        compiler_params=limit(20),
        cost_estimate=cost(0, 3 * 10**6),
        name="select_rows",
    )(place, row_offsets, col_offsets, *chunks)
    sent, strip = lax.optimization_barrier((sent, object_strip))
    received = lax.all_to_all(sent, SLAB, split_axis=0, concat_axis=0, tiled=True)

    ends = patches - 1
    left_tail = lax.ppermute(
        strip[:, CORE - HALO :], ("z", "x"), [(i, i + 1) for i in range(ends)]
    )
    right_head = lax.ppermute(strip[:, :HALO], ("z", "x"), [(i + 1, i) for i in range(ends)])
    window = jnp.concatenate([strip, right_head, left_tail], axis=1)
    window = jnp.concatenate([window[HALO:], window[:HALO]], axis=0)
    base, spec_re, spec_im = pl.pallas_call(
        object_kernel,
        out_shape=[jax.ShapeDtypeStruct((4, SPAN, SPAN), jnp.bfloat16)] + [f32(SPAN, HALF)] * 2,
        in_specs=[VMEM],
        out_specs=[VMEM] * 3,
        scratch_shapes=[pltpu.VMEM((4, SPAN, 2 * SPAN), jnp.bfloat16)] * 2,
        compiler_params=limit(28),
        cost_estimate=cost(3 * 2 * 226 * 10**6, 7 * 10**6),
        name="object_spectrum",
    )(window)

    row_turns = lax.dynamic_slice(row_offsets, (frame_id, 0, patch), (1, 2, 1))[0, :, 0] % CORE
    col_turns = lax.dynamic_slice(col_offsets, (frame_id, 0, patch), (1, 2, 1))[0, :, 0] % CORE
    turns = jnp.stack([row_turns, col_turns], axis=1)
    placed = gradient_call(
        turns, received, amplitude, observed, base, spec_re, spec_im
    )
    returned = lax.all_to_all(placed, SLAB, split_axis=0, concat_axis=0, tiled=True)

    partial = pl.pallas_call(
        scatter_kernel,
        out_shape=[f32(4, 2, 8, 512)] * 16,
        in_specs=[SMEM] * 3 + [VMEM],
        out_specs=[VMEM] * 16,
        scratch_shapes=[pltpu.VMEM((8, 8, 2, 8, 512), jnp.float32)],
        compiler_params=limit(20),
        cost_estimate=cost(0, 3 * 10**6),
        name="scatter_rows",
    )(place, row_offsets, col_offsets, returned)
    summed = ring_scatter(partial)
    turned = lax.all_to_all(summed, FRAME, split_axis=0, concat_axis=0, tiled=True)
    return turned.transpose(1, 0, 2, 3).reshape(2, 64, 512)


def solution(mesh):
    fine = Mesh(mesh.devices.reshape(8, 4, 4, 2), ("z", "x", "y", "core"))
    patch = ("z", "x")
    in_specs = (
        P(None, patch, None), P(), P(), P(), P(None, patch), P(FRAME, None, patch),
    )
    out_specs = P(None, patch, FRAME)
    return jax.shard_map(body, mesh=fine, in_specs=in_specs, out_specs=out_specs, check_vma=False)
```

time: 155 us -> 146 us (0.942)
  waiting for transfers between devices: 56.9 us -> 26.7 us
  starting transfers between devices: 34.1 us -> 59.9 us
  Pallas kernels: 33.6 us -> 28.2 us
    ppermute x8 -> x14, starting transfers between devices: 17.5 us -> 45.4 us  [up(): lax.ppermute(values, 'z', [(i, (i + 1) % count) for i in range(count)])]
    ppermute x8 -> x14, waiting for transfers between devices: 22 us -> 8.45 us  [up(): lax.ppermute(values, 'z', [(i, (i + 1) % count) for i in range(count)])]
    all_to_all x1, waiting for transfers between devices: 10.2 us -> 0.01 us  [body(): lax.all_to_all(sent, SLAB, split_axis=0, concat_axis=0, tiled=True)]
    ppermute x8 -> x14, waiting for transfers between devices: 18.4 us -> 9.78 us  [down(): lax.ppermute(values, 'z', [((i + 1) % count, i) for i in range(count)])]
    ppermute x1, waiting for transfers between devices: 0.01 us -> 5.97 us  [body(): lax.ppermute(strip[:, :HALO], ('z', 'x'), [(i + 1, i) for i in range(ends)])]
    ppermute x1, waiting for transfers between devices: 6.42 us -> 2.49 us  [body(): lax.ppermute(strip[:, CORE - HALO:], ('z', 'x'), [(i, i + 1) for i in ran...]
    pallas_call x1, Pallas kernels: 19.2 us -> 15.5 us  [gradient_call(): pl.pallas_call(gradient_kernel, out_shape=f32(32, 2, 8, CORE), in_specs=[...]
    ppermute x8 -> x14, starting transfers between devices: 4.29 us -> 0.71 us  [down(): lax.ppermute(values, 'z', [((i + 1) % count, i) for i in range(count)])]
  transfers between devices with their start and end apart: 19 -> 31, of which waited for: 15 -> 13; matrix products, arithmetic and copies ran while one was open for 1% -> 1% of each run, Pallas kernels for 4% -> 2%
where the time goes in v4:
time: 146 us; the launch traced here: 144 us
  starting transfers between devices  59.9 us (41%)
  Pallas kernels  28.2 us (19%)
  waiting for transfers between devices  26.7 us (18%)
  blocking collectives  25.4 us (17%)
  local copies, waits for them, and re-layouts  2.69 us (2%)
    ppermute x14, starting transfers between devices, up(): lax.ppermute(values, 'z', [(i, (i + 1) % count) for i in range(count)])  45.4 us
    all_to_all x1, blocking collectives, body(): lax.all_to_all(placed, SLAB, split_axis=0, concat_axis=0, tiled=True)  15.5 us
    pallas_call x1, Pallas kernels, gradient_call(): pl.pallas_call(gradient_kernel, out_shape=f32(32, 2, 8, CORE), in_specs=[...  15.5 us
    all_to_all x1, blocking collectives, body(): lax.all_to_all(summed, FRAME, split_axis=0, concat_axis=0, tiled=True)  9.91 us
    ppermute x14, waiting for transfers between devices, down(): lax.ppermute(values, 'z', [((i + 1) % count, i) for i in range(count)])  9.78 us
    ppermute x14, waiting for transfers between devices, up(): lax.ppermute(values, 'z', [(i, (i + 1) % count) for i in range(count)])  8.45 us
    all_to_all x1, starting transfers between devices, body(): lax.all_to_all(sent, SLAB, split_axis=0, concat_axis=0, tiled=True)  7.32 us
    ppermute x1, waiting for transfers between devices, body(): lax.ppermute(strip[:, :HALO], ('z', 'x'), [(i + 1, i) for i in range(ends)])  5.97 us
  transfers between devices with their start and end apart: 31, of which 13 were waited for; matrix products, arithmetic and copies ran while one was open for 1% of the time, Pallas kernels for 2%

profile of v4, /device:TPU:64, one launch (start us, length us, event | category | flops | bytes accessed | tf_op | source)
XLA Modules:
  0.0 144.4 jit_solution(11863624340183507313)
XLA Ops:
  0.0 0.6 pad_add_fusion.1.place
  0.6 2.5 %cut_rows.1 = (f32[8,4096]{1,0:T(8,128)}, f32[8,4096]{1,0:T(8,128)}) custom-call(s32[3]{0:T(128)} %pad_add_fusion.1.place, f32[2,64,4096]{2,1,0:T(8,128)} %screens.1), custom_call_target="tpu_custom_call" | custom-call | tf_op jit(solution)/shard_map/cut_rows/pallas_call | solution.py:344
  3.1 2.0 %collective-permute-start.6 = (f32[8,4096]{1,0:T(8,128)}, f32[8,4096]{1,0:T(8,128)S(1)}, u32[]{:S(2)}, u32[]{:S(2)}) collective-permute-start(f32[8,4096]{1,0:T(8,128)} %get-tuple-element.28.refs_0_), channel_id=1, source_target_pairs={{0,32},{32,64},{64,96},{96,128},{128,160},{160,192},{192,224},{224... | collective-permute-start | bytes 393224 | tf_op jit(solution)/shard_map/ppermute | solution.py:301
  5.1 0.1 collective-permute-start.1
  5.2 0.1 collective-permute-start
  5.3 2.9 %collective-permute-start.11 = (f32[8,4096]{1,0:T(8,128)}, f32[8,4096]{1,0:T(8,128)S(1)}, u32[]{:S(2)}, u32[]{:S(2)}) collective-permute-start(f32[8,4096]{1,0:T(8,128)} %get-tuple-element.29.refs_1_), channel_id=1, source_target_pairs={{0,32},{32,64},{64,96},{96,128},{128,160},{160,192},{192,224},{224... | collective-permute-start | bytes 393224 | tf_op jit(solution)/shard_map/ppermute | solution.py:301
  8.2 0.4 collective-permute-done.6.refs_14_
  8.6 2.9 %collective-permute-start.7 = (f32[8,4096]{1,0:T(8,128)S(1)}, f32[8,4096]{1,0:T(8,128)S(1)}, u32[]{:S(2)}, u32[]{:S(2)}) collective-permute-start(f32[8,4096]{1,0:T(8,128)S(1)} %collective-permute-done.6.refs_14_), channel_id=1, source_target_pairs={{0,32},{32,64},{64,96},{96,128},{128,160},{160,192},{192,224},{224... | collective-permute-start | bytes 393224 | tf_op jit(solution)/shard_map/ppermute | solution.py:301
  11.5 1.3 collective-permute-done.1.refs_3_
  12.8 1.7 %collective-permute-done.refs_2_ = f32[8,4096]{1,0:T(8,128)S(1)} collective-permute-done((f32[8,4096]{1,0:T(8,128)}, f32[8,4096]{1,0:T(8,128)S(1)}, u32[]{:S(2)}, u32[]{:S(2)}) %collective-permute-start) | collective-permute-done | bytes 131104 | tf_op jit(solution)/shard_map/ppermute | solution.py:306
  14.5 3.0 %collective-permute-start.12 = (f32[8,4096]{1,0:T(8,128)S(1)}, f32[8,4096]{1,0:T(8,128)S(1)}, u32[]{:S(2)}, u32[]{:S(2)}) collective-permute-start(f32[8,4096]{1,0:T(8,128)S(1)} %collective-permute-done.11.refs_15_), channel_id=1, source_target_pairs={{0,32},{32,64},{64,96},{96,128},{128,160},{160,192},{192,224},{224... | collective-permute-start | bytes 393224 | tf_op jit(solution)/shard_map/ppermute | solution.py:301
  17.4 3.2 %collective-permute-start.8 = (f32[8,4096]{1,0:T(8,128)S(1)}, f32[8,4096]{1,0:T(8,128)S(1)}, u32[]{:S(2)}, u32[]{:S(2)}) collective-permute-start(f32[8,4096]{1,0:T(8,128)S(1)} %collective-permute-done.7.refs_12_), channel_id=1, source_target_pairs={{0,32},{32,64},{64,96},{96,128},{128,160},{160,192},{192,224},{224... | collective-permute-start | bytes 393224 | tf_op jit(solution)/shard_map/ppermute | solution.py:301
  20.7 0.6 collective-permute-done.2.refs_4_
  21.2 4.3 %collective-permute-start.13 = (f32[8,4096]{1,0:T(8,128)S(1)}, f32[8,4096]{1,0:T(8,128)S(1)}, u32[]{:S(2)}, u32[]{:S(2)}) collective-permute-start(f32[8,4096]{1,0:T(8,128)S(1)} %collective-permute-done.12.refs_13_), channel_id=1, source_target_pairs={{0,32},{32,64},{64,96},{96,128},{128,160},{160,192},{192,224},{224... | collective-permute-start | bytes 393224 | tf_op jit(solution)/shard_map/ppermute | solution.py:301
  25.5 3.2 %collective-permute-start.9 = (f32[8,4096]{1,0:T(8,128)S(1)}, f32[8,4096]{1,0:T(8,128)S(1)}, u32[]{:S(2)}, u32[]{:S(2)}) collective-permute-start(f32[8,4096]{1,0:T(8,128)S(1)} %collective-permute-done.8.refs_10_), channel_id=1, source_target_pairs={{0,32},{32,64},{64,96},{96,128},{128,160},{160,192},{192,224},{224... | collective-permute-start | bytes 393224 | tf_op jit(solution)/shard_map/ppermute | solution.py:301
  28.8 0.1 and_select_fusion
  28.9 0.9 collective-permute-done.4.refs_6_
  29.8 1.5 %collective-permute-done.9.refs_8_ = f32[8,4096]{1,0:T(8,128)S(1)} collective-permute-done((f32[8,4096]{1,0:T(8,128)S(1)}, f32[8,4096]{1,0:T(8,128)S(1)}, u32[]{:S(2)}, u32[]{:S(2)}) %collective-permute-start.9) | collective-permute-done | bytes 131104 | tf_op jit(solution)/shard_map/ppermute | solution.py:301
  31.3 2.4 %collective-permute-done.10.refs_9_ = f32[8,4096]{1,0:T(8,128)S(1)} collective-permute-done((f32[8,4096]{1,0:T(8,128)S(1)}, f32[8,4096]{1,0:T(8,128)S(1)}, u32[]{:S(2)}, u32[]{:S(2)}) %collective-permute-start.10) | collective-permute-done | bytes 131104 | tf_op jit(solution)/shard_map/ppermute | solution.py:306
  33.7 0.9 copy-done
  34.6 0.9 copy-done.1
  35.5 3.2 %select_rows.1 = f32[32,2,8,256]{3,2,1,0:T(8,128)} custom-call(s32[3]{0:T(128)S(1)} %copy-done.4, s32[8,2,32]{2,1,0:T(2,128)S(1)} %copy-done.2, s32[8,2,32]{2,1,0:T(2,128)S(1)} %copy-done.3, f32[8,4096]{1,0:T(8,128)S(1)} %copy-done, f32[8,4096]{1,0:T(8,128)S(1)} %copy-done.1, f32[8,4096]{1,0:T(8,128)S(1)} %collective-permute-done.refs_2_, ...), custom_call_target="tpu_custom_call" | custom-call | bytes 3000000 | tf_op jit(solution)/shard_map/select_rows/pallas_call | solution.py:354
  38.7 7.3 %all-to-all-start = ((f32[32,2,8,256]{3,2,1,0:T(8,128)}), f32[32,2,8,256]{3,2,1,0:T(8,128)S(1)}, u32[]{:S(2)}, u32[]{:S(2)}) async-start(f32[32,2,8,256]{3,2,1,0:T(8,128)} %select_rows.1), calls=%async_computation | async-start | bytes 1048576 | tf_op jit(solution)/shard_map/all_to_all | solution.py:365
  46.1 0.1 fusion.3
  46.2 4.4 %collective-permute-start.14 = (f32[384,64]{1,0:T(8,128)S(1)}, f32[384,64]{1,0:T(8,128)S(1)}, u32[]{:S(2)}, u32[]{:S(2)}) collective-permute-start(f32[384,64]{1,0:T(8,128)S(1)} %get-tuple-element.51), channel_id=1, source_target_pairs={{8,0},{16,8},{24,16},{32,24},{40,32},{48,40},{56,48},{64,56},{72,6... | collective-permute-start | bytes 294920 | tf_op jit(solution)/shard_map/ppermute | solution.py:371
  50.6 2.1 %collective-permute-start.15 = (f32[384,64]{1,0:T(8,128)S(1)}, f32[384,64]{1,0:T(8,128)S(1)}, u32[]{:S(2)}, u32[]{:S(2)}) collective-permute-start(f32[384,64]{1,0:T(8,128)S(1)} %get-tuple-element.52), channel_id=1, source_target_pairs={{0,8},{8,16},{16,24},{24,32},{32,40},{40,48},{48,56},{56,64},{64,7... | collective-permute-start | bytes 294920 | tf_op jit(solution)/shard_map/ppermute | solution.py:368
  52.8 6.0 %collective-permute-done.14 = f32[384,64]{1,0:T(8,128)S(1)} collective-permute-done((f32[384,64]{1,0:T(8,128)S(1)}, f32[384,64]{1,0:T(8,128)S(1)}, u32[]{:S(2)}, u32[]{:S(2)}) %collective-permute-start.14) | collective-permute-done | bytes 98336 | tf_op jit(solution)/shard_map/ppermute | solution.py:371
  58.8 2.5 %collective-permute-done.15 = f32[384,64]{1,0:T(8,128)S(1)} collective-permute-done((f32[384,64]{1,0:T(8,128)S(1)}, f32[384,64]{1,0:T(8,128)S(1)}, u32[]{:S(2)}, u32[]{:S(2)}) %collective-permute-start.15) | collective-permute-done | bytes 98336 | tf_op jit(solution)/shard_map/ppermute | solution.py:368
  61.3 0.1 pad_maximum_fusion.2
  61.4 0.1 fusion.window
  61.5 3.3 %object_spectrum.1 = (bf16[4,384,384]{2,1,0:T(8,128)(2,1)S(1)}, f32[384,256]{1,0:T(8,128)S(1)}, f32[384,256]{1,0:T(8,128)S(1)}) custom-call(f32[384,384]{1,0:T(8,128)S(1)} %fusion.window), custom_call_target="tpu_custom_call" | custom-call | flops 1356000000 | bytes 7000000 | tf_op jit(solution)/shard_map/object_spectrum/pallas_call | solution.py:374
  64.8 15.5 %gradient.1 = f32[32,2,8,256]{3,2,1,0:T(8,128)S(1)} custom-call(s32[2,2]{1,0:T(2,128)S(1)} %pad_add_fusion.turns, f32[32,2,8,256]{3,2,1,0:T(8,128)S(1)} %all-to-all-done.received, f32[256,256]{1,0:T(8,128)S(1)} %copy-done.5, f32[1,256,256]{2,1,0:T(8,128)S(1)} %copy-done.6, bf16[4,384,384]{2,1,0:T(8,128)(2,1)S(1)} %get-tuple-element.32.base, ...), custom_call_target="tpu_custom_call" | custom-call | flops 7331999744 | bytes 7000000 | tf_op jit(solution)/shard_map/gradient/pallas_call | solution.py:276
  80.3 15.5 %all_to_all.15.values = f32[32,2,8,256]{3,2,1,0:T(8,128)S(1)} all-to-all(f32[32,2,8,256]{3,2,1,0:T(8,128)S(1)} %gradient.1), channel_id=1, replica_groups=mesh['z'=8,'x'=4,'y'=4,'core'=2] {'x','y','core'}, dimensions={0} | all-to-all | bytes 1048576 | tf_op jit(solution)/shard_map/all_to_all | solution.py:391
  95.9 3.7 %scatter_rows.1 = (f32[4,2,8,512]{3,2,1,0:T(8,128)S(1)}, f32[4,2,8,512]{3,2,1,0:T(8,128)S(1)}, f32[4,2,8,512]{3,2,1,0:T(8,128)S(1)}, f32[4,2,8,512]{3,2,1,0:T(8,...) custom-call(s32[3]{0:T(128)S(1)} %copy-done.4, ...), custom_call_target="tpu_custom_call" | custom-call | bytes 3000000 | tf_op jit(solution)/shard_map/scatter_rows/pallas_call | solution.py:393
  99.6 2.2 %collective-permute-start.16 = (f32[4,2,8,512]{3,2,1,0:T(8,128)S(1)}, f32[4,2,8,512]{3,2,1,0:T(8,128)S(1)}, u32[]{:S(2)}, u32[]{:S(2)}) collective-permute-start(f32[4,2,8,512]{3,2,1,0:T(8,128)S(1)} %get-tuple-element.36), channel_id=1, source_target_pairs={{0,32},{32,64},{64,96},{96,128},{128,160},{160,192},{192,224},{224... | collective-permute-start | bytes 393224 | tf_op jit(solution)/shard_map/ppermute | solution.py:301
  101.8 4.1 %collective-permute-done.16 = f32[4,2,8,512]{3,2,1,0:T(8,128)S(1)} collective-permute-done((f32[4,2,8,512]{3,2,1,0:T(8,128)S(1)}, f32[4,2,8,512]{3,2,1,0:T(8,128)S(1)}, u32[]{:S(2)}, u32[]{:S(2)}) %collective-permute-start.16) | collective-permute-done | bytes 131104 | tf_op jit(solution)/shard_map/ppermute | solution.py:301
  105.9 3.4 %collective-permute-start.17 = (f32[4,2,8,512]{3,2,1,0:T(8,128)S(1)}, f32[4,2,8,512]{3,2,1,0:T(8,128)S(1)}, u32[]{:S(2)}, u32[]{:S(2)}) collective-permute-start(f32[4,2,8,512]{3,2,1,0:T(8,128)S(1)} %add.90), channel_id=1, source_target_pairs={{0,32},{32,64},{64,96},{96,128},{128,160},{160,192},{192,224},{224... | collective-permute-start | bytes 393224 | tf_op jit(solution)/shard_map/ppermute | solution.py:301
  109.3 3.7 %collective-permute-start.23 = (f32[4,2,8,512]{3,2,1,0:T(8,128)S(1)}, f32[4,2,8,512]{3,2,1,0:T(8,128)S(1)}, u32[]{:S(2)}, u32[]{:S(2)}) collective-permute-start(f32[4,2,8,512]{3,2,1,0:T(8,128)S(1)} %get-tuple-element.44), channel_id=1, source_target_pairs={{0,32},{32,64},{64,96},{96,128},{128,160},{160,192},{192,224},{224... | collective-permute-start | bytes 393224 | tf_op jit(solution)/shard_map/ppermute | solution.py:301
  113.3 3.7 %collective-permute-start.18 = (f32[4,2,8,512]{3,2,1,0:T(8,128)S(1)}, f32[4,2,8,512]{3,2,1,0:T(8,128)S(1)}, u32[]{:S(2)}, u32[]{:S(2)}) collective-permute-start(f32[4,2,8,512]{3,2,1,0:T(8,128)S(1)} %add.91), channel_id=1, source_target_pairs={{0,32},{32,64},{64,96},{96,128},{128,160},{160,192},{192,224},{224... | collective-permute-start | bytes 393224 | tf_op jit(solution)/shard_map/ppermute | solution.py:301
  117.0 3.8 %collective-permute-start.24 = (f32[4,2,8,512]{3,2,1,0:T(8,128)S(1)}, f32[4,2,8,512]{3,2,1,0:T(8,128)S(1)}, u32[]{:S(2)}, u32[]{:S(2)}) collective-permute-start(f32[4,2,8,512]{3,2,1,0:T(8,128)S(1)} %add.97), channel_id=1, source_target_pairs={{0,32},{32,64},{64,96},{96,128},{128,160},{160,192},{192,224},{224... | collective-permute-start | bytes 393224 | tf_op jit(solution)/shard_map/ppermute | solution.py:301
  120.9 0.1 collective-permute-start.22
  121.1 3.5 %collective-permute-start.19 = (f32[4,2,8,512]{3,2,1,0:T(8,128)S(1)}, f32[4,2,8,512]{3,2,1,0:T(8,128)S(1)}, u32[]{:S(2)}, u32[]{:S(2)}) collective-permute-start(f32[4,2,8,512]{3,2,1,0:T(8,128)S(1)} %add.92), channel_id=1, source_target_pairs={{0,32},{32,64},{64,96},{96,128},{128,160},{160,192},{192,224},{224... | collective-permute-start | bytes 393224 | tf_op jit(solution)/shard_map/ppermute | solution.py:301
  124.5 0.1 collective-permute-done.24
  124.6 3.7 %collective-permute-start.25 = (f32[4,2,8,512]{3,2,1,0:T(8,128)S(1)}, f32[4,2,8,512]{3,2,1,0:T(8,128)S(1)}, u32[]{:S(2)}, u32[]{:S(2)}) collective-permute-start(f32[4,2,8,512]{3,2,1,0:T(8,128)S(1)} %add.98), channel_id=1, source_target_pairs={{0,32},{32,64},{64,96},{96,128},{128,160},{160,192},{192,224},{224... | collective-permute-start | bytes 393224 | tf_op jit(solution)/shard_map/ppermute | solution.py:301
  128.5 2.3 %collective-permute-done.25 = f32[4,2,8,512]{3,2,1,0:T(8,128)S(1)} collective-permute-done((f32[4,2,8,512]{3,2,1,0:T(8,128)S(1)}, f32[4,2,8,512]{3,2,1,0:T(8,128)S(1)}, u32[]{:S(2)}, u32[]{:S(2)}) %collective-permute-start.25) | collective-permute-done | bytes 131104 | tf_op jit(solution)/shard_map/ppermute | solution.py:301
  130.8 2.9 %collective-permute-done.29 = f32[4,2,8,512]{3,2,1,0:T(8,128)S(1)} collective-permute-done((f32[4,2,8,512]{3,2,1,0:T(8,128)S(1)}, f32[4,2,8,512]{3,2,1,0:T(8,128)S(1)}, u32[]{:S(2)}, u32[]{:S(2)}) %collective-permute-start.29) | collective-permute-done | bytes 131104 | tf_op jit(solution)/shard_map/ppermute | solution.py:306
  133.8 9.9 %all_to_all.16 = f32[8,2,8,512]{3,2,1,0:T(8,128)S(1)} all-to-all(f32[8,2,8,512]{3,2,1,0:T(8,128)S(1)} %pad_maximum_fusion.3), channel_id=1, replica_groups=mesh['z'=8,'x'=4,'y'=4,'core'=2] {'y','core'}, dimensions={0} | all-to-all | bytes 524288 | tf_op jit(solution)/shard_map/all_to_all | solution.py:404
  143.7 0.7 copy_bitcast_fusion
  (58 shorter events, 0.8 us)
Async XLA Ops:
  0.0 28.8 %copy-start.3 = (s32[8,2,32]{2,1,0:T(2,128)S(1)}, s32[8,2,32]{2,1,0:T(2,128)}, u32[]{:S(2)}) copy-start(s32[8,2,32]{2,1,0:T(2,128)} %cols.3) | copy-start | bytes 6148
  0.0 28.8 %copy-start.2 = (s32[8,2,32]{2,1,0:T(2,128)S(1)}, s32[8,2,32]{2,1,0:T(2,128)}, u32[]{:S(2)}) copy-start(s32[8,2,32]{2,1,0:T(2,128)} %rows.3) | copy-start | bytes 6148
  0.6 33.1 %copy-start.4 = (s32[3]{0:T(128)S(1)}, s32[3]{0:T(128)}, u32[]{:S(2)}) copy-start(s32[3]{0:T(128)} %pad_add_fusion.1.place) | copy-start | bytes 40
  0.6 45.5 %copy-start.7 = (f32[384,256]{1,0:T(8,128)S(1)}, f32[384,256]{1,0:T(8,128)}, u32[]{:S(2)}) copy-start(f32[384,256]{1,0:T(8,128)} %param.10) | copy-start | bytes 1179652
  3.1 5.5 %collective-permute-start.6 = (f32[8,4096]{1,0:T(8,128)}, f32[8,4096]{1,0:T(8,128)S(1)}, u32[]{:S(2)}, u32[]{:S(2)}) collective-permute-start(f32[8,4096]{1,0:T(8,128)} %get-tuple-element.28.refs_0_), channel_id=1, source_target_pairs={{0,32},{32,64},{64,96},{96,128},{128,160},{160,192},{192,224},{224... | collective-permute-start | bytes 393224 | tf_op jit(solution)/shard_map/ppermute | solution.py:301
  5.1 7.7 %collective-permute-start.1 = (f32[8,4096]{1,0:T(8,128)}, f32[8,4096]{1,0:T(8,128)S(1)}, u32[]{:S(2)}, u32[]{:S(2)}) collective-permute-start(f32[8,4096]{1,0:T(8,128)} %get-tuple-element.29.refs_1_), channel_id=1, source_target_pairs={{32,0},{64,32},{96,64},{128,96},{160,128},{192,160},{224,192},{0,2... | collective-permute-start | bytes 393224 | tf_op jit(solution)/shard_map/ppermute | solution.py:306
  5.2 9.3 %collective-permute-start = (f32[8,4096]{1,0:T(8,128)}, f32[8,4096]{1,0:T(8,128)S(1)}, u32[]{:S(2)}, u32[]{:S(2)}) collective-permute-start(f32[8,4096]{1,0:T(8,128)} %get-tuple-element.28.refs_0_), channel_id=1, source_target_pairs={{32,0},{64,32},{96,64},{128,96},{160,128},{192,160},{224,192},{0,2... | collective-permute-start | bytes 393224 | tf_op jit(solution)/shard_map/ppermute | solution.py:306
  5.3 9.2 %collective-permute-start.11 = (f32[8,4096]{1,0:T(8,128)}, f32[8,4096]{1,0:T(8,128)S(1)}, u32[]{:S(2)}, u32[]{:S(2)}) collective-permute-start(f32[8,4096]{1,0:T(8,128)} %get-tuple-element.29.refs_1_), channel_id=1, source_target_pairs={{0,32},{32,64},{64,96},{96,128},{128,160},{160,192},{192,224},{224... | collective-permute-start | bytes 393224 | tf_op jit(solution)/shard_map/ppermute | solution.py:301
  8.6 8.8 %collective-permute-start.7 = (f32[8,4096]{1,0:T(8,128)S(1)}, f32[8,4096]{1,0:T(8,128)S(1)}, u32[]{:S(2)}, u32[]{:S(2)}) collective-permute-start(f32[8,4096]{1,0:T(8,128)S(1)} %collective-permute-done.6.refs_14_), channel_id=1, source_target_pairs={{0,32},{32,64},{64,96},{96,128},{128,160},{160,192},{192,224},{224... | collective-permute-start | bytes 393224 | tf_op jit(solution)/shard_map/ppermute | solution.py:301
  12.8 7.9 %collective-permute-start.3 = (f32[8,4096]{1,0:T(8,128)S(1)}, f32[8,4096]{1,0:T(8,128)S(1)}, u32[]{:S(2)}, u32[]{:S(2)}) collective-permute-start(f32[8,4096]{1,0:T(8,128)S(1)} %collective-permute-done.1.refs_3_), channel_id=1, source_target_pairs={{32,0},{64,32},{96,64},{128,96},{160,128},{192,160},{224,192},{0,2... | collective-permute-start | bytes 393224 | tf_op jit(solution)/shard_map/ppermute | solution.py:306
  14.4 6.8 %collective-permute-start.2 = (f32[8,4096]{1,0:T(8,128)S(1)}, f32[8,4096]{1,0:T(8,128)S(1)}, u32[]{:S(2)}, u32[]{:S(2)}) collective-permute-start(f32[8,4096]{1,0:T(8,128)S(1)} %collective-permute-done.refs_2_), channel_id=1, source_target_pairs={{32,0},{64,32},{96,64},{128,96},{160,128},{192,160},{224,192},{0,2... | collective-permute-start | bytes 393224 | tf_op jit(solution)/shard_map/ppermute | solution.py:306
  14.5 6.8 %collective-permute-start.12 = (f32[8,4096]{1,0:T(8,128)S(1)}, f32[8,4096]{1,0:T(8,128)S(1)}, u32[]{:S(2)}, u32[]{:S(2)}) collective-permute-start(f32[8,4096]{1,0:T(8,128)S(1)} %collective-permute-done.11.refs_15_), channel_id=1, source_target_pairs={{0,32},{32,64},{64,96},{96,128},{128,160},{160,192},{192,224},{224... | collective-permute-start | bytes 393224 | tf_op jit(solution)/shard_map/ppermute | solution.py:301
  17.4 8.1 %collective-permute-start.8 = (f32[8,4096]{1,0:T(8,128)S(1)}, f32[8,4096]{1,0:T(8,128)S(1)}, u32[]{:S(2)}, u32[]{:S(2)}) collective-permute-start(f32[8,4096]{1,0:T(8,128)S(1)} %collective-permute-done.7.refs_12_), channel_id=1, source_target_pairs={{0,32},{32,64},{64,96},{96,128},{128,160},{160,192},{192,224},{224... | collective-permute-start | bytes 393224 | tf_op jit(solution)/shard_map/ppermute | solution.py:301
  20.6 8.1 %collective-permute-start.5 = (f32[8,4096]{1,0:T(8,128)S(1)}, f32[8,4096]{1,0:T(8,128)S(1)}, u32[]{:S(2)}, u32[]{:S(2)}) collective-permute-start(f32[8,4096]{1,0:T(8,128)S(1)} %collective-permute-done.3.refs_5_), channel_id=1, source_target_pairs={{32,0},{64,32},{96,64},{128,96},{160,128},{192,160},{224,192},{0,2... | collective-permute-start | bytes 393224 | tf_op jit(solution)/shard_map/ppermute | solution.py:306
  21.2 8.5 %collective-permute-start.4 = (f32[8,4096]{1,0:T(8,128)S(1)}, f32[8,4096]{1,0:T(8,128)S(1)}, u32[]{:S(2)}, u32[]{:S(2)}) collective-permute-start(f32[8,4096]{1,0:T(8,128)S(1)} %collective-permute-done.2.refs_4_), channel_id=1, source_target_pairs={{32,0},{64,32},{96,64},{128,96},{160,128},{192,160},{224,192},{0,2... | collective-permute-start | bytes 393224 | tf_op jit(solution)/shard_map/ppermute | solution.py:306
  21.2 8.5 %collective-permute-start.13 = (f32[8,4096]{1,0:T(8,128)S(1)}, f32[8,4096]{1,0:T(8,128)S(1)}, u32[]{:S(2)}, u32[]{:S(2)}) collective-permute-start(f32[8,4096]{1,0:T(8,128)S(1)} %collective-permute-done.12.refs_13_), channel_id=1, source_target_pairs={{0,32},{32,64},{64,96},{96,128},{128,160},{160,192},{192,224},{224... | collective-permute-start | bytes 393224 | tf_op jit(solution)/shard_map/ppermute | solution.py:301
  25.5 5.8 %collective-permute-start.9 = (f32[8,4096]{1,0:T(8,128)S(1)}, f32[8,4096]{1,0:T(8,128)S(1)}, u32[]{:S(2)}, u32[]{:S(2)}) collective-permute-start(f32[8,4096]{1,0:T(8,128)S(1)} %collective-permute-done.8.refs_10_), channel_id=1, source_target_pairs={{0,32},{32,64},{64,96},{96,128},{128,160},{160,192},{192,224},{224... | collective-permute-start | bytes 393224 | tf_op jit(solution)/shard_map/ppermute | solution.py:301
  28.8 5.0 %collective-permute-start.10 = (f32[8,4096]{1,0:T(8,128)S(1)}, f32[8,4096]{1,0:T(8,128)S(1)}, u32[]{:S(2)}, u32[]{:S(2)}) collective-permute-start(f32[8,4096]{1,0:T(8,128)S(1)} %collective-permute-done.5.refs_7_), channel_id=1, source_target_pairs={{32,0},{64,32},{96,64},{128,96},{160,128},{192,160},{224,192},{0,2... | collective-permute-start | bytes 393224 | tf_op jit(solution)/shard_map/ppermute | solution.py:306
  33.7 0.9 copy-start
  34.6 0.9 copy-start.1
  38.7 26.0 %all-to-all-start = ((f32[32,2,8,256]{3,2,1,0:T(8,128)}), f32[32,2,8,256]{3,2,1,0:T(8,128)S(1)}, u32[]{:S(2)}, u32[]{:S(2)}) async-start(f32[32,2,8,256]{3,2,1,0:T(8,128)} %select_rows.1), calls=%async_computation | async-start | bytes 1048576 | tf_op jit(solution)/shard_map/all_to_all | solution.py:365
  46.2 12.6 %collective-permute-start.14 = (f32[384,64]{1,0:T(8,128)S(1)}, f32[384,64]{1,0:T(8,128)S(1)}, u32[]{:S(2)}, u32[]{:S(2)}) collective-permute-start(f32[384,64]{1,0:T(8,128)S(1)} %get-tuple-element.51), channel_id=1, source_target_pairs={{8,0},{16,8},{24,16},{32,24},{40,32},{48,40},{56,48},{64,56},{72,6... | collective-permute-start | bytes 294920 | tf_op jit(solution)/shard_map/ppermute | solution.py:371
  50.6 10.7 %collective-permute-start.15 = (f32[384,64]{1,0:T(8,128)S(1)}, f32[384,64]{1,0:T(8,128)S(1)}, u32[]{:S(2)}, u32[]{:S(2)}) collective-permute-start(f32[384,64]{1,0:T(8,128)S(1)} %get-tuple-element.52), channel_id=1, source_target_pairs={{0,8},{8,16},{16,24},{24,32},{32,40},{40,48},{48,56},{56,64},{64,7... | collective-permute-start | bytes 294920 | tf_op jit(solution)/shard_map/ppermute | solution.py:368
  61.5 3.3 %copy-start.5 = (f32[256,256]{1,0:T(8,128)S(1)}, f32[256,256]{1,0:T(8,128)}, u32[]{:S(2)}) copy-start(f32[256,256]{1,0:T(8,128)} %amp_ref.1) | copy-start | bytes 786436
  61.5 3.3 %copy-start.6 = (f32[1,256,256]{2,1,0:T(8,128)S(1)}, f32[1,256,256]{2,1,0:T(8,128)}, u32[]{:S(2)}) copy-start(f32[1,256,256]{2,1,0:T(8,128)} %observed.1) | copy-start | bytes 786436
  99.6 6.3 %collective-permute-start.16 = (f32[4,2,8,512]{3,2,1,0:T(8,128)S(1)}, f32[4,2,8,512]{3,2,1,0:T(8,128)S(1)}, u32[]{:S(2)}, u32[]{:S(2)}) collective-permute-start(f32[4,2,8,512]{3,2,1,0:T(8,128)S(1)} %get-tuple-element.36), channel_id=1, source_target_pairs={{0,32},{32,64},{64,96},{96,128},{128,160},{160,192},{192,224},{224... | collective-permute-start | bytes 393224 | tf_op jit(solution)/shard_map/ppermute | solution.py:301
  101.8 11.2 %collective-permute-start.26 = (f32[4,2,8,512]{3,2,1,0:T(8,128)S(1)}, f32[4,2,8,512]{3,2,1,0:T(8,128)S(1)}, u32[]{:S(2)}, u32[]{:S(2)}) collective-permute-start(f32[4,2,8,512]{3,2,1,0:T(8,128)S(1)} %get-tuple-element.47), channel_id=1, source_target_pairs={{32,0},{64,32},{96,64},{128,96},{160,128},{192,160},{224,192},{0,2... | collective-permute-start | bytes 393224 | tf_op jit(solution)/shard_map/ppermute | solution.py:306
  101.8 11.3 %collective-permute-start.20 = (f32[4,2,8,512]{3,2,1,0:T(8,128)S(1)}, f32[4,2,8,512]{3,2,1,0:T(8,128)S(1)}, u32[]{:S(2)}, u32[]{:S(2)}) collective-permute-start(f32[4,2,8,512]{3,2,1,0:T(8,128)S(1)} %get-tuple-element.40), channel_id=1, source_target_pairs={{32,0},{64,32},{96,64},{128,96},{160,128},{192,160},{224,192},{0,2... | collective-permute-start | bytes 393224 | tf_op jit(solution)/shard_map/ppermute | solution.py:306
  105.9 7.3 %collective-permute-start.17 = (f32[4,2,8,512]{3,2,1,0:T(8,128)S(1)}, f32[4,2,8,512]{3,2,1,0:T(8,128)S(1)}, u32[]{:S(2)}, u32[]{:S(2)}) collective-permute-start(f32[4,2,8,512]{3,2,1,0:T(8,128)S(1)} %add.90), channel_id=1, source_target_pairs={{0,32},{32,64},{64,96},{96,128},{128,160},{160,192},{192,224},{224... | collective-permute-start | bytes 393224 | tf_op jit(solution)/shard_map/ppermute | solution.py:301
  109.3 7.7 %collective-permute-start.23 = (f32[4,2,8,512]{3,2,1,0:T(8,128)S(1)}, f32[4,2,8,512]{3,2,1,0:T(8,128)S(1)}, u32[]{:S(2)}, u32[]{:S(2)}) collective-permute-start(f32[4,2,8,512]{3,2,1,0:T(8,128)S(1)} %get-tuple-element.44), channel_id=1, source_target_pairs={{0,32},{32,64},{64,96},{96,128},{128,160},{160,192},{192,224},{224... | collective-permute-start | bytes 393224 | tf_op jit(solution)/shard_map/ppermute | solution.py:301
  113.0 7.8 %collective-permute-start.27 = (f32[4,2,8,512]{3,2,1,0:T(8,128)S(1)}, f32[4,2,8,512]{3,2,1,0:T(8,128)S(1)}, u32[]{:S(2)}, u32[]{:S(2)}) collective-permute-start(f32[4,2,8,512]{3,2,1,0:T(8,128)S(1)} %add.100), channel_id=1, source_target_pairs={{32,0},{64,32},{96,64},{128,96},{160,128},{192,160},{224,192},{0,2... | collective-permute-start | bytes 393224 | tf_op jit(solution)/shard_map/ppermute | solution.py:306
  113.1 7.7 %collective-permute-start.21 = (f32[4,2,8,512]{3,2,1,0:T(8,128)S(1)}, f32[4,2,8,512]{3,2,1,0:T(8,128)S(1)}, u32[]{:S(2)}, u32[]{:S(2)}) collective-permute-start(f32[4,2,8,512]{3,2,1,0:T(8,128)S(1)} %add.94), channel_id=1, source_target_pairs={{32,0},{64,32},{96,64},{128,96},{160,128},{192,160},{224,192},{0,2... | collective-permute-start | bytes 393224 | tf_op jit(solution)/shard_map/ppermute | solution.py:306
  113.3 7.8 %collective-permute-start.18 = (f32[4,2,8,512]{3,2,1,0:T(8,128)S(1)}, f32[4,2,8,512]{3,2,1,0:T(8,128)S(1)}, u32[]{:S(2)}, u32[]{:S(2)}) collective-permute-start(f32[4,2,8,512]{3,2,1,0:T(8,128)S(1)} %add.91), channel_id=1, source_target_pairs={{0,32},{32,64},{64,96},{96,128},{128,160},{160,192},{192,224},{224... | collective-permute-start | bytes 393224 | tf_op jit(solution)/shard_map/ppermute | solution.py:301
  117.0 7.6 %collective-permute-start.24 = (f32[4,2,8,512]{3,2,1,0:T(8,128)S(1)}, f32[4,2,8,512]{3,2,1,0:T(8,128)S(1)}, u32[]{:S(2)}, u32[]{:S(2)}) collective-permute-start(f32[4,2,8,512]{3,2,1,0:T(8,128)S(1)} %add.97), channel_id=1, source_target_pairs={{0,32},{32,64},{64,96},{96,128},{128,160},{160,192},{192,224},{224... | collective-permute-start | bytes 393224 | tf_op jit(solution)/shard_map/ppermute | solution.py:301
  120.8 7.5 %collective-permute-start.28 = (f32[4,2,8,512]{3,2,1,0:T(8,128)S(1)}, f32[4,2,8,512]{3,2,1,0:T(8,128)S(1)}, u32[]{:S(2)}, u32[]{:S(2)}) collective-permute-start(f32[4,2,8,512]{3,2,1,0:T(8,128)S(1)} %add.101), channel_id=1, source_target_pairs={{32,0},{64,32},{96,64},{128,96},{160,128},{192,160},{224,192},{0,2... | collective-permute-start | bytes 393224 | tf_op jit(solution)/shard_map/ppermute | solution.py:306
  120.9 7.5 %collective-permute-start.22 = (f32[4,2,8,512]{3,2,1,0:T(8,128)S(1)}, f32[4,2,8,512]{3,2,1,0:T(8,128)S(1)}, u32[]{:S(2)}, u32[]{:S(2)}) collective-permute-start(f32[4,2,8,512]{3,2,1,0:T(8,128)S(1)} %add.95), channel_id=1, source_target_pairs={{32,0},{64,32},{96,64},{128,96},{160,128},{192,160},{224,192},{0,2... | collective-permute-start | bytes 393224 | tf_op jit(solution)/shard_map/ppermute | solution.py:306
  121.1 7.4 %collective-permute-start.19 = (f32[4,2,8,512]{3,2,1,0:T(8,128)S(1)}, f32[4,2,8,512]{3,2,1,0:T(8,128)S(1)}, u32[]{:S(2)}, u32[]{:S(2)}) collective-permute-start(f32[4,2,8,512]{3,2,1,0:T(8,128)S(1)} %add.92), channel_id=1, source_target_pairs={{0,32},{32,64},{64,96},{96,128},{128,160},{160,192},{192,224},{224... | collective-permute-start | bytes 393224 | tf_op jit(solution)/shard_map/ppermute | solution.py:301
  124.6 6.2 %collective-permute-start.25 = (f32[4,2,8,512]{3,2,1,0:T(8,128)S(1)}, f32[4,2,8,512]{3,2,1,0:T(8,128)S(1)}, u32[]{:S(2)}, u32[]{:S(2)}) collective-permute-start(f32[4,2,8,512]{3,2,1,0:T(8,128)S(1)} %add.98), channel_id=1, source_target_pairs={{0,32},{32,64},{64,96},{96,128},{128,160},{160,192},{192,224},{224... | collective-permute-start | bytes 393224 | tf_op jit(solution)/shard_map/ppermute | solution.py:301
  128.3 5.4 %collective-permute-start.29 = (f32[4,2,8,512]{3,2,1,0:T(8,128)S(1)}, f32[4,2,8,512]{3,2,1,0:T(8,128)S(1)}, u32[]{:S(2)}, u32[]{:S(2)}) collective-permute-start(f32[4,2,8,512]{3,2,1,0:T(8,128)S(1)} %add.102), channel_id=1, source_target_pairs={{32,0},{64,32},{96,64},{128,96},{160,128},{192,160},{224,192},{0,2... | collective-permute-start | bytes 393224 | tf_op jit(solution)/shard_map/ppermute | solution.py:306

commit v5 on v4

--- a/solution.py
+++ b/solution.py
@@ -1,4 +1,3 @@
-import functools
 import math
 
 import jax
@@ -8,6 +7,7 @@
 from jax.experimental.pallas import tpu as pltpu
 from jax.sharding import Mesh, PartitionSpec as P
 
+
 CORE = 256
 HALO = 64
 SPAN = 384
@@ -26,48 +26,47 @@
     return jnp.dot(left, right, preferred_element_type=jnp.float32)
 
 
-def product(left, right):
-    return dot(left[0], right[0]) + (dot(left[0], right[1]) + dot(left[1], right[0]))
-
-
 def left(matrix, rows, parts):
-    stacked, extra = None, None
+    totals = [None, None]
     for lanes, (high, low) in parts:
-        four = matrix[:, 0:rows, lanes].reshape(4 * rows, high.shape[0])
-        term, small = dot(four, high), dot(four[0 : 2 * rows], low)
-        stacked = term if stacked is None else stacked + term
-        extra = small if extra is None else extra + small
-    real = stacked[0:rows] + (stacked[2 * rows : 3 * rows] + extra[0:rows])
-    imag = stacked[rows : 2 * rows] + (stacked[3 * rows : 4 * rows] + extra[rows : 2 * rows])
-    return real, imag
+        for block in range(2):
+            both = matrix[2 * block : 2 * block + 2, 0:rows, lanes].reshape(2 * rows, high.shape[0])
+            term, small = dot(both, high), dot(both[0:rows], low)
+            before = totals[block]
+            totals[block] = (term, small) if before is None else (before[0] + term, before[1] + small)
+    return tuple(term[0:rows] + (term[rows : 2 * rows] + small) for term, small in totals)
 
 
 def right(parts, matrix, lanes):
-    stacked, extra = None, None
+    rows = parts[0][0].shape[0] // 2
+    totals = [None, None]
     for part, (high, low) in enumerate(parts):
         depth = high.shape[1]
-        term = dot(jnp.concatenate([high, low], axis=0), matrix[part, 0:depth, lanes])
-        small = dot(high, matrix[2 + part, 0:depth, lanes])
-        stacked = term if stacked is None else stacked + term
-        extra = small if extra is None else extra + small
-    rows = extra.shape[0]
-    return stacked[0:rows] + (stacked[rows : 2 * rows] + extra)
+        weights = (matrix[2 * part, 0:depth, lanes], matrix[2 * part + 1, 0:depth, lanes])
+        for block in range(2):
+            at = slice(block * rows, block * rows + rows)
+            term = dot(jnp.concatenate([high[at], low[at]], axis=0), weights[0])
+            small = dot(high[at], weights[1])
+            before = totals[block]
+            totals[block] = (term, small) if before is None else (before[0] + term, before[1] + small)
+    return jnp.concatenate(
+        [term[0:rows] + (term[rows : 2 * rows] + small) for term, small in totals], axis=0
+    )
 
 
 def build(matrix, base, sign):
     for part in range(2):
         cosine, sine = base[2 * part], base[2 * part + 1]
-        matrix[2 * part, :, FULL] = cosine
-        matrix[2 * part, :, REST] = sine if sign > 0 else -sine
-        matrix[2 * part + 1, :, FULL] = -sine if sign > 0 else sine
-        matrix[2 * part + 1, :, REST] = cosine
+        matrix[part, :, FULL] = cosine
+        matrix[part, :, REST] = sine if sign > 0 else -sine
+        matrix[2 + part, :, FULL] = -sine if sign > 0 else sine
+        matrix[2 + part, :, REST] = cosine
 
 
 def sine_cosine(angle):
     turns = jnp.round(angle * (2.0 / math.pi))
     rest = angle - turns * 1.5703125
-    rest = rest - turns * 4.837512969970703125e-4
-    rest = rest - turns * 7.549789948768648e-8
+    rest = rest - turns * 4.83826794896619e-4
     square = rest * rest
     sine = rest + rest * square * (
         -1.6666654611e-1 + square * (8.3321608736e-3 + square * -1.9515295891e-4)
@@ -224,8 +223,9 @@
         forward, SPAN, [(LOW, split(pupil_re[...])), (HIGH, split(pupil_im[...]))]
     )
     half = [split(half_re), split(half_im)]
-    far_re[...] = right(half, inverse, FULL)
-    far_im[...] = right(half, inverse, REST)
+    far = right(half, inverse, ALL)
+    far_re[...] = far[:, FULL]
+    far_im[...] = far[:, REST]
     spread = [split((far_re[...] * far_re[...] + far_im[...] * far_im[...]) * inverse_total)]
     put(mix_h, mix_l, FULL, right(spread, inverse, LOW))
     put(mix_h, mix_l, REST, right(spread, inverse, HIGH))
@@ -272,7 +272,7 @@
     return jax.ShapeDtypeStruct(shape, jnp.float32)
 
 
-def gradient_call(*operands, name="gradient"):
+def gradient_call(*operands):
     return pl.pallas_call(
         gradient_kernel,
         out_shape=f32(32, 2, 8, CORE),
@@ -292,7 +292,6 @@
         ],
         compiler_params=limit(28),
         cost_estimate=cost(3 * 2 * 1222 * 10**6, 7 * 10**6),
-        name=name,
     )(*operands)
 
 
@@ -341,13 +340,18 @@
     patch = slab * 4 + across
     patches = lax.axis_size("z") * lax.axis_size("x")
     place = jnp.stack([slab, across * 64 + frame_id * 8, frame_id * 8]).astype(jnp.int32)
+    ends = patches - 1
+    left_tail = lax.ppermute(
+        object_strip[:, CORE - HALO :], ("z", "x"), [(i, i + 1) for i in range(ends)]
+    )
+    right_head = lax.ppermute(object_strip[:, :HALO], ("z", "x"), [(i + 1, i) for i in range(ends)])
     own = pl.pallas_call(
         cut_kernel,
         out_shape=[f32(8, screens.shape[2])] * 2,
         in_specs=[SMEM, ANY],
         out_specs=[VMEM] * 2,
         scratch_shapes=[pltpu.SemaphoreType.DMA((2,))],
-        compiler_params=limit(61),
+        compiler_params=limit(20),
         name="cut_rows",
     )(place, screens)
     chunks = ring_gather(own)
@@ -361,15 +365,9 @@
         cost_estimate=cost(0, 3 * 10**6),
         name="select_rows",
     )(place, row_offsets, col_offsets, *chunks)
-    sent, strip = lax.optimization_barrier((sent, object_strip))
+    sent, left_tail, right_head = lax.optimization_barrier((sent, left_tail, right_head))
     received = lax.all_to_all(sent, SLAB, split_axis=0, concat_axis=0, tiled=True)
-
-    ends = patches - 1
-    left_tail = lax.ppermute(
-        strip[:, CORE - HALO :], ("z", "x"), [(i, i + 1) for i in range(ends)]
-    )
-    right_head = lax.ppermute(strip[:, :HALO], ("z", "x"), [(i + 1, i) for i in range(ends)])
-    window = jnp.concatenate([strip, right_head, left_tail], axis=1)
+    window = jnp.concatenate([object_strip, right_head, left_tail], axis=1)
     window = jnp.concatenate([window[HALO:], window[:HALO]], axis=0)
     base, spec_re, spec_im = pl.pallas_call(
         object_kernel,

time: 146 us -> 135 us (0.925)
  Pallas kernels: 28.2 us -> 22.3 us
  waiting for transfers between devices: 26.7 us -> 22.1 us
    all_to_all x1, waiting for transfers between devices: 0.01 us -> 7.22 us  [body(): lax.all_to_all(sent, SLAB, split_axis=0, concat_axis=0, tiled=True)]
    ppermute x2, waiting for transfers between devices: 8.47 us -> 3.45 us  [the longest x1 3.45 us: body(): lax.ppermute(object_strip[:, CORE - HALO:], ('z', 'x'), [(i, i + 1) for i...]
    pallas_call x1, Pallas kernels: 15.5 us -> 11.2 us  [gradient_call(): pl.pallas_call(gradient_kernel, out_shape=f32(32, 2, 8, CORE), in_specs=[...]
    ppermute x14, waiting for transfers between devices: 9.78 us -> 6.22 us  [down(): lax.ppermute(values, 'z', [((i + 1) % count, i) for i in range(count)])]
    ppermute x14, waiting for transfers between devices: 8.45 us -> 5.2 us  [up(): lax.ppermute(values, 'z', [(i, (i + 1) % count) for i in range(count)])]
    ppermute x14, starting transfers between devices: 45.4 us -> 47 us  [up(): lax.ppermute(values, 'z', [(i, (i + 1) % count) for i in range(count)])]
    pallas_call x1, Pallas kernels: 2.48 us -> 0.9 us  [body(): pl.pallas_call(cut_kernel, out_shape=[f32(8, screens.shape[2])] * 2, in_s...]
  transfers between devices with their start and end apart: 31 -> 31, of which waited for: 13 -> 10; matrix products, arithmetic and copies ran while one was open for 1% -> 1% of each run, Pallas kernels for 2% -> 5%
where the time goes in v5:
time: 135 us; the launch traced here: 133 us
  starting transfers between devices  60.6 us (45%)
  blocking collectives  24.9 us (18%)
  Pallas kernels  22.3 us (17%)
  waiting for transfers between devices  22.1 us (16%)
  local copies, waits for them, and re-layouts  2.47 us (2%)
    ppermute x14, starting transfers between devices, up(): lax.ppermute(values, 'z', [(i, (i + 1) % count) for i in range(count)])  47 us
    all_to_all x1, blocking collectives, body(): lax.all_to_all(placed, SLAB, split_axis=0, concat_axis=0, tiled=True)  15 us
    pallas_call x1, Pallas kernels, gradient_call(): pl.pallas_call(gradient_kernel, out_shape=f32(32, 2, 8, CORE), in_specs=[...  11.2 us
    all_to_all x1, blocking collectives, body(): lax.all_to_all(summed, FRAME, split_axis=0, concat_axis=0, tiled=True)  9.91 us
    all_to_all x1, waiting for transfers between devices, body(): lax.all_to_all(sent, SLAB, split_axis=0, concat_axis=0, tiled=True)  7.22 us
    ppermute x14, waiting for transfers between devices, down(): lax.ppermute(values, 'z', [((i + 1) % count, i) for i in range(count)])  6.22 us
    all_to_all x1, starting transfers between devices, body(): lax.all_to_all(sent, SLAB, split_axis=0, concat_axis=0, tiled=True)  5.9 us
    ppermute x14, waiting for transfers between devices, up(): lax.ppermute(values, 'z', [(i, (i + 1) % count) for i in range(count)])  5.2 us
  transfers between devices with their start and end apart: 31, of which 10 were waited for; matrix products, arithmetic and copies ran while one was open for 1% of the time, Pallas kernels for 5%

profile of v5, /device:TPU:64, one launch (start us, length us, event | category | flops | bytes accessed | tf_op | source)
XLA Modules:
  0.0 133.4 jit_solution(1947338981070883937)
XLA Ops:
  0.1 1.6 %copy-done = f32[2,64,4096]{2,1,0:T(8,128)S(1)} copy-done((f32[2,64,4096]{2,1,0:T(8,128)S(1)}, f32[2,64,4096]{2,1,0:T(8,128)}, u32[]{:S(2)}) %copy-start) | copy-done | bytes 2097176
  1.7 0.9 cut_rows.1
  2.6 2.0 %collective-permute-start.6 = (f32[8,4096]{1,0:T(8,128)S(1)}, f32[8,4096]{1,0:T(8,128)S(1)}, u32[]{:S(2)}, u32[]{:S(2)}) collective-permute-start(f32[8,4096]{1,0:T(8,128)S(1)} %get-tuple-element.29.refs_0_), channel_id=1, source_target_pairs={{0,32},{32,64},{64,96},{96,128},{128,160},{160,192},{192,224},{224... | collective-permute-start | bytes 393224 | tf_op jit(solution)/shard_map/ppermute | solution.py:300
  4.6 0.1 collective-permute-start.1
  4.7 0.1 collective-permute-start
  4.8 2.9 %collective-permute-start.11 = (f32[8,4096]{1,0:T(8,128)S(1)}, f32[8,4096]{1,0:T(8,128)S(1)}, u32[]{:S(2)}, u32[]{:S(2)}) collective-permute-start(f32[8,4096]{1,0:T(8,128)S(1)} %get-tuple-element.30.refs_1_), channel_id=1, source_target_pairs={{0,32},{32,64},{64,96},{96,128},{128,160},{160,192},{192,224},{224... | collective-permute-start | bytes 393224 | tf_op jit(solution)/shard_map/ppermute | solution.py:300
  7.7 0.2 collective-permute-done.6.refs_14_
  7.9 3.1 %collective-permute-start.7 = (f32[8,4096]{1,0:T(8,128)S(1)}, f32[8,4096]{1,0:T(8,128)S(1)}, u32[]{:S(2)}, u32[]{:S(2)}) collective-permute-start(f32[8,4096]{1,0:T(8,128)S(1)} %collective-permute-done.6.refs_14_), channel_id=1, source_target_pairs={{0,32},{32,64},{64,96},{96,128},{128,160},{160,192},{192,224},{224... | collective-permute-start | bytes 393224 | tf_op jit(solution)/shard_map/ppermute | solution.py:300
  11.0 1.1 collective-permute-done.1.refs_3_
  12.1 1.7 %collective-permute-done.refs_2_ = f32[8,4096]{1,0:T(8,128)S(1)} collective-permute-done((f32[8,4096]{1,0:T(8,128)S(1)}, f32[8,4096]{1,0:T(8,128)S(1)}, u32[]{:S(2)}, u32[]{:S(2)}) %collective-permute-start) | collective-permute-done | bytes 131104 | tf_op jit(solution)/shard_map/ppermute | solution.py:305
  13.8 3.0 %collective-permute-start.12 = (f32[8,4096]{1,0:T(8,128)S(1)}, f32[8,4096]{1,0:T(8,128)S(1)}, u32[]{:S(2)}, u32[]{:S(2)}) collective-permute-start(f32[8,4096]{1,0:T(8,128)S(1)} %collective-permute-done.11.refs_15_), channel_id=1, source_target_pairs={{0,32},{32,64},{64,96},{96,128},{128,160},{160,192},{192,224},{224... | collective-permute-start | bytes 393224 | tf_op jit(solution)/shard_map/ppermute | solution.py:300
  16.7 3.2 %collective-permute-start.8 = (f32[8,4096]{1,0:T(8,128)S(1)}, f32[8,4096]{1,0:T(8,128)S(1)}, u32[]{:S(2)}, u32[]{:S(2)}) collective-permute-start(f32[8,4096]{1,0:T(8,128)S(1)} %collective-permute-done.7.refs_12_), channel_id=1, source_target_pairs={{0,32},{32,64},{64,96},{96,128},{128,160},{160,192},{192,224},{224... | collective-permute-start | bytes 393224 | tf_op jit(solution)/shard_map/ppermute | solution.py:300
  20.0 0.6 collective-permute-done.2.refs_4_
  20.5 4.3 %collective-permute-start.13 = (f32[8,4096]{1,0:T(8,128)S(1)}, f32[8,4096]{1,0:T(8,128)S(1)}, u32[]{:S(2)}, u32[]{:S(2)}) collective-permute-start(f32[8,4096]{1,0:T(8,128)S(1)} %collective-permute-done.12.refs_13_), channel_id=1, source_target_pairs={{0,32},{32,64},{64,96},{96,128},{128,160},{160,192},{192,224},{224... | collective-permute-start | bytes 393224 | tf_op jit(solution)/shard_map/ppermute | solution.py:300
  24.8 3.2 %collective-permute-start.9 = (f32[8,4096]{1,0:T(8,128)S(1)}, f32[8,4096]{1,0:T(8,128)S(1)}, u32[]{:S(2)}, u32[]{:S(2)}) collective-permute-start(f32[8,4096]{1,0:T(8,128)S(1)} %collective-permute-done.8.refs_10_), channel_id=1, source_target_pairs={{0,32},{32,64},{64,96},{96,128},{128,160},{160,192},{192,224},{224... | collective-permute-start | bytes 393224 | tf_op jit(solution)/shard_map/ppermute | solution.py:300
  28.1 0.1 fusion.3
  28.2 2.9 %collective-permute-start.15 = (f32[384,64]{1,0:T(8,128)S(1)}, f32[384,64]{1,0:T(8,128)S(1)}, u32[]{:S(2)}, u32[]{:S(2)}) collective-permute-start(f32[384,64]{1,0:T(8,128)S(1)} %get-tuple-element.53), channel_id=1, source_target_pairs={{8,0},{16,8},{24,16},{32,24},{40,32},{48,40},{56,48},{64,56},{72,6... | collective-permute-start | bytes 294920 | tf_op jit(solution)/shard_map/ppermute | solution.py:347
  31.1 2.9 %collective-permute-start.14 = (f32[384,64]{1,0:T(8,128)S(1)}, f32[384,64]{1,0:T(8,128)S(1)}, u32[]{:S(2)}, u32[]{:S(2)}) collective-permute-start(f32[384,64]{1,0:T(8,128)S(1)} %get-tuple-element.54), channel_id=1, source_target_pairs={{0,8},{8,16},{16,24},{24,32},{32,40},{40,48},{48,56},{56,64},{64,7... | collective-permute-start | bytes 294920 | tf_op jit(solution)/shard_map/ppermute | solution.py:344
  34.1 3.2 %select_rows.1 = f32[32,2,8,256]{3,2,1,0:T(8,128)} custom-call(s32[3]{0:T(128)S(1)} %pad_add_fusion.1.place, s32[8,2,32]{2,1,0:T(2,128)S(1)} %copy-done.1, s32[8,2,32]{2,1,0:T(2,128)S(1)} %copy-done.2, f32[8,4096]{1,0:T(8,128)S(1)} %get-tuple-element.29.refs_0_, f32[8,4096]{1,0:T(8,128)S(1)} %get-tuple-element.30.refs_1_, ...), custom_call_target="tpu_custom_call" | custom-call | bytes 3000000 | tf_op jit(solution)/shard_map/select_rows/pallas_call | solution.py:358
  37.3 3.4 %collective-permute-done.14 = f32[384,64]{1,0:T(8,128)S(1)} collective-permute-done((f32[384,64]{1,0:T(8,128)S(1)}, f32[384,64]{1,0:T(8,128)S(1)}, u32[]{:S(2)}, u32[]{:S(2)}) %collective-permute-start.14) | collective-permute-done | bytes 98336 | tf_op jit(solution)/shard_map/ppermute | solution.py:344
  40.8 5.9 %all-to-all-start = ((f32[32,2,8,256]{3,2,1,0:T(8,128)}), f32[32,2,8,256]{3,2,1,0:T(8,128)S(1)}, u32[]{:S(2)}, u32[]{:S(2)}) async-start(f32[32,2,8,256]{3,2,1,0:T(8,128)} %select_rows.1), calls=%async_computation | async-start | bytes 1048576 | tf_op jit(solution)/shard_map/all_to_all | solution.py:369
  46.7 0.1 and_select_fusion
  46.8 0.1 pad_maximum_fusion.2
  47.0 0.1 fusion.window
  47.1 3.2 %object_spectrum.1 = (bf16[4,384,384]{2,1,0:T(8,128)(2,1)S(1)}, f32[384,256]{1,0:T(8,128)S(1)}, f32[384,256]{1,0:T(8,128)S(1)}) custom-call(f32[384,384]{1,0:T(8,128)S(1)} %fusion.window), custom_call_target="tpu_custom_call" | custom-call | flops 1356000000 | bytes 7000000 | tf_op jit(solution)/shard_map/object_spectrum/pallas_call | solution.py:372
  50.4 7.2 %all-to-all-done.received = f32[32,2,8,256]{3,2,1,0:T(8,128)S(1)} async-done(((f32[32,2,8,256]{3,2,1,0:T(8,128)}), f32[32,2,8,256]{3,2,1,0:T(8,128)S(1)}, u32[]{:S(2)}, u32[]{:S(2)}) %all-to-all-start) | async-done | bytes 524320 | tf_op jit(solution)/shard_map/all_to_all | solution.py:369
  57.6 11.2 %shard_map.64 = f32[32,2,8,256]{3,2,1,0:T(8,128)S(1)} custom-call(s32[2,2]{1,0:T(2,128)S(1)} %pad_add_fusion.turns, f32[32,2,8,256]{3,2,1,0:T(8,128)S(1)} %all-to-all-done.received, f32[256,256]{1,0:T(8,128)S(1)} %copy-done.3, f32[1,256,256]{2,1,0:T(8,128)S(1)} %copy-done.4, bf16[4,384,384]{2,1,0:T(8,128)(2,1)S(1)} %get-tuple-element.34.base, ...), custom_call_target="tpu_custom_call" | custom-call | flops 7331999744 | bytes 7000000 | tf_op jit(solution)/shard_map/pallas_call | solution.py:276
  68.8 15.0 %all_to_all.15.values = f32[32,2,8,256]{3,2,1,0:T(8,128)S(1)} all-to-all(f32[32,2,8,256]{3,2,1,0:T(8,128)S(1)} %shard_map.64), channel_id=1, replica_groups=mesh['z'=8,'x'=4,'y'=4,'core'=2] {'x','y','core'}, dimensions={0} | all-to-all | bytes 1048576 | tf_op jit(solution)/shard_map/all_to_all | solution.py:389
  83.8 3.7 %scatter_rows.1 = (f32[4,2,8,512]{3,2,1,0:T(8,128)S(1)}, f32[4,2,8,512]{3,2,1,0:T(8,128)S(1)}, f32[4,2,8,512]{3,2,1,0:T(8,128)S(1)}, f32[4,2,8,512]{3,2,1,0:T(8,...) custom-call(s32[3]{0:T(128)S(1)} %pad_add_fusion.1.place, ...), custom_call_target="tpu_custom_call" | custom-call | bytes 3000000 | tf_op jit(solution)/shard_map/scatter_rows/pallas_call | solution.py:391
  87.5 3.3 %collective-permute-start.16 = (f32[4,2,8,512]{3,2,1,0:T(8,128)S(1)}, f32[4,2,8,512]{3,2,1,0:T(8,128)S(1)}, u32[]{:S(2)}, u32[]{:S(2)}) collective-permute-start(f32[4,2,8,512]{3,2,1,0:T(8,128)S(1)} %get-tuple-element.38), channel_id=1, source_target_pairs={{0,32},{32,64},{64,96},{96,128},{128,160},{160,192},{192,224},{224... | collective-permute-start | bytes 393224 | tf_op jit(solution)/shard_map/ppermute | solution.py:300
  90.8 1.2 collective-permute-start.20
  92.0 2.5 %collective-permute-done.16 = f32[4,2,8,512]{3,2,1,0:T(8,128)S(1)} collective-permute-done((f32[4,2,8,512]{3,2,1,0:T(8,128)S(1)}, f32[4,2,8,512]{3,2,1,0:T(8,128)S(1)}, u32[]{:S(2)}, u32[]{:S(2)}) %collective-permute-start.16) | collective-permute-done | bytes 131104 | tf_op jit(solution)/shard_map/ppermute | solution.py:300
  94.6 3.7 %collective-permute-start.17 = (f32[4,2,8,512]{3,2,1,0:T(8,128)S(1)}, f32[4,2,8,512]{3,2,1,0:T(8,128)S(1)}, u32[]{:S(2)}, u32[]{:S(2)}) collective-permute-start(f32[4,2,8,512]{3,2,1,0:T(8,128)S(1)} %add.90), channel_id=1, source_target_pairs={{0,32},{32,64},{64,96},{96,128},{128,160},{160,192},{192,224},{224... | collective-permute-start | bytes 393224 | tf_op jit(solution)/shard_map/ppermute | solution.py:300
  98.2 3.7 %collective-permute-start.23 = (f32[4,2,8,512]{3,2,1,0:T(8,128)S(1)}, f32[4,2,8,512]{3,2,1,0:T(8,128)S(1)}, u32[]{:S(2)}, u32[]{:S(2)}) collective-permute-start(f32[4,2,8,512]{3,2,1,0:T(8,128)S(1)} %get-tuple-element.46), channel_id=1, source_target_pairs={{0,32},{32,64},{64,96},{96,128},{128,160},{160,192},{192,224},{224... | collective-permute-start | bytes 393224 | tf_op jit(solution)/shard_map/ppermute | solution.py:300
  101.9 0.1 collective-permute-start.27
  102.1 0.1 collective-permute-start.21
  102.2 3.7 %collective-permute-start.18 = (f32[4,2,8,512]{3,2,1,0:T(8,128)S(1)}, f32[4,2,8,512]{3,2,1,0:T(8,128)S(1)}, u32[]{:S(2)}, u32[]{:S(2)}) collective-permute-start(f32[4,2,8,512]{3,2,1,0:T(8,128)S(1)} %add.91), channel_id=1, source_target_pairs={{0,32},{32,64},{64,96},{96,128},{128,160},{160,192},{192,224},{224... | collective-permute-start | bytes 393224 | tf_op jit(solution)/shard_map/ppermute | solution.py:300
  105.9 3.8 %collective-permute-start.24 = (f32[4,2,8,512]{3,2,1,0:T(8,128)S(1)}, f32[4,2,8,512]{3,2,1,0:T(8,128)S(1)}, u32[]{:S(2)}, u32[]{:S(2)}) collective-permute-start(f32[4,2,8,512]{3,2,1,0:T(8,128)S(1)} %add.97), channel_id=1, source_target_pairs={{0,32},{32,64},{64,96},{96,128},{128,160},{160,192},{192,224},{224... | collective-permute-start | bytes 393224 | tf_op jit(solution)/shard_map/ppermute | solution.py:300
  109.7 0.1 collective-permute-start.28
  109.9 0.1 collective-permute-start.22
  110.0 3.5 %collective-permute-start.19 = (f32[4,2,8,512]{3,2,1,0:T(8,128)S(1)}, f32[4,2,8,512]{3,2,1,0:T(8,128)S(1)}, u32[]{:S(2)}, u32[]{:S(2)}) collective-permute-start(f32[4,2,8,512]{3,2,1,0:T(8,128)S(1)} %add.92), channel_id=1, source_target_pairs={{0,32},{32,64},{64,96},{96,128},{128,160},{160,192},{192,224},{224... | collective-permute-start | bytes 393224 | tf_op jit(solution)/shard_map/ppermute | solution.py:300
  113.5 0.1 collective-permute-done.24
  113.6 3.7 %collective-permute-start.25 = (f32[4,2,8,512]{3,2,1,0:T(8,128)S(1)}, f32[4,2,8,512]{3,2,1,0:T(8,128)S(1)}, u32[]{:S(2)}, u32[]{:S(2)}) collective-permute-start(f32[4,2,8,512]{3,2,1,0:T(8,128)S(1)} %add.98), channel_id=1, source_target_pairs={{0,32},{32,64},{64,96},{96,128},{128,160},{160,192},{192,224},{224... | collective-permute-start | bytes 393224 | tf_op jit(solution)/shard_map/ppermute | solution.py:300
  117.3 0.1 collective-permute-start.29
  117.4 2.3 %collective-permute-done.25 = f32[4,2,8,512]{3,2,1,0:T(8,128)S(1)} collective-permute-done((f32[4,2,8,512]{3,2,1,0:T(8,128)S(1)}, f32[4,2,8,512]{3,2,1,0:T(8,128)S(1)}, u32[]{:S(2)}, u32[]{:S(2)}) %collective-permute-start.25) | collective-permute-done | bytes 131104 | tf_op jit(solution)/shard_map/ppermute | solution.py:300
  119.8 2.9 %collective-permute-done.29 = f32[4,2,8,512]{3,2,1,0:T(8,128)S(1)} collective-permute-done((f32[4,2,8,512]{3,2,1,0:T(8,128)S(1)}, f32[4,2,8,512]{3,2,1,0:T(8,128)S(1)}, u32[]{:S(2)}, u32[]{:S(2)}) %collective-permute-start.29) | collective-permute-done | bytes 131104 | tf_op jit(solution)/shard_map/ppermute | solution.py:305
  122.7 9.9 %all_to_all.16 = f32[8,2,8,512]{3,2,1,0:T(8,128)S(1)} all-to-all(f32[8,2,8,512]{3,2,1,0:T(8,128)S(1)} %pad_maximum_fusion.3), channel_id=1, replica_groups=mesh['z'=8,'x'=4,'y'=4,'core'=2] {'y','core'}, dimensions={0} | all-to-all | bytes 524288 | tf_op jit(solution)/shard_map/all_to_all | solution.py:402
  132.6 0.7 copy_bitcast_fusion
  (54 shorter events, 0.6 us)
Async XLA Ops:
  0.0 34.1 %copy-start.2 = (s32[8,2,32]{2,1,0:T(2,128)S(1)}, s32[8,2,32]{2,1,0:T(2,128)}, u32[]{:S(2)}) copy-start(s32[8,2,32]{2,1,0:T(2,128)} %cols.3) | copy-start | bytes 6148
  0.0 34.1 %copy-start.1 = (s32[8,2,32]{2,1,0:T(2,128)S(1)}, s32[8,2,32]{2,1,0:T(2,128)}, u32[]{:S(2)}) copy-start(s32[8,2,32]{2,1,0:T(2,128)} %rows.3) | copy-start | bytes 6148
  0.1 1.6 %copy-start = (f32[2,64,4096]{2,1,0:T(8,128)S(1)}, f32[2,64,4096]{2,1,0:T(8,128)}, u32[]{:S(2)}) copy-start(f32[2,64,4096]{2,1,0:T(8,128)} %screens.1) | copy-start | bytes 6291460
  1.7 26.4 %copy-start.5 = (f32[384,256]{1,0:T(8,128)S(1)}, f32[384,256]{1,0:T(8,128)}, u32[]{:S(2)}) copy-start(f32[384,256]{1,0:T(8,128)} %param.10) | copy-start | bytes 1179652
  2.6 5.3 %collective-permute-start.6 = (f32[8,4096]{1,0:T(8,128)S(1)}, f32[8,4096]{1,0:T(8,128)S(1)}, u32[]{:S(2)}, u32[]{:S(2)}) collective-permute-start(f32[8,4096]{1,0:T(8,128)S(1)} %get-tuple-element.29.refs_0_), channel_id=1, source_target_pairs={{0,32},{32,64},{64,96},{96,128},{128,160},{160,192},{192,224},{224... | collective-permute-start | bytes 393224 | tf_op jit(solution)/shard_map/ppermute | solution.py:300
  4.6 7.5 %collective-permute-start.1 = (f32[8,4096]{1,0:T(8,128)S(1)}, f32[8,4096]{1,0:T(8,128)S(1)}, u32[]{:S(2)}, u32[]{:S(2)}) collective-permute-start(f32[8,4096]{1,0:T(8,128)S(1)} %get-tuple-element.30.refs_1_), channel_id=1, source_target_pairs={{32,0},{64,32},{96,64},{128,96},{160,128},{192,160},{224,192},{0,2... | collective-permute-start | bytes 393224 | tf_op jit(solution)/shard_map/ppermute | solution.py:305
  4.7 9.1 %collective-permute-start = (f32[8,4096]{1,0:T(8,128)S(1)}, f32[8,4096]{1,0:T(8,128)S(1)}, u32[]{:S(2)}, u32[]{:S(2)}) collective-permute-start(f32[8,4096]{1,0:T(8,128)S(1)} %get-tuple-element.29.refs_0_), channel_id=1, source_target_pairs={{32,0},{64,32},{96,64},{128,96},{160,128},{192,160},{224,192},{0,2... | collective-permute-start | bytes 393224 | tf_op jit(solution)/shard_map/ppermute | solution.py:305
  4.8 9.0 %collective-permute-start.11 = (f32[8,4096]{1,0:T(8,128)S(1)}, f32[8,4096]{1,0:T(8,128)S(1)}, u32[]{:S(2)}, u32[]{:S(2)}) collective-permute-start(f32[8,4096]{1,0:T(8,128)S(1)} %get-tuple-element.30.refs_1_), channel_id=1, source_target_pairs={{0,32},{32,64},{64,96},{96,128},{128,160},{160,192},{192,224},{224... | collective-permute-start | bytes 393224 | tf_op jit(solution)/shard_map/ppermute | solution.py:300
  7.9 8.8 %collective-permute-start.7 = (f32[8,4096]{1,0:T(8,128)S(1)}, f32[8,4096]{1,0:T(8,128)S(1)}, u32[]{:S(2)}, u32[]{:S(2)}) collective-permute-start(f32[8,4096]{1,0:T(8,128)S(1)} %collective-permute-done.6.refs_14_), channel_id=1, source_target_pairs={{0,32},{32,64},{64,96},{96,128},{128,160},{160,192},{192,224},{224... | collective-permute-start | bytes 393224 | tf_op jit(solution)/shard_map/ppermute | solution.py:300
  12.1 7.9 %collective-permute-start.3 = (f32[8,4096]{1,0:T(8,128)S(1)}, f32[8,4096]{1,0:T(8,128)S(1)}, u32[]{:S(2)}, u32[]{:S(2)}) collective-permute-start(f32[8,4096]{1,0:T(8,128)S(1)} %collective-permute-done.1.refs_3_), channel_id=1, source_target_pairs={{32,0},{64,32},{96,64},{128,96},{160,128},{192,160},{224,192},{0,2... | collective-permute-start | bytes 393224 | tf_op jit(solution)/shard_map/ppermute | solution.py:305
  13.7 6.8 %collective-permute-start.2 = (f32[8,4096]{1,0:T(8,128)S(1)}, f32[8,4096]{1,0:T(8,128)S(1)}, u32[]{:S(2)}, u32[]{:S(2)}) collective-permute-start(f32[8,4096]{1,0:T(8,128)S(1)} %collective-permute-done.refs_2_), channel_id=1, source_target_pairs={{32,0},{64,32},{96,64},{128,96},{160,128},{192,160},{224,192},{0,2... | collective-permute-start | bytes 393224 | tf_op jit(solution)/shard_map/ppermute | solution.py:305
  13.8 6.8 %collective-permute-start.12 = (f32[8,4096]{1,0:T(8,128)S(1)}, f32[8,4096]{1,0:T(8,128)S(1)}, u32[]{:S(2)}, u32[]{:S(2)}) collective-permute-start(f32[8,4096]{1,0:T(8,128)S(1)} %collective-permute-done.11.refs_15_), channel_id=1, source_target_pairs={{0,32},{32,64},{64,96},{96,128},{128,160},{160,192},{192,224},{224... | collective-permute-start | bytes 393224 | tf_op jit(solution)/shard_map/ppermute | solution.py:300
  16.7 8.1 %collective-permute-start.8 = (f32[8,4096]{1,0:T(8,128)S(1)}, f32[8,4096]{1,0:T(8,128)S(1)}, u32[]{:S(2)}, u32[]{:S(2)}) collective-permute-start(f32[8,4096]{1,0:T(8,128)S(1)} %collective-permute-done.7.refs_12_), channel_id=1, source_target_pairs={{0,32},{32,64},{64,96},{96,128},{128,160},{160,192},{192,224},{224... | collective-permute-start | bytes 393224 | tf_op jit(solution)/shard_map/ppermute | solution.py:300
  20.0 8.1 %collective-permute-start.5 = (f32[8,4096]{1,0:T(8,128)S(1)}, f32[8,4096]{1,0:T(8,128)S(1)}, u32[]{:S(2)}, u32[]{:S(2)}) collective-permute-start(f32[8,4096]{1,0:T(8,128)S(1)} %collective-permute-done.3.refs_5_), channel_id=1, source_target_pairs={{32,0},{64,32},{96,64},{128,96},{160,128},{192,160},{224,192},{0,2... | collective-permute-start | bytes 393224 | tf_op jit(solution)/shard_map/ppermute | solution.py:305
  20.5 10.6 %collective-permute-start.4 = (f32[8,4096]{1,0:T(8,128)S(1)}, f32[8,4096]{1,0:T(8,128)S(1)}, u32[]{:S(2)}, u32[]{:S(2)}) collective-permute-start(f32[8,4096]{1,0:T(8,128)S(1)} %collective-permute-done.2.refs_4_), channel_id=1, source_target_pairs={{32,0},{64,32},{96,64},{128,96},{160,128},{192,160},{224,192},{0,2... | collective-permute-start | bytes 393224 | tf_op jit(solution)/shard_map/ppermute | solution.py:305
  20.5 13.5 %collective-permute-start.13 = (f32[8,4096]{1,0:T(8,128)S(1)}, f32[8,4096]{1,0:T(8,128)S(1)}, u32[]{:S(2)}, u32[]{:S(2)}) collective-permute-start(f32[8,4096]{1,0:T(8,128)S(1)} %collective-permute-done.12.refs_13_), channel_id=1, source_target_pairs={{0,32},{32,64},{64,96},{96,128},{128,160},{160,192},{192,224},{224... | collective-permute-start | bytes 393224 | tf_op jit(solution)/shard_map/ppermute | solution.py:300
  24.8 9.3 %collective-permute-start.9 = (f32[8,4096]{1,0:T(8,128)S(1)}, f32[8,4096]{1,0:T(8,128)S(1)}, u32[]{:S(2)}, u32[]{:S(2)}) collective-permute-start(f32[8,4096]{1,0:T(8,128)S(1)} %collective-permute-done.8.refs_10_), channel_id=1, source_target_pairs={{0,32},{32,64},{64,96},{96,128},{128,160},{160,192},{192,224},{224... | collective-permute-start | bytes 393224 | tf_op jit(solution)/shard_map/ppermute | solution.py:300
  28.1 6.0 %collective-permute-start.10 = (f32[8,4096]{1,0:T(8,128)S(1)}, f32[8,4096]{1,0:T(8,128)S(1)}, u32[]{:S(2)}, u32[]{:S(2)}) collective-permute-start(f32[8,4096]{1,0:T(8,128)S(1)} %collective-permute-done.5.refs_7_), channel_id=1, source_target_pairs={{32,0},{64,32},{96,64},{128,96},{160,128},{192,160},{224,192},{0,2... | collective-permute-start | bytes 393224 | tf_op jit(solution)/shard_map/ppermute | solution.py:305
  28.2 9.1 %collective-permute-start.15 = (f32[384,64]{1,0:T(8,128)S(1)}, f32[384,64]{1,0:T(8,128)S(1)}, u32[]{:S(2)}, u32[]{:S(2)}) collective-permute-start(f32[384,64]{1,0:T(8,128)S(1)} %get-tuple-element.53), channel_id=1, source_target_pairs={{8,0},{16,8},{24,16},{32,24},{40,32},{48,40},{56,48},{64,56},{72,6... | collective-permute-start | bytes 294920 | tf_op jit(solution)/shard_map/ppermute | solution.py:347
  31.1 9.7 %collective-permute-start.14 = (f32[384,64]{1,0:T(8,128)S(1)}, f32[384,64]{1,0:T(8,128)S(1)}, u32[]{:S(2)}, u32[]{:S(2)}) collective-permute-start(f32[384,64]{1,0:T(8,128)S(1)} %get-tuple-element.54), channel_id=1, source_target_pairs={{0,8},{8,16},{16,24},{24,32},{32,40},{40,48},{48,56},{56,64},{64,7... | collective-permute-start | bytes 294920 | tf_op jit(solution)/shard_map/ppermute | solution.py:344
  40.8 16.8 %all-to-all-start = ((f32[32,2,8,256]{3,2,1,0:T(8,128)}), f32[32,2,8,256]{3,2,1,0:T(8,128)S(1)}, u32[]{:S(2)}, u32[]{:S(2)}) async-start(f32[32,2,8,256]{3,2,1,0:T(8,128)} %select_rows.1), calls=%async_computation | async-start | bytes 1048576 | tf_op jit(solution)/shard_map/all_to_all | solution.py:369
  47.1 10.5 %copy-start.3 = (f32[256,256]{1,0:T(8,128)S(1)}, f32[256,256]{1,0:T(8,128)}, u32[]{:S(2)}) copy-start(f32[256,256]{1,0:T(8,128)} %amp_ref.1) | copy-start | bytes 786436
  47.1 10.5 %copy-start.4 = (f32[1,256,256]{2,1,0:T(8,128)S(1)}, f32[1,256,256]{2,1,0:T(8,128)}, u32[]{:S(2)}) copy-start(f32[1,256,256]{2,1,0:T(8,128)} %observed.1) | copy-start | bytes 786436
  87.5 7.0 %collective-permute-start.16 = (f32[4,2,8,512]{3,2,1,0:T(8,128)S(1)}, f32[4,2,8,512]{3,2,1,0:T(8,128)S(1)}, u32[]{:S(2)}, u32[]{:S(2)}) collective-permute-start(f32[4,2,8,512]{3,2,1,0:T(8,128)S(1)} %get-tuple-element.38), channel_id=1, source_target_pairs={{0,32},{32,64},{64,96},{96,128},{128,160},{160,192},{192,224},{224... | collective-permute-start | bytes 393224 | tf_op jit(solution)/shard_map/ppermute | solution.py:300
  90.8 11.1 %collective-permute-start.26 = (f32[4,2,8,512]{3,2,1,0:T(8,128)S(1)}, f32[4,2,8,512]{3,2,1,0:T(8,128)S(1)}, u32[]{:S(2)}, u32[]{:S(2)}) collective-permute-start(f32[4,2,8,512]{3,2,1,0:T(8,128)S(1)} %get-tuple-element.49), channel_id=1, source_target_pairs={{32,0},{64,32},{96,64},{128,96},{160,128},{192,160},{224,192},{0,2... | collective-permute-start | bytes 393224 | tf_op jit(solution)/shard_map/ppermute | solution.py:305
  90.8 11.2 %collective-permute-start.20 = (f32[4,2,8,512]{3,2,1,0:T(8,128)S(1)}, f32[4,2,8,512]{3,2,1,0:T(8,128)S(1)}, u32[]{:S(2)}, u32[]{:S(2)}) collective-permute-start(f32[4,2,8,512]{3,2,1,0:T(8,128)S(1)} %get-tuple-element.42), channel_id=1, source_target_pairs={{32,0},{64,32},{96,64},{128,96},{160,128},{192,160},{224,192},{0,2... | collective-permute-start | bytes 393224 | tf_op jit(solution)/shard_map/ppermute | solution.py:305
  94.6 7.6 %collective-permute-start.17 = (f32[4,2,8,512]{3,2,1,0:T(8,128)S(1)}, f32[4,2,8,512]{3,2,1,0:T(8,128)S(1)}, u32[]{:S(2)}, u32[]{:S(2)}) collective-permute-start(f32[4,2,8,512]{3,2,1,0:T(8,128)S(1)} %add.90), channel_id=1, source_target_pairs={{0,32},{32,64},{64,96},{96,128},{128,160},{160,192},{192,224},{224... | collective-permute-start | bytes 393224 | tf_op jit(solution)/shard_map/ppermute | solution.py:300
  98.2 7.7 %collective-permute-start.23 = (f32[4,2,8,512]{3,2,1,0:T(8,128)S(1)}, f32[4,2,8,512]{3,2,1,0:T(8,128)S(1)}, u32[]{:S(2)}, u32[]{:S(2)}) collective-permute-start(f32[4,2,8,512]{3,2,1,0:T(8,128)S(1)} %get-tuple-element.46), channel_id=1, source_target_pairs={{0,32},{32,64},{64,96},{96,128},{128,160},{160,192},{192,224},{224... | collective-permute-start | bytes 393224 | tf_op jit(solution)/shard_map/ppermute | solution.py:300
  101.9 7.8 %collective-permute-start.27 = (f32[4,2,8,512]{3,2,1,0:T(8,128)S(1)}, f32[4,2,8,512]{3,2,1,0:T(8,128)S(1)}, u32[]{:S(2)}, u32[]{:S(2)}) collective-permute-start(f32[4,2,8,512]{3,2,1,0:T(8,128)S(1)} %add.100), channel_id=1, source_target_pairs={{32,0},{64,32},{96,64},{128,96},{160,128},{192,160},{224,192},{0,2... | collective-permute-start | bytes 393224 | tf_op jit(solution)/shard_map/ppermute | solution.py:305
  102.1 7.7 %collective-permute-start.21 = (f32[4,2,8,512]{3,2,1,0:T(8,128)S(1)}, f32[4,2,8,512]{3,2,1,0:T(8,128)S(1)}, u32[]{:S(2)}, u32[]{:S(2)}) collective-permute-start(f32[4,2,8,512]{3,2,1,0:T(8,128)S(1)} %add.94), channel_id=1, source_target_pairs={{32,0},{64,32},{96,64},{128,96},{160,128},{192,160},{224,192},{0,2... | collective-permute-start | bytes 393224 | tf_op jit(solution)/shard_map/ppermute | solution.py:305
  102.2 7.8 %collective-permute-start.18 = (f32[4,2,8,512]{3,2,1,0:T(8,128)S(1)}, f32[4,2,8,512]{3,2,1,0:T(8,128)S(1)}, u32[]{:S(2)}, u32[]{:S(2)}) collective-permute-start(f32[4,2,8,512]{3,2,1,0:T(8,128)S(1)} %add.91), channel_id=1, source_target_pairs={{0,32},{32,64},{64,96},{96,128},{128,160},{160,192},{192,224},{224... | collective-permute-start | bytes 393224 | tf_op jit(solution)/shard_map/ppermute | solution.py:300
  105.9 7.6 %collective-permute-start.24 = (f32[4,2,8,512]{3,2,1,0:T(8,128)S(1)}, f32[4,2,8,512]{3,2,1,0:T(8,128)S(1)}, u32[]{:S(2)}, u32[]{:S(2)}) collective-permute-start(f32[4,2,8,512]{3,2,1,0:T(8,128)S(1)} %add.97), channel_id=1, source_target_pairs={{0,32},{32,64},{64,96},{96,128},{128,160},{160,192},{192,224},{224... | collective-permute-start | bytes 393224 | tf_op jit(solution)/shard_map/ppermute | solution.py:300
  109.7 7.5 %collective-permute-start.28 = (f32[4,2,8,512]{3,2,1,0:T(8,128)S(1)}, f32[4,2,8,512]{3,2,1,0:T(8,128)S(1)}, u32[]{:S(2)}, u32[]{:S(2)}) collective-permute-start(f32[4,2,8,512]{3,2,1,0:T(8,128)S(1)} %add.101), channel_id=1, source_target_pairs={{32,0},{64,32},{96,64},{128,96},{160,128},{192,160},{224,192},{0,2... | collective-permute-start | bytes 393224 | tf_op jit(solution)/shard_map/ppermute | solution.py:305
  109.9 7.5 %collective-permute-start.22 = (f32[4,2,8,512]{3,2,1,0:T(8,128)S(1)}, f32[4,2,8,512]{3,2,1,0:T(8,128)S(1)}, u32[]{:S(2)}, u32[]{:S(2)}) collective-permute-start(f32[4,2,8,512]{3,2,1,0:T(8,128)S(1)} %add.95), channel_id=1, source_target_pairs={{32,0},{64,32},{96,64},{128,96},{160,128},{192,160},{224,192},{0,2... | collective-permute-start | bytes 393224 | tf_op jit(solution)/shard_map/ppermute | solution.py:305
  110.0 7.4 %collective-permute-start.19 = (f32[4,2,8,512]{3,2,1,0:T(8,128)S(1)}, f32[4,2,8,512]{3,2,1,0:T(8,128)S(1)}, u32[]{:S(2)}, u32[]{:S(2)}) collective-permute-start(f32[4,2,8,512]{3,2,1,0:T(8,128)S(1)} %add.92), channel_id=1, source_target_pairs={{0,32},{32,64},{64,96},{96,128},{128,160},{160,192},{192,224},{224... | collective-permute-start | bytes 393224 | tf_op jit(solution)/shard_map/ppermute | solution.py:300
  113.6 6.2 %collective-permute-start.25 = (f32[4,2,8,512]{3,2,1,0:T(8,128)S(1)}, f32[4,2,8,512]{3,2,1,0:T(8,128)S(1)}, u32[]{:S(2)}, u32[]{:S(2)}) collective-permute-start(f32[4,2,8,512]{3,2,1,0:T(8,128)S(1)} %add.98), channel_id=1, source_target_pairs={{0,32},{32,64},{64,96},{96,128},{128,160},{160,192},{192,224},{224... | collective-permute-start | bytes 393224 | tf_op jit(solution)/shard_map/ppermute | solution.py:300
  117.3 5.4 %collective-permute-start.29 = (f32[4,2,8,512]{3,2,1,0:T(8,128)S(1)}, f32[4,2,8,512]{3,2,1,0:T(8,128)S(1)}, u32[]{:S(2)}, u32[]{:S(2)}) collective-permute-start(f32[4,2,8,512]{3,2,1,0:T(8,128)S(1)} %add.102), channel_id=1, source_target_pairs={{32,0},{64,32},{96,64},{128,96},{160,128},{192,160},{224,192},{0,2... | collective-permute-start | bytes 393224 | tf_op jit(solution)/shard_map/ppermute | solution.py:305

commit v6 on v5

--- a/solution.py
+++ b/solution.py
@@ -89,7 +89,7 @@
 ALL = slice(None)
 
 
-def object_kernel(window, base, spec_re, spec_im, forward, inverse):
+def base_kernel(base):
     block = SPAN // 8
     row = lax.broadcasted_iota(jnp.int32, (block, SPAN), 0)
     column = lax.broadcasted_iota(jnp.int32, (block, SPAN), 1)
@@ -105,9 +105,19 @@
         return carry
 
     lax.fori_loop(0, 8, fill, 0)
+
+
+def object_kernel(base, strip, right_ref, left_ref, spec_re, spec_im, forward, inverse):
+    lane = lax.broadcasted_iota(jnp.int32, (SPAN // 2, 2 * HALO), 1)
+    after, before = right_ref[...], left_ref[...]
+    top = jnp.where(lane < HALO, after, pltpu.roll(before, HALO, 1))
+    bottom = jnp.where(lane < HALO, pltpu.roll(after, HALO, 1), before)
+    halo = jnp.concatenate([top, bottom], axis=0)
+    window = jnp.concatenate([strip[...], halo], axis=1)
+    window = jnp.concatenate([window[HALO:], window[:HALO]], axis=0)
     build(forward, base, 1)
     build(inverse, base, -1)
-    seen = split(window[...])
+    seen = split(window)
     part_re = split(right([seen], inverse, LOW))
     part_im = split(right([seen], inverse, HIGH))
     real, imag = left(forward, SPAN, [(FULL, part_re), (REST, part_im)])
@@ -161,7 +171,7 @@
             out[member, layer] = jnp.where(row_index >= residue, upper, lower)
         return carry
 
-    lax.fori_loop(0, 32, one, 0, unroll=2)
+    lax.fori_loop(0, 32, one, 0, unroll=8)
 
 
 def scatter_kernel(place, rows, cols, values, *refs):
@@ -194,7 +204,7 @@
                     )
         return carry
 
-    lax.fori_loop(0, 32, one, 0, unroll=2)
+    lax.fori_loop(0, 32, one, 0, unroll=4)
     for index, piece in enumerate(pieces):
         piece[...] = out[index // 2, 4 * (index % 2) : 4 * (index % 2) + 4]
 
@@ -340,11 +350,6 @@
     patch = slab * 4 + across
     patches = lax.axis_size("z") * lax.axis_size("x")
     place = jnp.stack([slab, across * 64 + frame_id * 8, frame_id * 8]).astype(jnp.int32)
-    ends = patches - 1
-    left_tail = lax.ppermute(
-        object_strip[:, CORE - HALO :], ("z", "x"), [(i, i + 1) for i in range(ends)]
-    )
-    right_head = lax.ppermute(object_strip[:, :HALO], ("z", "x"), [(i + 1, i) for i in range(ends)])
     own = pl.pallas_call(
         cut_kernel,
         out_shape=[f32(8, screens.shape[2])] * 2,
@@ -365,20 +370,40 @@
         cost_estimate=cost(0, 3 * 10**6),
         name="select_rows",
     )(place, row_offsets, col_offsets, *chunks)
-    sent, left_tail, right_head = lax.optimization_barrier((sent, left_tail, right_head))
+    sent, strip = lax.optimization_barrier((sent, object_strip))
     received = lax.all_to_all(sent, SLAB, split_axis=0, concat_axis=0, tiled=True)
-    window = jnp.concatenate([object_strip, right_head, left_tail], axis=1)
-    window = jnp.concatenate([window[HALO:], window[:HALO]], axis=0)
-    base, spec_re, spec_im = pl.pallas_call(
+    ends = patches - 1
+    half = SPAN // 2
+    tail = strip[:, CORE - HALO :]
+    left_tail = lax.ppermute(
+        jnp.concatenate([tail[:half], tail[half:]], axis=1),
+        ("z", "x"),
+        [(i, i + 1) for i in range(ends)],
+    )
+    head = strip[:, :HALO]
+    right_head = lax.ppermute(
+        jnp.concatenate([head[:half], head[half:]], axis=1),
+        ("z", "x"),
+        [(i + 1, i) for i in range(ends)],
+    )
+    base = pl.pallas_call(
+        base_kernel,
+        out_shape=jax.ShapeDtypeStruct((4, SPAN, SPAN), jnp.bfloat16),
+        out_specs=VMEM,
+        compiler_params=limit(20),
+        cost_estimate=cost(10**6, 10**6),
+        name="dft_base",
+    )()
+    spec_re, spec_im = pl.pallas_call(
         object_kernel,
-        out_shape=[jax.ShapeDtypeStruct((4, SPAN, SPAN), jnp.bfloat16)] + [f32(SPAN, HALF)] * 2,
-        in_specs=[VMEM],
-        out_specs=[VMEM] * 3,
+        out_shape=[f32(SPAN, HALF)] * 2,
+        in_specs=[VMEM] * 4,
+        out_specs=[VMEM] * 2,
         scratch_shapes=[pltpu.VMEM((4, SPAN, 2 * SPAN), jnp.bfloat16)] * 2,
         compiler_params=limit(28),
         cost_estimate=cost(3 * 2 * 226 * 10**6, 7 * 10**6),
         name="object_spectrum",
-    )(window)
+    )(base, strip, right_head, left_tail)
 
     row_turns = lax.dynamic_slice(row_offsets, (frame_id, 0, patch), (1, 2, 1))[0, :, 0] % CORE
     col_turns = lax.dynamic_slice(col_offsets, (frame_id, 0, patch), (1, 2, 1))[0, :, 0] % CORE

time: 135 us -> 139 us (1.030)
  local copies, waits for them, and re-layouts: 2.47 us -> 4.87 us
    all_to_all x1, waiting for transfers between devices: 7.22 us -> 0.01 us  [body(): lax.all_to_all(sent, SLAB, split_axis=0, concat_axis=0, tiled=True)]
    ppermute x2, waiting for transfers between devices: 3.45 us -> 6.59 us  [the longest x1 3.64 us: body(): lax.ppermute(jnp.concatenate([head[:half], head[half:]], axis=1), ('z', '...]
    ppermute x14, waiting for transfers between devices: 6.22 us -> 8.78 us  [down(): lax.ppermute(values, 'z', [((i + 1) % count, i) for i in range(count)])]
    unnamed x12 -> x26, local copies, waits for them, and re-layouts: 1.61 us -> 4.04 us
    ppermute x14, waiting for transfers between devices: 5.2 us -> 7.35 us  [up(): lax.ppermute(values, 'z', [(i, (i + 1) % count) for i in range(count)])]
    all_to_all x1, starting transfers between devices: 5.9 us -> 7.45 us  [body(): lax.all_to_all(sent, SLAB, split_axis=0, concat_axis=0, tiled=True)]
    pallas_call x1 -> x2, Pallas kernels: 3.25 us -> 3.25 us  [the longest x1 2.16 us: body(): pl.pallas_call(object_kernel, out_shape=[f32(SPAN, HALF)] * 2, in_specs=[...]
  transfers between devices with their start and end apart: 31 -> 31, of which waited for: 10 -> 12; matrix products, arithmetic and copies ran while one was open for 1% -> 1% of each run, Pallas kernels for 5% -> 2%
where the time goes in v6:
time: 139 us; the launch traced here: 137 us
  starting transfers between devices  60.3 us (43%)
  blocking collectives  25.4 us (18%)
  waiting for transfers between devices  22.7 us (16%)
  Pallas kernels  22.2 us (16%)
  local copies, waits for them, and re-layouts  4.87 us (4%)
    ppermute x14, starting transfers between devices, up(): lax.ppermute(values, 'z', [(i, (i + 1) % count) for i in range(count)])  45.7 us
    all_to_all x1, blocking collectives, body(): lax.all_to_all(placed, SLAB, split_axis=0, concat_axis=0, tiled=True)  15.5 us
    pallas_call x1, Pallas kernels, gradient_call(): pl.pallas_call(gradient_kernel, out_shape=f32(32, 2, 8, CORE), in_specs=[...  11.2 us
    all_to_all x1, blocking collectives, body(): lax.all_to_all(summed, FRAME, split_axis=0, concat_axis=0, tiled=True)  9.91 us
    ppermute x14, waiting for transfers between devices, down(): lax.ppermute(values, 'z', [((i + 1) % count, i) for i in range(count)])  8.78 us
    all_to_all x1, starting transfers between devices, body(): lax.all_to_all(sent, SLAB, split_axis=0, concat_axis=0, tiled=True)  7.45 us
    ppermute x14, waiting for transfers between devices, up(): lax.ppermute(values, 'z', [(i, (i + 1) % count) for i in range(count)])  7.35 us
    ppermute x1, starting transfers between devices, body(): lax.ppermute(jnp.concatenate([head[:half], head[half:]], axis=1), ('z', '...  4.57 us
  transfers between devices with their start and end apart: 31, of which 12 were waited for; matrix products, arithmetic and copies ran while one was open for 1% of the time, Pallas kernels for 2%

profile of v6, /device:TPU:64, one launch (start us, length us, event | category | flops | bytes accessed | tf_op | source)
XLA Modules:
  0.0 137.2 jit_solution(10117086502224458140)
XLA Ops:
  0.1 1.6 %copy-done = f32[2,64,4096]{2,1,0:T(8,128)S(1)} copy-done((f32[2,64,4096]{2,1,0:T(8,128)S(1)}, f32[2,64,4096]{2,1,0:T(8,128)}, u32[]{:S(2)}) %copy-start) | copy-done | bytes 2097176
  1.7 0.9 cut_rows.1
  2.6 2.0 %collective-permute-start.6 = (f32[8,4096]{1,0:T(8,128)S(1)}, f32[8,4096]{1,0:T(8,128)S(1)}, u32[]{:S(2)}, u32[]{:S(2)}) collective-permute-start(f32[8,4096]{1,0:T(8,128)S(1)} %get-tuple-element.27.refs_0_), channel_id=1, source_target_pairs={{0,32},{32,64},{64,96},{96,128},{128,160},{160,192},{192,224},{224... | collective-permute-start | bytes 393224 | tf_op jit(solution)/shard_map/ppermute | solution.py:310
  4.6 0.1 collective-permute-start.1
  4.7 0.1 collective-permute-start
  4.8 2.9 %collective-permute-start.11 = (f32[8,4096]{1,0:T(8,128)S(1)}, f32[8,4096]{1,0:T(8,128)S(1)}, u32[]{:S(2)}, u32[]{:S(2)}) collective-permute-start(f32[8,4096]{1,0:T(8,128)S(1)} %get-tuple-element.28.refs_1_), channel_id=1, source_target_pairs={{0,32},{32,64},{64,96},{96,128},{128,160},{160,192},{192,224},{224... | collective-permute-start | bytes 393224 | tf_op jit(solution)/shard_map/ppermute | solution.py:310
  7.7 0.2 collective-permute-done.6.refs_14_
  7.9 3.1 %collective-permute-start.7 = (f32[8,4096]{1,0:T(8,128)S(1)}, f32[8,4096]{1,0:T(8,128)S(1)}, u32[]{:S(2)}, u32[]{:S(2)}) collective-permute-start(f32[8,4096]{1,0:T(8,128)S(1)} %collective-permute-done.6.refs_14_), channel_id=1, source_target_pairs={{0,32},{32,64},{64,96},{96,128},{128,160},{160,192},{192,224},{224... | collective-permute-start | bytes 393224 | tf_op jit(solution)/shard_map/ppermute | solution.py:310
  11.0 1.1 collective-permute-done.1.refs_3_
  12.1 1.7 %collective-permute-done.refs_2_ = f32[8,4096]{1,0:T(8,128)S(1)} collective-permute-done((f32[8,4096]{1,0:T(8,128)S(1)}, f32[8,4096]{1,0:T(8,128)S(1)}, u32[]{:S(2)}, u32[]{:S(2)}) %collective-permute-start) | collective-permute-done | bytes 131104 | tf_op jit(solution)/shard_map/ppermute | solution.py:315
  13.8 3.0 %collective-permute-start.12 = (f32[8,4096]{1,0:T(8,128)S(1)}, f32[8,4096]{1,0:T(8,128)S(1)}, u32[]{:S(2)}, u32[]{:S(2)}) collective-permute-start(f32[8,4096]{1,0:T(8,128)S(1)} %collective-permute-done.11.refs_15_), channel_id=1, source_target_pairs={{0,32},{32,64},{64,96},{96,128},{128,160},{160,192},{192,224},{224... | collective-permute-start | bytes 393224 | tf_op jit(solution)/shard_map/ppermute | solution.py:310
  16.7 3.2 %collective-permute-start.8 = (f32[8,4096]{1,0:T(8,128)S(1)}, f32[8,4096]{1,0:T(8,128)S(1)}, u32[]{:S(2)}, u32[]{:S(2)}) collective-permute-start(f32[8,4096]{1,0:T(8,128)S(1)} %collective-permute-done.7.refs_12_), channel_id=1, source_target_pairs={{0,32},{32,64},{64,96},{96,128},{128,160},{160,192},{192,224},{224... | collective-permute-start | bytes 393224 | tf_op jit(solution)/shard_map/ppermute | solution.py:310
  20.0 0.6 collective-permute-done.2.refs_4_
  20.5 4.3 %collective-permute-start.13 = (f32[8,4096]{1,0:T(8,128)S(1)}, f32[8,4096]{1,0:T(8,128)S(1)}, u32[]{:S(2)}, u32[]{:S(2)}) collective-permute-start(f32[8,4096]{1,0:T(8,128)S(1)} %collective-permute-done.12.refs_13_), channel_id=1, source_target_pairs={{0,32},{32,64},{64,96},{96,128},{128,160},{160,192},{192,224},{224... | collective-permute-start | bytes 393224 | tf_op jit(solution)/shard_map/ppermute | solution.py:310
  24.8 3.2 %collective-permute-start.9 = (f32[8,4096]{1,0:T(8,128)S(1)}, f32[8,4096]{1,0:T(8,128)S(1)}, u32[]{:S(2)}, u32[]{:S(2)}) collective-permute-start(f32[8,4096]{1,0:T(8,128)S(1)} %collective-permute-done.8.refs_10_), channel_id=1, source_target_pairs={{0,32},{32,64},{64,96},{96,128},{128,160},{160,192},{192,224},{224... | collective-permute-start | bytes 393224 | tf_op jit(solution)/shard_map/ppermute | solution.py:310
  28.1 1.1 dft_base.1.base
  29.2 0.7 and_select_fusion
  29.9 0.7 collective-permute-done.9.refs_8_
  30.6 2.6 %collective-permute-done.10.refs_9_ = f32[8,4096]{1,0:T(8,128)} collective-permute-done((f32[8,4096]{1,0:T(8,128)S(1)}, f32[8,4096]{1,0:T(8,128)}, u32[]{:S(2)}, u32[]{:S(2)}) %collective-permute-start.10) | collective-permute-done | bytes 131104 | tf_op jit(solution)/shard_map/ppermute | solution.py:315
  33.1 0.7 copy-done.5
  33.8 3.3 %select_rows.1 = f32[32,2,8,256]{3,2,1,0:T(8,128)} custom-call(s32[3]{0:T(128)S(1)} %copy-done.5, s32[8,2,32]{2,1,0:T(2,128)S(1)} %copy-done.2, s32[8,2,32]{2,1,0:T(2,128)S(1)} %copy-done.3, f32[8,4096]{1,0:T(8,128)S(1)} %get-tuple-element.27.refs_0_, f32[8,4096]{1,0:T(8,128)S(1)} %get-tuple-element.28.refs_1_, f32[8,4096]{1,0:T(8,128)S(1)} %collective-permute-done.refs_2_, ...), custom_call_target="tpu_custom_call" | custom-call | bytes 3000000 | tf_op jit(solution)/shard_map/select_rows/pallas_call | solution.py:363
  37.1 7.5 %all-to-all-start = ((f32[32,2,8,256]{3,2,1,0:T(8,128)}), f32[32,2,8,256]{3,2,1,0:T(8,128)S(1)}, u32[]{:S(2)}, u32[]{:S(2)}) async-start(f32[32,2,8,256]{3,2,1,0:T(8,128)} %select_rows.1), calls=%async_computation | async-start | bytes 1048576 | tf_op jit(solution)/shard_map/all_to_all | solution.py:374
  44.5 0.1 fusion.2
  44.6 0.1 pad_maximum_fusion.1
  44.8 4.6 %collective-permute-start.14 = (f32[192,128]{1,0:T(8,128)S(1)}, f32[192,128]{1,0:T(8,128)S(1)}, u32[]{:S(2)}, u32[]{:S(2)}) collective-permute-start(f32[192,128]{1,0:T(8,128)S(1)} %pad_maximum_fusion.1), channel_id=1, source_target_pairs={{8,0},{16,8},{24,16},{32,24},{40,32},{48,40},{56,48},{64,56},{72,6... | collective-permute-start | bytes 294920 | tf_op jit(solution)/shard_map/ppermute | solution.py:384
  49.4 1.9 %collective-permute-start.15 = (f32[192,128]{1,0:T(8,128)S(1)}, f32[192,128]{1,0:T(8,128)S(1)}, u32[]{:S(2)}, u32[]{:S(2)}) collective-permute-start(f32[192,128]{1,0:T(8,128)S(1)} %pad_maximum_fusion.2), channel_id=1, source_target_pairs={{0,8},{8,16},{16,24},{24,32},{32,40},{40,48},{48,56},{56,64},{64,7... | collective-permute-start | bytes 294920 | tf_op jit(solution)/shard_map/ppermute | solution.py:378
  51.5 3.6 %collective-permute-done.14.right_ref = f32[192,128]{1,0:T(8,128)S(1)} collective-permute-done((f32[192,128]{1,0:T(8,128)S(1)}, f32[192,128]{1,0:T(8,128)S(1)}, u32[]{:S(2)}, u32[]{:S(2)}) %collective-permute-start.14) | collective-permute-done | bytes 98336 | tf_op jit(solution)/shard_map/ppermute | solution.py:384
  55.1 3.0 %collective-permute-done.15.left_ref = f32[192,128]{1,0:T(8,128)S(1)} collective-permute-done((f32[192,128]{1,0:T(8,128)S(1)}, f32[192,128]{1,0:T(8,128)S(1)}, u32[]{:S(2)}, u32[]{:S(2)}) %collective-permute-start.15) | collective-permute-done | bytes 98336 | tf_op jit(solution)/shard_map/ppermute | solution.py:378
  58.1 2.2 %object_spectrum.1 = (f32[384,256]{1,0:T(8,128)S(1)}, f32[384,256]{1,0:T(8,128)S(1)}) custom-call(bf16[4,384,384]{2,1,0:T(8,128)(2,1)S(1)} %dft_base.1.base, f32[384,256]{1,0:T(8,128)S(1)} %copy-done.1, f32[192,128]{1,0:T(8,128)S(1)} %collective-permute-done.14.right_ref, f32[192,128]{1,0:T(8,128)S(1)} %collective-permute-done.15.left_ref), custom_call_target="tpu_custom_call" | custom-call | flops 1356000000 | bytes 7000000 | tf_op jit(solution)/shard_map/object_spectrum/pallas_call | solution.py:397
  60.2 0.8 copy-done.9
  61.0 1.0 copy-done.10
  62.0 11.2 %shard_map.64 = f32[32,2,8,256]{3,2,1,0:T(8,128)S(1)} custom-call(s32[2,2]{1,0:T(2,128)S(1)} %pad_add_fusion.turns, f32[32,2,8,256]{3,2,1,0:T(8,128)S(1)} %all-to-all-done.received, f32[256,256]{1,0:T(8,128)S(1)} %copy-done.7, f32[1,256,256]{2,1,0:T(8,128)S(1)} %copy-done.8, bf16[4,384,384]{2,1,0:T(8,128)(2,1)S(1)} %dft_base.1.base, ...), custom_call_target="tpu_custom_call" | custom-call | flops 7331999744 | bytes 7000000 | tf_op jit(solution)/shard_map/pallas_call | solution.py:286
  73.2 15.5 %all_to_all.15.values = f32[32,2,8,256]{3,2,1,0:T(8,128)S(1)} all-to-all(f32[32,2,8,256]{3,2,1,0:T(8,128)S(1)} %shard_map.64), channel_id=1, replica_groups=mesh['z'=8,'x'=4,'y'=4,'core'=2] {'x','y','core'}, dimensions={0} | all-to-all | bytes 1048576 | tf_op jit(solution)/shard_map/all_to_all | solution.py:414
  88.7 3.6 %scatter_rows.1 = (f32[4,2,8,512]{3,2,1,0:T(8,128)S(1)}, f32[4,2,8,512]{3,2,1,0:T(8,128)S(1)}, f32[4,2,8,512]{3,2,1,0:T(8,128)S(1)}, f32[4,2,8,512]{3,2,1,0:T(8,...) custom-call(s32[3]{0:T(128)S(1)} %copy-done.6, ...), custom_call_target="tpu_custom_call" | custom-call | bytes 3000000 | tf_op jit(solution)/shard_map/scatter_rows/pallas_call | solution.py:416
  92.3 2.3 %collective-permute-start.16 = (f32[4,2,8,512]{3,2,1,0:T(8,128)S(1)}, f32[4,2,8,512]{3,2,1,0:T(8,128)S(1)}, u32[]{:S(2)}, u32[]{:S(2)}) collective-permute-start(f32[4,2,8,512]{3,2,1,0:T(8,128)S(1)} %get-tuple-element.34), channel_id=1, source_target_pairs={{0,32},{32,64},{64,96},{96,128},{128,160},{160,192},{192,224},{224... | collective-permute-start | bytes 393224 | tf_op jit(solution)/shard_map/ppermute | solution.py:310
  94.6 4.0 %collective-permute-done.16 = f32[4,2,8,512]{3,2,1,0:T(8,128)S(1)} collective-permute-done((f32[4,2,8,512]{3,2,1,0:T(8,128)S(1)}, f32[4,2,8,512]{3,2,1,0:T(8,128)S(1)}, u32[]{:S(2)}, u32[]{:S(2)}) %collective-permute-start.16) | collective-permute-done | bytes 131104 | tf_op jit(solution)/shard_map/ppermute | solution.py:310
  98.6 3.4 %collective-permute-start.17 = (f32[4,2,8,512]{3,2,1,0:T(8,128)S(1)}, f32[4,2,8,512]{3,2,1,0:T(8,128)S(1)}, u32[]{:S(2)}, u32[]{:S(2)}) collective-permute-start(f32[4,2,8,512]{3,2,1,0:T(8,128)S(1)} %add.90), channel_id=1, source_target_pairs={{0,32},{32,64},{64,96},{96,128},{128,160},{160,192},{192,224},{224... | collective-permute-start | bytes 393224 | tf_op jit(solution)/shard_map/ppermute | solution.py:310
  102.0 3.7 %collective-permute-start.23 = (f32[4,2,8,512]{3,2,1,0:T(8,128)S(1)}, f32[4,2,8,512]{3,2,1,0:T(8,128)S(1)}, u32[]{:S(2)}, u32[]{:S(2)}) collective-permute-start(f32[4,2,8,512]{3,2,1,0:T(8,128)S(1)} %get-tuple-element.42), channel_id=1, source_target_pairs={{0,32},{32,64},{64,96},{96,128},{128,160},{160,192},{192,224},{224... | collective-permute-start | bytes 393224 | tf_op jit(solution)/shard_map/ppermute | solution.py:310
  106.0 3.7 %collective-permute-start.18 = (f32[4,2,8,512]{3,2,1,0:T(8,128)S(1)}, f32[4,2,8,512]{3,2,1,0:T(8,128)S(1)}, u32[]{:S(2)}, u32[]{:S(2)}) collective-permute-start(f32[4,2,8,512]{3,2,1,0:T(8,128)S(1)} %add.91), channel_id=1, source_target_pairs={{0,32},{32,64},{64,96},{96,128},{128,160},{160,192},{192,224},{224... | collective-permute-start | bytes 393224 | tf_op jit(solution)/shard_map/ppermute | solution.py:310
  109.8 3.8 %collective-permute-start.24 = (f32[4,2,8,512]{3,2,1,0:T(8,128)S(1)}, f32[4,2,8,512]{3,2,1,0:T(8,128)S(1)}, u32[]{:S(2)}, u32[]{:S(2)}) collective-permute-start(f32[4,2,8,512]{3,2,1,0:T(8,128)S(1)} %add.97), channel_id=1, source_target_pairs={{0,32},{32,64},{64,96},{96,128},{128,160},{160,192},{192,224},{224... | collective-permute-start | bytes 393224 | tf_op jit(solution)/shard_map/ppermute | solution.py:310
  113.7 0.1 collective-permute-start.22
  113.8 3.5 %collective-permute-start.19 = (f32[4,2,8,512]{3,2,1,0:T(8,128)S(1)}, f32[4,2,8,512]{3,2,1,0:T(8,128)S(1)}, u32[]{:S(2)}, u32[]{:S(2)}) collective-permute-start(f32[4,2,8,512]{3,2,1,0:T(8,128)S(1)} %add.92), channel_id=1, source_target_pairs={{0,32},{32,64},{64,96},{96,128},{128,160},{160,192},{192,224},{224... | collective-permute-start | bytes 393224 | tf_op jit(solution)/shard_map/ppermute | solution.py:310
  117.3 0.1 collective-permute-done.24
  117.4 3.7 %collective-permute-start.25 = (f32[4,2,8,512]{3,2,1,0:T(8,128)S(1)}, f32[4,2,8,512]{3,2,1,0:T(8,128)S(1)}, u32[]{:S(2)}, u32[]{:S(2)}) collective-permute-start(f32[4,2,8,512]{3,2,1,0:T(8,128)S(1)} %add.98), channel_id=1, source_target_pairs={{0,32},{32,64},{64,96},{96,128},{128,160},{160,192},{192,224},{224... | collective-permute-start | bytes 393224 | tf_op jit(solution)/shard_map/ppermute | solution.py:310
  121.3 2.3 %collective-permute-done.25 = f32[4,2,8,512]{3,2,1,0:T(8,128)S(1)} collective-permute-done((f32[4,2,8,512]{3,2,1,0:T(8,128)S(1)}, f32[4,2,8,512]{3,2,1,0:T(8,128)S(1)}, u32[]{:S(2)}, u32[]{:S(2)}) %collective-permute-start.25) | collective-permute-done | bytes 131104 | tf_op jit(solution)/shard_map/ppermute | solution.py:310
  123.6 2.9 %collective-permute-done.29 = f32[4,2,8,512]{3,2,1,0:T(8,128)S(1)} collective-permute-done((f32[4,2,8,512]{3,2,1,0:T(8,128)S(1)}, f32[4,2,8,512]{3,2,1,0:T(8,128)S(1)}, u32[]{:S(2)}, u32[]{:S(2)}) %collective-permute-start.29) | collective-permute-done | bytes 131104 | tf_op jit(solution)/shard_map/ppermute | solution.py:315
  126.5 9.9 %all_to_all.16 = f32[8,2,8,512]{3,2,1,0:T(8,128)S(1)} all-to-all(f32[8,2,8,512]{3,2,1,0:T(8,128)S(1)} %pad_maximum_fusion), channel_id=1, replica_groups=mesh['z'=8,'x'=4,'y'=4,'core'=2] {'y','core'}, dimensions={0} | all-to-all | bytes 524288 | tf_op jit(solution)/shard_map/all_to_all | solution.py:427
  136.5 0.7 copy_bitcast_fusion
  (68 shorter events, 1.0 us)
Async XLA Ops:
  0.0 29.2 %copy-start.3 = (s32[8,2,32]{2,1,0:T(2,128)S(1)}, s32[8,2,32]{2,1,0:T(2,128)}, u32[]{:S(2)}) copy-start(s32[8,2,32]{2,1,0:T(2,128)} %cols.3) | copy-start | bytes 6148
  0.0 29.2 %copy-start.2 = (s32[8,2,32]{2,1,0:T(2,128)S(1)}, s32[8,2,32]{2,1,0:T(2,128)}, u32[]{:S(2)}) copy-start(s32[8,2,32]{2,1,0:T(2,128)} %rows.3) | copy-start | bytes 6148
  0.1 1.6 %copy-start = (f32[2,64,4096]{2,1,0:T(8,128)S(1)}, f32[2,64,4096]{2,1,0:T(8,128)}, u32[]{:S(2)}) copy-start(f32[2,64,4096]{2,1,0:T(8,128)} %screens.1) | copy-start | bytes 6291460
  1.7 26.4 %copy-start.4 = (s32[3]{0:T(128)}, s32[3]{0:T(128)S(1)}, u32[]{:S(2)}) copy-start(s32[3]{0:T(128)S(1)} %pad_add_fusion.1.place) | copy-start | bytes 40
  2.6 5.3 %collective-permute-start.6 = (f32[8,4096]{1,0:T(8,128)S(1)}, f32[8,4096]{1,0:T(8,128)S(1)}, u32[]{:S(2)}, u32[]{:S(2)}) collective-permute-start(f32[8,4096]{1,0:T(8,128)S(1)} %get-tuple-element.27.refs_0_), channel_id=1, source_target_pairs={{0,32},{32,64},{64,96},{96,128},{128,160},{160,192},{192,224},{224... | collective-permute-start | bytes 393224 | tf_op jit(solution)/shard_map/ppermute | solution.py:310
  4.6 7.5 %collective-permute-start.1 = (f32[8,4096]{1,0:T(8,128)S(1)}, f32[8,4096]{1,0:T(8,128)S(1)}, u32[]{:S(2)}, u32[]{:S(2)}) collective-permute-start(f32[8,4096]{1,0:T(8,128)S(1)} %get-tuple-element.28.refs_1_), channel_id=1, source_target_pairs={{32,0},{64,32},{96,64},{128,96},{160,128},{192,160},{224,192},{0,2... | collective-permute-start | bytes 393224 | tf_op jit(solution)/shard_map/ppermute | solution.py:315
  4.7 9.1 %collective-permute-start = (f32[8,4096]{1,0:T(8,128)S(1)}, f32[8,4096]{1,0:T(8,128)S(1)}, u32[]{:S(2)}, u32[]{:S(2)}) collective-permute-start(f32[8,4096]{1,0:T(8,128)S(1)} %get-tuple-element.27.refs_0_), channel_id=1, source_target_pairs={{32,0},{64,32},{96,64},{128,96},{160,128},{192,160},{224,192},{0,2... | collective-permute-start | bytes 393224 | tf_op jit(solution)/shard_map/ppermute | solution.py:315
  4.8 9.0 %collective-permute-start.11 = (f32[8,4096]{1,0:T(8,128)S(1)}, f32[8,4096]{1,0:T(8,128)S(1)}, u32[]{:S(2)}, u32[]{:S(2)}) collective-permute-start(f32[8,4096]{1,0:T(8,128)S(1)} %get-tuple-element.28.refs_1_), channel_id=1, source_target_pairs={{0,32},{32,64},{64,96},{96,128},{128,160},{160,192},{192,224},{224... | collective-permute-start | bytes 393224 | tf_op jit(solution)/shard_map/ppermute | solution.py:310
  7.9 8.8 %collective-permute-start.7 = (f32[8,4096]{1,0:T(8,128)S(1)}, f32[8,4096]{1,0:T(8,128)S(1)}, u32[]{:S(2)}, u32[]{:S(2)}) collective-permute-start(f32[8,4096]{1,0:T(8,128)S(1)} %collective-permute-done.6.refs_14_), channel_id=1, source_target_pairs={{0,32},{32,64},{64,96},{96,128},{128,160},{160,192},{192,224},{224... | collective-permute-start | bytes 393224 | tf_op jit(solution)/shard_map/ppermute | solution.py:310
  12.1 7.9 %collective-permute-start.3 = (f32[8,4096]{1,0:T(8,128)S(1)}, f32[8,4096]{1,0:T(8,128)S(1)}, u32[]{:S(2)}, u32[]{:S(2)}) collective-permute-start(f32[8,4096]{1,0:T(8,128)S(1)} %collective-permute-done.1.refs_3_), channel_id=1, source_target_pairs={{32,0},{64,32},{96,64},{128,96},{160,128},{192,160},{224,192},{0,2... | collective-permute-start | bytes 393224 | tf_op jit(solution)/shard_map/ppermute | solution.py:315
  13.7 6.8 %collective-permute-start.2 = (f32[8,4096]{1,0:T(8,128)S(1)}, f32[8,4096]{1,0:T(8,128)S(1)}, u32[]{:S(2)}, u32[]{:S(2)}) collective-permute-start(f32[8,4096]{1,0:T(8,128)S(1)} %collective-permute-done.refs_2_), channel_id=1, source_target_pairs={{32,0},{64,32},{96,64},{128,96},{160,128},{192,160},{224,192},{0,2... | collective-permute-start | bytes 393224 | tf_op jit(solution)/shard_map/ppermute | solution.py:315
  13.8 6.8 %collective-permute-start.12 = (f32[8,4096]{1,0:T(8,128)S(1)}, f32[8,4096]{1,0:T(8,128)S(1)}, u32[]{:S(2)}, u32[]{:S(2)}) collective-permute-start(f32[8,4096]{1,0:T(8,128)S(1)} %collective-permute-done.11.refs_15_), channel_id=1, source_target_pairs={{0,32},{32,64},{64,96},{96,128},{128,160},{160,192},{192,224},{224... | collective-permute-start | bytes 393224 | tf_op jit(solution)/shard_map/ppermute | solution.py:310
  16.7 8.1 %collective-permute-start.8 = (f32[8,4096]{1,0:T(8,128)S(1)}, f32[8,4096]{1,0:T(8,128)S(1)}, u32[]{:S(2)}, u32[]{:S(2)}) collective-permute-start(f32[8,4096]{1,0:T(8,128)S(1)} %collective-permute-done.7.refs_12_), channel_id=1, source_target_pairs={{0,32},{32,64},{64,96},{96,128},{128,160},{160,192},{192,224},{224... | collective-permute-start | bytes 393224 | tf_op jit(solution)/shard_map/ppermute | solution.py:310
  20.0 8.1 %collective-permute-start.5 = (f32[8,4096]{1,0:T(8,128)S(1)}, f32[8,4096]{1,0:T(8,128)S(1)}, u32[]{:S(2)}, u32[]{:S(2)}) collective-permute-start(f32[8,4096]{1,0:T(8,128)S(1)} %collective-permute-done.3.refs_5_), channel_id=1, source_target_pairs={{32,0},{64,32},{96,64},{128,96},{160,128},{192,160},{224,192},{0,2... | collective-permute-start | bytes 393224 | tf_op jit(solution)/shard_map/ppermute | solution.py:315
  20.5 9.4 %collective-permute-start.4 = (f32[8,4096]{1,0:T(8,128)S(1)}, f32[8,4096]{1,0:T(8,128)S(1)}, u32[]{:S(2)}, u32[]{:S(2)}) collective-permute-start(f32[8,4096]{1,0:T(8,128)S(1)} %collective-permute-done.2.refs_4_), channel_id=1, source_target_pairs={{32,0},{64,32},{96,64},{128,96},{160,128},{192,160},{224,192},{0,2... | collective-permute-start | bytes 393224 | tf_op jit(solution)/shard_map/ppermute | solution.py:315
  20.5 9.4 %collective-permute-start.13 = (f32[8,4096]{1,0:T(8,128)S(1)}, f32[8,4096]{1,0:T(8,128)S(1)}, u32[]{:S(2)}, u32[]{:S(2)}) collective-permute-start(f32[8,4096]{1,0:T(8,128)S(1)} %collective-permute-done.12.refs_13_), channel_id=1, source_target_pairs={{0,32},{32,64},{64,96},{96,128},{128,160},{160,192},{192,224},{224... | collective-permute-start | bytes 393224 | tf_op jit(solution)/shard_map/ppermute | solution.py:310
  24.8 5.8 %collective-permute-start.9 = (f32[8,4096]{1,0:T(8,128)S(1)}, f32[8,4096]{1,0:T(8,128)S(1)}, u32[]{:S(2)}, u32[]{:S(2)}) collective-permute-start(f32[8,4096]{1,0:T(8,128)S(1)} %collective-permute-done.8.refs_10_), channel_id=1, source_target_pairs={{0,32},{32,64},{64,96},{96,128},{128,160},{160,192},{192,224},{224... | collective-permute-start | bytes 393224 | tf_op jit(solution)/shard_map/ppermute | solution.py:310
  28.1 5.1 %collective-permute-start.10 = (f32[8,4096]{1,0:T(8,128)S(1)}, f32[8,4096]{1,0:T(8,128)}, u32[]{:S(2)}, u32[]{:S(2)}) collective-permute-start(f32[8,4096]{1,0:T(8,128)S(1)} %collective-permute-done.5.refs_7_), channel_id=1, source_target_pairs={{32,0},{64,32},{96,64},{128,96},{160,128},{192,160},{224,192},{0,2... | collective-permute-start | bytes 393224 | tf_op jit(solution)/shard_map/ppermute | solution.py:315
  29.2 15.3 %copy-start.1 = (f32[384,256]{1,0:T(8,128)S(1)}, f32[384,256]{1,0:T(8,128)}, u32[]{:S(2)}) copy-start(f32[384,256]{1,0:T(8,128)} %strip) | copy-start | bytes 1179652
  33.1 0.7 copy-start.5
  37.1 14.3 %copy-start.11 = (s32[2,1]{1,0:T(2,128)S(1)}, s32[2,1]{1,0:T(2,128)}, u32[]{:S(2)}) copy-start(s32[2,1]{1,0:T(2,128)} %get-tuple-element.53) | copy-start | bytes 28
  37.1 14.3 %copy-start.12 = (s32[2,1]{1,0:T(2,128)S(1)}, s32[2,1]{1,0:T(2,128)}, u32[]{:S(2)}) copy-start(s32[2,1]{1,0:T(2,128)} %get-tuple-element.54) | copy-start | bytes 28
  37.1 23.9 %all-to-all-start = ((f32[32,2,8,256]{3,2,1,0:T(8,128)}), f32[32,2,8,256]{3,2,1,0:T(8,128)S(1)}, u32[]{:S(2)}, u32[]{:S(2)}) async-start(f32[32,2,8,256]{3,2,1,0:T(8,128)} %select_rows.1), calls=%async_computation | async-start | bytes 1048576 | tf_op jit(solution)/shard_map/all_to_all | solution.py:374
  44.8 10.3 %collective-permute-start.14 = (f32[192,128]{1,0:T(8,128)S(1)}, f32[192,128]{1,0:T(8,128)S(1)}, u32[]{:S(2)}, u32[]{:S(2)}) collective-permute-start(f32[192,128]{1,0:T(8,128)S(1)} %pad_maximum_fusion.1), channel_id=1, source_target_pairs={{8,0},{16,8},{24,16},{32,24},{40,32},{48,40},{56,48},{64,56},{72,6... | collective-permute-start | bytes 294920 | tf_op jit(solution)/shard_map/ppermute | solution.py:384
  49.4 8.6 %collective-permute-start.15 = (f32[192,128]{1,0:T(8,128)S(1)}, f32[192,128]{1,0:T(8,128)S(1)}, u32[]{:S(2)}, u32[]{:S(2)}) collective-permute-start(f32[192,128]{1,0:T(8,128)S(1)} %pad_maximum_fusion.2), channel_id=1, source_target_pairs={{0,8},{8,16},{16,24},{24,32},{32,40},{40,48},{48,56},{56,64},{64,7... | collective-permute-start | bytes 294920 | tf_op jit(solution)/shard_map/ppermute | solution.py:378
  51.5 9.5 %copy-start.7 = (f32[256,256]{1,0:T(8,128)S(1)}, f32[256,256]{1,0:T(8,128)}, u32[]{:S(2)}) copy-start(f32[256,256]{1,0:T(8,128)} %amp_ref.1) | copy-start | bytes 786436
  51.5 9.5 %copy-start.8 = (f32[1,256,256]{2,1,0:T(8,128)S(1)}, f32[1,256,256]{2,1,0:T(8,128)}, u32[]{:S(2)}) copy-start(f32[1,256,256]{2,1,0:T(8,128)} %observed.1) | copy-start | bytes 786436
  60.2 0.8 copy-start.9
  61.0 1.0 copy-start.10
  62.0 26.7 %copy-start.6 = (s32[3]{0:T(128)S(1)}, s32[3]{0:T(128)}, u32[]{:S(2)}) copy-start(s32[3]{0:T(128)} %copy-done.4) | copy-start | bytes 40
  92.3 6.3 %collective-permute-start.16 = (f32[4,2,8,512]{3,2,1,0:T(8,128)S(1)}, f32[4,2,8,512]{3,2,1,0:T(8,128)S(1)}, u32[]{:S(2)}, u32[]{:S(2)}) collective-permute-start(f32[4,2,8,512]{3,2,1,0:T(8,128)S(1)} %get-tuple-element.34), channel_id=1, source_target_pairs={{0,32},{32,64},{64,96},{96,128},{128,160},{160,192},{192,224},{224... | collective-permute-start | bytes 393224 | tf_op jit(solution)/shard_map/ppermute | solution.py:310
  94.6 11.1 %collective-permute-start.26 = (f32[4,2,8,512]{3,2,1,0:T(8,128)S(1)}, f32[4,2,8,512]{3,2,1,0:T(8,128)S(1)}, u32[]{:S(2)}, u32[]{:S(2)}) collective-permute-start(f32[4,2,8,512]{3,2,1,0:T(8,128)S(1)} %get-tuple-element.45), channel_id=1, source_target_pairs={{32,0},{64,32},{96,64},{128,96},{160,128},{192,160},{224,192},{0,2... | collective-permute-start | bytes 393224 | tf_op jit(solution)/shard_map/ppermute | solution.py:315
  94.6 11.2 %collective-permute-start.20 = (f32[4,2,8,512]{3,2,1,0:T(8,128)S(1)}, f32[4,2,8,512]{3,2,1,0:T(8,128)S(1)}, u32[]{:S(2)}, u32[]{:S(2)}) collective-permute-start(f32[4,2,8,512]{3,2,1,0:T(8,128)S(1)} %get-tuple-element.38), channel_id=1, source_target_pairs={{32,0},{64,32},{96,64},{128,96},{160,128},{192,160},{224,192},{0,2... | collective-permute-start | bytes 393224 | tf_op jit(solution)/shard_map/ppermute | solution.py:315
  98.6 7.3 %collective-permute-start.17 = (f32[4,2,8,512]{3,2,1,0:T(8,128)S(1)}, f32[4,2,8,512]{3,2,1,0:T(8,128)S(1)}, u32[]{:S(2)}, u32[]{:S(2)}) collective-permute-start(f32[4,2,8,512]{3,2,1,0:T(8,128)S(1)} %add.90), channel_id=1, source_target_pairs={{0,32},{32,64},{64,96},{96,128},{128,160},{160,192},{192,224},{224... | collective-permute-start | bytes 393224 | tf_op jit(solution)/shard_map/ppermute | solution.py:310
  102.0 7.7 %collective-permute-start.23 = (f32[4,2,8,512]{3,2,1,0:T(8,128)S(1)}, f32[4,2,8,512]{3,2,1,0:T(8,128)S(1)}, u32[]{:S(2)}, u32[]{:S(2)}) collective-permute-start(f32[4,2,8,512]{3,2,1,0:T(8,128)S(1)} %get-tuple-element.42), channel_id=1, source_target_pairs={{0,32},{32,64},{64,96},{96,128},{128,160},{160,192},{192,224},{224... | collective-permute-start | bytes 393224 | tf_op jit(solution)/shard_map/ppermute | solution.py:310
  105.8 7.8 %collective-permute-start.27 = (f32[4,2,8,512]{3,2,1,0:T(8,128)S(1)}, f32[4,2,8,512]{3,2,1,0:T(8,128)S(1)}, u32[]{:S(2)}, u32[]{:S(2)}) collective-permute-start(f32[4,2,8,512]{3,2,1,0:T(8,128)S(1)} %add.100), channel_id=1, source_target_pairs={{32,0},{64,32},{96,64},{128,96},{160,128},{192,160},{224,192},{0,2... | collective-permute-start | bytes 393224 | tf_op jit(solution)/shard_map/ppermute | solution.py:315
  105.9 7.7 %collective-permute-start.21 = (f32[4,2,8,512]{3,2,1,0:T(8,128)S(1)}, f32[4,2,8,512]{3,2,1,0:T(8,128)S(1)}, u32[]{:S(2)}, u32[]{:S(2)}) collective-permute-start(f32[4,2,8,512]{3,2,1,0:T(8,128)S(1)} %add.94), channel_id=1, source_target_pairs={{32,0},{64,32},{96,64},{128,96},{160,128},{192,160},{224,192},{0,2... | collective-permute-start | bytes 393224 | tf_op jit(solution)/shard_map/ppermute | solution.py:315
  106.0 7.8 %collective-permute-start.18 = (f32[4,2,8,512]{3,2,1,0:T(8,128)S(1)}, f32[4,2,8,512]{3,2,1,0:T(8,128)S(1)}, u32[]{:S(2)}, u32[]{:S(2)}) collective-permute-start(f32[4,2,8,512]{3,2,1,0:T(8,128)S(1)} %add.91), channel_id=1, source_target_pairs={{0,32},{32,64},{64,96},{96,128},{128,160},{160,192},{192,224},{224... | collective-permute-start | bytes 393224 | tf_op jit(solution)/shard_map/ppermute | solution.py:310
  109.8 7.6 %collective-permute-start.24 = (f32[4,2,8,512]{3,2,1,0:T(8,128)S(1)}, f32[4,2,8,512]{3,2,1,0:T(8,128)S(1)}, u32[]{:S(2)}, u32[]{:S(2)}) collective-permute-start(f32[4,2,8,512]{3,2,1,0:T(8,128)S(1)} %add.97), channel_id=1, source_target_pairs={{0,32},{32,64},{64,96},{96,128},{128,160},{160,192},{192,224},{224... | collective-permute-start | bytes 393224 | tf_op jit(solution)/shard_map/ppermute | solution.py:310
  113.5 7.5 %collective-permute-start.28 = (f32[4,2,8,512]{3,2,1,0:T(8,128)S(1)}, f32[4,2,8,512]{3,2,1,0:T(8,128)S(1)}, u32[]{:S(2)}, u32[]{:S(2)}) collective-permute-start(f32[4,2,8,512]{3,2,1,0:T(8,128)S(1)} %add.101), channel_id=1, source_target_pairs={{32,0},{64,32},{96,64},{128,96},{160,128},{192,160},{224,192},{0,2... | collective-permute-start | bytes 393224 | tf_op jit(solution)/shard_map/ppermute | solution.py:315
  113.7 7.5 %collective-permute-start.22 = (f32[4,2,8,512]{3,2,1,0:T(8,128)S(1)}, f32[4,2,8,512]{3,2,1,0:T(8,128)S(1)}, u32[]{:S(2)}, u32[]{:S(2)}) collective-permute-start(f32[4,2,8,512]{3,2,1,0:T(8,128)S(1)} %add.95), channel_id=1, source_target_pairs={{32,0},{64,32},{96,64},{128,96},{160,128},{192,160},{224,192},{0,2... | collective-permute-start | bytes 393224 | tf_op jit(solution)/shard_map/ppermute | solution.py:315
  113.8 7.4 %collective-permute-start.19 = (f32[4,2,8,512]{3,2,1,0:T(8,128)S(1)}, f32[4,2,8,512]{3,2,1,0:T(8,128)S(1)}, u32[]{:S(2)}, u32[]{:S(2)}) collective-permute-start(f32[4,2,8,512]{3,2,1,0:T(8,128)S(1)} %add.92), channel_id=1, source_target_pairs={{0,32},{32,64},{64,96},{96,128},{128,160},{160,192},{192,224},{224... | collective-permute-start | bytes 393224 | tf_op jit(solution)/shard_map/ppermute | solution.py:310
  117.4 6.2 %collective-permute-start.25 = (f32[4,2,8,512]{3,2,1,0:T(8,128)S(1)}, f32[4,2,8,512]{3,2,1,0:T(8,128)S(1)}, u32[]{:S(2)}, u32[]{:S(2)}) collective-permute-start(f32[4,2,8,512]{3,2,1,0:T(8,128)S(1)} %add.98), channel_id=1, source_target_pairs={{0,32},{32,64},{64,96},{96,128},{128,160},{160,192},{192,224},{224... | collective-permute-start | bytes 393224 | tf_op jit(solution)/shard_map/ppermute | solution.py:310
  121.1 5.4 %collective-permute-start.29 = (f32[4,2,8,512]{3,2,1,0:T(8,128)S(1)}, f32[4,2,8,512]{3,2,1,0:T(8,128)S(1)}, u32[]{:S(2)}, u32[]{:S(2)}) collective-permute-start(f32[4,2,8,512]{3,2,1,0:T(8,128)S(1)} %add.102), channel_id=1, source_target_pairs={{32,0},{64,32},{96,64},{128,96},{160,128},{192,160},{224,192},{0,2... | collective-permute-start | bytes 393224 | tf_op jit(solution)/shard_map/ppermute | solution.py:315

commit v7 on v6

--- a/solution.py
+++ b/solution.py
@@ -107,7 +107,7 @@
     lax.fori_loop(0, 8, fill, 0)
 
 
-def object_kernel(base, strip, right_ref, left_ref, spec_re, spec_im, forward, inverse):
+def object_kernel(forward, inverse, strip, right_ref, left_ref, spec_re, spec_im):
     lane = lax.broadcasted_iota(jnp.int32, (SPAN // 2, 2 * HALO), 1)
     after, before = right_ref[...], left_ref[...]
     top = jnp.where(lane < HALO, after, pltpu.roll(before, HALO, 1))
@@ -115,8 +115,6 @@
     halo = jnp.concatenate([top, bottom], axis=0)
     window = jnp.concatenate([strip[...], halo], axis=1)
     window = jnp.concatenate([window[HALO:], window[:HALO]], axis=0)
-    build(forward, base, 1)
-    build(inverse, base, -1)
     seen = split(window)
     part_re = split(right([seen], inverse, LOW))
     part_im = split(right([seen], inverse, HIGH))
@@ -209,13 +207,18 @@
         piece[...] = out[index // 2, 4 * (index % 2) : 4 * (index % 2) + 4]
 
 
-def gradient_kernel(
-    turns, received, amp_ref, observed, base, spec_re, spec_im, out,
-    forward, inverse, pupil_re, pupil_im, far_re, far_im, mix_h, mix_l, wide_h, wide_l,
+def put(high, low, at, values):
+    high[at], low[at] = split(values)
+
+
+def inverse_sum(amplitude):
+    return 1.0 / (SPAN * SPAN * jnp.sum(amplitude * amplitude))
+
+
+def far_kernel(
+    turns, received, amp_ref, base, forward, inverse, pupil_re, pupil_im, far_re, far_im,
+    spread_re, spread_im, mix_h, mix_l,
 ):
-    def put(high, low, at, values):
-        high[at], low[at] = split(values)
-
     build(forward, base, 1)
     build(inverse, base, -1)
     phases = None
@@ -225,7 +228,7 @@
         sheet = pltpu.roll(sheet, (CORE - turns[layer, 1]) % CORE, 1)
         phases = sheet if phases is None else phases + sheet
     amplitude = amp_ref[...]
-    inverse_total = 1.0 / (SPAN * SPAN * jnp.sum(amplitude * amplitude))
+    inverse_total = inverse_sum(amplitude)
     sine, cosine = sine_cosine(phases)
     pupil_re[...] = amplitude * cosine
     pupil_im[...] = amplitude * sine
@@ -239,7 +242,15 @@
     spread = [split((far_re[...] * far_re[...] + far_im[...] * far_im[...]) * inverse_total)]
     put(mix_h, mix_l, FULL, right(spread, inverse, LOW))
     put(mix_h, mix_l, REST, right(spread, inverse, HIGH))
-    first, second = left(forward, SPAN, [(ALL, (mix_h[...], mix_l[...]))])
+    spread_re[...], spread_im[...] = left(forward, SPAN, [(ALL, (mix_h[...], mix_l[...]))])
+
+
+def gradient_kernel(
+    turns, amp_ref, observed, forward, inverse, pupil_re, pupil_im, far_re, far_im,
+    spread_re, spread_im, spec_re, spec_im, out, mix_h, mix_l, wide_h, wide_l,
+):
+    inverse_total = inverse_sum(amp_ref[...])
+    first, second = spread_re[...], spread_im[...]
     put(mix_h, mix_l, FULL, first * spec_re[...] - second * spec_im[...])
     put(mix_h, mix_l, REST, first * spec_im[...] + second * spec_re[...])
     first, second = left(inverse, CORE, [(ALL, (mix_h[...], mix_l[...]))])
@@ -282,26 +293,35 @@
     return jax.ShapeDtypeStruct(shape, jnp.float32)
 
 
+def far_call(*operands):
+    matrix = jax.ShapeDtypeStruct((4, SPAN, 2 * SPAN), jnp.bfloat16)
+    return pl.pallas_call(
+        far_kernel,
+        out_shape=[matrix] * 2 + [f32(CORE, CORE)] * 2 + [f32(SPAN, SPAN)] * 2 + [f32(SPAN, HALF)] * 2,
+        in_specs=[SMEM] + [VMEM] * 3,
+        out_specs=[VMEM] * 8,
+        scratch_shapes=[pltpu.VMEM((2 * SPAN, HALF), jnp.bfloat16)] * 2,
+        compiler_params=limit(28),
+        cost_estimate=cost(3 * 2 * 500 * 10**6, 7 * 10**6),
+        name="far_field",
+    )(*operands)
+
+
 def gradient_call(*operands):
     return pl.pallas_call(
         gradient_kernel,
         out_shape=f32(32, 2, 8, CORE),
-        in_specs=[SMEM] + [VMEM] * 6,
+        in_specs=[SMEM] + [VMEM] * 12,
         out_specs=VMEM,
         scratch_shapes=[
-            pltpu.VMEM((4, SPAN, 2 * SPAN), jnp.bfloat16),
-            pltpu.VMEM((4, SPAN, 2 * SPAN), jnp.bfloat16),
-            pltpu.VMEM((CORE, CORE), jnp.float32),
-            pltpu.VMEM((CORE, CORE), jnp.float32),
-            pltpu.VMEM((SPAN, SPAN), jnp.float32),
-            pltpu.VMEM((SPAN, SPAN), jnp.float32),
             pltpu.VMEM((2 * SPAN, HALF), jnp.bfloat16),
             pltpu.VMEM((2 * SPAN, HALF), jnp.bfloat16),
             pltpu.VMEM((2 * SPAN, SPAN), jnp.bfloat16),
             pltpu.VMEM((2 * SPAN, SPAN), jnp.bfloat16),
         ],
         compiler_params=limit(28),
-        cost_estimate=cost(3 * 2 * 1222 * 10**6, 7 * 10**6),
+        cost_estimate=cost(3 * 2 * 722 * 10**6, 7 * 10**6),
+        name="gradient",
     )(*operands)
 
 
@@ -394,22 +414,21 @@
         cost_estimate=cost(10**6, 10**6),
         name="dft_base",
     )()
+    row_turns = lax.dynamic_slice(row_offsets, (frame_id, 0, patch), (1, 2, 1))[0, :, 0] % CORE
+    col_turns = lax.dynamic_slice(col_offsets, (frame_id, 0, patch), (1, 2, 1))[0, :, 0] % CORE
+    turns = jnp.stack([row_turns, col_turns], axis=1)
+    forward, inverse, *fields = far_call(turns, received, amplitude, base)
     spec_re, spec_im = pl.pallas_call(
         object_kernel,
         out_shape=[f32(SPAN, HALF)] * 2,
-        in_specs=[VMEM] * 4,
+        in_specs=[VMEM] * 5,
         out_specs=[VMEM] * 2,
-        scratch_shapes=[pltpu.VMEM((4, SPAN, 2 * SPAN), jnp.bfloat16)] * 2,
         compiler_params=limit(28),
         cost_estimate=cost(3 * 2 * 226 * 10**6, 7 * 10**6),
         name="object_spectrum",
-    )(base, strip, right_head, left_tail)
-
-    row_turns = lax.dynamic_slice(row_offsets, (frame_id, 0, patch), (1, 2, 1))[0, :, 0] % CORE
-    col_turns = lax.dynamic_slice(col_offsets, (frame_id, 0, patch), (1, 2, 1))[0, :, 0] % CORE
-    turns = jnp.stack([row_turns, col_turns], axis=1)
+    )(forward, inverse, strip, right_head, left_tail)
     placed = gradient_call(
-        turns, received, amplitude, observed, base, spec_re, spec_im
+        turns, amplitude, observed, forward, inverse, *fields, spec_re, spec_im
     )
     returned = lax.all_to_all(placed, SLAB, split_axis=0, concat_axis=0, tiled=True)
 

time: 139 us -> 136 us (0.978)
  the two profiles are of different devices: /device:TPU:64 before, /device:TPU:1 now
where the time goes in v7:
time: 136 us; the launch traced here: 135 us
  starting transfers between devices  52.2 us (38%)
  blocking collectives  28.9 us (21%)
  waiting for transfers between devices  25.9 us (19%)
  Pallas kernels  22.8 us (17%)
  local copies, waits for them, and re-layouts  3.85 us (3%)
  other arithmetic  1.38 us (1%)
    ppermute x14, starting transfers between devices, down(): lax.ppermute(values, 'z', [((i + 1) % count, i) for i in range(count)])  31.6 us
    ppermute x14, waiting for transfers between devices, up(): lax.ppermute(values, 'z', [(i, (i + 1) % count) for i in range(count)])  19.4 us
    all_to_all x1, blocking collectives, body(): lax.all_to_all(placed, SLAB, split_axis=0, concat_axis=0, tiled=True)  16.6 us
    all_to_all x1, blocking collectives, body(): lax.all_to_all(summed, FRAME, split_axis=0, concat_axis=0, tiled=True)  12.3 us
    all_to_all x1, starting transfers between devices, body(): lax.all_to_all(sent, SLAB, split_axis=0, concat_axis=0, tiled=True)  11.1 us
    pallas_call x1, Pallas kernels, gradient_call(): pl.pallas_call(gradient_kernel, out_shape=f32(32, 2, 8, CORE), in_specs=[...  7.08 us
    pallas_call x1, Pallas kernels, far_call(): pl.pallas_call(far_kernel, out_shape=[matrix] * 2 + [f32(CORE, CORE)] * 2...  4.85 us
    all_to_all x1, waiting for transfers between devices, body(): lax.all_to_all(sent, SLAB, split_axis=0, concat_axis=0, tiled=True)  4.61 us
  transfers between devices with their start and end apart: 31, of which 11 were waited for; matrix products, arithmetic and copies ran while one was open for 1% of the time, Pallas kernels for 4%

profile of v7, /device:TPU:1, one launch (start us, length us, event | category | flops | bytes accessed | tf_op | source)
XLA Modules:
  0.0 135.3 jit_solution(12401719972671309694)
XLA Ops:
  0.1 1.6 %copy-done = f32[2,64,4096]{2,1,0:T(8,128)S(1)} copy-done((f32[2,64,4096]{2,1,0:T(8,128)S(1)}, f32[2,64,4096]{2,1,0:T(8,128)}, u32[]{:S(2)}) %copy-start) | copy-done | bytes 2097176
  1.7 0.9 cut_rows.1
  2.6 6.5 %collective-permute-start.1 = (f32[8,4096]{1,0:T(8,128)S(1)}, f32[8,4096]{1,0:T(8,128)S(1)}, u32[]{:S(2)}, u32[]{:S(2)}) collective-permute-start(f32[8,4096]{1,0:T(8,128)S(1)} %get-tuple-element.36.refs_1_), channel_id=1, source_target_pairs={{32,0},{64,32},{96,64},{128,96},{160,128},{192,160},{224,192},{0,2... | collective-permute-start | bytes 393224 | tf_op jit(solution)/shard_map/ppermute | solution.py:335
  9.1 2.7 %collective-permute-start = (f32[8,4096]{1,0:T(8,128)S(1)}, f32[8,4096]{1,0:T(8,128)S(1)}, u32[]{:S(2)}, u32[]{:S(2)}) collective-permute-start(f32[8,4096]{1,0:T(8,128)S(1)} %get-tuple-element.35.refs_0_), channel_id=1, source_target_pairs={{32,0},{64,32},{96,64},{128,96},{160,128},{192,160},{224,192},{0,2... | collective-permute-start | bytes 393224 | tf_op jit(solution)/shard_map/ppermute | solution.py:335
  11.8 2.9 %collective-permute-start.3 = (f32[8,4096]{1,0:T(8,128)S(1)}, f32[8,4096]{1,0:T(8,128)S(1)}, u32[]{:S(2)}, u32[]{:S(2)}) collective-permute-start(f32[8,4096]{1,0:T(8,128)S(1)} %collective-permute-done.1.refs_3_), channel_id=1, source_target_pairs={{32,0},{64,32},{96,64},{128,96},{160,128},{192,160},{224,192},{0,2... | collective-permute-start | bytes 393224 | tf_op jit(solution)/shard_map/ppermute | solution.py:335
  14.7 2.5 %collective-permute-done.11.refs_15_ = f32[8,4096]{1,0:T(8,128)S(1)} collective-permute-done((f32[8,4096]{1,0:T(8,128)S(1)}, f32[8,4096]{1,0:T(8,128)S(1)}, u32[]{:S(2)}, u32[]{:S(2)}) %collective-permute-start.11) | collective-permute-done | bytes 131104 | tf_op jit(solution)/shard_map/ppermute | solution.py:330
  17.2 2.7 %collective-permute-start.2 = (f32[8,4096]{1,0:T(8,128)S(1)}, f32[8,4096]{1,0:T(8,128)S(1)}, u32[]{:S(2)}, u32[]{:S(2)}) collective-permute-start(f32[8,4096]{1,0:T(8,128)S(1)} %collective-permute-done.refs_2_), channel_id=1, source_target_pairs={{32,0},{64,32},{96,64},{128,96},{160,128},{192,160},{224,192},{0,2... | collective-permute-start | bytes 393224 | tf_op jit(solution)/shard_map/ppermute | solution.py:335
  19.9 1.4 %collective-permute-start.8 = (f32[8,4096]{1,0:T(8,128)S(1)}, f32[8,4096]{1,0:T(8,128)S(1)}, u32[]{:S(2)}, u32[]{:S(2)}) collective-permute-start(f32[8,4096]{1,0:T(8,128)S(1)} %collective-permute-done.7.refs_12_), channel_id=1, source_target_pairs={{0,32},{32,64},{64,96},{96,128},{128,160},{160,192},{192,224},{224... | collective-permute-start | bytes 393224 | tf_op jit(solution)/shard_map/ppermute | solution.py:330
  21.3 1.7 %collective-permute-done.12.refs_13_ = f32[8,4096]{1,0:T(8,128)S(1)} collective-permute-done((f32[8,4096]{1,0:T(8,128)S(1)}, f32[8,4096]{1,0:T(8,128)S(1)}, u32[]{:S(2)}, u32[]{:S(2)}) %collective-permute-start.12) | collective-permute-done | bytes 131104 | tf_op jit(solution)/shard_map/ppermute | solution.py:330
  23.0 2.7 %collective-permute-start.4 = (f32[8,4096]{1,0:T(8,128)S(1)}, f32[8,4096]{1,0:T(8,128)S(1)}, u32[]{:S(2)}, u32[]{:S(2)}) collective-permute-start(f32[8,4096]{1,0:T(8,128)S(1)} %collective-permute-done.2.refs_4_), channel_id=1, source_target_pairs={{32,0},{64,32},{96,64},{128,96},{160,128},{192,160},{224,192},{0,2... | collective-permute-start | bytes 393224 | tf_op jit(solution)/shard_map/ppermute | solution.py:335
  25.7 1.1 collective-permute-start.10
  26.8 0.4 collective-permute-start.9
  27.2 0.8 and_select_fusion
  28.0 0.1 collective-permute-done.13.refs_11_
  28.1 1.8 %collective-permute-done.10.refs_9_ = f32[8,4096]{1,0:T(8,128)S(1)} collective-permute-done((f32[8,4096]{1,0:T(8,128)S(1)}, f32[8,4096]{1,0:T(8,128)S(1)}, u32[]{:S(2)}, u32[]{:S(2)}) %collective-permute-start.10) | collective-permute-done | bytes 131104 | tf_op jit(solution)/shard_map/ppermute | solution.py:335
  29.8 3.0 %collective-permute-done.9.refs_8_ = f32[8,4096]{1,0:T(8,128)S(1)} collective-permute-done((f32[8,4096]{1,0:T(8,128)S(1)}, f32[8,4096]{1,0:T(8,128)S(1)}, u32[]{:S(2)}, u32[]{:S(2)}) %collective-permute-start.9) | collective-permute-done | bytes 131104 | tf_op jit(solution)/shard_map/ppermute | solution.py:330
  32.8 0.7 copy-done.2
  33.5 0.7 copy-done.4
  34.2 3.1 %select_rows.1 = f32[32,2,8,256]{3,2,1,0:T(8,128)} custom-call(s32[3]{0:T(128)S(1)} %pad_add_fusion.1.place, s32[8,2,32]{2,1,0:T(2,128)S(1)} %copy-done.2, s32[8,2,32]{2,1,0:T(2,128)S(1)} %copy-done.4, f32[8,4096]{1,0:T(8,128)S(1)} %get-tuple-element.35.refs_0_, f32[8,4096]{1,0:T(8,128)S(1)} %get-tuple-element.36.refs_1_, ...), custom_call_target="tpu_custom_call" | custom-call | bytes 3000000 | tf_op jit(solution)/shard_map/select_rows/pallas_call | solution.py:383
  37.3 11.1 %all-to-all-start = ((f32[32,2,8,256]{3,2,1,0:T(8,128)}), f32[32,2,8,256]{3,2,1,0:T(8,128)S(1)}, u32[]{:S(2)}, u32[]{:S(2)}) async-start(f32[32,2,8,256]{3,2,1,0:T(8,128)} %select_rows.1), calls=%async_computation | async-start | bytes 1048576 | tf_op jit(solution)/shard_map/all_to_all | solution.py:394
  48.5 1.1 dft_base.1.base
  49.6 0.1 fusion.2
  49.7 0.1 pad_maximum_fusion.1
  49.8 1.5 %collective-permute-start.14 = (f32[192,128]{1,0:T(8,128)S(1)}, f32[192,128]{1,0:T(8,128)S(1)}, u32[]{:S(2)}, u32[]{:S(2)}) collective-permute-start(f32[192,128]{1,0:T(8,128)S(1)} %pad_maximum_fusion.1), channel_id=1, source_target_pairs={{8,0},{16,8},{24,16},{32,24},{40,32},{48,40},{56,48},{64,56},{72,6... | collective-permute-start | bytes 294920 | tf_op jit(solution)/shard_map/ppermute | solution.py:404
  51.3 0.1 pad_maximum_fusion.2
  51.4 4.0 %collective-permute-start.15 = (f32[192,128]{1,0:T(8,128)S(1)}, f32[192,128]{1,0:T(8,128)S(1)}, u32[]{:S(2)}, u32[]{:S(2)}) collective-permute-start(f32[192,128]{1,0:T(8,128)S(1)} %pad_maximum_fusion.2), channel_id=1, source_target_pairs={{0,8},{8,16},{16,24},{24,32},{32,40},{40,48},{48,56},{56,64},{64,7... | collective-permute-start | bytes 294920 | tf_op jit(solution)/shard_map/ppermute | solution.py:398
  55.4 4.6 %all-to-all-done.received = f32[32,2,8,256]{3,2,1,0:T(8,128)S(1)} async-done(((f32[32,2,8,256]{3,2,1,0:T(8,128)}), f32[32,2,8,256]{3,2,1,0:T(8,128)S(1)}, u32[]{:S(2)}, u32[]{:S(2)}) %all-to-all-start) | async-done | bytes 524320 | tf_op jit(solution)/shard_map/all_to_all | solution.py:394
  60.0 4.9 %far_field.1 = (bf16[4,384,768]{2,1,0:T(8,128)(2,1)S(1)}, bf16[4,384,768]{2,1,0:T(8,128)(2,1)S(1)}, f32[256,256]{1,0:T(8,128)S(1)}, f32[256,256]{1,0:T(8,128)S(1...) custom-call(s32[2,2]{1,0:T(2,128)S(1)} %pad_add_fusion.turns, ...), custom_call_target="tpu_custom_call" | custom-call | flops 3000000000 | bytes 7000000 | tf_op jit(solution)/shard_map/far_field/pallas_call | solution.py:298
  64.9 2.1 %object_spectrum.1 = (f32[384,256]{1,0:T(8,128)S(1)}, f32[384,256]{1,0:T(8,128)S(1)}) custom-call(bf16[4,384,768]{2,1,0:T(8,128)(2,1)S(1)} %get-tuple-element.38.forward, bf16[4,384,768]{2,1,0:T(8,128)(2,1)S(1)} %get-tuple-element.39.inverse, f32[384,256]{1,0:T(8,128)S(1)} %copy-done.1, f32[192,128]{1,0:T(8,128)S(1)} %collective-permute-done.14.right_ref, ...), custom_call_target="tpu_custom_call" | custom-call | flops 1356000000 | bytes 7000000 | tf_op jit(solution)/shard_map/object_spectrum/pallas_call | solution.py:421
  67.1 7.1 %gradient.1 = f32[32,2,8,256]{3,2,1,0:T(8,128)S(1)} custom-call(s32[2,2]{1,0:T(2,128)S(1)} %pad_add_fusion.turns, f32[256,256]{1,0:T(8,128)S(1)} %copy-done.6, f32[1,256,256]{2,1,0:T(8,128)S(1)} %copy-done.7, bf16[4,384,768]{2,1,0:T(8,128)(2,1)S(1)} %get-tuple-element.38.forward, bf16[4,384,768]{2,1,0:T(8,128)(2,1)S(1)} %get-tuple-element.39.inverse, ...), custom_call_target="tpu_custom_call" | custom-call | flops 4332000256 | bytes 7000000 | tf_op jit(solution)/shard_map/gradient/pallas_call | solution.py:311
  74.2 16.6 %all_to_all.15.values = f32[32,2,8,256]{3,2,1,0:T(8,128)S(1)} all-to-all(f32[32,2,8,256]{3,2,1,0:T(8,128)S(1)} %gradient.1), channel_id=1, replica_groups=mesh['z'=8,'x'=4,'y'=4,'core'=2] {'x','y','core'}, dimensions={0} | all-to-all | bytes 1048576 | tf_op jit(solution)/shard_map/all_to_all | solution.py:433
  90.8 3.6 %scatter_rows.1 = (f32[4,2,8,512]{3,2,1,0:T(8,128)S(1)}, f32[4,2,8,512]{3,2,1,0:T(8,128)S(1)}, f32[4,2,8,512]{3,2,1,0:T(8,128)S(1)}, f32[4,2,8,512]{3,2,1,0:T(8,...) custom-call(s32[3]{0:T(128)S(1)} %pad_add_fusion.1.place, ...), custom_call_target="tpu_custom_call" | custom-call | bytes 3000000 | tf_op jit(solution)/shard_map/scatter_rows/pallas_call | solution.py:435
  94.5 0.5 collective-permute-start.16
  94.9 2.3 %collective-permute-start.26 = (f32[4,2,8,512]{3,2,1,0:T(8,128)S(1)}, f32[4,2,8,512]{3,2,1,0:T(8,128)S(1)}, u32[]{:S(2)}, u32[]{:S(2)}) collective-permute-start(f32[4,2,8,512]{3,2,1,0:T(8,128)S(1)} %get-tuple-element.61), channel_id=1, source_target_pairs={{32,0},{64,32},{96,64},{128,96},{160,128},{192,160},{224,192},{0,2... | collective-permute-start | bytes 393224 | tf_op jit(solution)/shard_map/ppermute | solution.py:335
  97.3 3.8 %collective-permute-done.16 = f32[4,2,8,512]{3,2,1,0:T(8,128)S(1)} collective-permute-done((f32[4,2,8,512]{3,2,1,0:T(8,128)S(1)}, f32[4,2,8,512]{3,2,1,0:T(8,128)S(1)}, u32[]{:S(2)}, u32[]{:S(2)}) %collective-permute-start.16) | collective-permute-done | bytes 131104 | tf_op jit(solution)/shard_map/ppermute | solution.py:330
  101.1 0.1 collective-permute-start.17
  101.4 2.7 %collective-permute-start.27 = (f32[4,2,8,512]{3,2,1,0:T(8,128)S(1)}, f32[4,2,8,512]{3,2,1,0:T(8,128)S(1)}, u32[]{:S(2)}, u32[]{:S(2)}) collective-permute-start(f32[4,2,8,512]{3,2,1,0:T(8,128)S(1)} %add.100), channel_id=1, source_target_pairs={{32,0},{64,32},{96,64},{128,96},{160,128},{192,160},{224,192},{0,2... | collective-permute-start | bytes 393224 | tf_op jit(solution)/shard_map/ppermute | solution.py:335
  104.1 2.3 %collective-permute-start.21 = (f32[4,2,8,512]{3,2,1,0:T(8,128)S(1)}, f32[4,2,8,512]{3,2,1,0:T(8,128)S(1)}, u32[]{:S(2)}, u32[]{:S(2)}) collective-permute-start(f32[4,2,8,512]{3,2,1,0:T(8,128)S(1)} %add.94), channel_id=1, source_target_pairs={{32,0},{64,32},{96,64},{128,96},{160,128},{192,160},{224,192},{0,2... | collective-permute-start | bytes 393224 | tf_op jit(solution)/shard_map/ppermute | solution.py:335
  106.4 0.5 collective-permute-done.17
  107.0 2.7 %collective-permute-done.23 = f32[4,2,8,512]{3,2,1,0:T(8,128)S(1)} collective-permute-done((f32[4,2,8,512]{3,2,1,0:T(8,128)S(1)}, f32[4,2,8,512]{3,2,1,0:T(8,128)S(1)}, u32[]{:S(2)}, u32[]{:S(2)}) %collective-permute-start.23) | collective-permute-done | bytes 131104 | tf_op jit(solution)/shard_map/ppermute | solution.py:330
  109.9 2.7 %collective-permute-start.28 = (f32[4,2,8,512]{3,2,1,0:T(8,128)S(1)}, f32[4,2,8,512]{3,2,1,0:T(8,128)S(1)}, u32[]{:S(2)}, u32[]{:S(2)}) collective-permute-start(f32[4,2,8,512]{3,2,1,0:T(8,128)S(1)} %add.101), channel_id=1, source_target_pairs={{32,0},{64,32},{96,64},{128,96},{160,128},{192,160},{224,192},{0,2... | collective-permute-start | bytes 393224 | tf_op jit(solution)/shard_map/ppermute | solution.py:335
  112.6 0.3 collective-permute-start.22
  112.9 1.4 %collective-permute-start.19 = (f32[4,2,8,512]{3,2,1,0:T(8,128)S(1)}, f32[4,2,8,512]{3,2,1,0:T(8,128)S(1)}, u32[]{:S(2)}, u32[]{:S(2)}) collective-permute-start(f32[4,2,8,512]{3,2,1,0:T(8,128)S(1)} %add.92), channel_id=1, source_target_pairs={{0,32},{32,64},{64,96},{96,128},{128,160},{160,192},{192,224},{224... | collective-permute-start | bytes 393224 | tf_op jit(solution)/shard_map/ppermute | solution.py:330
  114.3 2.2 %collective-permute-done.24 = f32[4,2,8,512]{3,2,1,0:T(8,128)S(1)} collective-permute-done((f32[4,2,8,512]{3,2,1,0:T(8,128)S(1)}, f32[4,2,8,512]{3,2,1,0:T(8,128)S(1)}, u32[]{:S(2)}, u32[]{:S(2)}) %collective-permute-start.24) | collective-permute-done | bytes 131104 | tf_op jit(solution)/shard_map/ppermute | solution.py:330
  116.6 2.7 %collective-permute-start.29 = (f32[4,2,8,512]{3,2,1,0:T(8,128)S(1)}, f32[4,2,8,512]{3,2,1,0:T(8,128)S(1)}, u32[]{:S(2)}, u32[]{:S(2)}) collective-permute-start(f32[4,2,8,512]{3,2,1,0:T(8,128)S(1)} %add.102), channel_id=1, source_target_pairs={{32,0},{64,32},{96,64},{128,96},{160,128},{192,160},{224,192},{0,2... | collective-permute-start | bytes 393224 | tf_op jit(solution)/shard_map/ppermute | solution.py:335
  119.3 2.9 %collective-permute-done.25 = f32[4,2,8,512]{3,2,1,0:T(8,128)S(1)} collective-permute-done((f32[4,2,8,512]{3,2,1,0:T(8,128)S(1)}, f32[4,2,8,512]{3,2,1,0:T(8,128)S(1)}, u32[]{:S(2)}, u32[]{:S(2)}) %collective-permute-start.25) | collective-permute-done | bytes 131104 | tf_op jit(solution)/shard_map/ppermute | solution.py:330
  122.3 12.3 %all_to_all.16 = f32[8,2,8,512]{3,2,1,0:T(8,128)S(1)} all-to-all(f32[8,2,8,512]{3,2,1,0:T(8,128)S(1)} %pad_maximum_fusion), channel_id=1, replica_groups=mesh['z'=8,'x'=4,'y'=4,'core'=2] {'y','core'}, dimensions={0} | all-to-all | bytes 524288 | tf_op jit(solution)/shard_map/all_to_all | solution.py:446
  134.6 0.7 copy_bitcast_fusion
  (59 shorter events, 1.0 us)
Async XLA Ops:
  0.1 1.6 %copy-start = (f32[2,64,4096]{2,1,0:T(8,128)S(1)}, f32[2,64,4096]{2,1,0:T(8,128)}, u32[]{:S(2)}) copy-start(f32[2,64,4096]{2,1,0:T(8,128)} %screens.1) | copy-start | bytes 6291460
  2.6 9.2 %collective-permute-start.1 = (f32[8,4096]{1,0:T(8,128)S(1)}, f32[8,4096]{1,0:T(8,128)S(1)}, u32[]{:S(2)}, u32[]{:S(2)}) collective-permute-start(f32[8,4096]{1,0:T(8,128)S(1)} %get-tuple-element.36.refs_1_), channel_id=1, source_target_pairs={{32,0},{64,32},{96,64},{128,96},{160,128},{192,160},{224,192},{0,2... | collective-permute-start | bytes 393224 | tf_op jit(solution)/shard_map/ppermute | solution.py:335
  9.1 5.6 %collective-permute-start.6 = (f32[8,4096]{1,0:T(8,128)S(1)}, f32[8,4096]{1,0:T(8,128)S(1)}, u32[]{:S(2)}, u32[]{:S(2)}) collective-permute-start(f32[8,4096]{1,0:T(8,128)S(1)} %get-tuple-element.35.refs_0_), channel_id=1, source_target_pairs={{0,32},{32,64},{64,96},{96,128},{128,160},{160,192},{192,224},{224... | collective-permute-start | bytes 393224 | tf_op jit(solution)/shard_map/ppermute | solution.py:330
  9.1 8.1 %collective-permute-start.11 = (f32[8,4096]{1,0:T(8,128)S(1)}, f32[8,4096]{1,0:T(8,128)S(1)}, u32[]{:S(2)}, u32[]{:S(2)}) collective-permute-start(f32[8,4096]{1,0:T(8,128)S(1)} %get-tuple-element.36.refs_1_), channel_id=1, source_target_pairs={{0,32},{32,64},{64,96},{96,128},{128,160},{160,192},{192,224},{224... | collective-permute-start | bytes 393224 | tf_op jit(solution)/shard_map/ppermute | solution.py:330
  9.1 8.1 %collective-permute-start = (f32[8,4096]{1,0:T(8,128)S(1)}, f32[8,4096]{1,0:T(8,128)S(1)}, u32[]{:S(2)}, u32[]{:S(2)}) collective-permute-start(f32[8,4096]{1,0:T(8,128)S(1)} %get-tuple-element.35.refs_0_), channel_id=1, source_target_pairs={{32,0},{64,32},{96,64},{128,96},{160,128},{192,160},{224,192},{0,2... | collective-permute-start | bytes 393224 | tf_op jit(solution)/shard_map/ppermute | solution.py:335
  11.8 8.1 %collective-permute-start.3 = (f32[8,4096]{1,0:T(8,128)S(1)}, f32[8,4096]{1,0:T(8,128)S(1)}, u32[]{:S(2)}, u32[]{:S(2)}) collective-permute-start(f32[8,4096]{1,0:T(8,128)S(1)} %collective-permute-done.1.refs_3_), channel_id=1, source_target_pairs={{32,0},{64,32},{96,64},{128,96},{160,128},{192,160},{224,192},{0,2... | collective-permute-start | bytes 393224 | tf_op jit(solution)/shard_map/ppermute | solution.py:335
  14.6 5.3 %collective-permute-start.7 = (f32[8,4096]{1,0:T(8,128)S(1)}, f32[8,4096]{1,0:T(8,128)S(1)}, u32[]{:S(2)}, u32[]{:S(2)}) collective-permute-start(f32[8,4096]{1,0:T(8,128)S(1)} %collective-permute-done.6.refs_14_), channel_id=1, source_target_pairs={{0,32},{32,64},{64,96},{96,128},{128,160},{160,192},{192,224},{224... | collective-permute-start | bytes 393224 | tf_op jit(solution)/shard_map/ppermute | solution.py:330
  17.2 5.9 %collective-permute-start.12 = (f32[8,4096]{1,0:T(8,128)S(1)}, f32[8,4096]{1,0:T(8,128)S(1)}, u32[]{:S(2)}, u32[]{:S(2)}) collective-permute-start(f32[8,4096]{1,0:T(8,128)S(1)} %collective-permute-done.11.refs_15_), channel_id=1, source_target_pairs={{0,32},{32,64},{64,96},{96,128},{128,160},{160,192},{192,224},{224... | collective-permute-start | bytes 393224 | tf_op jit(solution)/shard_map/ppermute | solution.py:330
  17.2 5.9 %collective-permute-start.2 = (f32[8,4096]{1,0:T(8,128)S(1)}, f32[8,4096]{1,0:T(8,128)S(1)}, u32[]{:S(2)}, u32[]{:S(2)}) collective-permute-start(f32[8,4096]{1,0:T(8,128)S(1)} %collective-permute-done.refs_2_), channel_id=1, source_target_pairs={{32,0},{64,32},{96,64},{128,96},{160,128},{192,160},{224,192},{0,2... | collective-permute-start | bytes 393224 | tf_op jit(solution)/shard_map/ppermute | solution.py:335
  19.9 5.9 %collective-permute-start.5 = (f32[8,4096]{1,0:T(8,128)S(1)}, f32[8,4096]{1,0:T(8,128)S(1)}, u32[]{:S(2)}, u32[]{:S(2)}) collective-permute-start(f32[8,4096]{1,0:T(8,128)S(1)} %collective-permute-done.3.refs_5_), channel_id=1, source_target_pairs={{32,0},{64,32},{96,64},{128,96},{160,128},{192,160},{224,192},{0,2... | collective-permute-start | bytes 393224 | tf_op jit(solution)/shard_map/ppermute | solution.py:335
  19.9 6.9 %collective-permute-start.8 = (f32[8,4096]{1,0:T(8,128)S(1)}, f32[8,4096]{1,0:T(8,128)S(1)}, u32[]{:S(2)}, u32[]{:S(2)}) collective-permute-start(f32[8,4096]{1,0:T(8,128)S(1)} %collective-permute-done.7.refs_12_), channel_id=1, source_target_pairs={{0,32},{32,64},{64,96},{96,128},{128,160},{160,192},{192,224},{224... | collective-permute-start | bytes 393224 | tf_op jit(solution)/shard_map/ppermute | solution.py:330
  23.0 5.0 %collective-permute-start.13 = (f32[8,4096]{1,0:T(8,128)S(1)}, f32[8,4096]{1,0:T(8,128)S(1)}, u32[]{:S(2)}, u32[]{:S(2)}) collective-permute-start(f32[8,4096]{1,0:T(8,128)S(1)} %collective-permute-done.12.refs_13_), channel_id=1, source_target_pairs={{0,32},{32,64},{64,96},{96,128},{128,160},{160,192},{192,224},{224... | collective-permute-start | bytes 393224 | tf_op jit(solution)/shard_map/ppermute | solution.py:330
  23.0 5.0 %collective-permute-start.4 = (f32[8,4096]{1,0:T(8,128)S(1)}, f32[8,4096]{1,0:T(8,128)S(1)}, u32[]{:S(2)}, u32[]{:S(2)}) collective-permute-start(f32[8,4096]{1,0:T(8,128)S(1)} %collective-permute-done.2.refs_4_), channel_id=1, source_target_pairs={{32,0},{64,32},{96,64},{128,96},{160,128},{192,160},{224,192},{0,2... | collective-permute-start | bytes 393224 | tf_op jit(solution)/shard_map/ppermute | solution.py:335
  25.7 4.1 %collective-permute-start.10 = (f32[8,4096]{1,0:T(8,128)S(1)}, f32[8,4096]{1,0:T(8,128)S(1)}, u32[]{:S(2)}, u32[]{:S(2)}) collective-permute-start(f32[8,4096]{1,0:T(8,128)S(1)} %collective-permute-done.5.refs_7_), channel_id=1, source_target_pairs={{32,0},{64,32},{96,64},{128,96},{160,128},{192,160},{224,192},{0,2... | collective-permute-start | bytes 393224 | tf_op jit(solution)/shard_map/ppermute | solution.py:335
  26.8 6.0 %collective-permute-start.9 = (f32[8,4096]{1,0:T(8,128)S(1)}, f32[8,4096]{1,0:T(8,128)S(1)}, u32[]{:S(2)}, u32[]{:S(2)}) collective-permute-start(f32[8,4096]{1,0:T(8,128)S(1)} %collective-permute-done.8.refs_10_), channel_id=1, source_target_pairs={{0,32},{32,64},{64,96},{96,128},{128,160},{160,192},{192,224},{224... | collective-permute-start | bytes 393224 | tf_op jit(solution)/shard_map/ppermute | solution.py:330
  28.0 21.7 %copy-start.1 = (f32[384,256]{1,0:T(8,128)S(1)}, f32[384,256]{1,0:T(8,128)}, u32[]{:S(2)}) copy-start(f32[384,256]{1,0:T(8,128)} %strip) | copy-start | bytes 1179652
  32.8 0.7 copy-start.2
  33.5 0.7 copy-start.4
  37.3 22.7 %copy-start.6 = (f32[256,256]{1,0:T(8,128)S(1)}, f32[256,256]{1,0:T(8,128)}, u32[]{:S(2)}) copy-start(f32[256,256]{1,0:T(8,128)} %amp_ref.3) | copy-start | bytes 786436
  37.3 22.7 %all-to-all-start = ((f32[32,2,8,256]{3,2,1,0:T(8,128)}), f32[32,2,8,256]{3,2,1,0:T(8,128)S(1)}, u32[]{:S(2)}, u32[]{:S(2)}) async-start(f32[32,2,8,256]{3,2,1,0:T(8,128)} %select_rows.1), calls=%async_computation | async-start | bytes 1048576 | tf_op jit(solution)/shard_map/all_to_all | solution.py:394
  49.8 15.1 %collective-permute-start.14 = (f32[192,128]{1,0:T(8,128)S(1)}, f32[192,128]{1,0:T(8,128)S(1)}, u32[]{:S(2)}, u32[]{:S(2)}) collective-permute-start(f32[192,128]{1,0:T(8,128)S(1)} %pad_maximum_fusion.1), channel_id=1, source_target_pairs={{8,0},{16,8},{24,16},{32,24},{40,32},{48,40},{56,48},{64,56},{72,6... | collective-permute-start | bytes 294920 | tf_op jit(solution)/shard_map/ppermute | solution.py:404
  51.4 13.5 %collective-permute-start.15 = (f32[192,128]{1,0:T(8,128)S(1)}, f32[192,128]{1,0:T(8,128)S(1)}, u32[]{:S(2)}, u32[]{:S(2)}) collective-permute-start(f32[192,128]{1,0:T(8,128)S(1)} %pad_maximum_fusion.2), channel_id=1, source_target_pairs={{0,8},{8,16},{16,24},{24,32},{32,40},{40,48},{48,56},{56,64},{64,7... | collective-permute-start | bytes 294920 | tf_op jit(solution)/shard_map/ppermute | solution.py:398
  64.9 2.2 %copy-start.7 = (f32[1,256,256]{2,1,0:T(8,128)S(1)}, f32[1,256,256]{2,1,0:T(8,128)}, u32[]{:S(2)}) copy-start(f32[1,256,256]{2,1,0:T(8,128)} %observed.1) | copy-start | bytes 786436
  67.1 23.7 %copy-start.3 = (s32[8,2,32]{2,1,0:T(2,128)S(1)}, s32[8,2,32]{2,1,0:T(2,128)}, u32[]{:S(2)}) copy-start(s32[8,2,32]{2,1,0:T(2,128)} %rows.3) | copy-start | bytes 6148
  67.1 23.7 %copy-start.5 = (s32[8,2,32]{2,1,0:T(2,128)S(1)}, s32[8,2,32]{2,1,0:T(2,128)}, u32[]{:S(2)}) copy-start(s32[8,2,32]{2,1,0:T(2,128)} %cols.3) | copy-start | bytes 6148
  94.5 6.6 %collective-permute-start.16 = (f32[4,2,8,512]{3,2,1,0:T(8,128)S(1)}, f32[4,2,8,512]{3,2,1,0:T(8,128)S(1)}, u32[]{:S(2)}, u32[]{:S(2)}) collective-permute-start(f32[4,2,8,512]{3,2,1,0:T(8,128)S(1)} %get-tuple-element.50), channel_id=1, source_target_pairs={{0,32},{32,64},{64,96},{96,128},{128,160},{160,192},{192,224},{224... | collective-permute-start | bytes 393224 | tf_op jit(solution)/shard_map/ppermute | solution.py:330
  94.9 6.4 %collective-permute-start.26 = (f32[4,2,8,512]{3,2,1,0:T(8,128)S(1)}, f32[4,2,8,512]{3,2,1,0:T(8,128)S(1)}, u32[]{:S(2)}, u32[]{:S(2)}) collective-permute-start(f32[4,2,8,512]{3,2,1,0:T(8,128)S(1)} %get-tuple-element.61), channel_id=1, source_target_pairs={{32,0},{64,32},{96,64},{128,96},{160,128},{192,160},{224,192},{0,2... | collective-permute-start | bytes 393224 | tf_op jit(solution)/shard_map/ppermute | solution.py:335
  97.2 6.8 %collective-permute-start.20 = (f32[4,2,8,512]{3,2,1,0:T(8,128)S(1)}, f32[4,2,8,512]{3,2,1,0:T(8,128)S(1)}, u32[]{:S(2)}, u32[]{:S(2)}) collective-permute-start(f32[4,2,8,512]{3,2,1,0:T(8,128)S(1)} %get-tuple-element.54), channel_id=1, source_target_pairs={{32,0},{64,32},{96,64},{128,96},{160,128},{192,160},{224,192},{0,2... | collective-permute-start | bytes 393224 | tf_op jit(solution)/shard_map/ppermute | solution.py:335
  101.1 5.8 %collective-permute-start.17 = (f32[4,2,8,512]{3,2,1,0:T(8,128)S(1)}, f32[4,2,8,512]{3,2,1,0:T(8,128)S(1)}, u32[]{:S(2)}, u32[]{:S(2)}) collective-permute-start(f32[4,2,8,512]{3,2,1,0:T(8,128)S(1)} %add.90), channel_id=1, source_target_pairs={{0,32},{32,64},{64,96},{96,128},{128,160},{160,192},{192,224},{224... | collective-permute-start | bytes 393224 | tf_op jit(solution)/shard_map/ppermute | solution.py:330
  101.2 8.5 %collective-permute-start.23 = (f32[4,2,8,512]{3,2,1,0:T(8,128)S(1)}, f32[4,2,8,512]{3,2,1,0:T(8,128)S(1)}, u32[]{:S(2)}, u32[]{:S(2)}) collective-permute-start(f32[4,2,8,512]{3,2,1,0:T(8,128)S(1)} %get-tuple-element.58), channel_id=1, source_target_pairs={{0,32},{32,64},{64,96},{96,128},{128,160},{160,192},{192,224},{224... | collective-permute-start | bytes 393224 | tf_op jit(solution)/shard_map/ppermute | solution.py:330
  101.4 8.5 %collective-permute-start.27 = (f32[4,2,8,512]{3,2,1,0:T(8,128)S(1)}, f32[4,2,8,512]{3,2,1,0:T(8,128)S(1)}, u32[]{:S(2)}, u32[]{:S(2)}) collective-permute-start(f32[4,2,8,512]{3,2,1,0:T(8,128)S(1)} %add.100), channel_id=1, source_target_pairs={{32,0},{64,32},{96,64},{128,96},{160,128},{192,160},{224,192},{0,2... | collective-permute-start | bytes 393224 | tf_op jit(solution)/shard_map/ppermute | solution.py:335
  104.1 8.5 %collective-permute-start.21 = (f32[4,2,8,512]{3,2,1,0:T(8,128)S(1)}, f32[4,2,8,512]{3,2,1,0:T(8,128)S(1)}, u32[]{:S(2)}, u32[]{:S(2)}) collective-permute-start(f32[4,2,8,512]{3,2,1,0:T(8,128)S(1)} %add.94), channel_id=1, source_target_pairs={{32,0},{64,32},{96,64},{128,96},{160,128},{192,160},{224,192},{0,2... | collective-permute-start | bytes 393224 | tf_op jit(solution)/shard_map/ppermute | solution.py:335
  106.9 6.0 %collective-permute-start.18 = (f32[4,2,8,512]{3,2,1,0:T(8,128)S(1)}, f32[4,2,8,512]{3,2,1,0:T(8,128)S(1)}, u32[]{:S(2)}, u32[]{:S(2)}) collective-permute-start(f32[4,2,8,512]{3,2,1,0:T(8,128)S(1)} %add.91), channel_id=1, source_target_pairs={{0,32},{32,64},{64,96},{96,128},{128,160},{160,192},{192,224},{224... | collective-permute-start | bytes 393224 | tf_op jit(solution)/shard_map/ppermute | solution.py:330
  109.7 6.7 %collective-permute-start.24 = (f32[4,2,8,512]{3,2,1,0:T(8,128)S(1)}, f32[4,2,8,512]{3,2,1,0:T(8,128)S(1)}, u32[]{:S(2)}, u32[]{:S(2)}) collective-permute-start(f32[4,2,8,512]{3,2,1,0:T(8,128)S(1)} %add.97), channel_id=1, source_target_pairs={{0,32},{32,64},{64,96},{96,128},{128,160},{160,192},{192,224},{224... | collective-permute-start | bytes 393224 | tf_op jit(solution)/shard_map/ppermute | solution.py:330
  109.9 6.7 %collective-permute-start.28 = (f32[4,2,8,512]{3,2,1,0:T(8,128)S(1)}, f32[4,2,8,512]{3,2,1,0:T(8,128)S(1)}, u32[]{:S(2)}, u32[]{:S(2)}) collective-permute-start(f32[4,2,8,512]{3,2,1,0:T(8,128)S(1)} %add.101), channel_id=1, source_target_pairs={{32,0},{64,32},{96,64},{128,96},{160,128},{192,160},{224,192},{0,2... | collective-permute-start | bytes 393224 | tf_op jit(solution)/shard_map/ppermute | solution.py:335
  112.6 6.7 %collective-permute-start.22 = (f32[4,2,8,512]{3,2,1,0:T(8,128)S(1)}, f32[4,2,8,512]{3,2,1,0:T(8,128)S(1)}, u32[]{:S(2)}, u32[]{:S(2)}) collective-permute-start(f32[4,2,8,512]{3,2,1,0:T(8,128)S(1)} %add.95), channel_id=1, source_target_pairs={{32,0},{64,32},{96,64},{128,96},{160,128},{192,160},{224,192},{0,2... | collective-permute-start | bytes 393224 | tf_op jit(solution)/shard_map/ppermute | solution.py:335
  112.9 6.4 %collective-permute-start.19 = (f32[4,2,8,512]{3,2,1,0:T(8,128)S(1)}, f32[4,2,8,512]{3,2,1,0:T(8,128)S(1)}, u32[]{:S(2)}, u32[]{:S(2)}) collective-permute-start(f32[4,2,8,512]{3,2,1,0:T(8,128)S(1)} %add.92), channel_id=1, source_target_pairs={{0,32},{32,64},{64,96},{96,128},{128,160},{160,192},{192,224},{224... | collective-permute-start | bytes 393224 | tf_op jit(solution)/shard_map/ppermute | solution.py:330
  116.4 5.8 %collective-permute-start.25 = (f32[4,2,8,512]{3,2,1,0:T(8,128)S(1)}, f32[4,2,8,512]{3,2,1,0:T(8,128)S(1)}, u32[]{:S(2)}, u32[]{:S(2)}) collective-permute-start(f32[4,2,8,512]{3,2,1,0:T(8,128)S(1)} %add.98), channel_id=1, source_target_pairs={{0,32},{32,64},{64,96},{96,128},{128,160},{160,192},{192,224},{224... | collective-permute-start | bytes 393224 | tf_op jit(solution)/shard_map/ppermute | solution.py:330
  116.6 5.7 %collective-permute-start.29 = (f32[4,2,8,512]{3,2,1,0:T(8,128)S(1)}, f32[4,2,8,512]{3,2,1,0:T(8,128)S(1)}, u32[]{:S(2)}, u32[]{:S(2)}) collective-permute-start(f32[4,2,8,512]{3,2,1,0:T(8,128)S(1)} %add.102), channel_id=1, source_target_pairs={{32,0},{64,32},{96,64},{128,96},{160,128},{192,160},{224,192},{0,2... | collective-permute-start | bytes 393224 | tf_op jit(solution)/shard_map/ppermute | solution.py:335

commit v8 on v7

--- a/solution.py
+++ b/solution.py
@@ -127,7 +127,7 @@
 
 
 def cut_kernel(place, screens, first, second, sems):
-    at = pl.ds(pl.multiple_of(place[2], 8), 8)
+    at = pl.ds(pl.multiple_of(place[0] * 8, 8), 8)
     copies = [
         pltpu.make_async_copy(screens.at[layer, at, :], target, sems.at[layer])
         for layer, target in enumerate((first, second))
@@ -138,25 +138,25 @@
         copy.wait()
 
 
-def select_kernel(place, rows, cols, *refs):
+def select_kernel(place, table, *refs):
     chunks, out, gathered = refs[:16], refs[16], refs[17]
     slab, first = place[0], place[1]
     for step in range(8):
-        source = (slab + step) % 8
+        source = (slab + step) & 7
         for layer in range(2):
             gathered[source * 2 + layer] = chunks[step * 2 + layer][...]
     row_index = first + lax.broadcasted_iota(jnp.int32, (8, CORE), 0)
     lane = lax.broadcasted_iota(jnp.int32, (8, CORE), 1)
 
     def one(member, carry):
-        patch = slab * 4 + member // 8
-        frame = member % 8
+        patch = slab * 4 + (member >> 3)
+        frame = member & 7
         for layer in range(2):
-            row = rows[frame, layer, patch]
-            col = cols[frame, layer, patch]
-            block, residue = row // CORE, row % CORE
+            row = table[frame, layer, patch]
+            col = table[8 + frame, layer, patch]
+            block, residue = row >> 8, row & 255
             after = jnp.minimum(block + 1, 7)
-            strip, turn = col // CORE, col % CORE
+            strip, turn = col >> 8, col & 255
             at = pl.ds(pl.multiple_of(strip * CORE, CORE), CORE)
             beside = pl.ds(pl.multiple_of(jnp.minimum(strip + 1, 15) * CORE, CORE), CORE)
             right = lane >= turn
@@ -172,7 +172,7 @@
     lax.fori_loop(0, 32, one, 0, unroll=8)
 
 
-def scatter_kernel(place, rows, cols, values, *refs):
+def scatter_kernel(place, table, values, *refs):
     pieces, out = refs[:16], refs[16]
     slab, first = place[0], place[1]
     row_index = first + lax.broadcasted_iota(jnp.int32, (8, CORE), 0)
@@ -180,23 +180,23 @@
     out[...] = jnp.zeros_like(out)
 
     def one(member, carry):
-        patch = slab * 4 + member // 8
-        frame = member % 8
+        patch = slab * 4 + (member >> 3)
+        frame = member & 7
         for layer in range(2):
-            row = rows[frame, layer, patch]
-            col = cols[frame, layer, patch]
-            block, residue = row // CORE, row % CORE
+            row = table[frame, layer, patch]
+            col = table[8 + frame, layer, patch]
+            block, residue = row >> 8, row & 255
             after = jnp.minimum(block + 1, 7)
-            strip, turn = col // CORE, col % CORE
+            strip, turn = col >> 8, col & 255
             beside = jnp.minimum(strip + 1, 15)
             value = values[member, layer]
             here = row_index >= residue
             right = lane >= turn
             for target, keep_row in ((block, here), (after, ~here)):
-                where = (target + 8 - slab) % 8
+                where = (target + 8 - slab) & 7
                 for place_col, keep_col in ((strip, right), (beside, ~right)):
-                    at = pl.ds(pl.multiple_of((place_col % 2) * CORE, CORE), CORE)
-                    chunk = place_col // 2
+                    at = pl.ds(pl.multiple_of((place_col & 1) * CORE, CORE), CORE)
+                    chunk = place_col >> 1
                     out[where, chunk, layer, :, at] = out[where, chunk, layer, :, at] + jnp.where(
                         keep_row & keep_col, value, 0.0
                     )
@@ -215,17 +215,24 @@
     return 1.0 / (SPAN * SPAN * jnp.sum(amplitude * amplitude))
 
 
+def turns_of(place, table):
+    frame = place[2] >> 3
+    patch = place[0] * 4 + (place[1] >> 6)
+    return [(table[frame, layer, patch] & 255, table[8 + frame, layer, patch] & 255) for layer in range(2)]
+
+
 def far_kernel(
-    turns, received, amp_ref, base, forward, inverse, pupil_re, pupil_im, far_re, far_im,
+    place, table, received, amp_ref, base, forward, inverse, pupil_re, pupil_im, far_re, far_im,
     spread_re, spread_im, mix_h, mix_l,
 ):
     build(forward, base, 1)
     build(inverse, base, -1)
+    turns = turns_of(place, table)
     phases = None
     for layer in range(2):
         sheet = received[:, layer].reshape(CORE, CORE)
-        sheet = pltpu.roll(sheet, (CORE - turns[layer, 0]) % CORE, 0)
-        sheet = pltpu.roll(sheet, (CORE - turns[layer, 1]) % CORE, 1)
+        sheet = pltpu.roll(sheet, (CORE - turns[layer][0]) & 255, 0)
+        sheet = pltpu.roll(sheet, (CORE - turns[layer][1]) & 255, 1)
         phases = sheet if phases is None else phases + sheet
     amplitude = amp_ref[...]
     inverse_total = inverse_sum(amplitude)
@@ -246,7 +253,7 @@
 
 
 def gradient_kernel(
-    turns, amp_ref, observed, forward, inverse, pupil_re, pupil_im, far_re, far_im,
+    place, table, amp_ref, observed, forward, inverse, pupil_re, pupil_im, far_re, far_im,
     spread_re, spread_im, spec_re, spec_im, out, mix_h, mix_l, wide_h, wide_l,
 ):
     inverse_total = inverse_sum(amp_ref[...])
@@ -270,9 +277,10 @@
     out_re = right(back, forward, LOW)
     out_im = right(back, forward, HIGH)
     gradient = (2.0 * inverse_total) * (pupil_re[...] * out_im - pupil_im[...] * out_re)
+    turns = turns_of(place, table)
     for layer in range(2):
-        sheet = pltpu.roll(gradient, turns[layer, 1], 1)
-        sheet = pltpu.roll(sheet, turns[layer, 0], 0)
+        sheet = pltpu.roll(gradient, turns[layer][1], 1)
+        sheet = pltpu.roll(sheet, turns[layer][0], 0)
         out[:, layer] = sheet.reshape(32, 8, CORE)
 
 
@@ -298,7 +306,7 @@
     return pl.pallas_call(
         far_kernel,
         out_shape=[matrix] * 2 + [f32(CORE, CORE)] * 2 + [f32(SPAN, SPAN)] * 2 + [f32(SPAN, HALF)] * 2,
-        in_specs=[SMEM] + [VMEM] * 3,
+        in_specs=[SMEM] * 2 + [VMEM] * 3,
         out_specs=[VMEM] * 8,
         scratch_shapes=[pltpu.VMEM((2 * SPAN, HALF), jnp.bfloat16)] * 2,
         compiler_params=limit(28),
@@ -311,7 +319,7 @@
     return pl.pallas_call(
         gradient_kernel,
         out_shape=f32(32, 2, 8, CORE),
-        in_specs=[SMEM] + [VMEM] * 12,
+        in_specs=[SMEM] * 2 + [VMEM] * 12,
         out_specs=VMEM,
         scratch_shapes=[
             pltpu.VMEM((2 * SPAN, HALF), jnp.bfloat16),
@@ -367,29 +375,29 @@
     slab = lax.axis_index("z")
     across = lax.axis_index("x")
     frame_id = lax.axis_index(FRAME)
-    patch = slab * 4 + across
     patches = lax.axis_size("z") * lax.axis_size("x")
     place = jnp.stack([slab, across * 64 + frame_id * 8, frame_id * 8]).astype(jnp.int32)
+    table = jnp.concatenate([row_offsets, col_offsets], axis=0)
     own = pl.pallas_call(
         cut_kernel,
-        out_shape=[f32(8, screens.shape[2])] * 2,
+        out_shape=[pltpu.VMEM((8, screens.shape[2]), jnp.float32)] * 2,
         in_specs=[SMEM, ANY],
         out_specs=[VMEM] * 2,
         scratch_shapes=[pltpu.SemaphoreType.DMA((2,))],
-        compiler_params=limit(20),
+        compiler_params=limit(58),
         name="cut_rows",
-    )(place, screens)
+    )(jnp.reshape(frame_id, (1,)).astype(jnp.int32), screens)
     chunks = ring_gather(own)
     sent = pl.pallas_call(
         select_kernel,
         out_shape=f32(32, 2, 8, CORE),
-        in_specs=[SMEM] * 3 + [VMEM] * 16,
+        in_specs=[SMEM] * 2 + [VMEM] * 16,
         out_specs=VMEM,
         scratch_shapes=[pltpu.VMEM((16, 8, screens.shape[2]), jnp.float32)],
         compiler_params=limit(20),
         cost_estimate=cost(0, 3 * 10**6),
         name="select_rows",
-    )(place, row_offsets, col_offsets, *chunks)
+    )(place, table, *chunks)
     sent, strip = lax.optimization_barrier((sent, object_strip))
     received = lax.all_to_all(sent, SLAB, split_axis=0, concat_axis=0, tiled=True)
     ends = patches - 1
@@ -414,10 +422,7 @@
         cost_estimate=cost(10**6, 10**6),
         name="dft_base",
     )()
-    row_turns = lax.dynamic_slice(row_offsets, (frame_id, 0, patch), (1, 2, 1))[0, :, 0] % CORE
-    col_turns = lax.dynamic_slice(col_offsets, (frame_id, 0, patch), (1, 2, 1))[0, :, 0] % CORE
-    turns = jnp.stack([row_turns, col_turns], axis=1)
-    forward, inverse, *fields = far_call(turns, received, amplitude, base)
+    forward, inverse, *fields = far_call(place, table, received, amplitude, base)
     spec_re, spec_im = pl.pallas_call(
         object_kernel,
         out_shape=[f32(SPAN, HALF)] * 2,
@@ -428,20 +433,20 @@
         name="object_spectrum",
     )(forward, inverse, strip, right_head, left_tail)
     placed = gradient_call(
-        turns, amplitude, observed, forward, inverse, *fields, spec_re, spec_im
+        place, table, amplitude, observed, forward, inverse, *fields, spec_re, spec_im
     )
     returned = lax.all_to_all(placed, SLAB, split_axis=0, concat_axis=0, tiled=True)
 
     partial = pl.pallas_call(
         scatter_kernel,
         out_shape=[f32(4, 2, 8, 512)] * 16,
-        in_specs=[SMEM] * 3 + [VMEM],
+        in_specs=[SMEM] * 2 + [VMEM],
         out_specs=[VMEM] * 16,
         scratch_shapes=[pltpu.VMEM((8, 8, 2, 8, 512), jnp.float32)],
         compiler_params=limit(20),
         cost_estimate=cost(0, 3 * 10**6),
         name="scatter_rows",
-    )(place, row_offsets, col_offsets, returned)
+    )(place, table, returned)
     summed = ring_scatter(partial)
     turned = lax.all_to_all(summed, FRAME, split_axis=0, concat_axis=0, tiled=True)
     return turned.transpose(1, 0, 2, 3).reshape(2, 64, 512)

time: 136 us -> 131 us (0.963)
  local copies, waits for them, and re-layouts: 3.85 us -> 2.25 us
  Pallas kernels: 22.8 us -> 21.4 us
    unnamed x16 -> x7, local copies, waits for them, and re-layouts: 3.01 us -> 0.71 us
  transfers between devices with their start and end apart: 31 -> 31, of which waited for: 11 -> 11; matrix products, arithmetic and copies ran while one was open for 1% -> 2% of each run, Pallas kernels for 4% -> 5%
where the time goes in v8:
time: 131 us
  starting transfers between devices  52.2 us (40%)
  blocking collectives  28.8 us (22%)
  waiting for transfers between devices  25.2 us (19%)
  Pallas kernels  21.4 us (16%)
  local copies, waits for them, and re-layouts  2.25 us (2%)
    ppermute x14, starting transfers between devices, down(): lax.ppermute(values, 'z', [((i + 1) % count, i) for i in range(count)])  31.6 us
    ppermute x14, waiting for transfers between devices, up(): lax.ppermute(values, 'z', [(i, (i + 1) % count) for i in range(count)])  18.7 us
    all_to_all x1, blocking collectives, body(): lax.all_to_all(placed, SLAB, split_axis=0, concat_axis=0, tiled=True)  16.5 us
    all_to_all x1, blocking collectives, body(): lax.all_to_all(summed, FRAME, split_axis=0, concat_axis=0, tiled=True)  12.3 us
    all_to_all x1, starting transfers between devices, body(): lax.all_to_all(sent, SLAB, split_axis=0, concat_axis=0, tiled=True)  11.1 us
    pallas_call x1, Pallas kernels, gradient_call(): pl.pallas_call(gradient_kernel, out_shape=f32(32, 2, 8, CORE), in_specs=[...  7.34 us
    pallas_call x1, Pallas kernels, far_call(): pl.pallas_call(far_kernel, out_shape=[matrix] * 2 + [f32(CORE, CORE)] * 2...  5.12 us
    all_to_all x1, waiting for transfers between devices, body(): lax.all_to_all(sent, SLAB, split_axis=0, concat_axis=0, tiled=True)  4.68 us
  transfers between devices with their start and end apart: 31, of which 11 were waited for; matrix products, arithmetic and copies ran while one was open for 2% of the time, Pallas kernels for 5%

profile of v8, /device:TPU:1, one launch (start us, length us, event | category | flops | bytes accessed | tf_op | source)
XLA Modules:
  0.0 130.7 jit_solution(17340545716602121685)
XLA Ops:
  0.0 1.0 cut_rows.1
  1.0 6.5 %collective-permute-start.1 = (f32[8,4096]{1,0:T(8,128)S(1)}, f32[8,4096]{1,0:T(8,128)S(1)}, u32[]{:S(2)}, u32[]{:S(2)}) collective-permute-start(f32[8,4096]{1,0:T(8,128)S(1)} %get-tuple-element.36.refs_1_), channel_id=1, source_target_pairs={{32,0},{64,32},{96,64},{128,96},{160,128},{192,160},{224,192},{0,2... | collective-permute-start | bytes 393224 | tf_op jit(solution)/shard_map/ppermute | solution.py:343
  7.5 2.7 %collective-permute-start = (f32[8,4096]{1,0:T(8,128)S(1)}, f32[8,4096]{1,0:T(8,128)S(1)}, u32[]{:S(2)}, u32[]{:S(2)}) collective-permute-start(f32[8,4096]{1,0:T(8,128)S(1)} %get-tuple-element.35.refs_0_), channel_id=1, source_target_pairs={{32,0},{64,32},{96,64},{128,96},{160,128},{192,160},{224,192},{0,2... | collective-permute-start | bytes 393224 | tf_op jit(solution)/shard_map/ppermute | solution.py:343
  10.2 2.9 %collective-permute-start.3 = (f32[8,4096]{1,0:T(8,128)S(1)}, f32[8,4096]{1,0:T(8,128)S(1)}, u32[]{:S(2)}, u32[]{:S(2)}) collective-permute-start(f32[8,4096]{1,0:T(8,128)S(1)} %collective-permute-done.1.refs_3_), channel_id=1, source_target_pairs={{32,0},{64,32},{96,64},{128,96},{160,128},{192,160},{224,192},{0,2... | collective-permute-start | bytes 393224 | tf_op jit(solution)/shard_map/ppermute | solution.py:343
  13.1 2.5 %collective-permute-done.11.refs_15_ = f32[8,4096]{1,0:T(8,128)S(1)} collective-permute-done((f32[8,4096]{1,0:T(8,128)S(1)}, f32[8,4096]{1,0:T(8,128)S(1)}, u32[]{:S(2)}, u32[]{:S(2)}) %collective-permute-start.11) | collective-permute-done | bytes 131104 | tf_op jit(solution)/shard_map/ppermute | solution.py:338
  15.6 2.7 %collective-permute-start.2 = (f32[8,4096]{1,0:T(8,128)S(1)}, f32[8,4096]{1,0:T(8,128)S(1)}, u32[]{:S(2)}, u32[]{:S(2)}) collective-permute-start(f32[8,4096]{1,0:T(8,128)S(1)} %collective-permute-done.refs_2_), channel_id=1, source_target_pairs={{32,0},{64,32},{96,64},{128,96},{160,128},{192,160},{224,192},{0,2... | collective-permute-start | bytes 393224 | tf_op jit(solution)/shard_map/ppermute | solution.py:343
  18.4 1.4 %collective-permute-start.8 = (f32[8,4096]{1,0:T(8,128)S(1)}, f32[8,4096]{1,0:T(8,128)S(1)}, u32[]{:S(2)}, u32[]{:S(2)}) collective-permute-start(f32[8,4096]{1,0:T(8,128)S(1)} %collective-permute-done.7.refs_12_), channel_id=1, source_target_pairs={{0,32},{32,64},{64,96},{96,128},{128,160},{160,192},{192,224},{224... | collective-permute-start | bytes 393224 | tf_op jit(solution)/shard_map/ppermute | solution.py:338
  19.7 0.7 constant_dynamic-update-slice_fusion.1
  20.4 1.0 collective-permute-done.12.refs_13_
  21.5 2.7 %collective-permute-start.4 = (f32[8,4096]{1,0:T(8,128)S(1)}, f32[8,4096]{1,0:T(8,128)S(1)}, u32[]{:S(2)}, u32[]{:S(2)}) collective-permute-start(f32[8,4096]{1,0:T(8,128)S(1)} %collective-permute-done.2.refs_4_), channel_id=1, source_target_pairs={{32,0},{64,32},{96,64},{128,96},{160,128},{192,160},{224,192},{0,2... | collective-permute-start | bytes 393224 | tf_op jit(solution)/shard_map/ppermute | solution.py:343
  24.1 1.1 collective-permute-start.10
  25.2 0.4 collective-permute-start.9
  25.7 0.7 constant_dynamic-update-slice_fusion.table
  26.4 0.1 collective-permute-done.13.refs_11_
  26.5 1.8 %collective-permute-done.10.refs_9_ = f32[8,4096]{1,0:T(8,128)S(1)} collective-permute-done((f32[8,4096]{1,0:T(8,128)S(1)}, f32[8,4096]{1,0:T(8,128)S(1)}, u32[]{:S(2)}, u32[]{:S(2)}) %collective-permute-start.10) | collective-permute-done | bytes 131104 | tf_op jit(solution)/shard_map/ppermute | solution.py:343
  28.2 3.0 %collective-permute-done.9.refs_8_ = f32[8,4096]{1,0:T(8,128)S(1)} collective-permute-done((f32[8,4096]{1,0:T(8,128)S(1)}, f32[8,4096]{1,0:T(8,128)S(1)}, u32[]{:S(2)}, u32[]{:S(2)}) %collective-permute-start.9) | collective-permute-done | bytes 131104 | tf_op jit(solution)/shard_map/ppermute | solution.py:338
  31.2 2.4 %select_rows.1 = f32[32,2,8,256]{3,2,1,0:T(8,128)} custom-call(s32[3]{0:T(128)S(1)} %pad_add_fusion.place, s32[16,2,32]{2,1,0:T(2,128)S(1)} %constant_dynamic-update-slice_fusion.table, f32[8,4096]{1,0:T(8,128)S(1)} %get-tuple-element.35.refs_0_, f32[8,4096]{1,0:T(8,128)S(1)} %get-tuple-element.36.refs_1_, f32[8,4096]{1,0:T(8,128)S(1)} %collective-permute-done.refs_2_, ...), custom_call_target="tpu_custom_call" | custom-call | bytes 3000000 | tf_op jit(solution)/shard_map/select_rows/pallas_call | solution.py:391
  33.7 11.1 %all-to-all-start = ((f32[32,2,8,256]{3,2,1,0:T(8,128)}), f32[32,2,8,256]{3,2,1,0:T(8,128)S(1)}, u32[]{:S(2)}, u32[]{:S(2)}) async-start(f32[32,2,8,256]{3,2,1,0:T(8,128)} %select_rows.1), calls=%async_computation | async-start | bytes 1048576 | tf_op jit(solution)/shard_map/all_to_all | solution.py:402
  44.8 1.1 dft_base.1.base
  45.9 0.1 fusion
  46.0 0.1 pad_maximum_fusion.1
  46.1 1.3 collective-permute-start.14
  47.4 0.1 pad_maximum_fusion.2
  47.5 4.2 %collective-permute-start.15 = (f32[192,128]{1,0:T(8,128)S(1)}, f32[192,128]{1,0:T(8,128)S(1)}, u32[]{:S(2)}, u32[]{:S(2)}) collective-permute-start(f32[192,128]{1,0:T(8,128)S(1)} %pad_maximum_fusion.2), channel_id=1, source_target_pairs={{0,8},{8,16},{16,24},{24,32},{32,40},{40,48},{48,56},{56,64},{64,7... | collective-permute-start | bytes 294920 | tf_op jit(solution)/shard_map/ppermute | solution.py:406
  51.7 4.7 %all-to-all-done.received = f32[32,2,8,256]{3,2,1,0:T(8,128)S(1)} async-done(((f32[32,2,8,256]{3,2,1,0:T(8,128)}), f32[32,2,8,256]{3,2,1,0:T(8,128)S(1)}, u32[]{:S(2)}, u32[]{:S(2)}) %all-to-all-start) | async-done | bytes 524320 | tf_op jit(solution)/shard_map/all_to_all | solution.py:402
  56.4 5.1 %far_field.1 = (bf16[4,384,768]{2,1,0:T(8,128)(2,1)S(1)}, bf16[4,384,768]{2,1,0:T(8,128)(2,1)S(1)}, f32[256,256]{1,0:T(8,128)S(1)}, f32[256,256]{1,0:T(8,128)S(1...) custom-call(s32[3]{0:T(128)S(1)} %pad_add_fusion.place, ...), custom_call_target="tpu_custom_call" | custom-call | flops 3000000000 | bytes 7000000 | tf_op jit(solution)/shard_map/far_field/pallas_call | solution.py:306
  61.5 2.1 %object_spectrum.1 = (f32[384,256]{1,0:T(8,128)S(1)}, f32[384,256]{1,0:T(8,128)S(1)}) custom-call(bf16[4,384,768]{2,1,0:T(8,128)(2,1)S(1)} %get-tuple-element.38.forward, bf16[4,384,768]{2,1,0:T(8,128)(2,1)S(1)} %get-tuple-element.39.inverse, f32[384,256]{1,0:T(8,128)S(1)} %copy-done, f32[192,128]{1,0:T(8,128)S(1)} %collective-permute-done.14.right_ref, ...), custom_call_target="tpu_custom_call" | custom-call | flops 1356000000 | bytes 7000000 | tf_op jit(solution)/shard_map/object_spectrum/pallas_call | solution.py:426
  63.7 7.3 %gradient.1 = f32[32,2,8,256]{3,2,1,0:T(8,128)S(1)} custom-call(s32[3]{0:T(128)S(1)} %pad_add_fusion.place, s32[16,2,32]{2,1,0:T(2,128)S(1)} %constant_dynamic-update-slice_fusion.table, f32[256,256]{1,0:T(8,128)S(1)} %copy-done.1, f32[1,256,256]{2,1,0:T(8,128)S(1)} %copy-done.2, bf16[4,384,768]{2,1,0:T(8,128)(2,1)S(1)} %get-tuple-element.38.forward, ...), custom_call_target="tpu_custom_call" | custom-call | flops 4332000256 | bytes 7000000 | tf_op jit(solution)/shard_map/gradient/pallas_call | solution.py:319
  71.0 16.5 %all_to_all.15.values = f32[32,2,8,256]{3,2,1,0:T(8,128)S(1)} all-to-all(f32[32,2,8,256]{3,2,1,0:T(8,128)S(1)} %gradient.1), channel_id=1, replica_groups=mesh['z'=8,'x'=4,'y'=4,'core'=2] {'x','y','core'}, dimensions={0} | all-to-all | bytes 1048576 | tf_op jit(solution)/shard_map/all_to_all | solution.py:438
  87.6 2.3 %scatter_rows.1 = (f32[4,2,8,512]{3,2,1,0:T(8,128)S(1)}, f32[4,2,8,512]{3,2,1,0:T(8,128)S(1)}, f32[4,2,8,512]{3,2,1,0:T(8,128)S(1)}, f32[4,2,8,512]{3,2,1,0:T(8,...) custom-call(s32[3]{0:T(128)S(1)} %pad_add_fusion.place, ...), custom_call_target="tpu_custom_call" | custom-call | bytes 3000000 | tf_op jit(solution)/shard_map/scatter_rows/pallas_call | solution.py:440
  89.9 0.5 collective-permute-start.16
  90.3 2.3 %collective-permute-start.26 = (f32[4,2,8,512]{3,2,1,0:T(8,128)S(1)}, f32[4,2,8,512]{3,2,1,0:T(8,128)S(1)}, u32[]{:S(2)}, u32[]{:S(2)}) collective-permute-start(f32[4,2,8,512]{3,2,1,0:T(8,128)S(1)} %get-tuple-element.61), channel_id=1, source_target_pairs={{32,0},{64,32},{96,64},{128,96},{160,128},{192,160},{224,192},{0,2... | collective-permute-start | bytes 393224 | tf_op jit(solution)/shard_map/ppermute | solution.py:343
  92.7 3.8 %collective-permute-done.16 = f32[4,2,8,512]{3,2,1,0:T(8,128)S(1)} collective-permute-done((f32[4,2,8,512]{3,2,1,0:T(8,128)S(1)}, f32[4,2,8,512]{3,2,1,0:T(8,128)S(1)}, u32[]{:S(2)}, u32[]{:S(2)}) %collective-permute-start.16) | collective-permute-done | bytes 131104 | tf_op jit(solution)/shard_map/ppermute | solution.py:338
  96.5 0.1 collective-permute-start.17
  96.7 2.7 %collective-permute-start.27 = (f32[4,2,8,512]{3,2,1,0:T(8,128)S(1)}, f32[4,2,8,512]{3,2,1,0:T(8,128)S(1)}, u32[]{:S(2)}, u32[]{:S(2)}) collective-permute-start(f32[4,2,8,512]{3,2,1,0:T(8,128)S(1)} %add.60), channel_id=1, source_target_pairs={{32,0},{64,32},{96,64},{128,96},{160,128},{192,160},{224,192},{0,2... | collective-permute-start | bytes 393224 | tf_op jit(solution)/shard_map/ppermute | solution.py:343
  99.5 2.3 %collective-permute-start.21 = (f32[4,2,8,512]{3,2,1,0:T(8,128)S(1)}, f32[4,2,8,512]{3,2,1,0:T(8,128)S(1)}, u32[]{:S(2)}, u32[]{:S(2)}) collective-permute-start(f32[4,2,8,512]{3,2,1,0:T(8,128)S(1)} %add.54), channel_id=1, source_target_pairs={{32,0},{64,32},{96,64},{128,96},{160,128},{192,160},{224,192},{0,2... | collective-permute-start | bytes 393224 | tf_op jit(solution)/shard_map/ppermute | solution.py:343
  101.8 0.5 collective-permute-done.17
  102.4 2.7 %collective-permute-done.23 = f32[4,2,8,512]{3,2,1,0:T(8,128)S(1)} collective-permute-done((f32[4,2,8,512]{3,2,1,0:T(8,128)S(1)}, f32[4,2,8,512]{3,2,1,0:T(8,128)S(1)}, u32[]{:S(2)}, u32[]{:S(2)}) %collective-permute-start.23) | collective-permute-done | bytes 131104 | tf_op jit(solution)/shard_map/ppermute | solution.py:338
  105.1 0.1 collective-permute-start.24
  105.3 2.7 %collective-permute-start.28 = (f32[4,2,8,512]{3,2,1,0:T(8,128)S(1)}, f32[4,2,8,512]{3,2,1,0:T(8,128)S(1)}, u32[]{:S(2)}, u32[]{:S(2)}) collective-permute-start(f32[4,2,8,512]{3,2,1,0:T(8,128)S(1)} %add.61), channel_id=1, source_target_pairs={{32,0},{64,32},{96,64},{128,96},{160,128},{192,160},{224,192},{0,2... | collective-permute-start | bytes 393224 | tf_op jit(solution)/shard_map/ppermute | solution.py:343
  108.0 0.3 collective-permute-start.22
  108.3 1.4 %collective-permute-start.19 = (f32[4,2,8,512]{3,2,1,0:T(8,128)S(1)}, f32[4,2,8,512]{3,2,1,0:T(8,128)S(1)}, u32[]{:S(2)}, u32[]{:S(2)}) collective-permute-start(f32[4,2,8,512]{3,2,1,0:T(8,128)S(1)} %add.52), channel_id=1, source_target_pairs={{0,32},{32,64},{64,96},{96,128},{128,160},{160,192},{192,224},{224... | collective-permute-start | bytes 393224 | tf_op jit(solution)/shard_map/ppermute | solution.py:338
  109.7 2.2 %collective-permute-done.24 = f32[4,2,8,512]{3,2,1,0:T(8,128)S(1)} collective-permute-done((f32[4,2,8,512]{3,2,1,0:T(8,128)S(1)}, f32[4,2,8,512]{3,2,1,0:T(8,128)S(1)}, u32[]{:S(2)}, u32[]{:S(2)}) %collective-permute-start.24) | collective-permute-done | bytes 131104 | tf_op jit(solution)/shard_map/ppermute | solution.py:338
  111.8 0.1 collective-permute-start.25
  112.0 2.7 %collective-permute-start.29 = (f32[4,2,8,512]{3,2,1,0:T(8,128)S(1)}, f32[4,2,8,512]{3,2,1,0:T(8,128)S(1)}, u32[]{:S(2)}, u32[]{:S(2)}) collective-permute-start(f32[4,2,8,512]{3,2,1,0:T(8,128)S(1)} %add.62), channel_id=1, source_target_pairs={{32,0},{64,32},{96,64},{128,96},{160,128},{192,160},{224,192},{0,2... | collective-permute-start | bytes 393224 | tf_op jit(solution)/shard_map/ppermute | solution.py:343
  114.7 2.9 %collective-permute-done.25 = f32[4,2,8,512]{3,2,1,0:T(8,128)S(1)} collective-permute-done((f32[4,2,8,512]{3,2,1,0:T(8,128)S(1)}, f32[4,2,8,512]{3,2,1,0:T(8,128)S(1)}, u32[]{:S(2)}, u32[]{:S(2)}) %collective-permute-start.25) | collective-permute-done | bytes 131104 | tf_op jit(solution)/shard_map/ppermute | solution.py:338
  117.7 12.3 %all_to_all.16 = f32[8,2,8,512]{3,2,1,0:T(8,128)S(1)} all-to-all(f32[8,2,8,512]{3,2,1,0:T(8,128)S(1)} %pad_maximum_fusion), channel_id=1, replica_groups=mesh['z'=8,'x'=4,'y'=4,'core'=2] {'y','core'}, dimensions={0} | all-to-all | bytes 524288 | tf_op jit(solution)/shard_map/all_to_all | solution.py:451
  130.0 0.7 copy_bitcast_fusion
  (49 shorter events, 0.7 us)
Async XLA Ops:
  1.0 9.2 %collective-permute-start.1 = (f32[8,4096]{1,0:T(8,128)S(1)}, f32[8,4096]{1,0:T(8,128)S(1)}, u32[]{:S(2)}, u32[]{:S(2)}) collective-permute-start(f32[8,4096]{1,0:T(8,128)S(1)} %get-tuple-element.36.refs_1_), channel_id=1, source_target_pairs={{32,0},{64,32},{96,64},{128,96},{160,128},{192,160},{224,192},{0,2... | collective-permute-start | bytes 393224 | tf_op jit(solution)/shard_map/ppermute | solution.py:343
  7.5 5.6 %collective-permute-start.6 = (f32[8,4096]{1,0:T(8,128)S(1)}, f32[8,4096]{1,0:T(8,128)S(1)}, u32[]{:S(2)}, u32[]{:S(2)}) collective-permute-start(f32[8,4096]{1,0:T(8,128)S(1)} %get-tuple-element.35.refs_0_), channel_id=1, source_target_pairs={{0,32},{32,64},{64,96},{96,128},{128,160},{160,192},{192,224},{224... | collective-permute-start | bytes 393224 | tf_op jit(solution)/shard_map/ppermute | solution.py:338
  7.5 8.1 %collective-permute-start.11 = (f32[8,4096]{1,0:T(8,128)S(1)}, f32[8,4096]{1,0:T(8,128)S(1)}, u32[]{:S(2)}, u32[]{:S(2)}) collective-permute-start(f32[8,4096]{1,0:T(8,128)S(1)} %get-tuple-element.36.refs_1_), channel_id=1, source_target_pairs={{0,32},{32,64},{64,96},{96,128},{128,160},{160,192},{192,224},{224... | collective-permute-start | bytes 393224 | tf_op jit(solution)/shard_map/ppermute | solution.py:338
  7.5 8.1 %collective-permute-start = (f32[8,4096]{1,0:T(8,128)S(1)}, f32[8,4096]{1,0:T(8,128)S(1)}, u32[]{:S(2)}, u32[]{:S(2)}) collective-permute-start(f32[8,4096]{1,0:T(8,128)S(1)} %get-tuple-element.35.refs_0_), channel_id=1, source_target_pairs={{32,0},{64,32},{96,64},{128,96},{160,128},{192,160},{224,192},{0,2... | collective-permute-start | bytes 393224 | tf_op jit(solution)/shard_map/ppermute | solution.py:343
  10.2 8.1 %collective-permute-start.3 = (f32[8,4096]{1,0:T(8,128)S(1)}, f32[8,4096]{1,0:T(8,128)S(1)}, u32[]{:S(2)}, u32[]{:S(2)}) collective-permute-start(f32[8,4096]{1,0:T(8,128)S(1)} %collective-permute-done.1.refs_3_), channel_id=1, source_target_pairs={{32,0},{64,32},{96,64},{128,96},{160,128},{192,160},{224,192},{0,2... | collective-permute-start | bytes 393224 | tf_op jit(solution)/shard_map/ppermute | solution.py:343
  13.1 5.3 %collective-permute-start.7 = (f32[8,4096]{1,0:T(8,128)S(1)}, f32[8,4096]{1,0:T(8,128)S(1)}, u32[]{:S(2)}, u32[]{:S(2)}) collective-permute-start(f32[8,4096]{1,0:T(8,128)S(1)} %collective-permute-done.6.refs_14_), channel_id=1, source_target_pairs={{0,32},{32,64},{64,96},{96,128},{128,160},{160,192},{192,224},{224... | collective-permute-start | bytes 393224 | tf_op jit(solution)/shard_map/ppermute | solution.py:338
  15.6 5.9 %collective-permute-start.12 = (f32[8,4096]{1,0:T(8,128)S(1)}, f32[8,4096]{1,0:T(8,128)S(1)}, u32[]{:S(2)}, u32[]{:S(2)}) collective-permute-start(f32[8,4096]{1,0:T(8,128)S(1)} %collective-permute-done.11.refs_15_), channel_id=1, source_target_pairs={{0,32},{32,64},{64,96},{96,128},{128,160},{160,192},{192,224},{224... | collective-permute-start | bytes 393224 | tf_op jit(solution)/shard_map/ppermute | solution.py:338
  15.6 5.9 %collective-permute-start.2 = (f32[8,4096]{1,0:T(8,128)S(1)}, f32[8,4096]{1,0:T(8,128)S(1)}, u32[]{:S(2)}, u32[]{:S(2)}) collective-permute-start(f32[8,4096]{1,0:T(8,128)S(1)} %collective-permute-done.refs_2_), channel_id=1, source_target_pairs={{32,0},{64,32},{96,64},{128,96},{160,128},{192,160},{224,192},{0,2... | collective-permute-start | bytes 393224 | tf_op jit(solution)/shard_map/ppermute | solution.py:343
  18.3 5.9 %collective-permute-start.5 = (f32[8,4096]{1,0:T(8,128)S(1)}, f32[8,4096]{1,0:T(8,128)S(1)}, u32[]{:S(2)}, u32[]{:S(2)}) collective-permute-start(f32[8,4096]{1,0:T(8,128)S(1)} %collective-permute-done.3.refs_5_), channel_id=1, source_target_pairs={{32,0},{64,32},{96,64},{128,96},{160,128},{192,160},{224,192},{0,2... | collective-permute-start | bytes 393224 | tf_op jit(solution)/shard_map/ppermute | solution.py:343
  18.4 6.9 %collective-permute-start.8 = (f32[8,4096]{1,0:T(8,128)S(1)}, f32[8,4096]{1,0:T(8,128)S(1)}, u32[]{:S(2)}, u32[]{:S(2)}) collective-permute-start(f32[8,4096]{1,0:T(8,128)S(1)} %collective-permute-done.7.refs_12_), channel_id=1, source_target_pairs={{0,32},{32,64},{64,96},{96,128},{128,160},{160,192},{192,224},{224... | collective-permute-start | bytes 393224 | tf_op jit(solution)/shard_map/ppermute | solution.py:338
  21.4 5.0 %collective-permute-start.13 = (f32[8,4096]{1,0:T(8,128)S(1)}, f32[8,4096]{1,0:T(8,128)S(1)}, u32[]{:S(2)}, u32[]{:S(2)}) collective-permute-start(f32[8,4096]{1,0:T(8,128)S(1)} %collective-permute-done.12.refs_13_), channel_id=1, source_target_pairs={{0,32},{32,64},{64,96},{96,128},{128,160},{160,192},{192,224},{224... | collective-permute-start | bytes 393224 | tf_op jit(solution)/shard_map/ppermute | solution.py:338
  21.5 5.0 %collective-permute-start.4 = (f32[8,4096]{1,0:T(8,128)S(1)}, f32[8,4096]{1,0:T(8,128)S(1)}, u32[]{:S(2)}, u32[]{:S(2)}) collective-permute-start(f32[8,4096]{1,0:T(8,128)S(1)} %collective-permute-done.2.refs_4_), channel_id=1, source_target_pairs={{32,0},{64,32},{96,64},{128,96},{160,128},{192,160},{224,192},{0,2... | collective-permute-start | bytes 393224 | tf_op jit(solution)/shard_map/ppermute | solution.py:343
  24.1 4.1 %collective-permute-start.10 = (f32[8,4096]{1,0:T(8,128)S(1)}, f32[8,4096]{1,0:T(8,128)S(1)}, u32[]{:S(2)}, u32[]{:S(2)}) collective-permute-start(f32[8,4096]{1,0:T(8,128)S(1)} %collective-permute-done.5.refs_7_), channel_id=1, source_target_pairs={{32,0},{64,32},{96,64},{128,96},{160,128},{192,160},{224,192},{0,2... | collective-permute-start | bytes 393224 | tf_op jit(solution)/shard_map/ppermute | solution.py:343
  25.2 6.0 %collective-permute-start.9 = (f32[8,4096]{1,0:T(8,128)S(1)}, f32[8,4096]{1,0:T(8,128)S(1)}, u32[]{:S(2)}, u32[]{:S(2)}) collective-permute-start(f32[8,4096]{1,0:T(8,128)S(1)} %collective-permute-done.8.refs_10_), channel_id=1, source_target_pairs={{0,32},{32,64},{64,96},{96,128},{128,160},{160,192},{192,224},{224... | collective-permute-start | bytes 393224 | tf_op jit(solution)/shard_map/ppermute | solution.py:338
  26.4 19.5 %copy-start = (f32[384,256]{1,0:T(8,128)S(1)}, f32[384,256]{1,0:T(8,128)}, u32[]{:S(2)}) copy-start(f32[384,256]{1,0:T(8,128)} %strip) | copy-start | bytes 1179652
  33.7 22.7 %copy-start.1 = (f32[256,256]{1,0:T(8,128)S(1)}, f32[256,256]{1,0:T(8,128)}, u32[]{:S(2)}) copy-start(f32[256,256]{1,0:T(8,128)} %amp_ref.3) | copy-start | bytes 786436
  33.7 22.7 %all-to-all-start = ((f32[32,2,8,256]{3,2,1,0:T(8,128)}), f32[32,2,8,256]{3,2,1,0:T(8,128)S(1)}, u32[]{:S(2)}, u32[]{:S(2)}) async-start(f32[32,2,8,256]{3,2,1,0:T(8,128)} %select_rows.1), calls=%async_computation | async-start | bytes 1048576 | tf_op jit(solution)/shard_map/all_to_all | solution.py:402
  46.1 15.4 %collective-permute-start.14 = (f32[192,128]{1,0:T(8,128)S(1)}, f32[192,128]{1,0:T(8,128)S(1)}, u32[]{:S(2)}, u32[]{:S(2)}) collective-permute-start(f32[192,128]{1,0:T(8,128)S(1)} %pad_maximum_fusion.1), channel_id=1, source_target_pairs={{8,0},{16,8},{24,16},{32,24},{40,32},{48,40},{56,48},{64,56},{72,6... | collective-permute-start | bytes 294920 | tf_op jit(solution)/shard_map/ppermute | solution.py:412
  47.5 14.0 %collective-permute-start.15 = (f32[192,128]{1,0:T(8,128)S(1)}, f32[192,128]{1,0:T(8,128)S(1)}, u32[]{:S(2)}, u32[]{:S(2)}) collective-permute-start(f32[192,128]{1,0:T(8,128)S(1)} %pad_maximum_fusion.2), channel_id=1, source_target_pairs={{0,8},{8,16},{16,24},{24,32},{32,40},{40,48},{48,56},{56,64},{64,7... | collective-permute-start | bytes 294920 | tf_op jit(solution)/shard_map/ppermute | solution.py:406
  61.5 2.2 %copy-start.2 = (f32[1,256,256]{2,1,0:T(8,128)S(1)}, f32[1,256,256]{2,1,0:T(8,128)}, u32[]{:S(2)}) copy-start(f32[1,256,256]{2,1,0:T(8,128)} %observed.1) | copy-start | bytes 786436
  89.9 6.6 %collective-permute-start.16 = (f32[4,2,8,512]{3,2,1,0:T(8,128)S(1)}, f32[4,2,8,512]{3,2,1,0:T(8,128)S(1)}, u32[]{:S(2)}, u32[]{:S(2)}) collective-permute-start(f32[4,2,8,512]{3,2,1,0:T(8,128)S(1)} %get-tuple-element.50), channel_id=1, source_target_pairs={{0,32},{32,64},{64,96},{96,128},{128,160},{160,192},{192,224},{224... | collective-permute-start | bytes 393224 | tf_op jit(solution)/shard_map/ppermute | solution.py:338
  90.3 6.4 %collective-permute-start.26 = (f32[4,2,8,512]{3,2,1,0:T(8,128)S(1)}, f32[4,2,8,512]{3,2,1,0:T(8,128)S(1)}, u32[]{:S(2)}, u32[]{:S(2)}) collective-permute-start(f32[4,2,8,512]{3,2,1,0:T(8,128)S(1)} %get-tuple-element.61), channel_id=1, source_target_pairs={{32,0},{64,32},{96,64},{128,96},{160,128},{192,160},{224,192},{0,2... | collective-permute-start | bytes 393224 | tf_op jit(solution)/shard_map/ppermute | solution.py:343
  92.6 6.8 %collective-permute-start.20 = (f32[4,2,8,512]{3,2,1,0:T(8,128)S(1)}, f32[4,2,8,512]{3,2,1,0:T(8,128)S(1)}, u32[]{:S(2)}, u32[]{:S(2)}) collective-permute-start(f32[4,2,8,512]{3,2,1,0:T(8,128)S(1)} %get-tuple-element.54), channel_id=1, source_target_pairs={{32,0},{64,32},{96,64},{128,96},{160,128},{192,160},{224,192},{0,2... | collective-permute-start | bytes 393224 | tf_op jit(solution)/shard_map/ppermute | solution.py:343
  96.5 5.8 %collective-permute-start.17 = (f32[4,2,8,512]{3,2,1,0:T(8,128)S(1)}, f32[4,2,8,512]{3,2,1,0:T(8,128)S(1)}, u32[]{:S(2)}, u32[]{:S(2)}) collective-permute-start(f32[4,2,8,512]{3,2,1,0:T(8,128)S(1)} %add.50), channel_id=1, source_target_pairs={{0,32},{32,64},{64,96},{96,128},{128,160},{160,192},{192,224},{224... | collective-permute-start | bytes 393224 | tf_op jit(solution)/shard_map/ppermute | solution.py:338
  96.6 8.5 %collective-permute-start.23 = (f32[4,2,8,512]{3,2,1,0:T(8,128)S(1)}, f32[4,2,8,512]{3,2,1,0:T(8,128)S(1)}, u32[]{:S(2)}, u32[]{:S(2)}) collective-permute-start(f32[4,2,8,512]{3,2,1,0:T(8,128)S(1)} %get-tuple-element.58), channel_id=1, source_target_pairs={{0,32},{32,64},{64,96},{96,128},{128,160},{160,192},{192,224},{224... | collective-permute-start | bytes 393224 | tf_op jit(solution)/shard_map/ppermute | solution.py:338
  96.7 8.5 %collective-permute-start.27 = (f32[4,2,8,512]{3,2,1,0:T(8,128)S(1)}, f32[4,2,8,512]{3,2,1,0:T(8,128)S(1)}, u32[]{:S(2)}, u32[]{:S(2)}) collective-permute-start(f32[4,2,8,512]{3,2,1,0:T(8,128)S(1)} %add.60), channel_id=1, source_target_pairs={{32,0},{64,32},{96,64},{128,96},{160,128},{192,160},{224,192},{0,2... | collective-permute-start | bytes 393224 | tf_op jit(solution)/shard_map/ppermute | solution.py:343
  99.5 8.5 %collective-permute-start.21 = (f32[4,2,8,512]{3,2,1,0:T(8,128)S(1)}, f32[4,2,8,512]{3,2,1,0:T(8,128)S(1)}, u32[]{:S(2)}, u32[]{:S(2)}) collective-permute-start(f32[4,2,8,512]{3,2,1,0:T(8,128)S(1)} %add.54), channel_id=1, source_target_pairs={{32,0},{64,32},{96,64},{128,96},{160,128},{192,160},{224,192},{0,2... | collective-permute-start | bytes 393224 | tf_op jit(solution)/shard_map/ppermute | solution.py:343
  102.3 6.0 %collective-permute-start.18 = (f32[4,2,8,512]{3,2,1,0:T(8,128)S(1)}, f32[4,2,8,512]{3,2,1,0:T(8,128)S(1)}, u32[]{:S(2)}, u32[]{:S(2)}) collective-permute-start(f32[4,2,8,512]{3,2,1,0:T(8,128)S(1)} %add.51), channel_id=1, source_target_pairs={{0,32},{32,64},{64,96},{96,128},{128,160},{160,192},{192,224},{224... | collective-permute-start | bytes 393224 | tf_op jit(solution)/shard_map/ppermute | solution.py:338
  105.1 6.7 %collective-permute-start.24 = (f32[4,2,8,512]{3,2,1,0:T(8,128)S(1)}, f32[4,2,8,512]{3,2,1,0:T(8,128)S(1)}, u32[]{:S(2)}, u32[]{:S(2)}) collective-permute-start(f32[4,2,8,512]{3,2,1,0:T(8,128)S(1)} %add.57), channel_id=1, source_target_pairs={{0,32},{32,64},{64,96},{96,128},{128,160},{160,192},{192,224},{224... | collective-permute-start | bytes 393224 | tf_op jit(solution)/shard_map/ppermute | solution.py:338
  105.3 6.7 %collective-permute-start.28 = (f32[4,2,8,512]{3,2,1,0:T(8,128)S(1)}, f32[4,2,8,512]{3,2,1,0:T(8,128)S(1)}, u32[]{:S(2)}, u32[]{:S(2)}) collective-permute-start(f32[4,2,8,512]{3,2,1,0:T(8,128)S(1)} %add.61), channel_id=1, source_target_pairs={{32,0},{64,32},{96,64},{128,96},{160,128},{192,160},{224,192},{0,2... | collective-permute-start | bytes 393224 | tf_op jit(solution)/shard_map/ppermute | solution.py:343
  108.0 6.7 %collective-permute-start.22 = (f32[4,2,8,512]{3,2,1,0:T(8,128)S(1)}, f32[4,2,8,512]{3,2,1,0:T(8,128)S(1)}, u32[]{:S(2)}, u32[]{:S(2)}) collective-permute-start(f32[4,2,8,512]{3,2,1,0:T(8,128)S(1)} %add.55), channel_id=1, source_target_pairs={{32,0},{64,32},{96,64},{128,96},{160,128},{192,160},{224,192},{0,2... | collective-permute-start | bytes 393224 | tf_op jit(solution)/shard_map/ppermute | solution.py:343
  108.3 6.4 %collective-permute-start.19 = (f32[4,2,8,512]{3,2,1,0:T(8,128)S(1)}, f32[4,2,8,512]{3,2,1,0:T(8,128)S(1)}, u32[]{:S(2)}, u32[]{:S(2)}) collective-permute-start(f32[4,2,8,512]{3,2,1,0:T(8,128)S(1)} %add.52), channel_id=1, source_target_pairs={{0,32},{32,64},{64,96},{96,128},{128,160},{160,192},{192,224},{224... | collective-permute-start | bytes 393224 | tf_op jit(solution)/shard_map/ppermute | solution.py:338
  111.8 5.8 %collective-permute-start.25 = (f32[4,2,8,512]{3,2,1,0:T(8,128)S(1)}, f32[4,2,8,512]{3,2,1,0:T(8,128)S(1)}, u32[]{:S(2)}, u32[]{:S(2)}) collective-permute-start(f32[4,2,8,512]{3,2,1,0:T(8,128)S(1)} %add.58), channel_id=1, source_target_pairs={{0,32},{32,64},{64,96},{96,128},{128,160},{160,192},{192,224},{224... | collective-permute-start | bytes 393224 | tf_op jit(solution)/shard_map/ppermute | solution.py:338
  112.0 5.7 %collective-permute-start.29 = (f32[4,2,8,512]{3,2,1,0:T(8,128)S(1)}, f32[4,2,8,512]{3,2,1,0:T(8,128)S(1)}, u32[]{:S(2)}, u32[]{:S(2)}) collective-permute-start(f32[4,2,8,512]{3,2,1,0:T(8,128)S(1)} %add.62), channel_id=1, source_target_pairs={{32,0},{64,32},{96,64},{128,96},{160,128},{192,160},{224,192},{0,2... | collective-permute-start | bytes 393224 | tf_op jit(solution)/shard_map/ppermute | solution.py:343

commit v9 on v8

--- a/solution.py
+++ b/solution.py
@@ -11,6 +11,7 @@
 CORE = 256
 HALO = 64
 SPAN = 384
+SCOLS = 4096
 HALF = 256
 SLAB = ("x", "y", "core")
 FRAME = ("y", "core")
@@ -107,9 +108,11 @@
     lax.fori_loop(0, 8, fill, 0)
 
 
-def object_kernel(forward, inverse, strip, right_ref, left_ref, spec_re, spec_im):
+def object_kernel(place, forward, inverse, strip, mine, other, spec_re, spec_im):
     lane = lax.broadcasted_iota(jnp.int32, (SPAN // 2, 2 * HALO), 1)
-    after, before = right_ref[...], left_ref[...]
+    first = ((place[2] >> 3) & 1) == 0
+    before = jnp.where(first, mine[...], other[...])
+    after = jnp.where(first, other[...], mine[...])
     top = jnp.where(lane < HALO, after, pltpu.roll(before, HALO, 1))
     bottom = jnp.where(lane < HALO, pltpu.roll(after, HALO, 1), before)
     halo = jnp.concatenate([top, bottom], axis=0)
@@ -152,8 +155,8 @@
         patch = slab * 4 + (member >> 3)
         frame = member & 7
         for layer in range(2):
-            row = table[frame, layer, patch]
-            col = table[8 + frame, layer, patch]
+            both = table[frame, layer, patch]
+            row, col = both >> 12, both & (SCOLS - 1)
             block, residue = row >> 8, row & 255
             after = jnp.minimum(block + 1, 7)
             strip, turn = col >> 8, col & 255
@@ -183,8 +186,8 @@
         patch = slab * 4 + (member >> 3)
         frame = member & 7
         for layer in range(2):
-            row = table[frame, layer, patch]
-            col = table[8 + frame, layer, patch]
+            both = table[frame, layer, patch]
+            row, col = both >> 12, both & (SCOLS - 1)
             block, residue = row >> 8, row & 255
             after = jnp.minimum(block + 1, 7)
             strip, turn = col >> 8, col & 255
@@ -218,7 +221,8 @@
 def turns_of(place, table):
     frame = place[2] >> 3
     patch = place[0] * 4 + (place[1] >> 6)
-    return [(table[frame, layer, patch] & 255, table[8 + frame, layer, patch] & 255) for layer in range(2)]
+    both = [table[frame, layer, patch] for layer in range(2)]
+    return [((value >> 12) & 255, value & 255) for value in both]
 
 
 def far_kernel(
@@ -377,7 +381,7 @@
     frame_id = lax.axis_index(FRAME)
     patches = lax.axis_size("z") * lax.axis_size("x")
     place = jnp.stack([slab, across * 64 + frame_id * 8, frame_id * 8]).astype(jnp.int32)
-    table = jnp.concatenate([row_offsets, col_offsets], axis=0)
+    table = row_offsets * SCOLS + col_offsets
     own = pl.pallas_call(
         cut_kernel,
         out_shape=[pltpu.VMEM((8, screens.shape[2]), jnp.float32)] * 2,
@@ -402,18 +406,16 @@
     received = lax.all_to_all(sent, SLAB, split_axis=0, concat_axis=0, tiled=True)
     ends = patches - 1
     half = SPAN // 2
-    tail = strip[:, CORE - HALO :]
-    left_tail = lax.ppermute(
-        jnp.concatenate([tail[:half], tail[half:]], axis=1),
-        ("z", "x"),
-        [(i, i + 1) for i in range(ends)],
-    )
-    head = strip[:, :HALO]
-    right_head = lax.ppermute(
-        jnp.concatenate([head[:half], head[half:]], axis=1),
-        ("z", "x"),
-        [(i + 1, i) for i in range(ends)],
-    )
+    core = lax.axis_index("core")
+    tail, head = strip[:, CORE - HALO :], strip[:, :HALO]
+    edge = jnp.where(core == 0, tail, head)
+    mine = lax.ppermute(
+        jnp.concatenate([edge[:half], edge[half:]], axis=1),
+        ("z", "x", "core"),
+        [(2 * i, 2 * i + 2) for i in range(ends)]
+        + [(2 * i + 3, 2 * i + 1) for i in range(ends)],
+    )
+    other = lax.ppermute(mine, "core", [(0, 1), (1, 0)])
     base = pl.pallas_call(
         base_kernel,
         out_shape=jax.ShapeDtypeStruct((4, SPAN, SPAN), jnp.bfloat16),
@@ -426,12 +428,12 @@
     spec_re, spec_im = pl.pallas_call(
         object_kernel,
         out_shape=[f32(SPAN, HALF)] * 2,
-        in_specs=[VMEM] * 5,
+        in_specs=[SMEM] + [VMEM] * 5,
         out_specs=[VMEM] * 2,
         compiler_params=limit(28),
         cost_estimate=cost(3 * 2 * 226 * 10**6, 7 * 10**6),
         name="object_spectrum",
-    )(forward, inverse, strip, right_head, left_tail)
+    )(place, forward, inverse, strip, mine, other)
     placed = gradient_call(
         place, table, amplitude, observed, forward, inverse, *fields, spec_re, spec_im
     )

time: 131 us -> 130 us (level)
  waiting for transfers between devices: 25.2 us -> 30.1 us
  starting transfers between devices: 52.2 us -> 48 us
  local copies, waits for them, and re-layouts: 2.25 us -> 0.75 us
    ppermute x2, waiting for transfers between devices: 0.01 us -> 6.71 us  [the longest x1 6.7 us: body(): lax.ppermute(jnp.concatenate([edge[:half], edge[half:]], axis=1), ('z', '...]
    ppermute x2, starting transfers between devices: 5.46 us -> 1.3 us  [the longest x1 1.29 us: body(): lax.ppermute(jnp.concatenate([edge[:half], edge[half:]], axis=1), ('z', '...]
    all_to_all x1, waiting for transfers between devices: 4.68 us -> 2.23 us  [body(): lax.all_to_all(sent, SLAB, split_axis=0, concat_axis=0, tiled=True)]
  transfers between devices with their start and end apart: 31 -> 31, of which waited for: 11 -> 12; matrix products, arithmetic and copies ran while one was open for 2% -> 1% of each run, Pallas kernels for 5% -> 5%
where the time goes in v9:
time: 130 us
  starting transfers between devices  48 us (37%)
  waiting for transfers between devices  30.1 us (23%)
  blocking collectives  28.2 us (22%)
  Pallas kernels  21.4 us (16%)
    ppermute x14, starting transfers between devices, down(): lax.ppermute(values, 'z', [((i + 1) % count, i) for i in range(count)])  31.7 us
    ppermute x14, waiting for transfers between devices, up(): lax.ppermute(values, 'z', [(i, (i + 1) % count) for i in range(count)])  19.4 us
    all_to_all x1, blocking collectives, body(): lax.all_to_all(placed, SLAB, split_axis=0, concat_axis=0, tiled=True)  16 us
    all_to_all x1, blocking collectives, body(): lax.all_to_all(summed, FRAME, split_axis=0, concat_axis=0, tiled=True)  12.3 us
    all_to_all x1, starting transfers between devices, body(): lax.all_to_all(sent, SLAB, split_axis=0, concat_axis=0, tiled=True)  11.1 us
    pallas_call x1, Pallas kernels, gradient_call(): pl.pallas_call(gradient_kernel, out_shape=f32(32, 2, 8, CORE), in_specs=[...  7.18 us
    ppermute x1, waiting for transfers between devices, body(): lax.ppermute(jnp.concatenate([edge[:half], edge[half:]], axis=1), ('z', '...  6.7 us
    pallas_call x1, Pallas kernels, far_call(): pl.pallas_call(far_kernel, out_shape=[matrix] * 2 + [f32(CORE, CORE)] * 2...  4.98 us
  transfers between devices with their start and end apart: 31, of which 12 were waited for; matrix products, arithmetic and copies ran while one was open for 1% of the time, Pallas kernels for 5%

profile of v9, /device:TPU:1, one launch (start us, length us, event | category | flops | bytes accessed | tf_op | source)
XLA Modules:
  0.0 130.1 jit_solution(15548419563030120731)
XLA Ops:
  0.0 1.0 cut_rows.1
  1.0 6.5 %collective-permute-start.1 = (f32[8,4096]{1,0:T(8,128)S(1)}, f32[8,4096]{1,0:T(8,128)S(1)}, u32[]{:S(2)}, u32[]{:S(2)}) collective-permute-start(f32[8,4096]{1,0:T(8,128)S(1)} %get-tuple-element.36.refs_1_), channel_id=1, source_target_pairs={{32,0},{64,32},{96,64},{128,96},{160,128},{192,160},{224,192},{0,2... | collective-permute-start | bytes 393224 | tf_op jit(solution)/shard_map/ppermute | solution.py:347
  7.5 2.7 %collective-permute-start = (f32[8,4096]{1,0:T(8,128)S(1)}, f32[8,4096]{1,0:T(8,128)S(1)}, u32[]{:S(2)}, u32[]{:S(2)}) collective-permute-start(f32[8,4096]{1,0:T(8,128)S(1)} %get-tuple-element.35.refs_0_), channel_id=1, source_target_pairs={{32,0},{64,32},{96,64},{128,96},{160,128},{192,160},{224,192},{0,2... | collective-permute-start | bytes 393224 | tf_op jit(solution)/shard_map/ppermute | solution.py:347
  10.2 2.9 %collective-permute-start.3 = (f32[8,4096]{1,0:T(8,128)S(1)}, f32[8,4096]{1,0:T(8,128)S(1)}, u32[]{:S(2)}, u32[]{:S(2)}) collective-permute-start(f32[8,4096]{1,0:T(8,128)S(1)} %collective-permute-done.1.refs_3_), channel_id=1, source_target_pairs={{32,0},{64,32},{96,64},{128,96},{160,128},{192,160},{224,192},{0,2... | collective-permute-start | bytes 393224 | tf_op jit(solution)/shard_map/ppermute | solution.py:347
  13.1 2.5 %collective-permute-done.11.refs_15_ = f32[8,4096]{1,0:T(8,128)S(1)} collective-permute-done((f32[8,4096]{1,0:T(8,128)S(1)}, f32[8,4096]{1,0:T(8,128)S(1)}, u32[]{:S(2)}, u32[]{:S(2)}) %collective-permute-start.11) | collective-permute-done | bytes 131104 | tf_op jit(solution)/shard_map/ppermute | solution.py:342
  15.6 2.7 %collective-permute-start.2 = (f32[8,4096]{1,0:T(8,128)S(1)}, f32[8,4096]{1,0:T(8,128)S(1)}, u32[]{:S(2)}, u32[]{:S(2)}) collective-permute-start(f32[8,4096]{1,0:T(8,128)S(1)} %collective-permute-done.refs_2_), channel_id=1, source_target_pairs={{32,0},{64,32},{96,64},{128,96},{160,128},{192,160},{224,192},{0,2... | collective-permute-start | bytes 393224 | tf_op jit(solution)/shard_map/ppermute | solution.py:347
  18.3 0.1 collective-permute-start.5
  18.4 1.4 %collective-permute-start.8 = (f32[8,4096]{1,0:T(8,128)S(1)}, f32[8,4096]{1,0:T(8,128)S(1)}, u32[]{:S(2)}, u32[]{:S(2)}) collective-permute-start(f32[8,4096]{1,0:T(8,128)S(1)} %collective-permute-done.7.refs_12_), channel_id=1, source_target_pairs={{0,32},{32,64},{64,96},{96,128},{128,160},{160,192},{192,224},{224... | collective-permute-start | bytes 393224 | tf_op jit(solution)/shard_map/ppermute | solution.py:342
  19.8 1.7 %collective-permute-done.12.refs_13_ = f32[8,4096]{1,0:T(8,128)S(1)} collective-permute-done((f32[8,4096]{1,0:T(8,128)S(1)}, f32[8,4096]{1,0:T(8,128)S(1)}, u32[]{:S(2)}, u32[]{:S(2)}) %collective-permute-start.12) | collective-permute-done | bytes 131104 | tf_op jit(solution)/shard_map/ppermute | solution.py:342
  21.5 2.7 %collective-permute-start.4 = (f32[8,4096]{1,0:T(8,128)S(1)}, f32[8,4096]{1,0:T(8,128)S(1)}, u32[]{:S(2)}, u32[]{:S(2)}) collective-permute-start(f32[8,4096]{1,0:T(8,128)S(1)} %collective-permute-done.2.refs_4_), channel_id=1, source_target_pairs={{32,0},{64,32},{96,64},{128,96},{160,128},{192,160},{224,192},{0,2... | collective-permute-start | bytes 393224 | tf_op jit(solution)/shard_map/ppermute | solution.py:347
  24.1 1.1 collective-permute-start.10
  25.3 0.4 collective-permute-start.9
  25.6 0.7 multiply_add_fusion.table
  26.5 1.8 %collective-permute-done.10.refs_9_ = f32[8,4096]{1,0:T(8,128)S(1)} collective-permute-done((f32[8,4096]{1,0:T(8,128)S(1)}, f32[8,4096]{1,0:T(8,128)S(1)}, u32[]{:S(2)}, u32[]{:S(2)}) %collective-permute-start.10) | collective-permute-done | bytes 131104 | tf_op jit(solution)/shard_map/ppermute | solution.py:347
  28.3 3.0 %collective-permute-done.9.refs_8_ = f32[8,4096]{1,0:T(8,128)S(1)} collective-permute-done((f32[8,4096]{1,0:T(8,128)S(1)}, f32[8,4096]{1,0:T(8,128)S(1)}, u32[]{:S(2)}, u32[]{:S(2)}) %collective-permute-start.9) | collective-permute-done | bytes 131104 | tf_op jit(solution)/shard_map/ppermute | solution.py:342
  31.2 2.3 %select_rows.1 = f32[32,2,8,256]{3,2,1,0:T(8,128)} custom-call(s32[3]{0:T(128)S(1)} %pad_add_fusion.place, s32[8,2,32]{2,1,0:T(2,128)S(1)} %multiply_add_fusion.table, f32[8,4096]{1,0:T(8,128)S(1)} %get-tuple-element.35.refs_0_, f32[8,4096]{1,0:T(8,128)S(1)} %get-tuple-element.36.refs_1_, f32[8,4096]{1,0:T(8,128)S(1)} %collective-permute-done.refs_2_, ...), custom_call_target="tpu_custom_call" | custom-call | bytes 3000000 | tf_op jit(solution)/shard_map/select_rows/pallas_call | solution.py:395
  33.5 11.1 %all-to-all-start = ((f32[32,2,8,256]{3,2,1,0:T(8,128)}), f32[32,2,8,256]{3,2,1,0:T(8,128)S(1)}, u32[]{:S(2)}, u32[]{:S(2)}) async-start(f32[32,2,8,256]{3,2,1,0:T(8,128)} %select_rows.1), calls=%async_computation | async-start | bytes 1048576 | tf_op jit(solution)/shard_map/all_to_all | solution.py:406
  44.6 0.1 slice_select_fusion
  44.8 0.1 pad_maximum_fusion.1
  44.9 1.3 collective-permute-start.14
  46.2 1.1 dft_base.1.base
  47.3 6.7 %collective-permute-done.14.mine = f32[192,128]{1,0:T(8,128)S(1)} collective-permute-done((f32[192,128]{1,0:T(8,128)S(1)}, f32[192,128]{1,0:T(8,128)S(1)}, u32[]{:S(2)}, u32[]{:S(2)}) %collective-permute-start.14) | collective-permute-done | bytes 98336 | tf_op jit(solution)/shard_map/ppermute | solution.py:412
  54.0 2.2 %all-to-all-done.received = f32[32,2,8,256]{3,2,1,0:T(8,128)S(1)} async-done(((f32[32,2,8,256]{3,2,1,0:T(8,128)}), f32[32,2,8,256]{3,2,1,0:T(8,128)S(1)}, u32[]{:S(2)}, u32[]{:S(2)}) %all-to-all-start) | async-done | bytes 524320 | tf_op jit(solution)/shard_map/all_to_all | solution.py:406
  56.2 5.0 %far_field.1 = (bf16[4,384,768]{2,1,0:T(8,128)(2,1)S(1)}, bf16[4,384,768]{2,1,0:T(8,128)(2,1)S(1)}, f32[256,256]{1,0:T(8,128)S(1)}, f32[256,256]{1,0:T(8,128)S(1...) custom-call(s32[3]{0:T(128)S(1)} %pad_add_fusion.place, ...), custom_call_target="tpu_custom_call" | custom-call | flops 3000000000 | bytes 7000000 | tf_op jit(solution)/shard_map/far_field/pallas_call | solution.py:310
  61.2 2.7 %object_spectrum.1 = (f32[384,256]{1,0:T(8,128)S(1)}, f32[384,256]{1,0:T(8,128)S(1)}) custom-call(s32[3]{0:T(128)S(1)} %pad_add_fusion.place, bf16[4,384,768]{2,1,0:T(8,128)(2,1)S(1)} %get-tuple-element.38.forward, bf16[4,384,768]{2,1,0:T(8,128)(2,1)S(1)} %get-tuple-element.39.inverse, f32[384,256]{1,0:T(8,128)S(1)} %copy-done, ...), custom_call_target="tpu_custom_call" | custom-call | flops 1356000000 | bytes 7000000 | tf_op jit(solution)/shard_map/object_spectrum/pallas_call | solution.py:428
  63.9 7.2 %gradient.1 = f32[32,2,8,256]{3,2,1,0:T(8,128)S(1)} custom-call(s32[3]{0:T(128)S(1)} %pad_add_fusion.place, s32[8,2,32]{2,1,0:T(2,128)S(1)} %multiply_add_fusion.table, f32[256,256]{1,0:T(8,128)S(1)} %copy-done.1, f32[1,256,256]{2,1,0:T(8,128)S(1)} %copy-done.2, bf16[4,384,768]{2,1,0:T(8,128)(2,1)S(1)} %get-tuple-element.38.forward, ...), custom_call_target="tpu_custom_call" | custom-call | flops 4332000256 | bytes 7000000 | tf_op jit(solution)/shard_map/gradient/pallas_call | solution.py:323
  71.1 16.0 %all_to_all.15.values = f32[32,2,8,256]{3,2,1,0:T(8,128)S(1)} all-to-all(f32[32,2,8,256]{3,2,1,0:T(8,128)S(1)} %gradient.1), channel_id=1, replica_groups=mesh['z'=8,'x'=4,'y'=4,'core'=2] {'x','y','core'}, dimensions={0} | all-to-all | bytes 1048576 | tf_op jit(solution)/shard_map/all_to_all | solution.py:440
  87.1 2.2 %scatter_rows.1 = (f32[4,2,8,512]{3,2,1,0:T(8,128)S(1)}, f32[4,2,8,512]{3,2,1,0:T(8,128)S(1)}, f32[4,2,8,512]{3,2,1,0:T(8,128)S(1)}, f32[4,2,8,512]{3,2,1,0:T(8,...) custom-call(s32[3]{0:T(128)S(1)} %pad_add_fusion.place, ...), custom_call_target="tpu_custom_call" | custom-call | bytes 3000000 | tf_op jit(solution)/shard_map/scatter_rows/pallas_call | solution.py:442
  89.3 0.5 collective-permute-start.16
  89.7 2.3 %collective-permute-start.26 = (f32[4,2,8,512]{3,2,1,0:T(8,128)S(1)}, f32[4,2,8,512]{3,2,1,0:T(8,128)S(1)}, u32[]{:S(2)}, u32[]{:S(2)}) collective-permute-start(f32[4,2,8,512]{3,2,1,0:T(8,128)S(1)} %get-tuple-element.61), channel_id=1, source_target_pairs={{32,0},{64,32},{96,64},{128,96},{160,128},{192,160},{224,192},{0,2... | collective-permute-start | bytes 393224 | tf_op jit(solution)/shard_map/ppermute | solution.py:347
  92.1 3.8 %collective-permute-done.16 = f32[4,2,8,512]{3,2,1,0:T(8,128)S(1)} collective-permute-done((f32[4,2,8,512]{3,2,1,0:T(8,128)S(1)}, f32[4,2,8,512]{3,2,1,0:T(8,128)S(1)}, u32[]{:S(2)}, u32[]{:S(2)}) %collective-permute-start.16) | collective-permute-done | bytes 131104 | tf_op jit(solution)/shard_map/ppermute | solution.py:342
  95.9 0.1 collective-permute-start.17
  96.0 0.1 collective-permute-start.23
  96.2 2.7 %collective-permute-start.27 = (f32[4,2,8,512]{3,2,1,0:T(8,128)S(1)}, f32[4,2,8,512]{3,2,1,0:T(8,128)S(1)}, u32[]{:S(2)}, u32[]{:S(2)}) collective-permute-start(f32[4,2,8,512]{3,2,1,0:T(8,128)S(1)} %add.64), channel_id=1, source_target_pairs={{32,0},{64,32},{96,64},{128,96},{160,128},{192,160},{224,192},{0,2... | collective-permute-start | bytes 393224 | tf_op jit(solution)/shard_map/ppermute | solution.py:347
  98.9 2.3 %collective-permute-start.21 = (f32[4,2,8,512]{3,2,1,0:T(8,128)S(1)}, f32[4,2,8,512]{3,2,1,0:T(8,128)S(1)}, u32[]{:S(2)}, u32[]{:S(2)}) collective-permute-start(f32[4,2,8,512]{3,2,1,0:T(8,128)S(1)} %add.58), channel_id=1, source_target_pairs={{32,0},{64,32},{96,64},{128,96},{160,128},{192,160},{224,192},{0,2... | collective-permute-start | bytes 393224 | tf_op jit(solution)/shard_map/ppermute | solution.py:347
  101.2 0.5 collective-permute-done.17
  101.7 0.1 collective-permute-start.18
  101.8 2.7 %collective-permute-done.23 = f32[4,2,8,512]{3,2,1,0:T(8,128)S(1)} collective-permute-done((f32[4,2,8,512]{3,2,1,0:T(8,128)S(1)}, f32[4,2,8,512]{3,2,1,0:T(8,128)S(1)}, u32[]{:S(2)}, u32[]{:S(2)}) %collective-permute-start.23) | collective-permute-done | bytes 131104 | tf_op jit(solution)/shard_map/ppermute | solution.py:342
  104.5 0.1 collective-permute-start.24
  104.7 2.7 %collective-permute-start.28 = (f32[4,2,8,512]{3,2,1,0:T(8,128)S(1)}, f32[4,2,8,512]{3,2,1,0:T(8,128)S(1)}, u32[]{:S(2)}, u32[]{:S(2)}) collective-permute-start(f32[4,2,8,512]{3,2,1,0:T(8,128)S(1)} %add.65), channel_id=1, source_target_pairs={{32,0},{64,32},{96,64},{128,96},{160,128},{192,160},{224,192},{0,2... | collective-permute-start | bytes 393224 | tf_op jit(solution)/shard_map/ppermute | solution.py:347
  107.4 0.3 collective-permute-start.22
  107.7 1.4 %collective-permute-start.19 = (f32[4,2,8,512]{3,2,1,0:T(8,128)S(1)}, f32[4,2,8,512]{3,2,1,0:T(8,128)S(1)}, u32[]{:S(2)}, u32[]{:S(2)}) collective-permute-start(f32[4,2,8,512]{3,2,1,0:T(8,128)S(1)} %add.56), channel_id=1, source_target_pairs={{0,32},{32,64},{64,96},{96,128},{128,160},{160,192},{192,224},{224... | collective-permute-start | bytes 393224 | tf_op jit(solution)/shard_map/ppermute | solution.py:342
  109.1 2.2 %collective-permute-done.24 = f32[4,2,8,512]{3,2,1,0:T(8,128)S(1)} collective-permute-done((f32[4,2,8,512]{3,2,1,0:T(8,128)S(1)}, f32[4,2,8,512]{3,2,1,0:T(8,128)S(1)}, u32[]{:S(2)}, u32[]{:S(2)}) %collective-permute-start.24) | collective-permute-done | bytes 131104 | tf_op jit(solution)/shard_map/ppermute | solution.py:342
  111.2 0.1 collective-permute-start.25
  111.4 2.7 %collective-permute-start.29 = (f32[4,2,8,512]{3,2,1,0:T(8,128)S(1)}, f32[4,2,8,512]{3,2,1,0:T(8,128)S(1)}, u32[]{:S(2)}, u32[]{:S(2)}) collective-permute-start(f32[4,2,8,512]{3,2,1,0:T(8,128)S(1)} %add.66), channel_id=1, source_target_pairs={{32,0},{64,32},{96,64},{128,96},{160,128},{192,160},{224,192},{0,2... | collective-permute-start | bytes 393224 | tf_op jit(solution)/shard_map/ppermute | solution.py:347
  114.1 2.9 %collective-permute-done.25 = f32[4,2,8,512]{3,2,1,0:T(8,128)S(1)} collective-permute-done((f32[4,2,8,512]{3,2,1,0:T(8,128)S(1)}, f32[4,2,8,512]{3,2,1,0:T(8,128)S(1)}, u32[]{:S(2)}, u32[]{:S(2)}) %collective-permute-start.25) | collective-permute-done | bytes 131104 | tf_op jit(solution)/shard_map/ppermute | solution.py:342
  117.1 12.3 %all_to_all.16 = f32[8,2,8,512]{3,2,1,0:T(8,128)S(1)} all-to-all(f32[8,2,8,512]{3,2,1,0:T(8,128)S(1)} %pad_maximum_fusion), channel_id=1, replica_groups=mesh['z'=8,'x'=4,'y'=4,'core'=2] {'y','core'}, dimensions={0} | all-to-all | bytes 524288 | tf_op jit(solution)/shard_map/all_to_all | solution.py:453
  129.4 0.7 copy_bitcast_fusion
  (48 shorter events, 0.6 us)
Async XLA Ops:
  1.0 43.6 %copy-start = (f32[384,256]{1,0:T(8,128)S(1)}, f32[384,256]{1,0:T(8,128)}, u32[]{:S(2)}) copy-start(f32[384,256]{1,0:T(8,128)} %strip) | copy-start | bytes 1179652
  1.0 9.2 %collective-permute-start.1 = (f32[8,4096]{1,0:T(8,128)S(1)}, f32[8,4096]{1,0:T(8,128)S(1)}, u32[]{:S(2)}, u32[]{:S(2)}) collective-permute-start(f32[8,4096]{1,0:T(8,128)S(1)} %get-tuple-element.36.refs_1_), channel_id=1, source_target_pairs={{32,0},{64,32},{96,64},{128,96},{160,128},{192,160},{224,192},{0,2... | collective-permute-start | bytes 393224 | tf_op jit(solution)/shard_map/ppermute | solution.py:347
  7.5 5.6 %collective-permute-start.6 = (f32[8,4096]{1,0:T(8,128)S(1)}, f32[8,4096]{1,0:T(8,128)S(1)}, u32[]{:S(2)}, u32[]{:S(2)}) collective-permute-start(f32[8,4096]{1,0:T(8,128)S(1)} %get-tuple-element.35.refs_0_), channel_id=1, source_target_pairs={{0,32},{32,64},{64,96},{96,128},{128,160},{160,192},{192,224},{224... | collective-permute-start | bytes 393224 | tf_op jit(solution)/shard_map/ppermute | solution.py:342
  7.5 8.1 %collective-permute-start.11 = (f32[8,4096]{1,0:T(8,128)S(1)}, f32[8,4096]{1,0:T(8,128)S(1)}, u32[]{:S(2)}, u32[]{:S(2)}) collective-permute-start(f32[8,4096]{1,0:T(8,128)S(1)} %get-tuple-element.36.refs_1_), channel_id=1, source_target_pairs={{0,32},{32,64},{64,96},{96,128},{128,160},{160,192},{192,224},{224... | collective-permute-start | bytes 393224 | tf_op jit(solution)/shard_map/ppermute | solution.py:342
  7.5 8.1 %collective-permute-start = (f32[8,4096]{1,0:T(8,128)S(1)}, f32[8,4096]{1,0:T(8,128)S(1)}, u32[]{:S(2)}, u32[]{:S(2)}) collective-permute-start(f32[8,4096]{1,0:T(8,128)S(1)} %get-tuple-element.35.refs_0_), channel_id=1, source_target_pairs={{32,0},{64,32},{96,64},{128,96},{160,128},{192,160},{224,192},{0,2... | collective-permute-start | bytes 393224 | tf_op jit(solution)/shard_map/ppermute | solution.py:347
  10.2 8.1 %collective-permute-start.3 = (f32[8,4096]{1,0:T(8,128)S(1)}, f32[8,4096]{1,0:T(8,128)S(1)}, u32[]{:S(2)}, u32[]{:S(2)}) collective-permute-start(f32[8,4096]{1,0:T(8,128)S(1)} %collective-permute-done.1.refs_3_), channel_id=1, source_target_pairs={{32,0},{64,32},{96,64},{128,96},{160,128},{192,160},{224,192},{0,2... | collective-permute-start | bytes 393224 | tf_op jit(solution)/shard_map/ppermute | solution.py:347
  13.1 5.3 %collective-permute-start.7 = (f32[8,4096]{1,0:T(8,128)S(1)}, f32[8,4096]{1,0:T(8,128)S(1)}, u32[]{:S(2)}, u32[]{:S(2)}) collective-permute-start(f32[8,4096]{1,0:T(8,128)S(1)} %collective-permute-done.6.refs_14_), channel_id=1, source_target_pairs={{0,32},{32,64},{64,96},{96,128},{128,160},{160,192},{192,224},{224... | collective-permute-start | bytes 393224 | tf_op jit(solution)/shard_map/ppermute | solution.py:342
  15.6 5.9 %collective-permute-start.12 = (f32[8,4096]{1,0:T(8,128)S(1)}, f32[8,4096]{1,0:T(8,128)S(1)}, u32[]{:S(2)}, u32[]{:S(2)}) collective-permute-start(f32[8,4096]{1,0:T(8,128)S(1)} %collective-permute-done.11.refs_15_), channel_id=1, source_target_pairs={{0,32},{32,64},{64,96},{96,128},{128,160},{160,192},{192,224},{224... | collective-permute-start | bytes 393224 | tf_op jit(solution)/shard_map/ppermute | solution.py:342
  15.6 5.9 %collective-permute-start.2 = (f32[8,4096]{1,0:T(8,128)S(1)}, f32[8,4096]{1,0:T(8,128)S(1)}, u32[]{:S(2)}, u32[]{:S(2)}) collective-permute-start(f32[8,4096]{1,0:T(8,128)S(1)} %collective-permute-done.refs_2_), channel_id=1, source_target_pairs={{32,0},{64,32},{96,64},{128,96},{160,128},{192,160},{224,192},{0,2... | collective-permute-start | bytes 393224 | tf_op jit(solution)/shard_map/ppermute | solution.py:347
  18.3 5.9 %collective-permute-start.5 = (f32[8,4096]{1,0:T(8,128)S(1)}, f32[8,4096]{1,0:T(8,128)S(1)}, u32[]{:S(2)}, u32[]{:S(2)}) collective-permute-start(f32[8,4096]{1,0:T(8,128)S(1)} %collective-permute-done.3.refs_5_), channel_id=1, source_target_pairs={{32,0},{64,32},{96,64},{128,96},{160,128},{192,160},{224,192},{0,2... | collective-permute-start | bytes 393224 | tf_op jit(solution)/shard_map/ppermute | solution.py:347
  18.4 6.9 %collective-permute-start.8 = (f32[8,4096]{1,0:T(8,128)S(1)}, f32[8,4096]{1,0:T(8,128)S(1)}, u32[]{:S(2)}, u32[]{:S(2)}) collective-permute-start(f32[8,4096]{1,0:T(8,128)S(1)} %collective-permute-done.7.refs_12_), channel_id=1, source_target_pairs={{0,32},{32,64},{64,96},{96,128},{128,160},{160,192},{192,224},{224... | collective-permute-start | bytes 393224 | tf_op jit(solution)/shard_map/ppermute | solution.py:342
  21.5 5.0 %collective-permute-start.13 = (f32[8,4096]{1,0:T(8,128)S(1)}, f32[8,4096]{1,0:T(8,128)S(1)}, u32[]{:S(2)}, u32[]{:S(2)}) collective-permute-start(f32[8,4096]{1,0:T(8,128)S(1)} %collective-permute-done.12.refs_13_), channel_id=1, source_target_pairs={{0,32},{32,64},{64,96},{96,128},{128,160},{160,192},{192,224},{224... | collective-permute-start | bytes 393224 | tf_op jit(solution)/shard_map/ppermute | solution.py:342
  21.5 5.0 %collective-permute-start.4 = (f32[8,4096]{1,0:T(8,128)S(1)}, f32[8,4096]{1,0:T(8,128)S(1)}, u32[]{:S(2)}, u32[]{:S(2)}) collective-permute-start(f32[8,4096]{1,0:T(8,128)S(1)} %collective-permute-done.2.refs_4_), channel_id=1, source_target_pairs={{32,0},{64,32},{96,64},{128,96},{160,128},{192,160},{224,192},{0,2... | collective-permute-start | bytes 393224 | tf_op jit(solution)/shard_map/ppermute | solution.py:347
  24.1 4.1 %collective-permute-start.10 = (f32[8,4096]{1,0:T(8,128)S(1)}, f32[8,4096]{1,0:T(8,128)S(1)}, u32[]{:S(2)}, u32[]{:S(2)}) collective-permute-start(f32[8,4096]{1,0:T(8,128)S(1)} %collective-permute-done.5.refs_7_), channel_id=1, source_target_pairs={{32,0},{64,32},{96,64},{128,96},{160,128},{192,160},{224,192},{0,2... | collective-permute-start | bytes 393224 | tf_op jit(solution)/shard_map/ppermute | solution.py:347
  25.3 6.0 %collective-permute-start.9 = (f32[8,4096]{1,0:T(8,128)S(1)}, f32[8,4096]{1,0:T(8,128)S(1)}, u32[]{:S(2)}, u32[]{:S(2)}) collective-permute-start(f32[8,4096]{1,0:T(8,128)S(1)} %collective-permute-done.8.refs_10_), channel_id=1, source_target_pairs={{0,32},{32,64},{64,96},{96,128},{128,160},{160,192},{192,224},{224... | collective-permute-start | bytes 393224 | tf_op jit(solution)/shard_map/ppermute | solution.py:342
  33.5 22.7 %copy-start.1 = (f32[256,256]{1,0:T(8,128)S(1)}, f32[256,256]{1,0:T(8,128)}, u32[]{:S(2)}) copy-start(f32[256,256]{1,0:T(8,128)} %amp_ref.3) | copy-start | bytes 786436
  33.5 22.7 %all-to-all-start = ((f32[32,2,8,256]{3,2,1,0:T(8,128)}), f32[32,2,8,256]{3,2,1,0:T(8,128)S(1)}, u32[]{:S(2)}, u32[]{:S(2)}) async-start(f32[32,2,8,256]{3,2,1,0:T(8,128)} %select_rows.1), calls=%async_computation | async-start | bytes 1048576 | tf_op jit(solution)/shard_map/all_to_all | solution.py:406
  44.9 9.1 %collective-permute-start.14 = (f32[192,128]{1,0:T(8,128)S(1)}, f32[192,128]{1,0:T(8,128)S(1)}, u32[]{:S(2)}, u32[]{:S(2)}) collective-permute-start(f32[192,128]{1,0:T(8,128)S(1)} %pad_maximum_fusion.1), channel_id=1, source_target_pairs={{0,8},{8,16},{16,24},{24,32},{32,40},{40,48},{48,56},{56,64},{64,7... | collective-permute-start | bytes 294920 | tf_op jit(solution)/shard_map/ppermute | solution.py:412
  54.0 7.2 %collective-permute-start.15 = (f32[192,128]{1,0:T(8,128)S(1)}, f32[192,128]{1,0:T(8,128)S(1)}, u32[]{:S(2)}, u32[]{:S(2)}) collective-permute-start(f32[192,128]{1,0:T(8,128)S(1)} %collective-permute-done.14.mine), channel_id=1, source_target_pairs={{0,1},{1,0},{2,3},{3,2},{4,5},{5,4},{6,7},{7,6},{8,9},{9,8},{10,11... | collective-permute-start | bytes 294920 | tf_op jit(solution)/shard_map/ppermute | solution.py:418
  61.2 2.7 %copy-start.2 = (f32[1,256,256]{2,1,0:T(8,128)S(1)}, f32[1,256,256]{2,1,0:T(8,128)}, u32[]{:S(2)}) copy-start(f32[1,256,256]{2,1,0:T(8,128)} %observed.1) | copy-start | bytes 786436
  89.3 6.6 %collective-permute-start.16 = (f32[4,2,8,512]{3,2,1,0:T(8,128)S(1)}, f32[4,2,8,512]{3,2,1,0:T(8,128)S(1)}, u32[]{:S(2)}, u32[]{:S(2)}) collective-permute-start(f32[4,2,8,512]{3,2,1,0:T(8,128)S(1)} %get-tuple-element.50), channel_id=1, source_target_pairs={{0,32},{32,64},{64,96},{96,128},{128,160},{160,192},{192,224},{224... | collective-permute-start | bytes 393224 | tf_op jit(solution)/shard_map/ppermute | solution.py:342
  89.7 6.4 %collective-permute-start.26 = (f32[4,2,8,512]{3,2,1,0:T(8,128)S(1)}, f32[4,2,8,512]{3,2,1,0:T(8,128)S(1)}, u32[]{:S(2)}, u32[]{:S(2)}) collective-permute-start(f32[4,2,8,512]{3,2,1,0:T(8,128)S(1)} %get-tuple-element.61), channel_id=1, source_target_pairs={{32,0},{64,32},{96,64},{128,96},{160,128},{192,160},{224,192},{0,2... | collective-permute-start | bytes 393224 | tf_op jit(solution)/shard_map/ppermute | solution.py:347
  92.0 6.8 %collective-permute-start.20 = (f32[4,2,8,512]{3,2,1,0:T(8,128)S(1)}, f32[4,2,8,512]{3,2,1,0:T(8,128)S(1)}, u32[]{:S(2)}, u32[]{:S(2)}) collective-permute-start(f32[4,2,8,512]{3,2,1,0:T(8,128)S(1)} %get-tuple-element.54), channel_id=1, source_target_pairs={{32,0},{64,32},{96,64},{128,96},{160,128},{192,160},{224,192},{0,2... | collective-permute-start | bytes 393224 | tf_op jit(solution)/shard_map/ppermute | solution.py:347
  95.9 5.8 %collective-permute-start.17 = (f32[4,2,8,512]{3,2,1,0:T(8,128)S(1)}, f32[4,2,8,512]{3,2,1,0:T(8,128)S(1)}, u32[]{:S(2)}, u32[]{:S(2)}) collective-permute-start(f32[4,2,8,512]{3,2,1,0:T(8,128)S(1)} %add.54), channel_id=1, source_target_pairs={{0,32},{32,64},{64,96},{96,128},{128,160},{160,192},{192,224},{224... | collective-permute-start | bytes 393224 | tf_op jit(solution)/shard_map/ppermute | solution.py:342
  96.0 8.5 %collective-permute-start.23 = (f32[4,2,8,512]{3,2,1,0:T(8,128)S(1)}, f32[4,2,8,512]{3,2,1,0:T(8,128)S(1)}, u32[]{:S(2)}, u32[]{:S(2)}) collective-permute-start(f32[4,2,8,512]{3,2,1,0:T(8,128)S(1)} %get-tuple-element.58), channel_id=1, source_target_pairs={{0,32},{32,64},{64,96},{96,128},{128,160},{160,192},{192,224},{224... | collective-permute-start | bytes 393224 | tf_op jit(solution)/shard_map/ppermute | solution.py:342
  96.2 8.5 %collective-permute-start.27 = (f32[4,2,8,512]{3,2,1,0:T(8,128)S(1)}, f32[4,2,8,512]{3,2,1,0:T(8,128)S(1)}, u32[]{:S(2)}, u32[]{:S(2)}) collective-permute-start(f32[4,2,8,512]{3,2,1,0:T(8,128)S(1)} %add.64), channel_id=1, source_target_pairs={{32,0},{64,32},{96,64},{128,96},{160,128},{192,160},{224,192},{0,2... | collective-permute-start | bytes 393224 | tf_op jit(solution)/shard_map/ppermute | solution.py:347
  98.9 8.5 %collective-permute-start.21 = (f32[4,2,8,512]{3,2,1,0:T(8,128)S(1)}, f32[4,2,8,512]{3,2,1,0:T(8,128)S(1)}, u32[]{:S(2)}, u32[]{:S(2)}) collective-permute-start(f32[4,2,8,512]{3,2,1,0:T(8,128)S(1)} %add.58), channel_id=1, source_target_pairs={{32,0},{64,32},{96,64},{128,96},{160,128},{192,160},{224,192},{0,2... | collective-permute-start | bytes 393224 | tf_op jit(solution)/shard_map/ppermute | solution.py:347
  101.7 6.0 %collective-permute-start.18 = (f32[4,2,8,512]{3,2,1,0:T(8,128)S(1)}, f32[4,2,8,512]{3,2,1,0:T(8,128)S(1)}, u32[]{:S(2)}, u32[]{:S(2)}) collective-permute-start(f32[4,2,8,512]{3,2,1,0:T(8,128)S(1)} %add.55), channel_id=1, source_target_pairs={{0,32},{32,64},{64,96},{96,128},{128,160},{160,192},{192,224},{224... | collective-permute-start | bytes 393224 | tf_op jit(solution)/shard_map/ppermute | solution.py:342
  104.5 6.7 %collective-permute-start.24 = (f32[4,2,8,512]{3,2,1,0:T(8,128)S(1)}, f32[4,2,8,512]{3,2,1,0:T(8,128)S(1)}, u32[]{:S(2)}, u32[]{:S(2)}) collective-permute-start(f32[4,2,8,512]{3,2,1,0:T(8,128)S(1)} %add.61), channel_id=1, source_target_pairs={{0,32},{32,64},{64,96},{96,128},{128,160},{160,192},{192,224},{224... | collective-permute-start | bytes 393224 | tf_op jit(solution)/shard_map/ppermute | solution.py:342
  104.7 6.7 %collective-permute-start.28 = (f32[4,2,8,512]{3,2,1,0:T(8,128)S(1)}, f32[4,2,8,512]{3,2,1,0:T(8,128)S(1)}, u32[]{:S(2)}, u32[]{:S(2)}) collective-permute-start(f32[4,2,8,512]{3,2,1,0:T(8,128)S(1)} %add.65), channel_id=1, source_target_pairs={{32,0},{64,32},{96,64},{128,96},{160,128},{192,160},{224,192},{0,2... | collective-permute-start | bytes 393224 | tf_op jit(solution)/shard_map/ppermute | solution.py:347
  107.4 6.7 %collective-permute-start.22 = (f32[4,2,8,512]{3,2,1,0:T(8,128)S(1)}, f32[4,2,8,512]{3,2,1,0:T(8,128)S(1)}, u32[]{:S(2)}, u32[]{:S(2)}) collective-permute-start(f32[4,2,8,512]{3,2,1,0:T(8,128)S(1)} %add.59), channel_id=1, source_target_pairs={{32,0},{64,32},{96,64},{128,96},{160,128},{192,160},{224,192},{0,2... | collective-permute-start | bytes 393224 | tf_op jit(solution)/shard_map/ppermute | solution.py:347
  107.7 6.4 %collective-permute-start.19 = (f32[4,2,8,512]{3,2,1,0:T(8,128)S(1)}, f32[4,2,8,512]{3,2,1,0:T(8,128)S(1)}, u32[]{:S(2)}, u32[]{:S(2)}) collective-permute-start(f32[4,2,8,512]{3,2,1,0:T(8,128)S(1)} %add.56), channel_id=1, source_target_pairs={{0,32},{32,64},{64,96},{96,128},{128,160},{160,192},{192,224},{224... | collective-permute-start | bytes 393224 | tf_op jit(solution)/shard_map/ppermute | solution.py:342
  111.2 5.8 %collective-permute-start.25 = (f32[4,2,8,512]{3,2,1,0:T(8,128)S(1)}, f32[4,2,8,512]{3,2,1,0:T(8,128)S(1)}, u32[]{:S(2)}, u32[]{:S(2)}) collective-permute-start(f32[4,2,8,512]{3,2,1,0:T(8,128)S(1)} %add.62), channel_id=1, source_target_pairs={{0,32},{32,64},{64,96},{96,128},{128,160},{160,192},{192,224},{224... | collective-permute-start | bytes 393224 | tf_op jit(solution)/shard_map/ppermute | solution.py:342
  111.4 5.7 %collective-permute-start.29 = (f32[4,2,8,512]{3,2,1,0:T(8,128)S(1)}, f32[4,2,8,512]{3,2,1,0:T(8,128)S(1)}, u32[]{:S(2)}, u32[]{:S(2)}) collective-permute-start(f32[4,2,8,512]{3,2,1,0:T(8,128)S(1)} %add.66), channel_id=1, source_target_pairs={{32,0},{64,32},{96,64},{128,96},{160,128},{192,160},{224,192},{0,2... | collective-permute-start | bytes 393224 | tf_op jit(solution)/shard_map/ppermute | solution.py:347

commit v10 on v9

--- a/solution.py
+++ b/solution.py
@@ -90,6 +90,10 @@
 ALL = slice(None)
 
 
+def frame_index():
+    return lax.axis_index("y") * 2 + lax.axis_index("core")
+
+
 def base_kernel(base):
     block = SPAN // 8
     row = lax.broadcasted_iota(jnp.int32, (block, SPAN), 0)
@@ -108,9 +112,9 @@
     lax.fori_loop(0, 8, fill, 0)
 
 
-def object_kernel(place, forward, inverse, strip, mine, other, spec_re, spec_im):
+def object_kernel(forward, inverse, strip, mine, other, spec_re, spec_im):
     lane = lax.broadcasted_iota(jnp.int32, (SPAN // 2, 2 * HALO), 1)
-    first = ((place[2] >> 3) & 1) == 0
+    first = lax.axis_index("core") == 0
     before = jnp.where(first, mine[...], other[...])
     after = jnp.where(first, other[...], mine[...])
     top = jnp.where(lane < HALO, after, pltpu.roll(before, HALO, 1))
@@ -129,8 +133,8 @@
     spec_im[...] = imag * weight
 
 
-def cut_kernel(place, screens, first, second, sems):
-    at = pl.ds(pl.multiple_of(place[0] * 8, 8), 8)
+def cut_kernel(screens, first, second, sems):
+    at = pl.ds(pl.multiple_of(frame_index() * 8, 8), 8)
     copies = [
         pltpu.make_async_copy(screens.at[layer, at, :], target, sems.at[layer])
         for layer, target in enumerate((first, second))
@@ -141,9 +145,9 @@
         copy.wait()
 
 
-def select_kernel(place, table, *refs):
+def select_kernel(table, *refs):
     chunks, out, gathered = refs[:16], refs[16], refs[17]
-    slab, first = place[0], place[1]
+    slab, first = lax.axis_index("z"), lax.axis_index("x") * 64 + frame_index() * 8
     for step in range(8):
         source = (slab + step) & 7
         for layer in range(2):
@@ -175,9 +179,9 @@
     lax.fori_loop(0, 32, one, 0, unroll=8)
 
 
-def scatter_kernel(place, table, values, *refs):
+def scatter_kernel(table, values, *refs):
     pieces, out = refs[:16], refs[16]
-    slab, first = place[0], place[1]
+    slab, first = lax.axis_index("z"), lax.axis_index("x") * 64 + frame_index() * 8
     row_index = first + lax.broadcasted_iota(jnp.int32, (8, CORE), 0)
     lane = lax.broadcasted_iota(jnp.int32, (8, CORE), 1)
     out[...] = jnp.zeros_like(out)
@@ -218,20 +222,20 @@
     return 1.0 / (SPAN * SPAN * jnp.sum(amplitude * amplitude))
 
 
-def turns_of(place, table):
-    frame = place[2] >> 3
-    patch = place[0] * 4 + (place[1] >> 6)
+def turns_of(table):
+    frame = frame_index()
+    patch = lax.axis_index("z") * 4 + lax.axis_index("x")
     both = [table[frame, layer, patch] for layer in range(2)]
     return [((value >> 12) & 255, value & 255) for value in both]
 
 
 def far_kernel(
-    place, table, received, amp_ref, base, forward, inverse, pupil_re, pupil_im, far_re, far_im,
+    table, received, amp_ref, base, forward, inverse, pupil_re, pupil_im, far_re, far_im,
     spread_re, spread_im, mix_h, mix_l,
 ):
     build(forward, base, 1)
     build(inverse, base, -1)
-    turns = turns_of(place, table)
+    turns = turns_of(table)
     phases = None
     for layer in range(2):
         sheet = received[:, layer].reshape(CORE, CORE)
@@ -257,7 +261,7 @@
 
 
 def gradient_kernel(
-    place, table, amp_ref, observed, forward, inverse, pupil_re, pupil_im, far_re, far_im,
+    table, amp_ref, observed, forward, inverse, pupil_re, pupil_im, far_re, far_im,
     spread_re, spread_im, spec_re, spec_im, out, mix_h, mix_l, wide_h, wide_l,
 ):
     inverse_total = inverse_sum(amp_ref[...])
@@ -281,7 +285,7 @@
     out_re = right(back, forward, LOW)
     out_im = right(back, forward, HIGH)
     gradient = (2.0 * inverse_total) * (pupil_re[...] * out_im - pupil_im[...] * out_re)
-    turns = turns_of(place, table)
+    turns = turns_of(table)
     for layer in range(2):
         sheet = pltpu.roll(gradient, turns[layer][1], 1)
         sheet = pltpu.roll(sheet, turns[layer][0], 0)
@@ -310,7 +314,7 @@
     return pl.pallas_call(
         far_kernel,
         out_shape=[matrix] * 2 + [f32(CORE, CORE)] * 2 + [f32(SPAN, SPAN)] * 2 + [f32(SPAN, HALF)] * 2,
-        in_specs=[SMEM] * 2 + [VMEM] * 3,
+        in_specs=[SMEM] + [VMEM] * 3,
         out_specs=[VMEM] * 8,
         scratch_shapes=[pltpu.VMEM((2 * SPAN, HALF), jnp.bfloat16)] * 2,
         compiler_params=limit(28),
@@ -323,7 +327,7 @@
     return pl.pallas_call(
         gradient_kernel,
         out_shape=f32(32, 2, 8, CORE),
-        in_specs=[SMEM] * 2 + [VMEM] * 12,
+        in_specs=[SMEM] + [VMEM] * 12,
         out_specs=VMEM,
         scratch_shapes=[
             pltpu.VMEM((2 * SPAN, HALF), jnp.bfloat16),
@@ -376,32 +380,28 @@
 
 
 def body(screens, row_offsets, col_offsets, amplitude, object_strip, observed):
-    slab = lax.axis_index("z")
-    across = lax.axis_index("x")
-    frame_id = lax.axis_index(FRAME)
     patches = lax.axis_size("z") * lax.axis_size("x")
-    place = jnp.stack([slab, across * 64 + frame_id * 8, frame_id * 8]).astype(jnp.int32)
     table = row_offsets * SCOLS + col_offsets
     own = pl.pallas_call(
         cut_kernel,
         out_shape=[pltpu.VMEM((8, screens.shape[2]), jnp.float32)] * 2,
-        in_specs=[SMEM, ANY],
+        in_specs=[ANY],
         out_specs=[VMEM] * 2,
         scratch_shapes=[pltpu.SemaphoreType.DMA((2,))],
         compiler_params=limit(58),
         name="cut_rows",
-    )(jnp.reshape(frame_id, (1,)).astype(jnp.int32), screens)
+    )(screens)
     chunks = ring_gather(own)
     sent = pl.pallas_call(
         select_kernel,
         out_shape=f32(32, 2, 8, CORE),
-        in_specs=[SMEM] * 2 + [VMEM] * 16,
+        in_specs=[SMEM] + [VMEM] * 16,
         out_specs=VMEM,
         scratch_shapes=[pltpu.VMEM((16, 8, screens.shape[2]), jnp.float32)],
         compiler_params=limit(20),
         cost_estimate=cost(0, 3 * 10**6),
         name="select_rows",
-    )(place, table, *chunks)
+    )(table, *chunks)
     sent, strip = lax.optimization_barrier((sent, object_strip))
     received = lax.all_to_all(sent, SLAB, split_axis=0, concat_axis=0, tiled=True)
     ends = patches - 1
@@ -424,31 +424,31 @@
         cost_estimate=cost(10**6, 10**6),
         name="dft_base",
     )()
-    forward, inverse, *fields = far_call(place, table, received, amplitude, base)
+    forward, inverse, *fields = far_call(table, received, amplitude, base)
     spec_re, spec_im = pl.pallas_call(
         object_kernel,
         out_shape=[f32(SPAN, HALF)] * 2,
-        in_specs=[SMEM] + [VMEM] * 5,
+        in_specs=[VMEM] * 5,
         out_specs=[VMEM] * 2,
         compiler_params=limit(28),
         cost_estimate=cost(3 * 2 * 226 * 10**6, 7 * 10**6),
         name="object_spectrum",
-    )(place, forward, inverse, strip, mine, other)
+    )(forward, inverse, strip, mine, other)
     placed = gradient_call(
-        place, table, amplitude, observed, forward, inverse, *fields, spec_re, spec_im
+        table, amplitude, observed, forward, inverse, *fields, spec_re, spec_im
     )
     returned = lax.all_to_all(placed, SLAB, split_axis=0, concat_axis=0, tiled=True)
 
     partial = pl.pallas_call(
         scatter_kernel,
         out_shape=[f32(4, 2, 8, 512)] * 16,
-        in_specs=[SMEM] * 2 + [VMEM],
+        in_specs=[SMEM] + [VMEM],
         out_specs=[VMEM] * 16,
         scratch_shapes=[pltpu.VMEM((8, 8, 2, 8, 512), jnp.float32)],
         compiler_params=limit(20),
         cost_estimate=cost(0, 3 * 10**6),
         name="scatter_rows",
-    )(place, table, returned)
+    )(table, returned)
     summed = ring_scatter(partial)
     turned = lax.all_to_all(summed, FRAME, split_axis=0, concat_axis=0, tiled=True)
     return turned.transpose(1, 0, 2, 3).reshape(2, 64, 512)

time: 130 us -> 131 us (level)
  starting transfers between devices: 48 us -> 54.8 us
  waiting for transfers between devices: 30.1 us -> 23.4 us
    ppermute x14, waiting for transfers between devices: 19.4 us -> 10.3 us  [up(): lax.ppermute(values, 'z', [(i, (i + 1) % count) for i in range(count)])]
    ppermute x14, starting transfers between devices: 31.7 us -> 37.4 us  [down(): lax.ppermute(values, 'z', [((i + 1) % count, i) for i in range(count)])]
    ppermute x14, waiting for transfers between devices: 1.8 us -> 4.14 us  [down(): lax.ppermute(values, 'z', [((i + 1) % count, i) for i in range(count)])]
  transfers between devices with their start and end apart: 31 -> 31, of which waited for: 12 -> 13; matrix products, arithmetic and copies ran while one was open for 1% -> 1% of each run, Pallas kernels for 5% -> 5%
where the time goes in v10:
time: 131 us
  starting transfers between devices  54.8 us (42%)
  blocking collectives  29.2 us (22%)
  waiting for transfers between devices  23.4 us (18%)
  Pallas kernels  20.9 us (16%)
    ppermute x14, starting transfers between devices, down(): lax.ppermute(values, 'z', [((i + 1) % count, i) for i in range(count)])  37.4 us
    all_to_all x1, blocking collectives, body(): lax.all_to_all(placed, SLAB, split_axis=0, concat_axis=0, tiled=True)  16 us
    all_to_all x1, blocking collectives, body(): lax.all_to_all(summed, FRAME, split_axis=0, concat_axis=0, tiled=True)  13.3 us
    all_to_all x1, starting transfers between devices, body(): lax.all_to_all(sent, SLAB, split_axis=0, concat_axis=0, tiled=True)  11.1 us
    ppermute x14, waiting for transfers between devices, up(): lax.ppermute(values, 'z', [(i, (i + 1) % count) for i in range(count)])  10.3 us
    pallas_call x1, Pallas kernels, gradient_call(): pl.pallas_call(gradient_kernel, out_shape=f32(32, 2, 8, CORE), in_specs=[...  7.2 us
    ppermute x1, waiting for transfers between devices, body(): lax.ppermute(jnp.concatenate([edge[:half], edge[half:]], axis=1), ('z', '...  6.71 us
    pallas_call x1, Pallas kernels, far_call(): pl.pallas_call(far_kernel, out_shape=[matrix] * 2 + [f32(CORE, CORE)] * 2...  5.03 us
  transfers between devices with their start and end apart: 31, of which 13 were waited for; matrix products, arithmetic and copies ran while one was open for 1% of the time, Pallas kernels for 5%

profile of v10, /device:TPU:1, one launch (start us, length us, event | category | flops | bytes accessed | tf_op | source)
XLA Modules:
  0.0 130.6 jit_solution(10473015525621876940)
XLA Ops:
  0.0 1.0 cut_rows.1
  1.0 2.5 %collective-permute-start.6 = (f32[8,4096]{1,0:T(8,128)S(1)}, f32[8,4096]{1,0:T(8,128)S(1)}, u32[]{:S(2)}, u32[]{:S(2)}) collective-permute-start(f32[8,4096]{1,0:T(8,128)S(1)} %get-tuple-element.35.refs_0_), channel_id=1, source_target_pairs={{0,32},{32,64},{64,96},{96,128},{128,160},{160,192},{192,224},{224... | collective-permute-start | bytes 393224 | tf_op jit(solution)/shard_map/ppermute | solution.py:346
  3.5 4.0 %collective-permute-start.1 = (f32[8,4096]{1,0:T(8,128)S(1)}, f32[8,4096]{1,0:T(8,128)S(1)}, u32[]{:S(2)}, u32[]{:S(2)}) collective-permute-start(f32[8,4096]{1,0:T(8,128)S(1)} %get-tuple-element.36.refs_1_), channel_id=1, source_target_pairs={{32,0},{64,32},{96,64},{128,96},{160,128},{192,160},{224,192},{0,2... | collective-permute-start | bytes 393224 | tf_op jit(solution)/shard_map/ppermute | solution.py:351
  7.6 1.4 %collective-permute-start = (f32[8,4096]{1,0:T(8,128)S(1)}, f32[8,4096]{1,0:T(8,128)S(1)}, u32[]{:S(2)}, u32[]{:S(2)}) collective-permute-start(f32[8,4096]{1,0:T(8,128)S(1)} %get-tuple-element.35.refs_0_), channel_id=1, source_target_pairs={{32,0},{64,32},{96,64},{128,96},{160,128},{192,160},{224,192},{0,2... | collective-permute-start | bytes 393224 | tf_op jit(solution)/shard_map/ppermute | solution.py:351
  8.9 0.1 collective-permute-start.11
  9.0 1.6 %collective-permute-done.6.refs_14_ = f32[8,4096]{1,0:T(8,128)S(1)} collective-permute-done((f32[8,4096]{1,0:T(8,128)S(1)}, f32[8,4096]{1,0:T(8,128)S(1)}, u32[]{:S(2)}, u32[]{:S(2)}) %collective-permute-start.6) | collective-permute-done | bytes 131104 | tf_op jit(solution)/shard_map/ppermute | solution.py:346
  10.7 2.7 %collective-permute-start.3 = (f32[8,4096]{1,0:T(8,128)S(1)}, f32[8,4096]{1,0:T(8,128)S(1)}, u32[]{:S(2)}, u32[]{:S(2)}) collective-permute-start(f32[8,4096]{1,0:T(8,128)S(1)} %collective-permute-done.1.refs_3_), channel_id=1, source_target_pairs={{32,0},{64,32},{96,64},{128,96},{160,128},{192,160},{224,192},{0,2... | collective-permute-start | bytes 393224 | tf_op jit(solution)/shard_map/ppermute | solution.py:351
  13.4 2.6 %collective-permute-start.2 = (f32[8,4096]{1,0:T(8,128)S(1)}, f32[8,4096]{1,0:T(8,128)S(1)}, u32[]{:S(2)}, u32[]{:S(2)}) collective-permute-start(f32[8,4096]{1,0:T(8,128)S(1)} %collective-permute-done.refs_2_), channel_id=1, source_target_pairs={{32,0},{64,32},{96,64},{128,96},{160,128},{192,160},{224,192},{0,2... | collective-permute-start | bytes 393224 | tf_op jit(solution)/shard_map/ppermute | solution.py:351
  16.0 1.2 collective-permute-done.7.refs_12_
  17.2 2.7 %collective-permute-start.5 = (f32[8,4096]{1,0:T(8,128)S(1)}, f32[8,4096]{1,0:T(8,128)S(1)}, u32[]{:S(2)}, u32[]{:S(2)}) collective-permute-start(f32[8,4096]{1,0:T(8,128)S(1)} %collective-permute-done.3.refs_5_), channel_id=1, source_target_pairs={{32,0},{64,32},{96,64},{128,96},{160,128},{192,160},{224,192},{0,2... | collective-permute-start | bytes 393224 | tf_op jit(solution)/shard_map/ppermute | solution.py:351
  19.8 2.5 %collective-permute-start.4 = (f32[8,4096]{1,0:T(8,128)S(1)}, f32[8,4096]{1,0:T(8,128)S(1)}, u32[]{:S(2)}, u32[]{:S(2)}) collective-permute-start(f32[8,4096]{1,0:T(8,128)S(1)} %collective-permute-done.2.refs_4_), channel_id=1, source_target_pairs={{32,0},{64,32},{96,64},{128,96},{160,128},{192,160},{224,192},{0,2... | collective-permute-start | bytes 393224 | tf_op jit(solution)/shard_map/ppermute | solution.py:351
  22.4 0.8 collective-permute-done.8.refs_10_
  23.2 2.7 %collective-permute-start.10 = (f32[8,4096]{1,0:T(8,128)S(1)}, f32[8,4096]{1,0:T(8,128)S(1)}, u32[]{:S(2)}, u32[]{:S(2)}) collective-permute-start(f32[8,4096]{1,0:T(8,128)S(1)} %collective-permute-done.5.refs_7_), channel_id=1, source_target_pairs={{32,0},{64,32},{96,64},{128,96},{160,128},{192,160},{224,192},{0,2... | collective-permute-start | bytes 393224 | tf_op jit(solution)/shard_map/ppermute | solution.py:351
  25.9 0.7 multiply_add_fusion.table
  26.6 0.8 collective-permute-done.13.refs_11_
  27.4 1.4 %collective-permute-done.9.refs_8_ = f32[8,4096]{1,0:T(8,128)S(1)} collective-permute-done((f32[8,4096]{1,0:T(8,128)S(1)}, f32[8,4096]{1,0:T(8,128)S(1)}, u32[]{:S(2)}, u32[]{:S(2)}) %collective-permute-start.9) | collective-permute-done | bytes 131104 | tf_op jit(solution)/shard_map/ppermute | solution.py:346
  28.8 2.3 %select_rows.1 = f32[32,2,8,256]{3,2,1,0:T(8,128)} custom-call(s32[8,2,32]{2,1,0:T(2,128)S(1)} %multiply_add_fusion.table, f32[8,4096]{1,0:T(8,128)S(1)} %get-tuple-element.35.refs_0_, f32[8,4096]{1,0:T(8,128)S(1)} %get-tuple-element.36.refs_1_, f32[8,4096]{1,0:T(8,128)S(1)} %collective-permute-done.refs_2_, f32[8,4096]{1,0:T(8,128)S(1)} %collective-permute-done.1.refs_3_, ...), custom_call_target="tpu_custom_call" | custom-call | bytes 3000000 | tf_op jit(solution)/shard_map/select_rows/pallas_call | solution.py:395
  31.1 11.1 %all-to-all-start = ((f32[32,2,8,256]{3,2,1,0:T(8,128)}), f32[32,2,8,256]{3,2,1,0:T(8,128)S(1)}, u32[]{:S(2)}, u32[]{:S(2)}) async-start(f32[32,2,8,256]{3,2,1,0:T(8,128)} %select_rows.1), calls=%async_computation | async-start | bytes 1048576 | tf_op jit(solution)/shard_map/all_to_all | solution.py:406
  42.2 0.1 slice_select_fusion
  42.4 0.1 pad_maximum_fusion.1
  42.5 1.3 collective-permute-start.14
  43.8 1.1 dft_base.1.base
  44.9 6.7 %collective-permute-done.14.mine = f32[192,128]{1,0:T(8,128)S(1)} collective-permute-done((f32[192,128]{1,0:T(8,128)S(1)}, f32[192,128]{1,0:T(8,128)S(1)}, u32[]{:S(2)}, u32[]{:S(2)}) %collective-permute-start.14) | collective-permute-done | bytes 98336 | tf_op jit(solution)/shard_map/ppermute | solution.py:412
  51.6 2.2 %all-to-all-done.received = f32[32,2,8,256]{3,2,1,0:T(8,128)S(1)} async-done(((f32[32,2,8,256]{3,2,1,0:T(8,128)}), f32[32,2,8,256]{3,2,1,0:T(8,128)S(1)}, u32[]{:S(2)}, u32[]{:S(2)}) %all-to-all-start) | async-done | bytes 524320 | tf_op jit(solution)/shard_map/all_to_all | solution.py:406
  53.8 5.0 %far_field.1 = (bf16[4,384,768]{2,1,0:T(8,128)(2,1)S(1)}, bf16[4,384,768]{2,1,0:T(8,128)(2,1)S(1)}, f32[256,256]{1,0:T(8,128)S(1)}, f32[256,256]{1,0:T(8,128)S(1...) custom-call(s32[8,2,32]{2,1,0:T(2,128)S(1)} %multiply_add_fusion.table, ...), custom_call_target="tpu_custom_call" | custom-call | flops 3000000000 | bytes 7000000 | tf_op jit(solution)/shard_map/far_field/pallas_call | solution.py:314
  58.9 2.2 %object_spectrum.1 = (f32[384,256]{1,0:T(8,128)S(1)}, f32[384,256]{1,0:T(8,128)S(1)}) custom-call(bf16[4,384,768]{2,1,0:T(8,128)(2,1)S(1)} %get-tuple-element.38.forward, bf16[4,384,768]{2,1,0:T(8,128)(2,1)S(1)} %get-tuple-element.39.inverse, f32[384,256]{1,0:T(8,128)S(1)} %copy-done, f32[192,128]{1,0:T(8,128)S(1)} %collective-permute-done.14.mine, ...), custom_call_target="tpu_custom_call" | custom-call | flops 1356000000 | bytes 7000000 | tf_op jit(solution)/shard_map/object_spectrum/pallas_call | solution.py:428
  61.0 7.2 %gradient.1 = f32[32,2,8,256]{3,2,1,0:T(8,128)S(1)} custom-call(s32[8,2,32]{2,1,0:T(2,128)S(1)} %multiply_add_fusion.table, f32[256,256]{1,0:T(8,128)S(1)} %copy-done.1, f32[1,256,256]{2,1,0:T(8,128)S(1)} %copy-done.2, bf16[4,384,768]{2,1,0:T(8,128)(2,1)S(1)} %get-tuple-element.38.forward, bf16[4,384,768]{2,1,0:T(8,128)(2,1)S(1)} %get-tuple-element.39.inverse, ...), custom_call_target="tpu_custom_call" | custom-call | flops 4332000256 | bytes 7000000 | tf_op jit(solution)/shard_map/gradient/pallas_call | solution.py:327
  68.2 16.0 %all_to_all.15.values = f32[32,2,8,256]{3,2,1,0:T(8,128)S(1)} all-to-all(f32[32,2,8,256]{3,2,1,0:T(8,128)S(1)} %gradient.1), channel_id=1, replica_groups=mesh['z'=8,'x'=4,'y'=4,'core'=2] {'x','y','core'}, dimensions={0} | all-to-all | bytes 1048576 | tf_op jit(solution)/shard_map/all_to_all | solution.py:440
  84.2 2.2 %scatter_rows.1 = (f32[4,2,8,512]{3,2,1,0:T(8,128)S(1)}, f32[4,2,8,512]{3,2,1,0:T(8,128)S(1)}, f32[4,2,8,512]{3,2,1,0:T(8,128)S(1)}, f32[4,2,8,512]{3,2,1,0:T(8,...) custom-call(s32[8,2,32]{2,1,0:T(2,128)S(1)} %multiply_add_fusion.tab, ...), custom_call_target="tpu_custom_call" | custom-call | bytes 3000000 | tf_op jit(solution)/shard_map/scatter_rows/pallas_call | solution.py:442
  86.4 3.1 %collective-permute-start.26 = (f32[4,2,8,512]{3,2,1,0:T(8,128)S(1)}, f32[4,2,8,512]{3,2,1,0:T(8,128)S(1)}, u32[]{:S(2)}, u32[]{:S(2)}) collective-permute-start(f32[4,2,8,512]{3,2,1,0:T(8,128)S(1)} %get-tuple-element.61), channel_id=1, source_target_pairs={{32,0},{64,32},{96,64},{128,96},{160,128},{192,160},{224,192},{0,2... | collective-permute-start | bytes 393224 | tf_op jit(solution)/shard_map/ppermute | solution.py:351
  89.5 0.6 collective-permute-start.23
  90.1 2.5 %collective-permute-done.26 = f32[4,2,8,512]{3,2,1,0:T(8,128)S(1)} collective-permute-done((f32[4,2,8,512]{3,2,1,0:T(8,128)S(1)}, f32[4,2,8,512]{3,2,1,0:T(8,128)S(1)}, u32[]{:S(2)}, u32[]{:S(2)}) %collective-permute-start.26) | collective-permute-done | bytes 131104 | tf_op jit(solution)/shard_map/ppermute | solution.py:351
  92.6 3.5 %collective-permute-start.27 = (f32[4,2,8,512]{3,2,1,0:T(8,128)S(1)}, f32[4,2,8,512]{3,2,1,0:T(8,128)S(1)}, u32[]{:S(2)}, u32[]{:S(2)}) collective-permute-start(f32[4,2,8,512]{3,2,1,0:T(8,128)S(1)} %add.56), channel_id=1, source_target_pairs={{32,0},{64,32},{96,64},{128,96},{160,128},{192,160},{224,192},{0,2... | collective-permute-start | bytes 393224 | tf_op jit(solution)/shard_map/ppermute | solution.py:351
  96.1 0.1 collective-permute-start.20
  96.2 1.5 %collective-permute-start.17 = (f32[4,2,8,512]{3,2,1,0:T(8,128)S(1)}, f32[4,2,8,512]{3,2,1,0:T(8,128)S(1)}, u32[]{:S(2)}, u32[]{:S(2)}) collective-permute-start(f32[4,2,8,512]{3,2,1,0:T(8,128)S(1)} %add.46), channel_id=1, source_target_pairs={{0,32},{32,64},{64,96},{96,128},{128,160},{160,192},{192,224},{224... | collective-permute-start | bytes 393224 | tf_op jit(solution)/shard_map/ppermute | solution.py:346
  97.7 0.9 collective-permute-done.23
  98.6 0.1 collective-permute-start.24
  98.7 3.2 %collective-permute-start.28 = (f32[4,2,8,512]{3,2,1,0:T(8,128)S(1)}, f32[4,2,8,512]{3,2,1,0:T(8,128)S(1)}, u32[]{:S(2)}, u32[]{:S(2)}) collective-permute-start(f32[4,2,8,512]{3,2,1,0:T(8,128)S(1)} %add.57), channel_id=1, source_target_pairs={{32,0},{64,32},{96,64},{128,96},{160,128},{192,160},{224,192},{0,2... | collective-permute-start | bytes 393224 | tf_op jit(solution)/shard_map/ppermute | solution.py:351
  101.9 2.8 %collective-permute-start.21 = (f32[4,2,8,512]{3,2,1,0:T(8,128)S(1)}, f32[4,2,8,512]{3,2,1,0:T(8,128)S(1)}, u32[]{:S(2)}, u32[]{:S(2)}) collective-permute-start(f32[4,2,8,512]{3,2,1,0:T(8,128)S(1)} %add.50), channel_id=1, source_target_pairs={{32,0},{64,32},{96,64},{128,96},{160,128},{192,160},{224,192},{0,2... | collective-permute-start | bytes 393224 | tf_op jit(solution)/shard_map/ppermute | solution.py:351
  104.8 0.2 collective-permute-done.24
  105.0 0.1 collective-permute-start.25
  105.1 2.7 %collective-permute-start.29 = (f32[4,2,8,512]{3,2,1,0:T(8,128)S(1)}, f32[4,2,8,512]{3,2,1,0:T(8,128)S(1)}, u32[]{:S(2)}, u32[]{:S(2)}) collective-permute-start(f32[4,2,8,512]{3,2,1,0:T(8,128)S(1)} %add.58), channel_id=1, source_target_pairs={{32,0},{64,32},{96,64},{128,96},{160,128},{192,160},{224,192},{0,2... | collective-permute-start | bytes 393224 | tf_op jit(solution)/shard_map/ppermute | solution.py:351
  107.9 3.5 %collective-permute-start.22 = (f32[4,2,8,512]{3,2,1,0:T(8,128)S(1)}, f32[4,2,8,512]{3,2,1,0:T(8,128)S(1)}, u32[]{:S(2)}, u32[]{:S(2)}) collective-permute-start(f32[4,2,8,512]{3,2,1,0:T(8,128)S(1)} %add.51), channel_id=1, source_target_pairs={{32,0},{64,32},{96,64},{128,96},{160,128},{192,160},{224,192},{0,2... | collective-permute-start | bytes 393224 | tf_op jit(solution)/shard_map/ppermute | solution.py:351
  111.5 0.6 collective-permute-done.25
  112.2 1.5 %collective-permute-done.22 = f32[4,2,8,512]{3,2,1,0:T(8,128)S(1)} collective-permute-done((f32[4,2,8,512]{3,2,1,0:T(8,128)S(1)}, f32[4,2,8,512]{3,2,1,0:T(8,128)S(1)}, u32[]{:S(2)}, u32[]{:S(2)}) %collective-permute-start.22) | collective-permute-done | bytes 131104 | tf_op jit(solution)/shard_map/ppermute | solution.py:351
  113.8 2.8 %collective-permute-done.19 = f32[4,2,8,512]{3,2,1,0:T(8,128)S(1)} collective-permute-done((f32[4,2,8,512]{3,2,1,0:T(8,128)S(1)}, f32[4,2,8,512]{3,2,1,0:T(8,128)S(1)}, u32[]{:S(2)}, u32[]{:S(2)}) %collective-permute-start.19) | collective-permute-done | bytes 131104 | tf_op jit(solution)/shard_map/ppermute | solution.py:346
  116.6 13.3 %all_to_all.16 = f32[8,2,8,512]{3,2,1,0:T(8,128)S(1)} all-to-all(f32[8,2,8,512]{3,2,1,0:T(8,128)S(1)} %pad_maximum_fusion), channel_id=1, replica_groups=mesh['z'=8,'x'=4,'y'=4,'core'=2] {'y','core'}, dimensions={0} | all-to-all | bytes 524288 | tf_op jit(solution)/shard_map/all_to_all | solution.py:453
  129.9 0.7 copy_bitcast_fusion
  (47 shorter events, 0.6 us)
Async XLA Ops:
  1.0 41.2 %copy-start = (f32[384,256]{1,0:T(8,128)S(1)}, f32[384,256]{1,0:T(8,128)}, u32[]{:S(2)}) copy-start(f32[384,256]{1,0:T(8,128)} %strip) | copy-start | bytes 1179652
  1.0 9.7 %collective-permute-start.6 = (f32[8,4096]{1,0:T(8,128)S(1)}, f32[8,4096]{1,0:T(8,128)S(1)}, u32[]{:S(2)}, u32[]{:S(2)}) collective-permute-start(f32[8,4096]{1,0:T(8,128)S(1)} %get-tuple-element.35.refs_0_), channel_id=1, source_target_pairs={{0,32},{32,64},{64,96},{96,128},{128,160},{160,192},{192,224},{224... | collective-permute-start | bytes 393224 | tf_op jit(solution)/shard_map/ppermute | solution.py:346
  3.5 7.1 %collective-permute-start.1 = (f32[8,4096]{1,0:T(8,128)S(1)}, f32[8,4096]{1,0:T(8,128)S(1)}, u32[]{:S(2)}, u32[]{:S(2)}) collective-permute-start(f32[8,4096]{1,0:T(8,128)S(1)} %get-tuple-element.36.refs_1_), channel_id=1, source_target_pairs={{32,0},{64,32},{96,64},{128,96},{160,128},{192,160},{224,192},{0,2... | collective-permute-start | bytes 393224 | tf_op jit(solution)/shard_map/ppermute | solution.py:351
  7.6 5.8 %collective-permute-start = (f32[8,4096]{1,0:T(8,128)S(1)}, f32[8,4096]{1,0:T(8,128)S(1)}, u32[]{:S(2)}, u32[]{:S(2)}) collective-permute-start(f32[8,4096]{1,0:T(8,128)S(1)} %get-tuple-element.35.refs_0_), channel_id=1, source_target_pairs={{32,0},{64,32},{96,64},{128,96},{160,128},{192,160},{224,192},{0,2... | collective-permute-start | bytes 393224 | tf_op jit(solution)/shard_map/ppermute | solution.py:351
  8.9 7.0 %collective-permute-start.11 = (f32[8,4096]{1,0:T(8,128)S(1)}, f32[8,4096]{1,0:T(8,128)S(1)}, u32[]{:S(2)}, u32[]{:S(2)}) collective-permute-start(f32[8,4096]{1,0:T(8,128)S(1)} %get-tuple-element.36.refs_1_), channel_id=1, source_target_pairs={{0,32},{32,64},{64,96},{96,128},{128,160},{160,192},{192,224},{224... | collective-permute-start | bytes 393224 | tf_op jit(solution)/shard_map/ppermute | solution.py:346
  10.7 6.5 %collective-permute-start.7 = (f32[8,4096]{1,0:T(8,128)S(1)}, f32[8,4096]{1,0:T(8,128)S(1)}, u32[]{:S(2)}, u32[]{:S(2)}) collective-permute-start(f32[8,4096]{1,0:T(8,128)S(1)} %collective-permute-done.6.refs_14_), channel_id=1, source_target_pairs={{0,32},{32,64},{64,96},{96,128},{128,160},{160,192},{192,224},{224... | collective-permute-start | bytes 393224 | tf_op jit(solution)/shard_map/ppermute | solution.py:346
  10.7 6.5 %collective-permute-start.3 = (f32[8,4096]{1,0:T(8,128)S(1)}, f32[8,4096]{1,0:T(8,128)S(1)}, u32[]{:S(2)}, u32[]{:S(2)}) collective-permute-start(f32[8,4096]{1,0:T(8,128)S(1)} %collective-permute-done.1.refs_3_), channel_id=1, source_target_pairs={{32,0},{64,32},{96,64},{128,96},{160,128},{192,160},{224,192},{0,2... | collective-permute-start | bytes 393224 | tf_op jit(solution)/shard_map/ppermute | solution.py:351
  13.4 6.5 %collective-permute-start.2 = (f32[8,4096]{1,0:T(8,128)S(1)}, f32[8,4096]{1,0:T(8,128)S(1)}, u32[]{:S(2)}, u32[]{:S(2)}) collective-permute-start(f32[8,4096]{1,0:T(8,128)S(1)} %collective-permute-done.refs_2_), channel_id=1, source_target_pairs={{32,0},{64,32},{96,64},{128,96},{160,128},{192,160},{224,192},{0,2... | collective-permute-start | bytes 393224 | tf_op jit(solution)/shard_map/ppermute | solution.py:351
  16.0 6.4 %collective-permute-start.12 = (f32[8,4096]{1,0:T(8,128)S(1)}, f32[8,4096]{1,0:T(8,128)S(1)}, u32[]{:S(2)}, u32[]{:S(2)}) collective-permute-start(f32[8,4096]{1,0:T(8,128)S(1)} %collective-permute-done.11.refs_15_), channel_id=1, source_target_pairs={{0,32},{32,64},{64,96},{96,128},{128,160},{160,192},{192,224},{224... | collective-permute-start | bytes 393224 | tf_op jit(solution)/shard_map/ppermute | solution.py:346
  17.2 6.0 %collective-permute-start.8 = (f32[8,4096]{1,0:T(8,128)S(1)}, f32[8,4096]{1,0:T(8,128)S(1)}, u32[]{:S(2)}, u32[]{:S(2)}) collective-permute-start(f32[8,4096]{1,0:T(8,128)S(1)} %collective-permute-done.7.refs_12_), channel_id=1, source_target_pairs={{0,32},{32,64},{64,96},{96,128},{128,160},{160,192},{192,224},{224... | collective-permute-start | bytes 393224 | tf_op jit(solution)/shard_map/ppermute | solution.py:346
  17.2 6.0 %collective-permute-start.5 = (f32[8,4096]{1,0:T(8,128)S(1)}, f32[8,4096]{1,0:T(8,128)S(1)}, u32[]{:S(2)}, u32[]{:S(2)}) collective-permute-start(f32[8,4096]{1,0:T(8,128)S(1)} %collective-permute-done.3.refs_5_), channel_id=1, source_target_pairs={{32,0},{64,32},{96,64},{128,96},{160,128},{192,160},{224,192},{0,2... | collective-permute-start | bytes 393224 | tf_op jit(solution)/shard_map/ppermute | solution.py:351
  19.8 6.8 %collective-permute-start.4 = (f32[8,4096]{1,0:T(8,128)S(1)}, f32[8,4096]{1,0:T(8,128)S(1)}, u32[]{:S(2)}, u32[]{:S(2)}) collective-permute-start(f32[8,4096]{1,0:T(8,128)S(1)} %collective-permute-done.2.refs_4_), channel_id=1, source_target_pairs={{32,0},{64,32},{96,64},{128,96},{160,128},{192,160},{224,192},{0,2... | collective-permute-start | bytes 393224 | tf_op jit(solution)/shard_map/ppermute | solution.py:351
  22.4 5.0 %collective-permute-start.13 = (f32[8,4096]{1,0:T(8,128)S(1)}, f32[8,4096]{1,0:T(8,128)S(1)}, u32[]{:S(2)}, u32[]{:S(2)}) collective-permute-start(f32[8,4096]{1,0:T(8,128)S(1)} %collective-permute-done.12.refs_13_), channel_id=1, source_target_pairs={{0,32},{32,64},{64,96},{96,128},{128,160},{160,192},{192,224},{224... | collective-permute-start | bytes 393224 | tf_op jit(solution)/shard_map/ppermute | solution.py:346
  23.2 5.6 %collective-permute-start.9 = (f32[8,4096]{1,0:T(8,128)S(1)}, f32[8,4096]{1,0:T(8,128)S(1)}, u32[]{:S(2)}, u32[]{:S(2)}) collective-permute-start(f32[8,4096]{1,0:T(8,128)S(1)} %collective-permute-done.8.refs_10_), channel_id=1, source_target_pairs={{0,32},{32,64},{64,96},{96,128},{128,160},{160,192},{192,224},{224... | collective-permute-start | bytes 393224 | tf_op jit(solution)/shard_map/ppermute | solution.py:346
  23.2 5.6 %collective-permute-start.10 = (f32[8,4096]{1,0:T(8,128)S(1)}, f32[8,4096]{1,0:T(8,128)S(1)}, u32[]{:S(2)}, u32[]{:S(2)}) collective-permute-start(f32[8,4096]{1,0:T(8,128)S(1)} %collective-permute-done.5.refs_7_), channel_id=1, source_target_pairs={{32,0},{64,32},{96,64},{128,96},{160,128},{192,160},{224,192},{0,2... | collective-permute-start | bytes 393224 | tf_op jit(solution)/shard_map/ppermute | solution.py:351
  31.1 22.7 %copy-start.1 = (f32[256,256]{1,0:T(8,128)S(1)}, f32[256,256]{1,0:T(8,128)}, u32[]{:S(2)}) copy-start(f32[256,256]{1,0:T(8,128)} %amp_ref.3) | copy-start | bytes 786436
  31.1 22.7 %all-to-all-start = ((f32[32,2,8,256]{3,2,1,0:T(8,128)}), f32[32,2,8,256]{3,2,1,0:T(8,128)S(1)}, u32[]{:S(2)}, u32[]{:S(2)}) async-start(f32[32,2,8,256]{3,2,1,0:T(8,128)} %select_rows.1), calls=%async_computation | async-start | bytes 1048576 | tf_op jit(solution)/shard_map/all_to_all | solution.py:406
  42.5 9.1 %collective-permute-start.14 = (f32[192,128]{1,0:T(8,128)S(1)}, f32[192,128]{1,0:T(8,128)S(1)}, u32[]{:S(2)}, u32[]{:S(2)}) collective-permute-start(f32[192,128]{1,0:T(8,128)S(1)} %pad_maximum_fusion.1), channel_id=1, source_target_pairs={{0,8},{8,16},{16,24},{24,32},{32,40},{40,48},{48,56},{56,64},{64,7... | collective-permute-start | bytes 294920 | tf_op jit(solution)/shard_map/ppermute | solution.py:412
  51.6 7.3 %collective-permute-start.15 = (f32[192,128]{1,0:T(8,128)S(1)}, f32[192,128]{1,0:T(8,128)S(1)}, u32[]{:S(2)}, u32[]{:S(2)}) collective-permute-start(f32[192,128]{1,0:T(8,128)S(1)} %collective-permute-done.14.mine), channel_id=1, source_target_pairs={{0,1},{1,0},{2,3},{3,2},{4,5},{5,4},{6,7},{7,6},{8,9},{9,8},{10,11... | collective-permute-start | bytes 294920 | tf_op jit(solution)/shard_map/ppermute | solution.py:418
  58.8 2.2 %copy-start.2 = (f32[1,256,256]{2,1,0:T(8,128)S(1)}, f32[1,256,256]{2,1,0:T(8,128)}, u32[]{:S(2)}) copy-start(f32[1,256,256]{2,1,0:T(8,128)} %observed.1) | copy-start | bytes 786436
  86.4 6.2 %collective-permute-start.26 = (f32[4,2,8,512]{3,2,1,0:T(8,128)S(1)}, f32[4,2,8,512]{3,2,1,0:T(8,128)S(1)}, u32[]{:S(2)}, u32[]{:S(2)}) collective-permute-start(f32[4,2,8,512]{3,2,1,0:T(8,128)S(1)} %get-tuple-element.61), channel_id=1, source_target_pairs={{32,0},{64,32},{96,64},{128,96},{160,128},{192,160},{224,192},{0,2... | collective-permute-start | bytes 393224 | tf_op jit(solution)/shard_map/ppermute | solution.py:351
  89.5 6.7 %collective-permute-start.16 = (f32[4,2,8,512]{3,2,1,0:T(8,128)S(1)}, f32[4,2,8,512]{3,2,1,0:T(8,128)S(1)}, u32[]{:S(2)}, u32[]{:S(2)}) collective-permute-start(f32[4,2,8,512]{3,2,1,0:T(8,128)S(1)} %get-tuple-element.50), channel_id=1, source_target_pairs={{0,32},{32,64},{64,96},{96,128},{128,160},{160,192},{192,224},{224... | collective-permute-start | bytes 393224 | tf_op jit(solution)/shard_map/ppermute | solution.py:346
  89.5 9.1 %collective-permute-start.23 = (f32[4,2,8,512]{3,2,1,0:T(8,128)S(1)}, f32[4,2,8,512]{3,2,1,0:T(8,128)S(1)}, u32[]{:S(2)}, u32[]{:S(2)}) collective-permute-start(f32[4,2,8,512]{3,2,1,0:T(8,128)S(1)} %get-tuple-element.58), channel_id=1, source_target_pairs={{0,32},{32,64},{64,96},{96,128},{128,160},{160,192},{192,224},{224... | collective-permute-start | bytes 393224 | tf_op jit(solution)/shard_map/ppermute | solution.py:346
  92.6 6.0 %collective-permute-start.27 = (f32[4,2,8,512]{3,2,1,0:T(8,128)S(1)}, f32[4,2,8,512]{3,2,1,0:T(8,128)S(1)}, u32[]{:S(2)}, u32[]{:S(2)}) collective-permute-start(f32[4,2,8,512]{3,2,1,0:T(8,128)S(1)} %add.56), channel_id=1, source_target_pairs={{32,0},{64,32},{96,64},{128,96},{160,128},{192,160},{224,192},{0,2... | collective-permute-start | bytes 393224 | tf_op jit(solution)/shard_map/ppermute | solution.py:351
  96.1 5.8 %collective-permute-start.20 = (f32[4,2,8,512]{3,2,1,0:T(8,128)S(1)}, f32[4,2,8,512]{3,2,1,0:T(8,128)S(1)}, u32[]{:S(2)}, u32[]{:S(2)}) collective-permute-start(f32[4,2,8,512]{3,2,1,0:T(8,128)S(1)} %get-tuple-element.54), channel_id=1, source_target_pairs={{32,0},{64,32},{96,64},{128,96},{160,128},{192,160},{224,192},{0,2... | collective-permute-start | bytes 393224 | tf_op jit(solution)/shard_map/ppermute | solution.py:351
  96.2 8.5 %collective-permute-start.17 = (f32[4,2,8,512]{3,2,1,0:T(8,128)S(1)}, f32[4,2,8,512]{3,2,1,0:T(8,128)S(1)}, u32[]{:S(2)}, u32[]{:S(2)}) collective-permute-start(f32[4,2,8,512]{3,2,1,0:T(8,128)S(1)} %add.46), channel_id=1, source_target_pairs={{0,32},{32,64},{64,96},{96,128},{128,160},{160,192},{192,224},{224... | collective-permute-start | bytes 393224 | tf_op jit(solution)/shard_map/ppermute | solution.py:346
  98.6 6.4 %collective-permute-start.24 = (f32[4,2,8,512]{3,2,1,0:T(8,128)S(1)}, f32[4,2,8,512]{3,2,1,0:T(8,128)S(1)}, u32[]{:S(2)}, u32[]{:S(2)}) collective-permute-start(f32[4,2,8,512]{3,2,1,0:T(8,128)S(1)} %add.53), channel_id=1, source_target_pairs={{0,32},{32,64},{64,96},{96,128},{128,160},{160,192},{192,224},{224... | collective-permute-start | bytes 393224 | tf_op jit(solution)/shard_map/ppermute | solution.py:346
  98.7 6.4 %collective-permute-start.28 = (f32[4,2,8,512]{3,2,1,0:T(8,128)S(1)}, f32[4,2,8,512]{3,2,1,0:T(8,128)S(1)}, u32[]{:S(2)}, u32[]{:S(2)}) collective-permute-start(f32[4,2,8,512]{3,2,1,0:T(8,128)S(1)} %add.57), channel_id=1, source_target_pairs={{32,0},{64,32},{96,64},{128,96},{160,128},{192,160},{224,192},{0,2... | collective-permute-start | bytes 393224 | tf_op jit(solution)/shard_map/ppermute | solution.py:351
  101.9 6.0 %collective-permute-start.21 = (f32[4,2,8,512]{3,2,1,0:T(8,128)S(1)}, f32[4,2,8,512]{3,2,1,0:T(8,128)S(1)}, u32[]{:S(2)}, u32[]{:S(2)}) collective-permute-start(f32[4,2,8,512]{3,2,1,0:T(8,128)S(1)} %add.50), channel_id=1, source_target_pairs={{32,0},{64,32},{96,64},{128,96},{160,128},{192,160},{224,192},{0,2... | collective-permute-start | bytes 393224 | tf_op jit(solution)/shard_map/ppermute | solution.py:351
  104.7 6.7 %collective-permute-start.18 = (f32[4,2,8,512]{3,2,1,0:T(8,128)S(1)}, f32[4,2,8,512]{3,2,1,0:T(8,128)S(1)}, u32[]{:S(2)}, u32[]{:S(2)}) collective-permute-start(f32[4,2,8,512]{3,2,1,0:T(8,128)S(1)} %add.47), channel_id=1, source_target_pairs={{0,32},{32,64},{64,96},{96,128},{128,160},{160,192},{192,224},{224... | collective-permute-start | bytes 393224 | tf_op jit(solution)/shard_map/ppermute | solution.py:346
  105.0 7.2 %collective-permute-start.25 = (f32[4,2,8,512]{3,2,1,0:T(8,128)S(1)}, f32[4,2,8,512]{3,2,1,0:T(8,128)S(1)}, u32[]{:S(2)}, u32[]{:S(2)}) collective-permute-start(f32[4,2,8,512]{3,2,1,0:T(8,128)S(1)} %add.54), channel_id=1, source_target_pairs={{0,32},{32,64},{64,96},{96,128},{128,160},{160,192},{192,224},{224... | collective-permute-start | bytes 393224 | tf_op jit(solution)/shard_map/ppermute | solution.py:346
  105.1 7.0 %collective-permute-start.29 = (f32[4,2,8,512]{3,2,1,0:T(8,128)S(1)}, f32[4,2,8,512]{3,2,1,0:T(8,128)S(1)}, u32[]{:S(2)}, u32[]{:S(2)}) collective-permute-start(f32[4,2,8,512]{3,2,1,0:T(8,128)S(1)} %add.58), channel_id=1, source_target_pairs={{32,0},{64,32},{96,64},{128,96},{160,128},{192,160},{224,192},{0,2... | collective-permute-start | bytes 393224 | tf_op jit(solution)/shard_map/ppermute | solution.py:351
  107.9 5.8 %collective-permute-start.22 = (f32[4,2,8,512]{3,2,1,0:T(8,128)S(1)}, f32[4,2,8,512]{3,2,1,0:T(8,128)S(1)}, u32[]{:S(2)}, u32[]{:S(2)}) collective-permute-start(f32[4,2,8,512]{3,2,1,0:T(8,128)S(1)} %add.51), channel_id=1, source_target_pairs={{32,0},{64,32},{96,64},{128,96},{160,128},{192,160},{224,192},{0,2... | collective-permute-start | bytes 393224 | tf_op jit(solution)/shard_map/ppermute | solution.py:351
  111.4 5.1 %collective-permute-start.19 = (f32[4,2,8,512]{3,2,1,0:T(8,128)S(1)}, f32[4,2,8,512]{3,2,1,0:T(8,128)S(1)}, u32[]{:S(2)}, u32[]{:S(2)}) collective-permute-start(f32[4,2,8,512]{3,2,1,0:T(8,128)S(1)} %add.48), channel_id=1, source_target_pairs={{0,32},{32,64},{64,96},{96,128},{128,160},{160,192},{192,224},{224... | collective-permute-start | bytes 393224 | tf_op jit(solution)/shard_map/ppermute | solution.py:346

commit v11 on v10

--- a/solution.py
+++ b/solution.py
@@ -351,14 +351,18 @@
     return lax.ppermute(values, "z", [((i + 1) % count, i) for i in range(count)])
 
 
+def send(way, values):
+    return up(values) if way == "up" else down(values)
+
+
 def ring_gather(own):
     chunks = {(0, 0): own[0], (0, 1): own[1]}
     for step in range(1, 4):
         for layer in range(2):
-            chunks[8 - step, layer] = up(chunks[(9 - step) % 8, layer])
-            chunks[step, layer] = down(chunks[step - 1, layer])
-    chunks[4, 0] = up(chunks[5, 0])
-    chunks[4, 1] = down(chunks[3, 1])
+            chunks[8 - step, layer] = send("up", chunks[(9 - step) % 8, layer])
+            chunks[step, layer] = send("down", chunks[step - 1, layer])
+    chunks[4, 0] = send("up", chunks[5, 0])
+    chunks[4, 1] = send("down", chunks[3, 1])
     return [chunks[step, layer] for step in range(8) for layer in range(2)]
 
 
@@ -369,11 +373,11 @@
     for step in range(1, 5):
         for half in range(2):
             if step <= top[half]:
-                rise[half] = up(rise[half])
+                rise[half] = send("up", rise[half])
                 if step < top[half]:
                     rise[half] = rise[half] + partial[2 * (top[half] - step) + half]
             if step <= bottom[half]:
-                fall[half] = down(fall[half])
+                fall[half] = send("down", fall[half])
                 if step < bottom[half]:
                     fall[half] = fall[half] + partial[2 * (8 - bottom[half] + step) + half]
     return jnp.concatenate([partial[half] + rise[half] + fall[half] for half in range(2)])

time: 131 us -> 131 us (level)
  no operation moved by 1% of the time
where the time goes in v11:
time: 131 us
  starting transfers between devices  54.8 us (42%)
  blocking collectives  29.2 us (22%)
  waiting for transfers between devices  23.4 us (18%)
  Pallas kernels  20.9 us (16%)
    ppermute x14, starting transfers between devices, down(): lax.ppermute(values, 'z', [((i + 1) % count, i) for i in range(count)])  37.4 us
    all_to_all x1, blocking collectives, body(): lax.all_to_all(placed, SLAB, split_axis=0, concat_axis=0, tiled=True)  16 us
    all_to_all x1, blocking collectives, body(): lax.all_to_all(summed, FRAME, split_axis=0, concat_axis=0, tiled=True)  13.3 us
    all_to_all x1, starting transfers between devices, body(): lax.all_to_all(sent, SLAB, split_axis=0, concat_axis=0, tiled=True)  11.1 us
    ppermute x14, waiting for transfers between devices, up(): lax.ppermute(values, 'z', [(i, (i + 1) % count) for i in range(count)])  10.3 us
    pallas_call x1, Pallas kernels, gradient_call(): pl.pallas_call(gradient_kernel, out_shape=f32(32, 2, 8, CORE), in_specs=[...  7.2 us
    ppermute x1, waiting for transfers between devices, body(): lax.ppermute(jnp.concatenate([edge[:half], edge[half:]], axis=1), ('z', '...  6.71 us
    pallas_call x1, Pallas kernels, far_call(): pl.pallas_call(far_kernel, out_shape=[matrix] * 2 + [f32(CORE, CORE)] * 2...  5.03 us
  transfers between devices with their start and end apart: 31, of which 13 were waited for; matrix products, arithmetic and copies ran while one was open for 1% of the time, Pallas kernels for 5%

profile of v11, /device:TPU:1, one launch (start us, length us, event | category | flops | bytes accessed | tf_op | source)
XLA Modules:
  0.0 130.6 jit_solution(10473015525621876940)
XLA Ops:
  0.0 1.0 cut_rows.1
  1.0 2.5 %collective-permute-start.6 = (f32[8,4096]{1,0:T(8,128)S(1)}, f32[8,4096]{1,0:T(8,128)S(1)}, u32[]{:S(2)}, u32[]{:S(2)}) collective-permute-start(f32[8,4096]{1,0:T(8,128)S(1)} %get-tuple-element.35.refs_0_), channel_id=1, source_target_pairs={{0,32},{32,64},{64,96},{96,128},{128,160},{160,192},{192,224},{224... | collective-permute-start | bytes 393224 | tf_op jit(solution)/shard_map/ppermute | solution.py:346
  3.5 4.0 %collective-permute-start.1 = (f32[8,4096]{1,0:T(8,128)S(1)}, f32[8,4096]{1,0:T(8,128)S(1)}, u32[]{:S(2)}, u32[]{:S(2)}) collective-permute-start(f32[8,4096]{1,0:T(8,128)S(1)} %get-tuple-element.36.refs_1_), channel_id=1, source_target_pairs={{32,0},{64,32},{96,64},{128,96},{160,128},{192,160},{224,192},{0,2... | collective-permute-start | bytes 393224 | tf_op jit(solution)/shard_map/ppermute | solution.py:351
  7.6 1.4 %collective-permute-start = (f32[8,4096]{1,0:T(8,128)S(1)}, f32[8,4096]{1,0:T(8,128)S(1)}, u32[]{:S(2)}, u32[]{:S(2)}) collective-permute-start(f32[8,4096]{1,0:T(8,128)S(1)} %get-tuple-element.35.refs_0_), channel_id=1, source_target_pairs={{32,0},{64,32},{96,64},{128,96},{160,128},{192,160},{224,192},{0,2... | collective-permute-start | bytes 393224 | tf_op jit(solution)/shard_map/ppermute | solution.py:351
  8.9 0.1 collective-permute-start.11
  9.0 1.6 %collective-permute-done.6.refs_14_ = f32[8,4096]{1,0:T(8,128)S(1)} collective-permute-done((f32[8,4096]{1,0:T(8,128)S(1)}, f32[8,4096]{1,0:T(8,128)S(1)}, u32[]{:S(2)}, u32[]{:S(2)}) %collective-permute-start.6) | collective-permute-done | bytes 131104 | tf_op jit(solution)/shard_map/ppermute | solution.py:346
  10.7 2.7 %collective-permute-start.3 = (f32[8,4096]{1,0:T(8,128)S(1)}, f32[8,4096]{1,0:T(8,128)S(1)}, u32[]{:S(2)}, u32[]{:S(2)}) collective-permute-start(f32[8,4096]{1,0:T(8,128)S(1)} %collective-permute-done.1.refs_3_), channel_id=1, source_target_pairs={{32,0},{64,32},{96,64},{128,96},{160,128},{192,160},{224,192},{0,2... | collective-permute-start | bytes 393224 | tf_op jit(solution)/shard_map/ppermute | solution.py:351
  13.4 2.6 %collective-permute-start.2 = (f32[8,4096]{1,0:T(8,128)S(1)}, f32[8,4096]{1,0:T(8,128)S(1)}, u32[]{:S(2)}, u32[]{:S(2)}) collective-permute-start(f32[8,4096]{1,0:T(8,128)S(1)} %collective-permute-done.refs_2_), channel_id=1, source_target_pairs={{32,0},{64,32},{96,64},{128,96},{160,128},{192,160},{224,192},{0,2... | collective-permute-start | bytes 393224 | tf_op jit(solution)/shard_map/ppermute | solution.py:351
  16.0 1.2 collective-permute-done.7.refs_12_
  17.2 2.7 %collective-permute-start.5 = (f32[8,4096]{1,0:T(8,128)S(1)}, f32[8,4096]{1,0:T(8,128)S(1)}, u32[]{:S(2)}, u32[]{:S(2)}) collective-permute-start(f32[8,4096]{1,0:T(8,128)S(1)} %collective-permute-done.3.refs_5_), channel_id=1, source_target_pairs={{32,0},{64,32},{96,64},{128,96},{160,128},{192,160},{224,192},{0,2... | collective-permute-start | bytes 393224 | tf_op jit(solution)/shard_map/ppermute | solution.py:351
  19.8 2.5 %collective-permute-start.4 = (f32[8,4096]{1,0:T(8,128)S(1)}, f32[8,4096]{1,0:T(8,128)S(1)}, u32[]{:S(2)}, u32[]{:S(2)}) collective-permute-start(f32[8,4096]{1,0:T(8,128)S(1)} %collective-permute-done.2.refs_4_), channel_id=1, source_target_pairs={{32,0},{64,32},{96,64},{128,96},{160,128},{192,160},{224,192},{0,2... | collective-permute-start | bytes 393224 | tf_op jit(solution)/shard_map/ppermute | solution.py:351
  22.4 0.8 collective-permute-done.8.refs_10_
  23.2 2.7 %collective-permute-start.10 = (f32[8,4096]{1,0:T(8,128)S(1)}, f32[8,4096]{1,0:T(8,128)S(1)}, u32[]{:S(2)}, u32[]{:S(2)}) collective-permute-start(f32[8,4096]{1,0:T(8,128)S(1)} %collective-permute-done.5.refs_7_), channel_id=1, source_target_pairs={{32,0},{64,32},{96,64},{128,96},{160,128},{192,160},{224,192},{0,2... | collective-permute-start | bytes 393224 | tf_op jit(solution)/shard_map/ppermute | solution.py:351
  25.9 0.7 multiply_add_fusion.table
  26.6 0.8 collective-permute-done.13.refs_11_
  27.4 1.4 %collective-permute-done.9.refs_8_ = f32[8,4096]{1,0:T(8,128)S(1)} collective-permute-done((f32[8,4096]{1,0:T(8,128)S(1)}, f32[8,4096]{1,0:T(8,128)S(1)}, u32[]{:S(2)}, u32[]{:S(2)}) %collective-permute-start.9) | collective-permute-done | bytes 131104 | tf_op jit(solution)/shard_map/ppermute | solution.py:346
  28.8 2.3 %select_rows.1 = f32[32,2,8,256]{3,2,1,0:T(8,128)} custom-call(s32[8,2,32]{2,1,0:T(2,128)S(1)} %multiply_add_fusion.table, f32[8,4096]{1,0:T(8,128)S(1)} %get-tuple-element.35.refs_0_, f32[8,4096]{1,0:T(8,128)S(1)} %get-tuple-element.36.refs_1_, f32[8,4096]{1,0:T(8,128)S(1)} %collective-permute-done.refs_2_, f32[8,4096]{1,0:T(8,128)S(1)} %collective-permute-done.1.refs_3_, ...), custom_call_target="tpu_custom_call" | custom-call | bytes 3000000 | tf_op jit(solution)/shard_map/select_rows/pallas_call | solution.py:399
  31.1 11.1 %all-to-all-start = ((f32[32,2,8,256]{3,2,1,0:T(8,128)}), f32[32,2,8,256]{3,2,1,0:T(8,128)S(1)}, u32[]{:S(2)}, u32[]{:S(2)}) async-start(f32[32,2,8,256]{3,2,1,0:T(8,128)} %select_rows.1), calls=%async_computation | async-start | bytes 1048576 | tf_op jit(solution)/shard_map/all_to_all | solution.py:410
  42.2 0.1 slice_select_fusion
  42.4 0.1 pad_maximum_fusion.1
  42.5 1.3 collective-permute-start.14
  43.8 1.1 dft_base.1.base
  44.9 6.7 %collective-permute-done.14.mine = f32[192,128]{1,0:T(8,128)S(1)} collective-permute-done((f32[192,128]{1,0:T(8,128)S(1)}, f32[192,128]{1,0:T(8,128)S(1)}, u32[]{:S(2)}, u32[]{:S(2)}) %collective-permute-start.14) | collective-permute-done | bytes 98336 | tf_op jit(solution)/shard_map/ppermute | solution.py:416
  51.6 2.2 %all-to-all-done.received = f32[32,2,8,256]{3,2,1,0:T(8,128)S(1)} async-done(((f32[32,2,8,256]{3,2,1,0:T(8,128)}), f32[32,2,8,256]{3,2,1,0:T(8,128)S(1)}, u32[]{:S(2)}, u32[]{:S(2)}) %all-to-all-start) | async-done | bytes 524320 | tf_op jit(solution)/shard_map/all_to_all | solution.py:410
  53.8 5.0 %far_field.1 = (bf16[4,384,768]{2,1,0:T(8,128)(2,1)S(1)}, bf16[4,384,768]{2,1,0:T(8,128)(2,1)S(1)}, f32[256,256]{1,0:T(8,128)S(1)}, f32[256,256]{1,0:T(8,128)S(1...) custom-call(s32[8,2,32]{2,1,0:T(2,128)S(1)} %multiply_add_fusion.table, ...), custom_call_target="tpu_custom_call" | custom-call | flops 3000000000 | bytes 7000000 | tf_op jit(solution)/shard_map/far_field/pallas_call | solution.py:314
  58.9 2.2 %object_spectrum.1 = (f32[384,256]{1,0:T(8,128)S(1)}, f32[384,256]{1,0:T(8,128)S(1)}) custom-call(bf16[4,384,768]{2,1,0:T(8,128)(2,1)S(1)} %get-tuple-element.38.forward, bf16[4,384,768]{2,1,0:T(8,128)(2,1)S(1)} %get-tuple-element.39.inverse, f32[384,256]{1,0:T(8,128)S(1)} %copy-done, f32[192,128]{1,0:T(8,128)S(1)} %collective-permute-done.14.mine, ...), custom_call_target="tpu_custom_call" | custom-call | flops 1356000000 | bytes 7000000 | tf_op jit(solution)/shard_map/object_spectrum/pallas_call | solution.py:432
  61.0 7.2 %gradient.1 = f32[32,2,8,256]{3,2,1,0:T(8,128)S(1)} custom-call(s32[8,2,32]{2,1,0:T(2,128)S(1)} %multiply_add_fusion.table, f32[256,256]{1,0:T(8,128)S(1)} %copy-done.1, f32[1,256,256]{2,1,0:T(8,128)S(1)} %copy-done.2, bf16[4,384,768]{2,1,0:T(8,128)(2,1)S(1)} %get-tuple-element.38.forward, bf16[4,384,768]{2,1,0:T(8,128)(2,1)S(1)} %get-tuple-element.39.inverse, ...), custom_call_target="tpu_custom_call" | custom-call | flops 4332000256 | bytes 7000000 | tf_op jit(solution)/shard_map/gradient/pallas_call | solution.py:327
  68.2 16.0 %all_to_all.15.values = f32[32,2,8,256]{3,2,1,0:T(8,128)S(1)} all-to-all(f32[32,2,8,256]{3,2,1,0:T(8,128)S(1)} %gradient.1), channel_id=1, replica_groups=mesh['z'=8,'x'=4,'y'=4,'core'=2] {'x','y','core'}, dimensions={0} | all-to-all | bytes 1048576 | tf_op jit(solution)/shard_map/all_to_all | solution.py:444
  84.2 2.2 %scatter_rows.1 = (f32[4,2,8,512]{3,2,1,0:T(8,128)S(1)}, f32[4,2,8,512]{3,2,1,0:T(8,128)S(1)}, f32[4,2,8,512]{3,2,1,0:T(8,128)S(1)}, f32[4,2,8,512]{3,2,1,0:T(8,...) custom-call(s32[8,2,32]{2,1,0:T(2,128)S(1)} %multiply_add_fusion.tab, ...), custom_call_target="tpu_custom_call" | custom-call | bytes 3000000 | tf_op jit(solution)/shard_map/scatter_rows/pallas_call | solution.py:446
  86.4 3.1 %collective-permute-start.26 = (f32[4,2,8,512]{3,2,1,0:T(8,128)S(1)}, f32[4,2,8,512]{3,2,1,0:T(8,128)S(1)}, u32[]{:S(2)}, u32[]{:S(2)}) collective-permute-start(f32[4,2,8,512]{3,2,1,0:T(8,128)S(1)} %get-tuple-element.61), channel_id=1, source_target_pairs={{32,0},{64,32},{96,64},{128,96},{160,128},{192,160},{224,192},{0,2... | collective-permute-start | bytes 393224 | tf_op jit(solution)/shard_map/ppermute | solution.py:351
  89.5 0.6 collective-permute-start.23
  90.1 2.5 %collective-permute-done.26 = f32[4,2,8,512]{3,2,1,0:T(8,128)S(1)} collective-permute-done((f32[4,2,8,512]{3,2,1,0:T(8,128)S(1)}, f32[4,2,8,512]{3,2,1,0:T(8,128)S(1)}, u32[]{:S(2)}, u32[]{:S(2)}) %collective-permute-start.26) | collective-permute-done | bytes 131104 | tf_op jit(solution)/shard_map/ppermute | solution.py:351
  92.6 3.5 %collective-permute-start.27 = (f32[4,2,8,512]{3,2,1,0:T(8,128)S(1)}, f32[4,2,8,512]{3,2,1,0:T(8,128)S(1)}, u32[]{:S(2)}, u32[]{:S(2)}) collective-permute-start(f32[4,2,8,512]{3,2,1,0:T(8,128)S(1)} %add.56), channel_id=1, source_target_pairs={{32,0},{64,32},{96,64},{128,96},{160,128},{192,160},{224,192},{0,2... | collective-permute-start | bytes 393224 | tf_op jit(solution)/shard_map/ppermute | solution.py:351
  96.1 0.1 collective-permute-start.20
  96.2 1.5 %collective-permute-start.17 = (f32[4,2,8,512]{3,2,1,0:T(8,128)S(1)}, f32[4,2,8,512]{3,2,1,0:T(8,128)S(1)}, u32[]{:S(2)}, u32[]{:S(2)}) collective-permute-start(f32[4,2,8,512]{3,2,1,0:T(8,128)S(1)} %add.46), channel_id=1, source_target_pairs={{0,32},{32,64},{64,96},{96,128},{128,160},{160,192},{192,224},{224... | collective-permute-start | bytes 393224 | tf_op jit(solution)/shard_map/ppermute | solution.py:346
  97.7 0.9 collective-permute-done.23
  98.6 0.1 collective-permute-start.24
  98.7 3.2 %collective-permute-start.28 = (f32[4,2,8,512]{3,2,1,0:T(8,128)S(1)}, f32[4,2,8,512]{3,2,1,0:T(8,128)S(1)}, u32[]{:S(2)}, u32[]{:S(2)}) collective-permute-start(f32[4,2,8,512]{3,2,1,0:T(8,128)S(1)} %add.57), channel_id=1, source_target_pairs={{32,0},{64,32},{96,64},{128,96},{160,128},{192,160},{224,192},{0,2... | collective-permute-start | bytes 393224 | tf_op jit(solution)/shard_map/ppermute | solution.py:351
  101.9 2.8 %collective-permute-start.21 = (f32[4,2,8,512]{3,2,1,0:T(8,128)S(1)}, f32[4,2,8,512]{3,2,1,0:T(8,128)S(1)}, u32[]{:S(2)}, u32[]{:S(2)}) collective-permute-start(f32[4,2,8,512]{3,2,1,0:T(8,128)S(1)} %add.50), channel_id=1, source_target_pairs={{32,0},{64,32},{96,64},{128,96},{160,128},{192,160},{224,192},{0,2... | collective-permute-start | bytes 393224 | tf_op jit(solution)/shard_map/ppermute | solution.py:351
  104.8 0.2 collective-permute-done.24
  105.0 0.1 collective-permute-start.25
  105.1 2.7 %collective-permute-start.29 = (f32[4,2,8,512]{3,2,1,0:T(8,128)S(1)}, f32[4,2,8,512]{3,2,1,0:T(8,128)S(1)}, u32[]{:S(2)}, u32[]{:S(2)}) collective-permute-start(f32[4,2,8,512]{3,2,1,0:T(8,128)S(1)} %add.58), channel_id=1, source_target_pairs={{32,0},{64,32},{96,64},{128,96},{160,128},{192,160},{224,192},{0,2... | collective-permute-start | bytes 393224 | tf_op jit(solution)/shard_map/ppermute | solution.py:351
  107.9 3.5 %collective-permute-start.22 = (f32[4,2,8,512]{3,2,1,0:T(8,128)S(1)}, f32[4,2,8,512]{3,2,1,0:T(8,128)S(1)}, u32[]{:S(2)}, u32[]{:S(2)}) collective-permute-start(f32[4,2,8,512]{3,2,1,0:T(8,128)S(1)} %add.51), channel_id=1, source_target_pairs={{32,0},{64,32},{96,64},{128,96},{160,128},{192,160},{224,192},{0,2... | collective-permute-start | bytes 393224 | tf_op jit(solution)/shard_map/ppermute | solution.py:351
  111.5 0.6 collective-permute-done.25
  112.2 1.5 %collective-permute-done.22 = f32[4,2,8,512]{3,2,1,0:T(8,128)S(1)} collective-permute-done((f32[4,2,8,512]{3,2,1,0:T(8,128)S(1)}, f32[4,2,8,512]{3,2,1,0:T(8,128)S(1)}, u32[]{:S(2)}, u32[]{:S(2)}) %collective-permute-start.22) | collective-permute-done | bytes 131104 | tf_op jit(solution)/shard_map/ppermute | solution.py:351
  113.8 2.8 %collective-permute-done.19 = f32[4,2,8,512]{3,2,1,0:T(8,128)S(1)} collective-permute-done((f32[4,2,8,512]{3,2,1,0:T(8,128)S(1)}, f32[4,2,8,512]{3,2,1,0:T(8,128)S(1)}, u32[]{:S(2)}, u32[]{:S(2)}) %collective-permute-start.19) | collective-permute-done | bytes 131104 | tf_op jit(solution)/shard_map/ppermute | solution.py:346
  116.6 13.3 %all_to_all.16 = f32[8,2,8,512]{3,2,1,0:T(8,128)S(1)} all-to-all(f32[8,2,8,512]{3,2,1,0:T(8,128)S(1)} %pad_maximum_fusion), channel_id=1, replica_groups=mesh['z'=8,'x'=4,'y'=4,'core'=2] {'y','core'}, dimensions={0} | all-to-all | bytes 524288 | tf_op jit(solution)/shard_map/all_to_all | solution.py:457
  129.9 0.7 copy_bitcast_fusion
  (47 shorter events, 0.6 us)
Async XLA Ops:
  1.0 41.2 %copy-start = (f32[384,256]{1,0:T(8,128)S(1)}, f32[384,256]{1,0:T(8,128)}, u32[]{:S(2)}) copy-start(f32[384,256]{1,0:T(8,128)} %strip) | copy-start | bytes 1179652
  1.0 9.7 %collective-permute-start.6 = (f32[8,4096]{1,0:T(8,128)S(1)}, f32[8,4096]{1,0:T(8,128)S(1)}, u32[]{:S(2)}, u32[]{:S(2)}) collective-permute-start(f32[8,4096]{1,0:T(8,128)S(1)} %get-tuple-element.35.refs_0_), channel_id=1, source_target_pairs={{0,32},{32,64},{64,96},{96,128},{128,160},{160,192},{192,224},{224... | collective-permute-start | bytes 393224 | tf_op jit(solution)/shard_map/ppermute | solution.py:346
  3.5 7.1 %collective-permute-start.1 = (f32[8,4096]{1,0:T(8,128)S(1)}, f32[8,4096]{1,0:T(8,128)S(1)}, u32[]{:S(2)}, u32[]{:S(2)}) collective-permute-start(f32[8,4096]{1,0:T(8,128)S(1)} %get-tuple-element.36.refs_1_), channel_id=1, source_target_pairs={{32,0},{64,32},{96,64},{128,96},{160,128},{192,160},{224,192},{0,2... | collective-permute-start | bytes 393224 | tf_op jit(solution)/shard_map/ppermute | solution.py:351
  7.6 5.8 %collective-permute-start = (f32[8,4096]{1,0:T(8,128)S(1)}, f32[8,4096]{1,0:T(8,128)S(1)}, u32[]{:S(2)}, u32[]{:S(2)}) collective-permute-start(f32[8,4096]{1,0:T(8,128)S(1)} %get-tuple-element.35.refs_0_), channel_id=1, source_target_pairs={{32,0},{64,32},{96,64},{128,96},{160,128},{192,160},{224,192},{0,2... | collective-permute-start | bytes 393224 | tf_op jit(solution)/shard_map/ppermute | solution.py:351
  8.9 7.0 %collective-permute-start.11 = (f32[8,4096]{1,0:T(8,128)S(1)}, f32[8,4096]{1,0:T(8,128)S(1)}, u32[]{:S(2)}, u32[]{:S(2)}) collective-permute-start(f32[8,4096]{1,0:T(8,128)S(1)} %get-tuple-element.36.refs_1_), channel_id=1, source_target_pairs={{0,32},{32,64},{64,96},{96,128},{128,160},{160,192},{192,224},{224... | collective-permute-start | bytes 393224 | tf_op jit(solution)/shard_map/ppermute | solution.py:346
  10.7 6.5 %collective-permute-start.7 = (f32[8,4096]{1,0:T(8,128)S(1)}, f32[8,4096]{1,0:T(8,128)S(1)}, u32[]{:S(2)}, u32[]{:S(2)}) collective-permute-start(f32[8,4096]{1,0:T(8,128)S(1)} %collective-permute-done.6.refs_14_), channel_id=1, source_target_pairs={{0,32},{32,64},{64,96},{96,128},{128,160},{160,192},{192,224},{224... | collective-permute-start | bytes 393224 | tf_op jit(solution)/shard_map/ppermute | solution.py:346
  10.7 6.5 %collective-permute-start.3 = (f32[8,4096]{1,0:T(8,128)S(1)}, f32[8,4096]{1,0:T(8,128)S(1)}, u32[]{:S(2)}, u32[]{:S(2)}) collective-permute-start(f32[8,4096]{1,0:T(8,128)S(1)} %collective-permute-done.1.refs_3_), channel_id=1, source_target_pairs={{32,0},{64,32},{96,64},{128,96},{160,128},{192,160},{224,192},{0,2... | collective-permute-start | bytes 393224 | tf_op jit(solution)/shard_map/ppermute | solution.py:351
  13.4 6.5 %collective-permute-start.2 = (f32[8,4096]{1,0:T(8,128)S(1)}, f32[8,4096]{1,0:T(8,128)S(1)}, u32[]{:S(2)}, u32[]{:S(2)}) collective-permute-start(f32[8,4096]{1,0:T(8,128)S(1)} %collective-permute-done.refs_2_), channel_id=1, source_target_pairs={{32,0},{64,32},{96,64},{128,96},{160,128},{192,160},{224,192},{0,2... | collective-permute-start | bytes 393224 | tf_op jit(solution)/shard_map/ppermute | solution.py:351
  16.0 6.4 %collective-permute-start.12 = (f32[8,4096]{1,0:T(8,128)S(1)}, f32[8,4096]{1,0:T(8,128)S(1)}, u32[]{:S(2)}, u32[]{:S(2)}) collective-permute-start(f32[8,4096]{1,0:T(8,128)S(1)} %collective-permute-done.11.refs_15_), channel_id=1, source_target_pairs={{0,32},{32,64},{64,96},{96,128},{128,160},{160,192},{192,224},{224... | collective-permute-start | bytes 393224 | tf_op jit(solution)/shard_map/ppermute | solution.py:346
  17.2 6.0 %collective-permute-start.8 = (f32[8,4096]{1,0:T(8,128)S(1)}, f32[8,4096]{1,0:T(8,128)S(1)}, u32[]{:S(2)}, u32[]{:S(2)}) collective-permute-start(f32[8,4096]{1,0:T(8,128)S(1)} %collective-permute-done.7.refs_12_), channel_id=1, source_target_pairs={{0,32},{32,64},{64,96},{96,128},{128,160},{160,192},{192,224},{224... | collective-permute-start | bytes 393224 | tf_op jit(solution)/shard_map/ppermute | solution.py:346
  17.2 6.0 %collective-permute-start.5 = (f32[8,4096]{1,0:T(8,128)S(1)}, f32[8,4096]{1,0:T(8,128)S(1)}, u32[]{:S(2)}, u32[]{:S(2)}) collective-permute-start(f32[8,4096]{1,0:T(8,128)S(1)} %collective-permute-done.3.refs_5_), channel_id=1, source_target_pairs={{32,0},{64,32},{96,64},{128,96},{160,128},{192,160},{224,192},{0,2... | collective-permute-start | bytes 393224 | tf_op jit(solution)/shard_map/ppermute | solution.py:351
  19.8 6.8 %collective-permute-start.4 = (f32[8,4096]{1,0:T(8,128)S(1)}, f32[8,4096]{1,0:T(8,128)S(1)}, u32[]{:S(2)}, u32[]{:S(2)}) collective-permute-start(f32[8,4096]{1,0:T(8,128)S(1)} %collective-permute-done.2.refs_4_), channel_id=1, source_target_pairs={{32,0},{64,32},{96,64},{128,96},{160,128},{192,160},{224,192},{0,2... | collective-permute-start | bytes 393224 | tf_op jit(solution)/shard_map/ppermute | solution.py:351
  22.4 5.0 %collective-permute-start.13 = (f32[8,4096]{1,0:T(8,128)S(1)}, f32[8,4096]{1,0:T(8,128)S(1)}, u32[]{:S(2)}, u32[]{:S(2)}) collective-permute-start(f32[8,4096]{1,0:T(8,128)S(1)} %collective-permute-done.12.refs_13_), channel_id=1, source_target_pairs={{0,32},{32,64},{64,96},{96,128},{128,160},{160,192},{192,224},{224... | collective-permute-start | bytes 393224 | tf_op jit(solution)/shard_map/ppermute | solution.py:346
  23.2 5.6 %collective-permute-start.9 = (f32[8,4096]{1,0:T(8,128)S(1)}, f32[8,4096]{1,0:T(8,128)S(1)}, u32[]{:S(2)}, u32[]{:S(2)}) collective-permute-start(f32[8,4096]{1,0:T(8,128)S(1)} %collective-permute-done.8.refs_10_), channel_id=1, source_target_pairs={{0,32},{32,64},{64,96},{96,128},{128,160},{160,192},{192,224},{224... | collective-permute-start | bytes 393224 | tf_op jit(solution)/shard_map/ppermute | solution.py:346
  23.2 5.6 %collective-permute-start.10 = (f32[8,4096]{1,0:T(8,128)S(1)}, f32[8,4096]{1,0:T(8,128)S(1)}, u32[]{:S(2)}, u32[]{:S(2)}) collective-permute-start(f32[8,4096]{1,0:T(8,128)S(1)} %collective-permute-done.5.refs_7_), channel_id=1, source_target_pairs={{32,0},{64,32},{96,64},{128,96},{160,128},{192,160},{224,192},{0,2... | collective-permute-start | bytes 393224 | tf_op jit(solution)/shard_map/ppermute | solution.py:351
  31.1 22.7 %copy-start.1 = (f32[256,256]{1,0:T(8,128)S(1)}, f32[256,256]{1,0:T(8,128)}, u32[]{:S(2)}) copy-start(f32[256,256]{1,0:T(8,128)} %amp_ref.3) | copy-start | bytes 786436
  31.1 22.7 %all-to-all-start = ((f32[32,2,8,256]{3,2,1,0:T(8,128)}), f32[32,2,8,256]{3,2,1,0:T(8,128)S(1)}, u32[]{:S(2)}, u32[]{:S(2)}) async-start(f32[32,2,8,256]{3,2,1,0:T(8,128)} %select_rows.1), calls=%async_computation | async-start | bytes 1048576 | tf_op jit(solution)/shard_map/all_to_all | solution.py:410
  42.5 9.1 %collective-permute-start.14 = (f32[192,128]{1,0:T(8,128)S(1)}, f32[192,128]{1,0:T(8,128)S(1)}, u32[]{:S(2)}, u32[]{:S(2)}) collective-permute-start(f32[192,128]{1,0:T(8,128)S(1)} %pad_maximum_fusion.1), channel_id=1, source_target_pairs={{0,8},{8,16},{16,24},{24,32},{32,40},{40,48},{48,56},{56,64},{64,7... | collective-permute-start | bytes 294920 | tf_op jit(solution)/shard_map/ppermute | solution.py:416
  51.6 7.3 %collective-permute-start.15 = (f32[192,128]{1,0:T(8,128)S(1)}, f32[192,128]{1,0:T(8,128)S(1)}, u32[]{:S(2)}, u32[]{:S(2)}) collective-permute-start(f32[192,128]{1,0:T(8,128)S(1)} %collective-permute-done.14.mine), channel_id=1, source_target_pairs={{0,1},{1,0},{2,3},{3,2},{4,5},{5,4},{6,7},{7,6},{8,9},{9,8},{10,11... | collective-permute-start | bytes 294920 | tf_op jit(solution)/shard_map/ppermute | solution.py:422
  58.8 2.2 %copy-start.2 = (f32[1,256,256]{2,1,0:T(8,128)S(1)}, f32[1,256,256]{2,1,0:T(8,128)}, u32[]{:S(2)}) copy-start(f32[1,256,256]{2,1,0:T(8,128)} %observed.1) | copy-start | bytes 786436
  86.4 6.2 %collective-permute-start.26 = (f32[4,2,8,512]{3,2,1,0:T(8,128)S(1)}, f32[4,2,8,512]{3,2,1,0:T(8,128)S(1)}, u32[]{:S(2)}, u32[]{:S(2)}) collective-permute-start(f32[4,2,8,512]{3,2,1,0:T(8,128)S(1)} %get-tuple-element.61), channel_id=1, source_target_pairs={{32,0},{64,32},{96,64},{128,96},{160,128},{192,160},{224,192},{0,2... | collective-permute-start | bytes 393224 | tf_op jit(solution)/shard_map/ppermute | solution.py:351
  89.5 6.7 %collective-permute-start.16 = (f32[4,2,8,512]{3,2,1,0:T(8,128)S(1)}, f32[4,2,8,512]{3,2,1,0:T(8,128)S(1)}, u32[]{:S(2)}, u32[]{:S(2)}) collective-permute-start(f32[4,2,8,512]{3,2,1,0:T(8,128)S(1)} %get-tuple-element.50), channel_id=1, source_target_pairs={{0,32},{32,64},{64,96},{96,128},{128,160},{160,192},{192,224},{224... | collective-permute-start | bytes 393224 | tf_op jit(solution)/shard_map/ppermute | solution.py:346
  89.5 9.1 %collective-permute-start.23 = (f32[4,2,8,512]{3,2,1,0:T(8,128)S(1)}, f32[4,2,8,512]{3,2,1,0:T(8,128)S(1)}, u32[]{:S(2)}, u32[]{:S(2)}) collective-permute-start(f32[4,2,8,512]{3,2,1,0:T(8,128)S(1)} %get-tuple-element.58), channel_id=1, source_target_pairs={{0,32},{32,64},{64,96},{96,128},{128,160},{160,192},{192,224},{224... | collective-permute-start | bytes 393224 | tf_op jit(solution)/shard_map/ppermute | solution.py:346
  92.6 6.0 %collective-permute-start.27 = (f32[4,2,8,512]{3,2,1,0:T(8,128)S(1)}, f32[4,2,8,512]{3,2,1,0:T(8,128)S(1)}, u32[]{:S(2)}, u32[]{:S(2)}) collective-permute-start(f32[4,2,8,512]{3,2,1,0:T(8,128)S(1)} %add.56), channel_id=1, source_target_pairs={{32,0},{64,32},{96,64},{128,96},{160,128},{192,160},{224,192},{0,2... | collective-permute-start | bytes 393224 | tf_op jit(solution)/shard_map/ppermute | solution.py:351
  96.1 5.8 %collective-permute-start.20 = (f32[4,2,8,512]{3,2,1,0:T(8,128)S(1)}, f32[4,2,8,512]{3,2,1,0:T(8,128)S(1)}, u32[]{:S(2)}, u32[]{:S(2)}) collective-permute-start(f32[4,2,8,512]{3,2,1,0:T(8,128)S(1)} %get-tuple-element.54), channel_id=1, source_target_pairs={{32,0},{64,32},{96,64},{128,96},{160,128},{192,160},{224,192},{0,2... | collective-permute-start | bytes 393224 | tf_op jit(solution)/shard_map/ppermute | solution.py:351
  96.2 8.5 %collective-permute-start.17 = (f32[4,2,8,512]{3,2,1,0:T(8,128)S(1)}, f32[4,2,8,512]{3,2,1,0:T(8,128)S(1)}, u32[]{:S(2)}, u32[]{:S(2)}) collective-permute-start(f32[4,2,8,512]{3,2,1,0:T(8,128)S(1)} %add.46), channel_id=1, source_target_pairs={{0,32},{32,64},{64,96},{96,128},{128,160},{160,192},{192,224},{224... | collective-permute-start | bytes 393224 | tf_op jit(solution)/shard_map/ppermute | solution.py:346
  98.6 6.4 %collective-permute-start.24 = (f32[4,2,8,512]{3,2,1,0:T(8,128)S(1)}, f32[4,2,8,512]{3,2,1,0:T(8,128)S(1)}, u32[]{:S(2)}, u32[]{:S(2)}) collective-permute-start(f32[4,2,8,512]{3,2,1,0:T(8,128)S(1)} %add.53), channel_id=1, source_target_pairs={{0,32},{32,64},{64,96},{96,128},{128,160},{160,192},{192,224},{224... | collective-permute-start | bytes 393224 | tf_op jit(solution)/shard_map/ppermute | solution.py:346
  98.7 6.4 %collective-permute-start.28 = (f32[4,2,8,512]{3,2,1,0:T(8,128)S(1)}, f32[4,2,8,512]{3,2,1,0:T(8,128)S(1)}, u32[]{:S(2)}, u32[]{:S(2)}) collective-permute-start(f32[4,2,8,512]{3,2,1,0:T(8,128)S(1)} %add.57), channel_id=1, source_target_pairs={{32,0},{64,32},{96,64},{128,96},{160,128},{192,160},{224,192},{0,2... | collective-permute-start | bytes 393224 | tf_op jit(solution)/shard_map/ppermute | solution.py:351
  101.9 6.0 %collective-permute-start.21 = (f32[4,2,8,512]{3,2,1,0:T(8,128)S(1)}, f32[4,2,8,512]{3,2,1,0:T(8,128)S(1)}, u32[]{:S(2)}, u32[]{:S(2)}) collective-permute-start(f32[4,2,8,512]{3,2,1,0:T(8,128)S(1)} %add.50), channel_id=1, source_target_pairs={{32,0},{64,32},{96,64},{128,96},{160,128},{192,160},{224,192},{0,2... | collective-permute-start | bytes 393224 | tf_op jit(solution)/shard_map/ppermute | solution.py:351
  104.7 6.7 %collective-permute-start.18 = (f32[4,2,8,512]{3,2,1,0:T(8,128)S(1)}, f32[4,2,8,512]{3,2,1,0:T(8,128)S(1)}, u32[]{:S(2)}, u32[]{:S(2)}) collective-permute-start(f32[4,2,8,512]{3,2,1,0:T(8,128)S(1)} %add.47), channel_id=1, source_target_pairs={{0,32},{32,64},{64,96},{96,128},{128,160},{160,192},{192,224},{224... | collective-permute-start | bytes 393224 | tf_op jit(solution)/shard_map/ppermute | solution.py:346
  105.0 7.2 %collective-permute-start.25 = (f32[4,2,8,512]{3,2,1,0:T(8,128)S(1)}, f32[4,2,8,512]{3,2,1,0:T(8,128)S(1)}, u32[]{:S(2)}, u32[]{:S(2)}) collective-permute-start(f32[4,2,8,512]{3,2,1,0:T(8,128)S(1)} %add.54), channel_id=1, source_target_pairs={{0,32},{32,64},{64,96},{96,128},{128,160},{160,192},{192,224},{224... | collective-permute-start | bytes 393224 | tf_op jit(solution)/shard_map/ppermute | solution.py:346
  105.1 7.0 %collective-permute-start.29 = (f32[4,2,8,512]{3,2,1,0:T(8,128)S(1)}, f32[4,2,8,512]{3,2,1,0:T(8,128)S(1)}, u32[]{:S(2)}, u32[]{:S(2)}) collective-permute-start(f32[4,2,8,512]{3,2,1,0:T(8,128)S(1)} %add.58), channel_id=1, source_target_pairs={{32,0},{64,32},{96,64},{128,96},{160,128},{192,160},{224,192},{0,2... | collective-permute-start | bytes 393224 | tf_op jit(solution)/shard_map/ppermute | solution.py:351
  107.9 5.8 %collective-permute-start.22 = (f32[4,2,8,512]{3,2,1,0:T(8,128)S(1)}, f32[4,2,8,512]{3,2,1,0:T(8,128)S(1)}, u32[]{:S(2)}, u32[]{:S(2)}) collective-permute-start(f32[4,2,8,512]{3,2,1,0:T(8,128)S(1)} %add.51), channel_id=1, source_target_pairs={{32,0},{64,32},{96,64},{128,96},{160,128},{192,160},{224,192},{0,2... | collective-permute-start | bytes 393224 | tf_op jit(solution)/shard_map/ppermute | solution.py:351
  111.4 5.1 %collective-permute-start.19 = (f32[4,2,8,512]{3,2,1,0:T(8,128)S(1)}, f32[4,2,8,512]{3,2,1,0:T(8,128)S(1)}, u32[]{:S(2)}, u32[]{:S(2)}) collective-permute-start(f32[4,2,8,512]{3,2,1,0:T(8,128)S(1)} %add.48), channel_id=1, source_target_pairs={{0,32},{32,64},{64,96},{96,128},{128,160},{160,192},{192,224},{224... | collective-permute-start | bytes 393224 | tf_op jit(solution)/shard_map/ppermute | solution.py:346
